TPU v7x, 32 devices: a whole 2x2x4 slice. The times are simulated.
32 devices in a mesh: parts: 4 (over x, core), ctx: 2 (over y), fsdp: 4 (over z).
Axes of the slice: x: 2, y: 2, z: 4, core: 2. Of those that a mesh axis runs over, the one named last changes fastest.
Arguments:
- decoder_in: bfloat16 [16, 2048, 768], P(('parts', 'fsdp'), 'ctx'), may hold values from -10 to 10
- encoder_out: bfloat16 [16, 2048, 768], P(('parts', 'fsdp'), 'ctx'), may hold values from -6 to 6
- segment_ids: int32 [16, 2048], P(('parts', 'fsdp')), may hold values from 0 to 1, never falling along the last dimension, each value on 1 to 1365 neighbouring positions
- block_order: int32 [16, 4], P(('parts', 'fsdp')), may hold values from 0 to 3, each once within a row
- prompt_len: int32 [16], P(('parts', 'fsdp')), may hold values from 512 to 2048
- self_query: bfloat16 [768, 768], P('fsdp'), may hold values from -0.21875 to 0.21875
- self_key: bfloat16 [768, 768], P('fsdp'), may hold values from -0.21875 to 0.21875
- self_value: bfloat16 [768, 768], P('fsdp'), may hold values from -0.21875 to 0.21875
- self_output: bfloat16 [768, 768], P('fsdp'), may hold values from -3.5 to 3.5
- cross_query: bfloat16 [768, 768], P('fsdp'), may hold values from -0.21875 to 0.21875
- cross_key: bfloat16 [768, 768], P('fsdp'), may hold values from -0.21875 to 0.21875
- cross_value: bfloat16 [768, 768], P('fsdp'), may hold values from -0.21875 to 0.21875
- cross_output: bfloat16 [768, 768], P('fsdp'), may hold values from -6 to 6
- gate_in: bfloat16 [768, 2048], P('fsdp'), may hold values from -0.21875 to 0.21875
- up_in: bfloat16 [768, 2048], P('fsdp'), may hold values from -0.21875 to 0.21875
- down_out: bfloat16 [2048, 768], P('fsdp'), may hold values from -0.125 to 0.125
- norm_self: bfloat16 [768], P('fsdp'), may hold values from 0.5 to 1.5
- norm_cross: bfloat16 [768], P('fsdp'), may hold values from 0.5 to 1.5
- norm_mlp: bfloat16 [768], P('fsdp'), may hold values from 0.5 to 1.5
- cotangent: bfloat16 [16, 2048, 768], P(('parts', 'fsdp'), 'ctx'), may hold values from -6 to 6
Outputs:
- layer_out: bfloat16 [16, 2048, 768], P(('parts', 'fsdp'), 'ctx')
- decoder_grad: float32 [16, 2048, 768], P(('parts', 'fsdp'), 'ctx')
- encoder_grad: float32 [16, 2048, 768], P(('parts', 'fsdp'), 'ctx')
- self_query_grad: float32 [768, 768], P('fsdp')
- self_key_grad: float32 [768, 768], P('fsdp')
- self_value_grad: float32 [768, 768], P('fsdp')
- self_output_grad: float32 [768, 768], P('fsdp')
- cross_query_grad: float32 [768, 768], P('fsdp')
- cross_key_grad: float32 [768, 768], P('fsdp')
- cross_value_grad: float32 [768, 768], P('fsdp')
- cross_output_grad: float32 [768, 768], P('fsdp')
- gate_in_grad: float32 [768, 2048], P('fsdp')
- up_in_grad: float32 [768, 2048], P('fsdp')
- down_out_grad: float32 [2048, 768], P('fsdp')
- norm_self_grad: float32 [768], P('fsdp')
- norm_cross_grad: float32 [768], P('fsdp')
- norm_mlp_grad: float32 [768], P('fsdp')
- rms_values: float32 [4], replicated
All inputs are finite; a program needn't handle non-finite values.
Results may differ from a plain program's by a relative error of at most 0.04.
Values may be sent and summed in bfloat16 or wider, within the bound.
No kernel may reach another device: no remote copies, remote signals or barrier semaphores. Data moves between devices by JAX's collectives and lax.ppermute only.
A program may use at most 320 MiB of HBM per device.

v0:
```python
import math

import jax
import jax.numpy as jnp
from jax import lax
from jax.sharding import PartitionSpec as P

HEADS = 12


SCALE = 0.125
NEG = -1e30
EPS = 1e-06


def normed(value, gain):
    return value * lax.rsqrt(jnp.mean(value * value, axis=-1, keepdims=True) + EPS) * gain


def gated(gate, upward):
    return jax.nn.gelu(gate, approximate=True) * upward


def forward_dot(left, right):
    return jnp.dot(left, right, preferred_element_type=jnp.float32)


def outer(left, right):
    return lax.dot_general(
        left, right, (((0,), (0,)), ((), ())), preferred_element_type=jnp.float32
    )


def back_dot(left, right):
    return lax.dot_general(
        left, right, (((1,), (1,)), ((), ())), preferred_element_type=jnp.float32
    )


def key_split(matrix, block):
    return matrix.reshape(matrix.shape[0] // block, block, HEADS, matrix.shape[1] // HEADS)


def block_scores(q_heads, key_block, allowed):
    scores = (
        jnp.einsum("qhd,khd->hqk", q_heads, key_block, preferred_element_type=jnp.float32) * SCALE
    )
    return jnp.where(allowed[None], scores, NEG)


def attention_forward(query, keys, values, allow_fn):
    rows = query.shape[0]
    total = keys.shape[0]
    block = math.gcd(1024, total)
    q_heads = query.reshape(rows, HEADS, query.shape[1] // HEADS)
    key_blocks = key_split(keys, block)
    value_blocks = key_split(values, block)
    starts = jnp.arange(total // block, dtype=jnp.int32) * block

    def attention_step(carry, items):
        top, total_exp, acc = carry
        key_block, value_block, start = items
        allowed = allow_fn(start, block)
        scores = block_scores(q_heads, key_block, allowed)
        new_top = jnp.maximum(top, scores.max(-1))
        factor = jnp.exp(top - new_top)
        weights = jnp.where(allowed[None], jnp.exp(scores - new_top[..., None]), 0.0)
        total_exp = total_exp * factor + weights.sum(-1)
        update = jnp.einsum(
            "hqk,khd->qhd",
            weights.astype(jnp.bfloat16),
            value_block,
            preferred_element_type=jnp.float32,
        )
        acc = acc * factor.T[:, :, None] + update
        return ((new_top, total_exp, acc), None)

    init = (
        jnp.full((HEADS, rows), NEG, jnp.float32),
        jnp.zeros((HEADS, rows), jnp.float32),
        jnp.zeros(q_heads.shape, jnp.float32),
    )
    (top, total_exp, acc), _ = lax.scan(attention_step, init, (key_blocks, value_blocks, starts))
    wide = (acc / total_exp.T[:, :, None]).reshape(rows, -1)
    logsum = top + jnp.log(total_exp)
    return (wide, logsum)


def row_delta(grad_mixed, wide):
    rows = wide.shape[0]
    product = grad_mixed.astype(jnp.float32) * wide
    return product.reshape(rows, HEADS, -1).sum(-1).T


def attention_backward(query, keys, values, grad_mixed, logsum, delta, allow_fn, want_keys):
    rows = query.shape[0]
    total = keys.shape[0]
    block = math.gcd(1024, total)
    q_heads = query.reshape(rows, HEADS, query.shape[1] // HEADS)
    g_heads = grad_mixed.reshape(rows, HEADS, grad_mixed.shape[1] // HEADS)
    key_blocks = key_split(keys, block)
    value_blocks = key_split(values, block)
    starts = jnp.arange(total // block, dtype=jnp.int32) * block

    def grad_step(acc, items):
        key_block, value_block, start = items
        allowed = allow_fn(start, block)
        probs = jnp.where(
            allowed[None],
            jnp.exp(block_scores(q_heads, key_block, allowed) - logsum[..., None]),
            0.0,
        )
        dprobs = jnp.einsum(
            "qhd,khd->hqk", g_heads, value_block, preferred_element_type=jnp.float32
        )
        dscores = (probs * (dprobs - delta[..., None])).astype(jnp.bfloat16)
        acc = (
            acc
            + jnp.einsum("hqk,khd->qhd", dscores, key_block, preferred_element_type=jnp.float32)
            * SCALE
        )
        if want_keys:
            key_grad = (
                jnp.einsum("hqk,qhd->khd", dscores, q_heads, preferred_element_type=jnp.float32)
                * SCALE
            )
            value_grad = jnp.einsum(
                "hqk,qhd->khd",
                probs.astype(jnp.bfloat16),
                g_heads,
                preferred_element_type=jnp.float32,
            )
            return (acc, (key_grad, value_grad))
        return (acc, None)

    query_grad, extra = lax.scan(
        grad_step, jnp.zeros(q_heads.shape, jnp.float32), (key_blocks, value_blocks, starts)
    )
    if want_keys:
        return (
            query_grad.reshape(rows, -1),
            extra[0].reshape(total, -1),
            extra[1].reshape(total, -1),
        )
    return (query_grad.reshape(rows, -1), None, None)


def key_side(own_keys, own_values, all_query, all_grad, all_lse, all_delta, allow_fn):
    total = all_query.shape[0]
    block = math.gcd(1024, total)
    key_rows = own_keys.shape[0]
    k_heads = own_keys.reshape(key_rows, HEADS, -1)
    v_heads = own_values.reshape(key_rows, HEADS, -1)
    q_blocks = key_split(all_query, block)
    g_blocks = key_split(all_grad, block)
    lse_blocks = all_lse.reshape(total // block, block, HEADS)
    delta_blocks = all_delta.reshape(total // block, block, HEADS)
    starts = jnp.arange(total // block, dtype=jnp.int32) * block

    def key_step(carry, items):
        key_acc, value_acc = carry
        q_block, g_block, lse_block, delta_block, start = items
        allowed = allow_fn(start, block)
        scores = block_scores(q_block, k_heads, allowed)
        probs = jnp.where(allowed[None], jnp.exp(scores - lse_block.T[..., None]), 0.0)
        dprobs = jnp.einsum("qhd,khd->hqk", g_block, v_heads, preferred_element_type=jnp.float32)
        dscores = (probs * (dprobs - delta_block.T[..., None])).astype(jnp.bfloat16)
        key_acc = (
            key_acc
            + jnp.einsum("hqk,qhd->khd", dscores, q_block, preferred_element_type=jnp.float32)
            * SCALE
        )
        value_acc = value_acc + jnp.einsum(
            "hqk,qhd->khd", probs.astype(jnp.bfloat16), g_block, preferred_element_type=jnp.float32
        )
        return ((key_acc, value_acc), None)

    init = (jnp.zeros(k_heads.shape, jnp.float32), jnp.zeros(v_heads.shape, jnp.float32))
    (key_acc, value_acc), _ = lax.scan(
        key_step, init, (q_blocks, g_blocks, lse_blocks, delta_blocks, starts)
    )
    return (key_acc.reshape(key_rows, -1), value_acc.reshape(key_rows, -1))


def local(
    decoder_in,
    encoder_out,
    segment_ids,
    block_order,
    prompt_len,
    self_query,
    self_key,
    self_value,
    self_output,
    cross_query,
    cross_key,
    cross_value,
    cross_output,
    gate_in,
    up_in,
    down_out,
    norm_self,
    norm_cross,
    norm_mlp,
    cotangent,
):
    full = (
        lax.all_gather(self_query, "fsdp", axis=0, tiled=True),
        lax.all_gather(self_key, "fsdp", axis=0, tiled=True),
        lax.all_gather(self_value, "fsdp", axis=0, tiled=True),
        lax.all_gather(self_output, "fsdp", axis=0, tiled=True),
        lax.all_gather(cross_query, "fsdp", axis=0, tiled=True),
        lax.all_gather(cross_key, "fsdp", axis=0, tiled=True),
        lax.all_gather(cross_value, "fsdp", axis=0, tiled=True),
        lax.all_gather(cross_output, "fsdp", axis=0, tiled=True),
        lax.all_gather(gate_in, "fsdp", axis=0, tiled=True),
        lax.all_gather(up_in, "fsdp", axis=0, tiled=True),
        lax.all_gather(down_out, "fsdp", axis=0, tiled=True),
        lax.all_gather(norm_self, "fsdp", axis=0, tiled=True),
        lax.all_gather(norm_cross, "fsdp", axis=0, tiled=True),
        lax.all_gather(norm_mlp, "fsdp", axis=0, tiled=True),
    )
    (
        w_query,
        w_key,
        w_value,
        w_out,
        c_query,
        c_key,
        c_value,
        c_out,
        w_gate,
        w_up,
        w_down,
        g_self,
        g_cross,
        g_mlp,
    ) = full
    gain_self = g_self.astype(jnp.float32)
    gain_cross = g_cross.astype(jnp.float32)
    gain_mlp = g_mlp.astype(jnp.float32)
    place = lax.axis_index("ctx")
    local_rows = decoder_in.shape[1]
    half = local_rows // 2
    order = block_order[0]
    segs = segment_ids[0]
    offsets = jnp.arange(half, dtype=jnp.int32)
    own_blocks = lax.dynamic_slice_in_dim(order, 2 * place, 2)
    own_pos = (own_blocks[:, None] * half + offsets[None, :]).reshape(-1)
    all_pos = (order[:, None] * half + offsets[None, :]).reshape(-1)
    own_seg = jnp.take(segs, own_pos)
    all_seg = jnp.take(segs, all_pos)
    inputs = decoder_in[0].astype(jnp.float32)
    encoder = encoder_out[0]
    n_self = normed(inputs, gain_self).astype(jnp.bfloat16)
    query = forward_dot(n_self, w_query).astype(jnp.bfloat16)
    keys = forward_dot(n_self, w_key).astype(jnp.bfloat16)
    values = forward_dot(n_self, w_value).astype(jnp.bfloat16)
    all_keys, all_values = (
        lax.all_gather(keys, "ctx", axis=0, tiled=True),
        lax.all_gather(values, "ctx", axis=0, tiled=True),
    )

    def self_allow(start, block):
        pos_block = lax.dynamic_slice_in_dim(all_pos, start, block)
        seg_block = lax.dynamic_slice_in_dim(all_seg, start, block)
        return (pos_block[None, :] <= own_pos[:, None]) & (seg_block[None, :] == own_seg[:, None])

    self_wide, self_lse = attention_forward(query, all_keys, all_values, self_allow)
    mixed = self_wide.astype(jnp.bfloat16)
    branch_self = forward_dot(mixed, w_out)
    after_self = inputs + branch_self
    n_cross = normed(after_self, gain_cross).astype(jnp.bfloat16)
    cross_q = forward_dot(n_cross, c_query).astype(jnp.bfloat16)
    own_ck = forward_dot(encoder, c_key).astype(jnp.bfloat16)
    own_cv = forward_dot(encoder, c_value).astype(jnp.bfloat16)
    cross_k, cross_v = (
        lax.all_gather(own_ck, "ctx", axis=0, tiled=True),
        lax.all_gather(own_cv, "ctx", axis=0, tiled=True),
    )
    valid = prompt_len[0]

    def cross_allow(start, block):
        index = start + jnp.arange(block, dtype=jnp.int32)
        return jnp.broadcast_to((index < valid)[None, :], (local_rows, block))

    cross_wide, cross_lse = attention_forward(cross_q, cross_k, cross_v, cross_allow)
    cross_mixed = cross_wide.astype(jnp.bfloat16)
    branch_cross = forward_dot(cross_mixed, c_out)
    after_cross = after_self + branch_cross
    n_mlp = normed(after_cross, gain_mlp).astype(jnp.bfloat16)
    gate = forward_dot(n_mlp, w_gate)
    upward = forward_dot(n_mlp, w_up)
    hidden = gated(gate, upward).astype(jnp.bfloat16)
    branch_mlp = forward_dot(hidden, w_down)
    leaving = after_cross + branch_mlp
    layer_out = leaving.astype(jnp.bfloat16)
    totals = lax.psum(
        (
            jnp.sum(inputs * inputs),
            jnp.sum(branch_self * branch_self),
            jnp.sum(branch_cross * branch_cross),
            jnp.sum(leaving * leaving),
        ),
        ("parts", "ctx", "fsdp"),
    )
    entries = float(
        lax.axis_size("parts")
        * lax.axis_size("ctx")
        * lax.axis_size("fsdp")
        * local_rows
        * inputs.shape[1]
    )
    rms_values = jnp.sqrt(jnp.stack(totals) / entries)
    grad_top = cotangent[0].astype(jnp.float32)
    d_mlp = cotangent[0]
    grad_down = outer(hidden, d_mlp)
    d_hidden = back_dot(d_mlp, w_down)
    _, gated_back = jax.vjp(gated, gate, upward)
    d_gate, d_up = gated_back(d_hidden)
    d_gate16 = d_gate.astype(jnp.bfloat16)
    d_up16 = d_up.astype(jnp.bfloat16)
    grad_gate = outer(n_mlp, d_gate16)
    grad_up = outer(n_mlp, d_up16)
    d_nmlp = back_dot(d_gate16, w_gate) + back_dot(d_up16, w_up)
    _, mlp_norm_back = jax.vjp(normed, after_cross, gain_mlp)
    d_after_cross, grad_gmlp = mlp_norm_back(d_nmlp)
    d_cross_res = grad_top + d_after_cross
    d_branch_c = d_cross_res.astype(jnp.bfloat16)
    grad_cout = outer(cross_mixed, d_branch_c)
    d_cmixed = back_dot(d_branch_c, c_out).astype(jnp.bfloat16)
    cross_delta = row_delta(d_cmixed, cross_wide)
    d_cq, d_ck_all, d_cv_all = attention_backward(
        cross_q, cross_k, cross_v, d_cmixed, cross_lse, cross_delta, cross_allow, True
    )
    d_cq16 = d_cq.astype(jnp.bfloat16)
    grad_cquery = outer(n_cross, d_cq16)
    d_ncross = back_dot(d_cq16, c_query)
    own_dk, own_dv = (
        lax.psum_scatter(
            d_ck_all.astype(jnp.bfloat16), "ctx", scatter_dimension=0, tiled=True
        ).astype(jnp.float32),
        lax.psum_scatter(
            d_cv_all.astype(jnp.bfloat16), "ctx", scatter_dimension=0, tiled=True
        ).astype(jnp.float32),
    )
    own_dk16 = own_dk.astype(jnp.bfloat16)
    own_dv16 = own_dv.astype(jnp.bfloat16)
    grad_ckey = outer(encoder, own_dk16)
    grad_cvalue = outer(encoder, own_dv16)
    enc_grad = back_dot(own_dk16, c_key) + back_dot(own_dv16, c_value)
    _, cross_norm_back = jax.vjp(normed, after_self, gain_cross)
    d_after_self, grad_gcross = cross_norm_back(d_ncross)
    d_self_res = d_cross_res + d_after_self
    d_branch_s = d_self_res.astype(jnp.bfloat16)
    grad_wout = outer(mixed, d_branch_s)
    d_mixed = back_dot(d_branch_s, w_out).astype(jnp.bfloat16)
    self_delta = row_delta(d_mixed, self_wide)
    d_query, _, _ = attention_backward(
        query, all_keys, all_values, d_mixed, self_lse, self_delta, self_allow, False
    )
    all_query, all_grad = (
        lax.all_gather(query, "ctx", axis=0, tiled=True),
        lax.all_gather(d_mixed, "ctx", axis=0, tiled=True),
    )
    all_lse, all_delta = (
        lax.all_gather(self_lse.T.astype(jnp.bfloat16), "ctx", axis=0, tiled=True).astype(
            jnp.float32
        ),
        lax.all_gather(self_delta.T.astype(jnp.bfloat16), "ctx", axis=0, tiled=True).astype(
            jnp.float32
        ),
    )

    def key_allow(start, block):
        pos_block = lax.dynamic_slice_in_dim(all_pos, start, block)
        seg_block = lax.dynamic_slice_in_dim(all_seg, start, block)
        return (own_pos[None, :] <= pos_block[:, None]) & (own_seg[None, :] == seg_block[:, None])

    own_dkeys, own_dvalues = key_side(
        keys, values, all_query, all_grad, all_lse, all_delta, key_allow
    )
    d_query16 = d_query.astype(jnp.bfloat16)
    d_keys16 = own_dkeys.astype(jnp.bfloat16)
    d_values16 = own_dvalues.astype(jnp.bfloat16)
    grad_query = outer(n_self, d_query16)
    grad_key = outer(n_self, d_keys16)
    grad_value = outer(n_self, d_values16)
    d_nself = (
        back_dot(d_query16, w_query) + back_dot(d_keys16, w_key) + back_dot(d_values16, w_value)
    )
    _, self_norm_back = jax.vjp(normed, inputs, gain_self)
    d_inputs, grad_gself = self_norm_back(d_nself)
    decoder_grad = d_self_res + d_inputs
    shares = (
        lax.psum_scatter(
            grad_query.astype(jnp.bfloat16), "fsdp", scatter_dimension=0, tiled=True
        ).astype(jnp.float32),
        lax.psum_scatter(
            grad_key.astype(jnp.bfloat16), "fsdp", scatter_dimension=0, tiled=True
        ).astype(jnp.float32),
        lax.psum_scatter(
            grad_value.astype(jnp.bfloat16), "fsdp", scatter_dimension=0, tiled=True
        ).astype(jnp.float32),
        lax.psum_scatter(
            grad_wout.astype(jnp.bfloat16), "fsdp", scatter_dimension=0, tiled=True
        ).astype(jnp.float32),
        lax.psum_scatter(
            grad_cquery.astype(jnp.bfloat16), "fsdp", scatter_dimension=0, tiled=True
        ).astype(jnp.float32),
        lax.psum_scatter(
            grad_ckey.astype(jnp.bfloat16), "fsdp", scatter_dimension=0, tiled=True
        ).astype(jnp.float32),
        lax.psum_scatter(
            grad_cvalue.astype(jnp.bfloat16), "fsdp", scatter_dimension=0, tiled=True
        ).astype(jnp.float32),
        lax.psum_scatter(
            grad_cout.astype(jnp.bfloat16), "fsdp", scatter_dimension=0, tiled=True
        ).astype(jnp.float32),
        lax.psum_scatter(
            grad_gate.astype(jnp.bfloat16), "fsdp", scatter_dimension=0, tiled=True
        ).astype(jnp.float32),
        lax.psum_scatter(
            grad_up.astype(jnp.bfloat16), "fsdp", scatter_dimension=0, tiled=True
        ).astype(jnp.float32),
        lax.psum_scatter(
            grad_down.astype(jnp.bfloat16), "fsdp", scatter_dimension=0, tiled=True
        ).astype(jnp.float32),
        lax.psum_scatter(
            grad_gself.astype(jnp.bfloat16), "fsdp", scatter_dimension=0, tiled=True
        ).astype(jnp.float32),
        lax.psum_scatter(
            grad_gcross.astype(jnp.bfloat16), "fsdp", scatter_dimension=0, tiled=True
        ).astype(jnp.float32),
        lax.psum_scatter(
            grad_gmlp.astype(jnp.bfloat16), "fsdp", scatter_dimension=0, tiled=True
        ).astype(jnp.float32),
    )
    summed = lax.psum(
        (
            shares[0],
            shares[1],
            shares[2],
            shares[3],
            shares[4],
            shares[5],
            shares[6],
            shares[7],
            shares[8],
            shares[9],
            shares[10],
            shares[11],
            shares[12],
            shares[13],
        ),
        ("parts", "ctx"),
    )
    return (
        layer_out[None],
        decoder_grad[None],
        enc_grad[None],
        summed[0],
        summed[1],
        summed[2],
        summed[3],
        summed[4],
        summed[5],
        summed[6],
        summed[7],
        summed[8],
        summed[9],
        summed[10],
        summed[11],
        summed[12],
        summed[13],
        rms_values,
    )


def solution(mesh):
    placed = (
        P(("parts", "fsdp"), "ctx", None),
        P(("parts", "fsdp"), "ctx", None),
        P(("parts", "fsdp"), None),
        P(("parts", "fsdp"), None),
        P(("parts", "fsdp")),
        P("fsdp", None),
        P("fsdp", None),
        P("fsdp", None),
        P("fsdp", None),
        P("fsdp", None),
        P("fsdp", None),
        P("fsdp", None),
        P("fsdp", None),
        P("fsdp", None),
        P("fsdp", None),
        P("fsdp", None),
        P("fsdp"),
        P("fsdp"),
        P("fsdp"),
        P(("parts", "fsdp"), "ctx", None),
    )
    return jax.shard_map(
        local,
        mesh=mesh,
        in_specs=placed,
        out_specs=(
            P(("parts", "fsdp"), "ctx", None),
            P(("parts", "fsdp"), "ctx", None),
            P(("parts", "fsdp"), "ctx", None),
            P("fsdp", None),
            P("fsdp", None),
            P("fsdp", None),
            P("fsdp", None),
            P("fsdp", None),
            P("fsdp", None),
            P("fsdp", None),
            P("fsdp", None),
            P("fsdp", None),
            P("fsdp", None),
            P("fsdp", None),
            P("fsdp"),
            P("fsdp"),
            P("fsdp"),
            P(),
        ),
        check_vma=False,
    )
```

profile of v0, /device:TPU:9, one launch (start us, length us, event | category | flops | bytes accessed | tf_op | source)
XLA Modules:
  0.0 1936.4 jit_solution(4971213738837510506)
XLA Ops:
  22.5 18.3 all-gather.18.cloned.1.call-done
  44.8 27.2 %all-gather.24.cloned.1.call-done = bf16[768,768]{1,0:T(8,128)(2,1)} async-done(((bf16[192,768]{1,0:T(8,128)(2,1)}), bf16[768,768]{1,0:T(8,128)(2,1)}) %all-gather.24.cloned.1.call-update) | async-done | bytes 1179664 | tf_op jit(solution)/shard_map/all_gather | solution.py:210
  76.0 27.1 %all-gather.30.cloned.1.call-done = bf16[768,768]{1,0:T(8,128)(2,1)} async-done(((bf16[192,768]{1,0:T(8,128)(2,1)}), bf16[768,768]{1,0:T(8,128)(2,1)}) %all-gather.30.cloned.1.call-update) | async-done | bytes 1179664 | tf_op jit(solution)/shard_map/all_gather | solution.py:213
  107.9 26.3 %all-gather.36.cloned.1.call-done = bf16[768,768]{1,0:T(8,128)(2,1)} async-done(((bf16[192,768]{1,0:T(8,128)(2,1)}), bf16[768,768]{1,0:T(8,128)(2,1)}) %all-gather.36.cloned.1.call-update) | async-done | bytes 1179664 | tf_op jit(solution)/shard_map/all_gather | solution.py:214
  169.5 42.5 %all-gather.20.cloned.1.call-done = bf16[2048,768]{0,1:T(8,128)(2,1)} async-done(((bf16[1024,768]{0,1:T(8,128)(2,1)}), bf16[2048,768]{0,1:T(8,128)(2,1)}) %all-gather.20.cloned.1.call-update) | async-done | bytes 3145744 | tf_op jit(solution)/shard_map/all_gather | solution.py:260
  222.6 36.4 %all-gather.26.cloned.1.call-done = bf16[2048,768]{0,1:T(8,128)(2,1)} async-done(((bf16[1024,768]{0,1:T(8,128)(2,1)}), bf16[2048,768]{0,1:T(8,128)(2,1)}) %all-gather.26.cloned.1.call-update) | async-done | bytes 3145744 | tf_op jit(solution)/shard_map/all_gather | solution.py:261
  269.7 139.6 %while.69 = (s32[]{:T(128)}, f32[12,1024]{1,0:T(8,128)S(1)}, f32[12,1024]{1,0:T(8,128)S(1)}, f32[1024,12,64]{0,2,1:T(8,128)}, s32[2]{0:T(128)S(1)}, /*index=5*/s...) while((s32[]{:T(128)}, f32[12,1024]{1,0:T(8,128)S(1)}, ...), condition=%wide.region_4.5_spmd.clone, body=%wide.region_1.4_spmd.clone.sunk | while | flops 3390383104 | bytes 204812624 | solution.py:83
  273.6 21.5 %fusion.299 = (f32[12,1024]{1,0:T(8,128)S(1)}, f32[12,1024,1024]{2,1,0:T(8,128)}) fusion(pred[1024,1024]{0,1:T(8,128)(4,1)S(1)} %compare_and_fusion.6, bf16[1024,12,64]{0,2,1:T(8,128)(2,1)} %get-tuple-element.1398, bf16[2,1024,12,64]{1,3,2,0:T(8,128)(2,1)} %get-tuple-element.1397, s32[]{:T(128)S(6)} %copy.183), kind=kOutput, calls=%fused_computation.7.clone.1 | convolution fusion | flops 1648349184 | bytes 54575108 | tf_op jit(solution)/shard_map/while/body/eval_jaxpr/qhd,khd->hqk/dot_general | solution.py:46
  295.2 22.8 %fusion.301 = f32[12,1024]{1,0:T(8,128)S(1)} fusion(f32[12,1024,1024]{2,1,0:T(8,128)} %get-tuple-element.1303, f32[12,1024]{1,0:T(8,128)S(1)} %get-tuple-element.1390, pred[1024,1024]{0,1:T(8,128)(4,1)S(1)} %compare_and_fusion.6), kind=kLoop, calls=%fused_computation.9.clone.1 | loop fusion | flops 62902272 | bytes 51478528 | tf_op jit(solution)/shard_map/while/body/eval_jaxpr/reduce_sum | solution.py:68
  318.0 19.4 %bitcast_add_fusion.12 = f32[1024,12,64]{0,2,1:T(8,128)S(1)} fusion(f32[1024,12,64]{0,2,1:T(8,128)S(1)} %copy-done.29, f32[12,1024,1024]{2,1,0:T(8,128)} %get-tuple-element.1303, f32[12,1024]{1,0:T(8,128)S(1)} %get-tuple-element.1390, pred[1024,1024]{0,1:T(8,128)(4,1)S(1)} %compare_and_fusion.6, bf16[2,1024,12,64]{1,3,2,0:T(8,128)(2,1)S(1)} %copy-done.25, ...), kind=kOutput, calls=%fused_computation.13.clone.1 | convolution fusion | flops 1675886592 | bytes 59375620 | tf_op jit(solution)/shard_map/while/body/eval_jaxpr/hqk,khd->qhd/dot_general | solution.py:69
  343.1 21.8 %fusion.299 = (f32[12,1024]{1,0:T(8,128)S(1)}, f32[12,1024,1024]{2,1,0:T(8,128)}) fusion(pred[1024,1024]{0,1:T(8,128)(4,1)S(1)} %compare_and_fusion.6, bf16[1024,12,64]{0,2,1:T(8,128)(2,1)} %get-tuple-element.1398, bf16[2,1024,12,64]{1,3,2,0:T(8,128)(2,1)} %get-tuple-element.1397, s32[]{:T(128)S(6)} %copy.183), kind=kOutput, calls=%fused_computation.7.clone.1 | convolution fusion | flops 1648349184 | bytes 54575108 | tf_op jit(solution)/shard_map/while/body/eval_jaxpr/qhd,khd->hqk/dot_general | solution.py:46
  364.9 22.6 %fusion.301 = f32[12,1024]{1,0:T(8,128)S(1)} fusion(f32[12,1024,1024]{2,1,0:T(8,128)} %get-tuple-element.1303, f32[12,1024]{1,0:T(8,128)S(1)} %get-tuple-element.1390, pred[1024,1024]{0,1:T(8,128)(4,1)S(1)} %compare_and_fusion.6), kind=kLoop, calls=%fused_computation.9.clone.1 | loop fusion | flops 62902272 | bytes 51478528 | tf_op jit(solution)/shard_map/while/body/eval_jaxpr/reduce_sum | solution.py:68
  387.6 19.6 %bitcast_add_fusion.12 = f32[1024,12,64]{0,2,1:T(8,128)S(1)} fusion(f32[1024,12,64]{0,2,1:T(8,128)S(1)} %copy-done.29, f32[12,1024,1024]{2,1,0:T(8,128)} %get-tuple-element.1303, f32[12,1024]{1,0:T(8,128)S(1)} %get-tuple-element.1390, pred[1024,1024]{0,1:T(8,128)(4,1)S(1)} %compare_and_fusion.6, bf16[2,1024,12,64]{1,3,2,0:T(8,128)(2,1)S(1)} %copy-done.25, ...), kind=kOutput, calls=%fused_computation.13.clone.1 | convolution fusion | flops 1675886592 | bytes 59375620 | tf_op jit(solution)/shard_map/while/body/eval_jaxpr/hqk,khd->qhd/dot_general | solution.py:69
  455.3 135.3 %while.70 = (s32[]{:T(128)}, f32[12,1024]{1,0:T(8,128)S(1)}, f32[12,1024]{1,0:T(8,128)S(1)}, f32[1024,12,64]{0,2,1:T(8,128)}, s32[2]{0:T(128)S(1)}, /*index=5*/s...) while((s32[]{:T(128)}, f32[12,1024]{1,0:T(8,128)S(1)}, ...), condition=%wide.region_9.10_spmd.clone, body=%wide.region_6.9_spmd.clone.sunk | while | flops 3387238400 | bytes 200578288 | solution.py:83
  457.4 20.2 %bitcast_reduce_fusion.2 = (f32[12,1024]{1,0:T(8,128)S(1)}, f32[12,1024,1024]{2,1,0:T(8,128)}) fusion(pred[1024]{0:T(1024)(128)(4,1)S(1)} %add_compare_fusion.4, bf16[1024,12,64]{0,2,1:T(8,128)(2,1)S(1)} %get-tuple-element.1433, bf16[2,1024,12,64]{1,3,2,0:T(8,128)(2,1)} %get-tuple-element.1432, s32[]{:T(128)S(6)} %copy.195), kind=kOutput, calls=%fused_computation.32.clone.1 | convolution fusion | flops 1648349184 | bytes 53527556 | tf_op jit(solution)/shard_map/while/body/eval_jaxpr/qhd,khd->hqk/dot_general | solution.py:46
  477.6 23.7 %fusion.307 = f32[12,1024]{1,0:T(8,128)S(1)} fusion(f32[12,1024,1024]{2,1,0:T(8,128)} %get-tuple-element.1316, f32[12,1024]{1,0:T(8,128)S(1)} %get-tuple-element.1427, pred[1024]{0:T(1024)(128)(4,1)S(1)} %add_compare_fusion.4), kind=kLoop, calls=%fused_computation.37.clone.1 | loop fusion | flops 62902272 | bytes 50430976 | tf_op jit(solution)/shard_map/while/body/eval_jaxpr/reduce_sum | solution.py:68
  501.4 19.6 %bitcast_add_fusion.13 = f32[1024,12,64]{0,2,1:T(8,128)S(1)} fusion(f32[1024,12,64]{0,2,1:T(8,128)S(1)} %copy-done.26, f32[12,1024,1024]{2,1,0:T(8,128)} %get-tuple-element.1316, f32[12,1024]{1,0:T(8,128)S(1)} %get-tuple-element.1427, pred[1024]{0:T(1024)(128)(4,1)S(1)} %add_compare_fusion.4, bf16[2,1024,12,64]{1,3,2,0:T(8,128)(2,1)S(1)} %copy-done.28, ...), kind=kOutput, calls=%fused_computation.41.clone.1 | convolution fusion | flops 1675886592 | bytes 58329092 | tf_op jit(solution)/shard_map/while/body/eval_jaxpr/hqk,khd->qhd/dot_general | solution.py:69
  524.5 20.2 %bitcast_reduce_fusion.2 = (f32[12,1024]{1,0:T(8,128)S(1)}, f32[12,1024,1024]{2,1,0:T(8,128)}) fusion(pred[1024]{0:T(1024)(128)(4,1)S(1)} %add_compare_fusion.4, bf16[1024,12,64]{0,2,1:T(8,128)(2,1)S(1)} %get-tuple-element.1433, bf16[2,1024,12,64]{1,3,2,0:T(8,128)(2,1)} %get-tuple-element.1432, s32[]{:T(128)S(6)} %copy.195), kind=kOutput, calls=%fused_computation.32.clone.1 | convolution fusion | flops 1648349184 | bytes 53527556 | tf_op jit(solution)/shard_map/while/body/eval_jaxpr/qhd,khd->hqk/dot_general | solution.py:46
  544.7 23.7 %fusion.307 = f32[12,1024]{1,0:T(8,128)S(1)} fusion(f32[12,1024,1024]{2,1,0:T(8,128)} %get-tuple-element.1316, f32[12,1024]{1,0:T(8,128)S(1)} %get-tuple-element.1427, pred[1024]{0:T(1024)(128)(4,1)S(1)} %add_compare_fusion.4), kind=kLoop, calls=%fused_computation.37.clone.1 | loop fusion | flops 62902272 | bytes 50430976 | tf_op jit(solution)/shard_map/while/body/eval_jaxpr/reduce_sum | solution.py:68
  568.5 20.3 %bitcast_add_fusion.13 = f32[1024,12,64]{0,2,1:T(8,128)S(1)} fusion(f32[1024,12,64]{0,2,1:T(8,128)S(1)} %copy-done.26, f32[12,1024,1024]{2,1,0:T(8,128)} %get-tuple-element.1316, f32[12,1024]{1,0:T(8,128)S(1)} %get-tuple-element.1427, pred[1024]{0:T(1024)(128)(4,1)S(1)} %add_compare_fusion.4, bf16[2,1024,12,64]{1,3,2,0:T(8,128)(2,1)S(1)} %copy-done.28, ...), kind=kOutput, calls=%fused_computation.41.clone.1 | convolution fusion | flops 1675886592 | bytes 58329092 | tf_op jit(solution)/shard_map/while/body/eval_jaxpr/hqk,khd->qhd/dot_general | solution.py:69
  635.2 17.4 multiply_convert_fusion.5
  672.0 206.8 %while.71 = (s32[]{:T(128)}, f32[1024,12,64]{0,2,1:T(8,128)}, bf16[2,1024,12,64]{1,3,2,0:T(8,128)(2,1)}, bf16[2,1024,12,64]{1,3,2,0:T(8,128)(2,1)}, bf16[2,1024,...) while((s32[]{:T(128)}, f32[1024,12,64]{0,2,1:T(8,128)}, ...), condition=%wide.region_14.15_spmd.clone, body=%wide.region_13.14_spmd.clone.sunk | while | flops 8207206400 | bytes 250236096 | solution.py:136
  672.2 20.7 %fusion.319 = f32[12,1024,1024]{2,1,0:T(8,128)} fusion(bf16[1024,12,64]{0,2,1:T(8,128)(2,1)S(1)} %get-tuple-element.1472, bf16[2,1024,12,64]{1,3,2,0:T(8,128)(2,1)} %get-tuple-element.1469, s32[]{:T(128)S(6)} %copy.207), kind=kOutput, calls=%fused_computation.69.clone.1 | convolution fusion | flops 1610612736 | bytes 53477380 | tf_op jit(solution)/shard_map/while/body/eval_jaxpr/qhd,khd->hqk/dot_general | solution.py:46
  694.9 31.3 %multiply_convert_fusion.13 = bf16[12,1024,1024]{2,1,0:T(8,128)(2,1)} fusion(f32[12,1024,1024]{2,1,0:T(8,128)} %fusion.319, f32[12,1024]{1,0:T(8,128)S(1)} %get-tuple-element.1476, f32[12,1024]{1,0:T(8,128)S(1)} %get-tuple-element.1473, pred[1024]{0:T(1024)(128)(4,1)S(1)} %add_compare_fusion.5, bf16[1024,12,64]{0,2,1:T(8,128)(2,1)} %get-tuple-element.1475, ...), kind=kOutput, calls=%fused_computation.59.clone.1 | convolution fusion | flops 1698693120 | bytes 78742528 | tf_op jit(solution)/shard_map/while/body/eval_jaxpr/qhd,khd->hqk/dot_general | solution.py:113
  726.2 14.8 bitcast_add_fusion.14
  754.8 20.2 %bitcast_dynamic-update-slice_fusion.5 = bf16[2,1024,12,64]{1,3,2,0:T(8,128)(2,1)} fusion(bf16[2,1024,12,64]{1,3,2,0:T(8,128)(2,1)} %get-tuple-element.1454, s32[]{:T(128)S(6)} %copy.207, bf16[1024,12,64]{0,2,1:T(8,128)(2,1)} %get-tuple-element.1475, f32[12,1024,1024]{2,1,0:T(8,128)} %fusion.319, f32[12,1024]{1,0:T(8,128)S(1)} %get-tuple-element.1473, ...), kind=kOutput, calls=%fused_computation.64.clone.1 | convolution fusion | flops 1673527296 | bytes 55100420 | tf_op jit(solution)/shard_map/while/body/eval_jaxpr/hqk,qhd->khd/dot_general | solution.py:127
  775.0 20.7 %fusion.319 = f32[12,1024,1024]{2,1,0:T(8,128)} fusion(bf16[1024,12,64]{0,2,1:T(8,128)(2,1)S(1)} %get-tuple-element.1472, bf16[2,1024,12,64]{1,3,2,0:T(8,128)(2,1)} %get-tuple-element.1469, s32[]{:T(128)S(6)} %copy.207), kind=kOutput, calls=%fused_computation.69.clone.1 | convolution fusion | flops 1610612736 | bytes 53477380 | tf_op jit(solution)/shard_map/while/body/eval_jaxpr/qhd,khd->hqk/dot_general | solution.py:46
  797.6 31.3 %multiply_convert_fusion.13 = bf16[12,1024,1024]{2,1,0:T(8,128)(2,1)} fusion(f32[12,1024,1024]{2,1,0:T(8,128)} %fusion.319, f32[12,1024]{1,0:T(8,128)S(1)} %get-tuple-element.1476, f32[12,1024]{1,0:T(8,128)S(1)} %get-tuple-element.1473, pred[1024]{0:T(1024)(128)(4,1)S(1)} %add_compare_fusion.5, bf16[1024,12,64]{0,2,1:T(8,128)(2,1)} %get-tuple-element.1475, ...), kind=kOutput, calls=%fused_computation.59.clone.1 | convolution fusion | flops 1698693120 | bytes 78742528 | tf_op jit(solution)/shard_map/while/body/eval_jaxpr/qhd,khd->hqk/dot_general | solution.py:113
  828.9 15.8 bitcast_add_fusion.14
  858.5 20.2 %bitcast_dynamic-update-slice_fusion.5 = bf16[2,1024,12,64]{1,3,2,0:T(8,128)(2,1)} fusion(bf16[2,1024,12,64]{1,3,2,0:T(8,128)(2,1)} %get-tuple-element.1454, s32[]{:T(128)S(6)} %copy.207, bf16[1024,12,64]{0,2,1:T(8,128)(2,1)} %get-tuple-element.1475, f32[12,1024,1024]{2,1,0:T(8,128)} %fusion.319, f32[12,1024]{1,0:T(8,128)S(1)} %get-tuple-element.1473, ...), kind=kOutput, calls=%fused_computation.64.clone.1 | convolution fusion | flops 1673527296 | bytes 55100420 | tf_op jit(solution)/shard_map/while/body/eval_jaxpr/hqk,qhd->khd/dot_general | solution.py:127
  902.0 108.3 %while.72 = (s32[]{:T(128)}, f32[1024,12,64]{0,2,1:T(8,128)}, bf16[2,1024,12,64]{1,3,2,0:T(8,128)(2,1)}, s32[2]{0:T(128)S(1)}, s32[2048]{0:T(1024)S(1)}, /*index...) while((s32[]{:T(128)}, f32[1024,12,64]{0,2,1:T(8,128)}, ...), condition=%wide.region_18.19_spmd.clone, body=%wide.region_17.18_spmd.clone.sunk | while | flops 4925424640 | bytes 117061352 | solution.py:136
  902.5 20.9 %fusion.326 = f32[12,1024,1024]{2,1,0:T(8,128)} fusion(bf16[1024,12,64]{0,2,1:T(8,128)(2,1)S(1)} %get-tuple-element.1569, bf16[2,1024,12,64]{1,3,2,0:T(8,128)(2,1)} %get-tuple-element.1564, s32[]{:T(128)S(6)} %copy.226), kind=kOutput, calls=%fused_computation.94.clone.1 | convolution fusion | flops 1610612736 | bytes 53477380 | tf_op jit(solution)/shard_map/while/body/eval_jaxpr/qhd,khd->hqk/dot_general | solution.py:46
  928.0 28.3 %bitcast_add_fusion.15 = f32[1024,12,64]{0,2,1:T(8,128)} fusion(f32[1024,12,64]{0,2,1:T(8,128)} %get-tuple-element.1547, f32[12,1024,1024]{2,1,0:T(8,128)} %fusion.326, f32[12,1024]{1,0:T(8,128)S(1)} %get-tuple-element.1573, f32[12,1024]{1,0:T(8,128)S(1)} %get-tuple-element.1570, pred[1024,1024]{0,1:T(8,128)(4,1)} %compare_and_fusion.7, ...), kind=kOutput, calls=%fused_computation.91.clone.1 | convolution fusion | flops 3311665152 | bytes 62490112 | tf_op jit(solution)/shard_map/while/body/eval_jaxpr/hqk,khd->qhd/dot_general | solution.py:119
  956.4 21.0 %fusion.326 = f32[12,1024,1024]{2,1,0:T(8,128)} fusion(bf16[1024,12,64]{0,2,1:T(8,128)(2,1)S(1)} %get-tuple-element.1569, bf16[2,1024,12,64]{1,3,2,0:T(8,128)(2,1)} %get-tuple-element.1564, s32[]{:T(128)S(6)} %copy.226), kind=kOutput, calls=%fused_computation.94.clone.1 | convolution fusion | flops 1610612736 | bytes 53477380 | tf_op jit(solution)/shard_map/while/body/eval_jaxpr/qhd,khd->hqk/dot_general | solution.py:46
  982.1 28.2 %bitcast_add_fusion.15 = f32[1024,12,64]{0,2,1:T(8,128)} fusion(f32[1024,12,64]{0,2,1:T(8,128)} %get-tuple-element.1547, f32[12,1024,1024]{2,1,0:T(8,128)} %fusion.326, f32[12,1024]{1,0:T(8,128)S(1)} %get-tuple-element.1573, f32[12,1024]{1,0:T(8,128)S(1)} %get-tuple-element.1570, pred[1024,1024]{0,1:T(8,128)(4,1)} %compare_and_fusion.7, ...), kind=kOutput, calls=%fused_computation.91.clone.1 | convolution fusion | flops 3311665152 | bytes 62490112 | tf_op jit(solution)/shard_map/while/body/eval_jaxpr/hqk,khd->qhd/dot_general | solution.py:119
  1067.2 157.8 %while.73 = (s32[]{:T(128)}, f32[1024,12,64]{0,2,1:T(8,128)}, f32[1024,12,64]{0,2,1:T(8,128)}, bf16[2,1024,12,64]{1,3,2,0:T(8,128)(2,1)}, s32[2]{0:T(128)S(1)}, ...) while((s32[]{:T(128)}, f32[1024,12,64]{0,2,1:T(8,128)}, ...), condition=%wide.region_20.21_spmd.clone, body=%wide.region_19.20_spmd.clone.sunk | while | flops 6600524800 | bytes 176748272 | solution.py:179
  1067.4 21.1 %fusion.334 = f32[12,1024,1024]{2,1,0:T(8,128)} fusion(bf16[1024,12,64]{0,2,1:T(8,128)(2,1)S(1)} %get-tuple-element.1521, bf16[2,1024,12,64]{1,3,2,0:T(8,128)(2,1)} %get-tuple-element.1516, s32[]{:T(128)S(6)} %copy.218), kind=kOutput, calls=%fused_computation.119.clone.1 | convolution fusion | flops 1610612736 | bytes 53477380 | tf_op jit(solution)/shard_map/while/body/eval_jaxpr/qhd,khd->hqk/dot_general | solution.py:46
  1093.3 29.4 %bitcast_add_fusion.16 = f32[1024,12,64]{0,2,1:T(8,128)} fusion(f32[1024,12,64]{0,2,1:T(8,128)} %get-tuple-element.1497, f32[12,1024,1024]{2,1,0:T(8,128)} %fusion.334, f32[12,1024]{1,0:T(8,128)S(1)} %bitcast.491, f32[12,1024]{1,0:T(8,128)S(1)} %bitcast.489, pred[1024,1024]{1,0:T(8,128)(4,1)} %compare_and_fusion.8, ...), kind=kOutput, calls=%fused_computation.115.clone.1 | convolution fusion | flops 3311665152 | bytes 62490112 | tf_op jit(solution)/shard_map/while/body/eval_jaxpr/hqk,qhd->khd/dot_general | solution.py:170
  1122.7 22.7 %bitcast_add_fusion.17 = f32[1024,12,64]{0,2,1:T(8,128)} fusion(f32[1024,12,64]{0,2,1:T(8,128)} %get-tuple-element.1498, f32[12,1024,1024]{2,1,0:T(8,128)} %fusion.334, f32[12,1024]{1,0:T(8,128)S(1)} %bitcast.490, pred[1024,1024]{1,0:T(8,128)(4,1)} %compare_and_fusion.8, pred[]{:T(512)S(6)} %compare.19, ...), kind=kOutput, calls=%fused_computation.114.clone.1 | convolution fusion | flops 1675100160 | bytes 59293700 | tf_op jit(solution)/shard_map/while/body/eval_jaxpr/hqk,qhd->khd/dot_general | solution.py:173
  1145.4 21.3 %fusion.334 = f32[12,1024,1024]{2,1,0:T(8,128)} fusion(bf16[1024,12,64]{0,2,1:T(8,128)(2,1)S(1)} %get-tuple-element.1521, bf16[2,1024,12,64]{1,3,2,0:T(8,128)(2,1)} %get-tuple-element.1516, s32[]{:T(128)S(6)} %copy.218), kind=kOutput, calls=%fused_computation.119.clone.1 | convolution fusion | flops 1610612736 | bytes 53477380 | tf_op jit(solution)/shard_map/while/body/eval_jaxpr/qhd,khd->hqk/dot_general | solution.py:46
  1171.5 29.7 %bitcast_add_fusion.16 = f32[1024,12,64]{0,2,1:T(8,128)} fusion(f32[1024,12,64]{0,2,1:T(8,128)} %get-tuple-element.1497, f32[12,1024,1024]{2,1,0:T(8,128)} %fusion.334, f32[12,1024]{1,0:T(8,128)S(1)} %bitcast.491, f32[12,1024]{1,0:T(8,128)S(1)} %bitcast.489, pred[1024,1024]{1,0:T(8,128)(4,1)} %compare_and_fusion.8, ...), kind=kOutput, calls=%fused_computation.115.clone.1 | convolution fusion | flops 3311665152 | bytes 62490112 | tf_op jit(solution)/shard_map/while/body/eval_jaxpr/hqk,qhd->khd/dot_general | solution.py:170
  1201.2 23.4 %bitcast_add_fusion.17 = f32[1024,12,64]{0,2,1:T(8,128)} fusion(f32[1024,12,64]{0,2,1:T(8,128)} %get-tuple-element.1498, f32[12,1024,1024]{2,1,0:T(8,128)} %fusion.334, f32[12,1024]{1,0:T(8,128)S(1)} %bitcast.490, pred[1024,1024]{1,0:T(8,128)(4,1)} %compare_and_fusion.8, pred[]{:T(512)S(6)} %compare.19, ...), kind=kOutput, calls=%fused_computation.114.clone.1 | convolution fusion | flops 1675100160 | bytes 59293700 | tf_op jit(solution)/shard_map/while/body/eval_jaxpr/hqk,qhd->khd/dot_general | solution.py:173
  1303.8 47.4 %all-reduce.6 = (f32[1]{0:T(128)}, f32[1]{0:T(128)}, f32[1]{0:T(128)}, f32[1]{0:T(128)}) all-reduce(f32[1]{0:T(128)} %bitcast.38, f32[1]{0:T(128)} %bitcast.37, f32[1]{0:T(128)} %bitcast.36, f32[1]{0:T(128)} %bitcast.35), channel_id=1, replica_groups=mesh['parts'=4,'ctx'=2,'fsdp'=4] {'parts','ctx','fsdp'}, use_global_device_ids=true, to_apply=%region_62.63 | all-reduce | flops 4 | bytes 32 | tf_op jit(solution)/shard_map/psum | solution.py:298
  1371.4 46.1 %reduce-scatter.36.cloned.1.call-done = bf16[192,2048]{1,0:T(8,128)(2,1)} async-done(((bf16[768,2048]{1,0:T(8,128)(2,1)}), bf16[192,2048]{1,0:T(8,128)(2,1)}) %reduce-scatter.36.cloned.1.call-update) | async-done | bytes 786448 | tf_op jit(solution)/shard_map/reduce_scatter | solution.py:423
  1417.5 62.6 %reduce-scatter.38.cloned.1.call-done = bf16[512,768]{1,0:T(8,128)(2,1)} async-done(((bf16[2048,768]{1,0:T(8,128)(2,1)}), bf16[512,768]{1,0:T(8,128)(2,1)}) %reduce-scatter.38.cloned.1.call-update) | async-done | bytes 786448 | tf_op jit(solution)/shard_map/reduce_scatter | solution.py:426
  1486.2 23.9 %reduce-scatter.40.cloned.1.call-done = bf16[192,768]{1,0:T(8,128)(2,1)} async-done(((bf16[768,768]{1,0:T(8,128)(2,1)}), bf16[192,768]{1,0:T(8,128)(2,1)}) %reduce-scatter.40.cloned.1.call-update) | async-done | bytes 294928
  1511.2 29.5 %reduce-scatter.42.cloned.1.call-done = bf16[192,768]{1,0:T(8,128)(2,1)} async-done(((bf16[768,768]{1,0:T(8,128)(2,1)}), bf16[192,768]{1,0:T(8,128)(2,1)}) %reduce-scatter.42.cloned.1.call-update) | async-done | bytes 294928
  1541.9 383.0 %all-reduce.11 = (f32[192,768]{1,0:T(8,128)}, f32[192,768]{1,0:T(8,128)}, f32[192,768]{1,0:T(8,128)}, f32[192,768]{1,0:T(8,128)}, f32[192,768]{1,0:T(8,128)}, /*...) all-reduce(bf16[192,768]{1,0:T(8,128)(2,1)S(1)} %copy-done.46, ...), channel_id=1, replica_groups=mesh['parts'=4,'ctx'=2,'fsdp'=4] {'parts','ctx'}, use_global_device_ids=true, to_apply=%region_25.26 | all-reduce | flops 2359872 | bytes 14160384 | tf_op jit(solution)/shard_map/psum | solution.py:439
  (454 shorter events, 440.7 us)
Async XLA Ops:
  7.2 96.0 %copy-start = (bf16[1,1024,768]{2,1,0:T(8,128)(2,1)S(1)}, bf16[1,1024,768]{2,1,0:T(8,128)(2,1)}, u32[]{:S(2)}) copy-start(bf16[1,1024,768]{2,1,0:T(8,128)(2,1)} %param.31) | copy-start | bytes 4718596
  7.2 33.5 %all-gather.18.cloned.1.call-start = ((), (), s32[]{:S(2)}) async-start(), calls=%async_computation.13 | async-start | bytes 1474560 | tf_op jit(solution)/shard_map/all_gather | solution.py:209
  8.0 64.0 %all-gather.24.cloned.1.call-start = ((), (), s32[]{:S(2)}) async-start(), calls=%async_computation.16 | async-start | bytes 1474560 | tf_op jit(solution)/shard_map/all_gather | solution.py:210
  8.7 94.4 %all-gather.30.cloned.1.call-start = ((), (), s32[]{:S(2)}) async-start(), calls=%async_computation.19 | async-start | bytes 1474560 | tf_op jit(solution)/shard_map/all_gather | solution.py:213
  9.5 124.7 %all-gather.36.cloned.1.call-start = ((), (), s32[]{:S(2)}) async-start(), calls=%async_computation.22 | async-start | bytes 1474560 | tf_op jit(solution)/shard_map/all_gather | solution.py:214
  10.0 155.2 %all-gather.22.cloned.1.call-start = ((), (), s32[]{:S(2)}) async-start(), calls=%async_computation.15 | async-start | bytes 1474560 | tf_op jit(solution)/shard_map/all_gather | solution.py:208
  10.6 201.3 %all-gather.20.cloned.1.call-start = ((), (), s32[]{:S(2)}) async-start(), calls=%async_computation.14 | async-start | bytes 4718592 | tf_op jit(solution)/shard_map/all_gather | solution.py:260
  12.4 152.8 %copy-start.11 = (bf16[1,1024,768]{1,2,0:T(8,128)(2,1)}, bf16[1,1024,768]{1,2,0:T(8,128)(2,1)S(1)}, u32[]{:S(2)}) copy-start(bf16[1,1024,768]{1,2,0:T(8,128)(2,1)S(1)} %copy.105) | copy-start | bytes 4718596
  22.1 143.1 %copy-start.50 = (f32[768]{0:T(1024)}, f32[768]{0:T(1024)S(1)}, u32[]{:S(2)}) copy-start(f32[768]{0:T(1024)S(1)} %convert_element_type.260) | copy-start | bytes 9220
  22.4 22.3 %copy-start.57 = (f32[1024]{0:T(1024)}, f32[1024]{0:T(1024)S(1)}, u32[]{:S(2)}) copy-start(f32[1024]{0:T(1024)S(1)} %fusion.137) | copy-start | bytes 12292
  22.5 142.7 %copy-start.53 = (f32[1024]{0:T(1024)}, f32[1024]{0:T(1024)S(1)}, u32[]{:S(2)}) copy-start(f32[1024]{0:T(1024)S(1)} %fusion.179) | copy-start | bytes 12292
  44.7 214.3 %all-gather.26.cloned.1.call-start = ((), (), s32[]{:S(2)}) async-start(), calls=%async_computation.17 | async-start | bytes 4718592 | tf_op jit(solution)/shard_map/all_gather | solution.py:261
  76.0 338.8 %all-gather.32.cloned.1.call-start = ((), (), s32[]{:S(2)}) async-start(), calls=%async_computation.20 | async-start | bytes 4718592 | tf_op jit(solution)/shard_map/all_gather | solution.py:278
  107.1 323.2 %all-gather.28.cloned.1.call-start = ((), (), s32[]{:S(2)}) async-start(), calls=%async_computation.18 | async-start | bytes 1474560 | tf_op jit(solution)/shard_map/all_gather | solution.py:211
  107.8 328.2 %all-gather.38.cloned.1.call-start = ((), (), s32[]{:S(2)}) async-start(), calls=%async_computation.23 | async-start | bytes 4718592 | tf_op jit(solution)/shard_map/all_gather | solution.py:279
  138.1 313.4 %all-gather.34.cloned.1.call-start = ((), (), s32[]{:S(2)}) async-start(), calls=%async_computation.21 | async-start | bytes 1474560 | tf_op jit(solution)/shard_map/all_gather | solution.py:212
  138.8 457.0 %all-gather.40.cloned.1.call-start = ((), (), s32[]{:S(2)}) async-start(), calls=%async_computation.24 | async-start | bytes 1474560 | tf_op jit(solution)/shard_map/all_gather | solution.py:215
  139.4 465.2 %all-gather.42.cloned.1.call-start = ((), (), s32[]{:S(2)}) async-start(), calls=%async_computation.25 | async-start | bytes 3932160 | tf_op jit(solution)/shard_map/all_gather | solution.py:216
  140.1 473.6 %all-gather.44.cloned.1.call-start = ((), (), s32[]{:S(2)}) async-start(), calls=%async_computation.26 | async-start | bytes 3932160 | tf_op jit(solution)/shard_map/all_gather | solution.py:217
  140.7 494.4 %all-gather.46.cloned.1.call-start = ((), (), s32[]{:S(2)}) async-start(), calls=%async_computation.27 | async-start | bytes 3932160 | tf_op jit(solution)/shard_map/all_gather | solution.py:218
  141.3 889.2 %all-gather.48.cloned.1.call-start = ((), (), s32[]{:S(2)}) async-start(), calls=%async_computation.28 | async-start | bytes 4718592 | tf_op jit(solution)/shard_map/all_gather | solution.py:363
  169.2 887.0 %all-gather.50.cloned.1.call-start = ((), (), s32[]{:S(2)}) async-start(), calls=%async_computation.29 | async-start | bytes 4718592 | tf_op jit(solution)/shard_map/all_gather | solution.py:364
  295.1 22.9 %copy-start.25 = (bf16[2,1024,12,64]{1,3,2,0:T(8,128)(2,1)S(1)}, bf16[2,1024,12,64]{1,3,2,0:T(8,128)(2,1)}, u32[]{:S(2)}) copy-start(bf16[2,1024,12,64]{1,3,2,0:T(8,128)(2,1)} %get-tuple-element.1399) | copy-start | bytes 9437188 | tf_op jit(solution)/shard_map/while
  295.2 22.9 %copy-start.29 = (f32[1024,12,64]{0,2,1:T(8,128)S(1)}, f32[1024,12,64]{0,2,1:T(8,128)}, u32[]{:S(2)}) copy-start(f32[1024,12,64]{0,2,1:T(8,128)} %get-tuple-element.1377) | copy-start | bytes 9437188 | tf_op jit(solution)/shard_map/while
  364.9 22.7 %copy-start.25 = (bf16[2,1024,12,64]{1,3,2,0:T(8,128)(2,1)S(1)}, bf16[2,1024,12,64]{1,3,2,0:T(8,128)(2,1)}, u32[]{:S(2)}) copy-start(bf16[2,1024,12,64]{1,3,2,0:T(8,128)(2,1)} %get-tuple-element.1399) | copy-start | bytes 9437188 | tf_op jit(solution)/shard_map/while
  364.9 22.7 %copy-start.29 = (f32[1024,12,64]{0,2,1:T(8,128)S(1)}, f32[1024,12,64]{0,2,1:T(8,128)}, u32[]{:S(2)}) copy-start(f32[1024,12,64]{0,2,1:T(8,128)} %get-tuple-element.1377) | copy-start | bytes 9437188 | tf_op jit(solution)/shard_map/while
  477.6 23.8 %copy-start.26 = (f32[1024,12,64]{0,2,1:T(8,128)S(1)}, f32[1024,12,64]{0,2,1:T(8,128)}, u32[]{:S(2)}) copy-start(f32[1024,12,64]{0,2,1:T(8,128)} %get-tuple-element.1418) | copy-start | bytes 9437188 | tf_op jit(solution)/shard_map/while
  477.6 23.8 %copy-start.28 = (bf16[2,1024,12,64]{1,3,2,0:T(8,128)(2,1)S(1)}, bf16[2,1024,12,64]{1,3,2,0:T(8,128)(2,1)}, u32[]{:S(2)}) copy-start(bf16[2,1024,12,64]{1,3,2,0:T(8,128)(2,1)} %get-tuple-element.1434) | copy-start | bytes 9437188 | tf_op jit(solution)/shard_map/while
  544.7 23.7 %copy-start.26 = (f32[1024,12,64]{0,2,1:T(8,128)S(1)}, f32[1024,12,64]{0,2,1:T(8,128)}, u32[]{:S(2)}) copy-start(f32[1024,12,64]{0,2,1:T(8,128)} %get-tuple-element.1418) | copy-start | bytes 9437188 | tf_op jit(solution)/shard_map/while
  544.7 23.7 %copy-start.28 = (bf16[2,1024,12,64]{1,3,2,0:T(8,128)(2,1)S(1)}, bf16[2,1024,12,64]{1,3,2,0:T(8,128)(2,1)}, u32[]{:S(2)}) copy-start(bf16[2,1024,12,64]{1,3,2,0:T(8,128)(2,1)} %get-tuple-element.1434) | copy-start | bytes 9437188 | tf_op jit(solution)/shard_map/while
  635.2 17.5 copy-start.70
  890.2 370.5 %reduce-scatter.18.cloned.1.call-start = ((), (), s32[]{:S(2)}) async-start(), calls=%async_computation.30 | async-start | bytes 4718592 | tf_op jit(solution)/shard_map/reduce_scatter | solution.py:340
  901.2 383.3 %reduce-scatter.22.cloned.1.call-start = ((), (), s32[]{:S(2)}) async-start(), calls=%async_computation.32 | async-start | bytes 1474560 | tf_op jit(solution)/shard_map/reduce_scatter | solution.py:396
  1016.3 268.3 %reduce-scatter.28.cloned.1.call-start = ((), (), s32[]{:S(2)}) async-start(), calls=%async_computation.35 | async-start | bytes 1474560 | tf_op jit(solution)/shard_map/reduce_scatter | solution.py:405
  1020.7 263.8 %reduce-scatter.30.cloned.1.call-start = ((), (), s32[]{:S(2)}) async-start(), calls=%async_computation.36 | async-start | bytes 1474560 | tf_op jit(solution)/shard_map/reduce_scatter | solution.py:408
  1025.9 258.6 %reduce-scatter.32.cloned.1.call-start = ((), (), s32[]{:S(2)}) async-start(), calls=%async_computation.37 | async-start | bytes 1474560 | tf_op jit(solution)/shard_map/reduce_scatter | solution.py:417
  1030.4 259.1 %reduce-scatter.20.cloned.1.call-start = ((), (), s32[]{:S(2)}) async-start(), calls=%async_computation.31 | async-start | bytes 4718592 | tf_op jit(solution)/shard_map/reduce_scatter | solution.py:343
  1056.2 315.2 %reduce-scatter.24.cloned.1.call-start = ((), (), s32[]{:S(2)}) async-start(), calls=%async_computation.33 | async-start | bytes 1474560 | tf_op jit(solution)/shard_map/reduce_scatter | solution.py:399
  1231.0 140.4 %reduce-scatter.26.cloned.1.call-start = ((), (), s32[]{:S(2)}) async-start(), calls=%async_computation.34 | async-start | bytes 1474560 | tf_op jit(solution)/shard_map/reduce_scatter | solution.py:402
  1236.8 134.5 %reduce-scatter.34.cloned.1.call-start = ((), (), s32[]{:S(2)}) async-start(), calls=%async_computation.38 | async-start | bytes 3932160 | tf_op jit(solution)/shard_map/reduce_scatter | solution.py:420
  1244.7 172.8 %reduce-scatter.36.cloned.1.call-start = ((), (), s32[]{:S(2)}) async-start(), calls=%async_computation.39 | async-start | bytes 3932160 | tf_op jit(solution)/shard_map/reduce_scatter | solution.py:423
  1252.5 227.6 %reduce-scatter.38.cloned.1.call-start = ((), (), s32[]{:S(2)}) async-start(), calls=%async_computation.40 | async-start | bytes 3932160 | tf_op jit(solution)/shard_map/reduce_scatter | solution.py:426
  1260.5 249.6 %reduce-scatter.40.cloned.1.call-start = ((), (), s32[]{:S(2)}) async-start(), calls=%async_computation.41 | async-start | bytes 1474560
  1266.9 273.8 %reduce-scatter.42.cloned.1.call-start = ((), (), s32[]{:S(2)}) async-start(), calls=%async_computation.42 | async-start | bytes 1474560
  1295.7 55.6 %copy-start.58 = (f32[1024]{0:T(1024)S(1)}, f32[1024]{0:T(1024)}, u32[]{:S(2)}) copy-start(f32[1024]{0:T(1024)} %copy-done.57) | copy-start | bytes 12292
  1356.5 123.5 %copy-start.72 = (bf16[1024,768]{0,1:T(8,128)(2,1)S(1)}, bf16[1024,768]{0,1:T(8,128)(2,1)}, u32[]{:S(2)}) copy-start(bf16[1024,768]{0,1:T(8,128)(2,1)} %reduce-scatter.18.cloned.1.call-done) | copy-start | bytes 4718596
  1483.0 58.9 %copy-start.41 = (bf16[192,2048]{1,0:T(8,128)(2,1)S(1)}, bf16[192,2048]{1,0:T(8,128)(2,1)}, u32[]{:S(2)}) copy-start(bf16[192,2048]{1,0:T(8,128)(2,1)} %reduce-scatter.34.cloned.1.call-done) | copy-start | bytes 2359300
  1483.0 58.9 %copy-start.46 = (bf16[192,768]{1,0:T(8,128)(2,1)S(1)}, bf16[192,768]{1,0:T(8,128)(2,1)}, u32[]{:S(2)}) copy-start(bf16[192,768]{1,0:T(8,128)(2,1)} %reduce-scatter.22.cloned.1.call-done) | copy-start | bytes 884740
  (71 other events, 243.9 us)
Sparse Core Ops, SparseCore 0:
  9.7 31.0 all-gather.17
  42.3 29.6 all-gather.23
  73.6 29.5 all-gather.29
  104.6 29.5 all-gather.35
  135.6 29.5 all-gather.21
  167.2 44.7 all-gather.19
  214.1 44.9 all-gather.25
  260.6 44.9 all-gather.31
  307.1 29.7 all-gather.27
  338.3 44.7 all-gather.37
  384.7 29.7 all-gather.33
  415.9 29.5 all-gather.39
  447.0 60.8 all-gather.41
  509.4 62.1 all-gather.43
  573.0 62.1 all-gather.45
  637.1 46.0 all-gather.47
  890.4 46.0 all-gather.49
  938.5 43.4 reduce-scatter.17
  1016.4 27.8 reduce-scatter.21
  1046.5 27.8 reduce-scatter.27
  1076.9 27.8 reduce-scatter.29
  1107.2 27.8 reduce-scatter.31
  1137.4 44.1 reduce-scatter.19
  1231.1 29.6 reduce-scatter.23
  1263.1 27.8 reduce-scatter.25
  1293.2 61.5 reduce-scatter.33
  1357.0 60.4 reduce-scatter.35
  1419.8 60.2 reduce-scatter.37
  1482.4 27.6 reduce-scatter.39
  1512.8 27.8 reduce-scatter.41
where the time goes:
time: 1950 us; the launch traced here: 1940 us
  matrix products  788 us (40%)
  blocking collectives  453 us (23%)
  waiting for transfers between devices  361 us (19%)
  local copies, waits for them, and re-layouts  158 us (8%)
  other arithmetic  144 us (7%)
    psum x1, blocking collectives, local(): lax.psum((shares[0], shares[1], shares[2], shares[3], shares[4], shares[5...  383 us
    dot_general x10, matrix products, block_scores(): jnp.einsum('qhd,khd->hqk', q_heads, key_block, preferred_element_type=jnp...  209 us
    reduce_sum x4, other arithmetic, attention_step(): total_exp = total_exp * factor + weights.sum(-1)  92.8 us
    dot_general x4, matrix products, grad_step(): jnp.einsum('hqk,khd->qhd', dscores, key_block, preferred_element_type=jnp...  87.1 us
    dot_general x4, matrix products, attention_step(): jnp.einsum('hqk,khd->qhd', weights.astype(jnp.bfloat16), value_block, pre...  79 us
    unnamed x183, local copies, waits for them, and re-layouts  69.6 us
    dot_general x2, matrix products, grad_step(): jnp.einsum('qhd,khd->hqk', g_heads, value_block, preferred_element_type=j...  62.6 us
    dot_general x11, matrix products, forward_dot(): return jnp.dot(left, right, preferred_element_type=jnp.float32)  62.6 us
  transfers between devices with their start and end apart: 30, of which 12 were waited for; matrix products, arithmetic and copies ran while one was open for 55% of the time, Pallas kernels for 0%

commit v1 on v0

v1 whole, which is shorter than its diff:
```python
import functools
import math

import jax
import jax.numpy as jnp
from jax import lax
from jax.experimental import pallas as pl
from jax.experimental.pallas import tpu as pltpu
from jax.sharding import PartitionSpec as P

HEADS = 12
HEAD = 64
SCALE = 0.125
EPS = 1e-06
BIG = 1e30
LN2 = math.log(2.0)
QSCALE = SCALE * math.log2(math.e)
PART0 = 16
SEGS = 16
BF = jnp.bfloat16
F32 = jnp.float32
MIB = 1 << 20
ALL = ("fsdp", "parts", "ctx")


def nn(a, b):
    return lax.dot_general(a, b, (((1,), (0,)), ((), ())), preferred_element_type=F32)


def nt(a, b):
    return lax.dot_general(a, b, (((1,), (1,)), ((), ())), preferred_element_type=F32)


def tn(a, b):
    return lax.dot_general(a, b, (((0,), (0,)), ((), ())), preferred_element_type=F32)


def lanes(shape):
    return lax.broadcasted_iota(jnp.int32, shape, len(shape) - 1)


def params(mib):
    return pltpu.CompilerParams(vmem_limit_bytes=mib * MIB)


def cost(flops, moved, exps=0):
    return pl.CostEstimate(flops=int(flops), bytes_accessed=int(moved), transcendentals=int(exps))


def rms_scale(h):
    return lax.rsqrt(jnp.mean(h * h, axis=-1, keepdims=True) + EPS)


def norm_back(h, gain, dn):
    r = rms_scale(h)
    t = dn * gain
    hr = h * r
    dh = r * (t - hr * jnp.mean(t * hr, axis=-1, keepdims=True))
    return dh, jnp.sum(dn * hr, axis=0, keepdims=True)


def with_parts(base, value):
    spot = lanes(base.shape) % HEAD
    hi = value.astype(BF)
    rest = value - hi.astype(F32)
    mid = rest.astype(BF)
    low = (rest - mid.astype(F32)).astype(BF)
    return jnp.where(
        spot == PART0, hi, jnp.where(spot == PART0 + 1, mid, jnp.where(spot == PART0 + 2, low, base))
    )


def pair_of(own, other):
    left = lanes(own.shape) < HEAD
    return jnp.where(left, own, other), jnp.where(left, other, own)


def forward_block(lo, n, diag, q_ref, qa_ref, kx, vx, o_ref, lse_ref, chunk):
    q = q_ref[...]
    rows = q.shape[0]
    left = lanes(q.shape) < HEAD
    sides = pair_of(q, qa_ref[...])
    scores, tops, accs = [], [], []
    for h in range(2):
        found = []
        for c in range(0, n, chunk):
            s = nt(sides[h], kx[h, pl.ds(lo + c, chunk), :])
            if diag and c + chunk > n - rows:
                r = lax.broadcasted_iota(jnp.int32, s.shape, 0) + (n - rows - c)
                s = jnp.where(lanes(s.shape) <= r, s, -BIG)
            found.append(s)
        scores.append(found)
    for h in range(2):
        top = functools.reduce(jnp.maximum, [jnp.max(s, axis=1, keepdims=True) for s in scores[h]])
        acc = None
        for i, s in enumerate(scores[h]):
            p = jnp.exp2(s - top).astype(BF)
            term = nn(p, vx[h, pl.ds(lo + i * chunk, chunk), :])
            acc = term if acc is None else acc + term
        accs.append(acc)
        tops.append(top)
    wide = jnp.where(left, accs[0], accs[1])
    total = jnp.where(left, accs[1], accs[0])
    o_ref[...] = (wide / pltpu.roll(total, HEAD, 1)).astype(o_ref.dtype)
    lse_ref[...] = jnp.where(left, tops[1], tops[0]) + jnp.log2(total)


def forward_prep(k_ref, v_ref, ka_ref, kx, vx):
    kx[0], kx[1] = pair_of(k_ref[...], ka_ref[...])
    v = v_ref[...]
    vx[0], vx[1] = pair_of(v, jnp.ones_like(v))


def backward_prep(k_ref, v_ref, ka_ref, kx, vx, km, dk_acc, dv_acc):
    k, v = k_ref[...], v_ref[...]
    spot = lanes(v.shape) % HEAD
    neg = jnp.where((spot >= PART0) & (spot < PART0 + 3), -1.0, 0.0).astype(BF)
    kx[0], kx[1] = pair_of(k, ka_ref[...])
    vx[0], vx[1] = pair_of(v, neg)
    km[0], km[1] = pair_of(k, jnp.zeros_like(k))
    dk_acc[...] = jnp.zeros_like(dk_acc)
    dv_acc[...] = jnp.zeros_like(dv_acc)


def backward_block(
    lo, n, diag, q_ref, do_ref, o_ref, lse_ref, qa_ref, kx, vx, km, dq_ref, dk_acc, dv_acc, chunk
):
    q, do = q_ref[...], do_ref[...]
    rows = q.shape[0]
    left = lanes(q.shape) < HEAD
    product = do.astype(F32) * o_ref[...].astype(F32)
    first = jnp.sum(jnp.where(left, product, 0.0), axis=1, keepdims=True)
    second = jnp.sum(jnp.where(left, 0.0, product), axis=1, keepdims=True)
    delta = jnp.where(left, second, first)
    zero = jnp.zeros_like(q)
    qx = pair_of(q, with_parts(qa_ref[...], lse_ref[...]))
    dx = pair_of(do, with_parts(zero, delta))
    qm = pair_of(q, zero)
    dm = pair_of(do, zero)
    dq = None
    for c in range(0, n, chunk):
        at = pl.ds(lo + c, chunk)
        dk = dv = None
        for h in range(2):
            st = nt(kx[h, at, :], qx[h])
            if diag and c + chunk > n - rows:
                r = lax.broadcasted_iota(jnp.int32, st.shape, 0) + (c - (n - rows))
                st = jnp.where(r <= lanes(st.shape), st, -BIG)
            pt = jnp.exp2(st)
            dp = nt(vx[h, at, :], dx[h])
            ds = (pt * dp).astype(BF)
            tv, tk, tq = nn(pt.astype(BF), dm[h]), nn(ds, qm[h]), tn(ds, km[h, at, :])
            dv = tv if dv is None else dv + tv
            dk = tk if dk is None else dk + tk
            dq = tq if dq is None else dq + tq
        dv_acc[at, :] += dv
        dk_acc[at, :] += dk
    dq_ref[...] = (dq * SCALE).astype(dq_ref.dtype)


def cross_forward_kernel(q_ref, k_ref, v_ref, qa_ref, ka_ref, o_ref, lse_ref, kx, vx):
    @pl.when(pl.program_id(1) == 0)
    def _():
        forward_prep(k_ref, v_ref, ka_ref, kx, vx)

    keys = k_ref.shape[0]
    forward_block(0, keys, False, q_ref, qa_ref, kx, vx, o_ref, lse_ref, math.gcd(512, keys))


def cross_forward(q, kv, qa, ka):
    rows, width = q.shape
    keys = kv.shape[0]
    block = min(512, rows)
    pairs = width // 128
    row = pl.BlockSpec((block, 128), lambda h, i: (i, h))
    return pl.pallas_call(
        cross_forward_kernel,
        grid=(pairs, rows // block),
        in_specs=[
            row,
            pl.BlockSpec((keys, 128), lambda h, i: (0, h)),
            pl.BlockSpec((keys, 128), lambda h, i: (0, h + pairs)),
            pl.BlockSpec((block, 128), lambda h, i: (i, 0)),
            pl.BlockSpec((keys, 128), lambda h, i: (0, 0)),
        ],
        out_specs=[row, row],
        out_shape=[
            jax.ShapeDtypeStruct((rows, width), BF),
            jax.ShapeDtypeStruct((rows, width), F32),
        ],
        scratch_shapes=[pltpu.VMEM((2, keys, 128), BF)] * 2,
        compiler_params=params(48),
        cost_estimate=cost(16 * rows * keys * width, 8 * rows * width, rows * keys * 12),
        name="cross_forward",
    )(q, kv, kv, qa, ka)


def cross_backward_kernel(
    q_ref, k_ref, v_ref, do_ref, o_ref, lse_ref, qa_ref, ka_ref,
    dq_ref, dk_ref, dv_ref, kx, vx, km, dk_acc, dv_acc,
):
    @pl.when(pl.program_id(1) == 0)
    def _():
        backward_prep(k_ref, v_ref, ka_ref, kx, vx, km, dk_acc, dv_acc)

    keys = k_ref.shape[0]
    backward_block(
        0, keys, False, q_ref, do_ref, o_ref, lse_ref, qa_ref, kx, vx, km,
        dq_ref, dk_acc, dv_acc, math.gcd(512, keys),
    )

    @pl.when(pl.program_id(1) == pl.num_programs(1) - 1)
    def _():
        dk_ref[...] = (dk_acc[...] * LN2).astype(BF)
        dv_ref[...] = dv_acc[...].astype(BF)


def cross_backward(q, kv, do, o, lse, qa, ka):
    rows, width = q.shape
    keys = kv.shape[0]
    block = min(512, rows)
    pairs = width // 128
    row = pl.BlockSpec((block, 128), lambda h, i: (i, h))
    col = pl.BlockSpec((keys, 128), lambda h, i: (0, h))
    return pl.pallas_call(
        cross_backward_kernel,
        grid=(pairs, rows // block),
        in_specs=[
            row,
            col,
            pl.BlockSpec((keys, 128), lambda h, i: (0, h + pairs)),
            row,
            row,
            row,
            pl.BlockSpec((block, 128), lambda h, i: (i, 0)),
            pl.BlockSpec((keys, 128), lambda h, i: (0, 0)),
        ],
        out_specs=[row, col, col],
        out_shape=[
            jax.ShapeDtypeStruct((rows, width), BF),
            jax.ShapeDtypeStruct((keys, width), BF),
            jax.ShapeDtypeStruct((keys, width), BF),
        ],
        scratch_shapes=[pltpu.VMEM((2, keys, 128), BF)] * 3 + [pltpu.VMEM((keys, 128), F32)] * 2,
        compiler_params=params(48),
        cost_estimate=cost(40 * rows * keys * width, 12 * rows * width, rows * keys * 12),
        name="cross_backward",
    )(q, kv, kv, do, o, lse, qa, ka)


def counts_for(blocks, least):
    return list(range(least, min(blocks, 8) + 1))


def grain_of(block):
    return min(256, block)


def needed_blocks(segs, block):
    total = segs.shape[0]
    grain = grain_of(block)
    first = segs.reshape(total // block, block)[:, 0]
    start = jnp.sum((segs[None, :] < first[:, None]).astype(jnp.int32), axis=1)
    ends = (jnp.arange(total // block, dtype=jnp.int32) + 1) * block
    need = (ends - start // grain * grain) // grain
    return jnp.minimum(need, counts_for(total // grain, block // grain)[-1])


def self_forward_kernel(
    count_ref, slot_ref, q_ref, k_ref, v_ref, qa_ref, ka_ref, o_ref, lse_ref, kx, vx
):
    i = pl.program_id(1)
    block = q_ref.shape[0]
    grain = grain_of(block)

    @pl.when(i == 0)
    def _():
        forward_prep(k_ref, v_ref, ka_ref, kx, vx)

    for n in counts_for(k_ref.shape[0] // grain, block // grain):

        @pl.when(count_ref[i] == n)
        def _():
            lo = pl.multiple_of((i + 1) * block - n * grain, grain)
            forward_block(lo, n * grain, True, q_ref, qa_ref, kx, vx, o_ref, lse_ref, grain)


def self_specs(block, total):
    row = pl.BlockSpec((block, 128), lambda h, i, n, s: (i, h))
    col = pl.BlockSpec((total, 128), lambda h, i, n, s: (0, h))
    dealt = pl.BlockSpec((block, 128), lambda h, i, n, s: (s[i], h))
    qa = pl.BlockSpec((block, 128), lambda h, i, n, s: (i, 0))
    ka = pl.BlockSpec((total, 128), lambda h, i, n, s: (0, 0))
    return row, col, dealt, qa, ka


def self_forward(counts, slots, q, k, v, qa, ka, block):
    total, width = q.shape
    row, col, dealt, qas, kas = self_specs(block, total)
    return pl.pallas_call(
        self_forward_kernel,
        grid_spec=pltpu.PrefetchScalarGridSpec(
            num_scalar_prefetch=2,
            grid=(width // 128, total // block),
            in_specs=[row, col, col, qas, kas],
            out_specs=[dealt, row],
            scratch_shapes=[pltpu.VMEM((2, total, 128), BF)] * 2,
        ),
        out_shape=[
            jax.ShapeDtypeStruct((total, width), BF),
            jax.ShapeDtypeStruct((total, width), F32),
        ],
        compiler_params=params(48),
        cost_estimate=cost(8 * total * total * width, 8 * total * width, total * total * 3),
        name="self_forward",
    )(counts, slots, q, k, v, qa, ka)


def self_backward_kernel(
    count_ref, slot_ref, q_ref, k_ref, v_ref, do_ref, o_ref, lse_ref, qa_ref, ka_ref,
    dq_ref, dk_ref, dv_ref, kx, vx, km, dk_acc, dv_acc,
):
    i = pl.program_id(1)
    block = q_ref.shape[0]
    grain = grain_of(block)

    @pl.when(i == 0)
    def _():
        backward_prep(k_ref, v_ref, ka_ref, kx, vx, km, dk_acc, dv_acc)

    for n in counts_for(k_ref.shape[0] // grain, block // grain):

        @pl.when(count_ref[i] == n)
        def _():
            lo = pl.multiple_of((i + 1) * block - n * grain, grain)
            backward_block(
                lo, n * grain, True, q_ref, do_ref, o_ref, lse_ref, qa_ref, kx, vx, km,
                dq_ref, dk_acc, dv_acc, grain,
            )

    @pl.when(i == pl.num_programs(1) - 1)
    def _():
        dk_ref[...] = (dk_acc[...] * LN2).astype(BF)
        dv_ref[...] = dv_acc[...].astype(BF)


def self_backward(counts, slots, q, k, v, do, o, lse, qa, ka, block):
    total, width = q.shape
    row, col, dealt, qas, kas = self_specs(block, total)
    return pl.pallas_call(
        self_backward_kernel,
        grid_spec=pltpu.PrefetchScalarGridSpec(
            num_scalar_prefetch=2,
            grid=(width // 128, total // block),
            in_specs=[row, col, col, dealt, dealt, row, qas, kas],
            out_specs=[row, col, col],
            scratch_shapes=[pltpu.VMEM((2, total, 128), BF)] * 3
            + [pltpu.VMEM((total, 128), F32)] * 2,
        ),
        out_shape=[jax.ShapeDtypeStruct((total, width), BF)] * 3,
        compiler_params=params(48),
        cost_estimate=cost(20 * total * total * width, 12 * total * width, total * total * 3),
        name="self_backward",
    )(counts, slots, q, k, v, do, o, lse, qa, ka)


def qkv_kernel(order_ref, x_ref, g_ref, w_ref, n_ref, q_ref, k_ref, v_ref):
    x = x_ref[...].astype(F32)
    n = (x * rms_scale(x) * g_ref[...]).astype(BF)
    n_ref[...] = n
    width = q_ref.shape[1]
    out = nn(n, w_ref[...])
    q_ref[...] = (out[:, :width] * QSCALE).astype(BF)
    k_ref[...] = out[:, width : 2 * width].astype(BF)
    v_ref[...] = out[:, 2 * width :].astype(BF)


def qkv_forward(order, x, gain, w, block):
    total, dim = x.shape
    width = w.shape[1] // 3
    here = lambda i, o: (o[i], 0)
    whole = lambda i, o: (0, 0)
    return pl.pallas_call(
        qkv_kernel,
        grid_spec=pltpu.PrefetchScalarGridSpec(
            num_scalar_prefetch=1,
            grid=(total // block,),
            in_specs=[
                pl.BlockSpec((block, dim), lambda i, o: (i, 0)),
                pl.BlockSpec((1, dim), whole),
                pl.BlockSpec(w.shape, whole),
            ],
            out_specs=[pl.BlockSpec((block, dim), here)] + [pl.BlockSpec((block, width), here)] * 3,
        ),
        out_shape=[jax.ShapeDtypeStruct((total, dim), BF)]
        + [jax.ShapeDtypeStruct((total, width), BF)] * 3,
        compiler_params=params(48),
        cost_estimate=cost(6 * total * dim * width, 8 * total * dim),
        name="qkv_forward",
    )(order, x, gain, w)


def after_self_kernel(x_ref, o_ref, wo_ref, g_ref, wq_ref, h_ref, n_ref, q_ref, s_ref):
    x = x_ref[...].astype(F32)
    a = nn(o_ref[...], wo_ref[...])
    h = x + a
    h_ref[...] = h
    n = (h * rms_scale(h) * g_ref[...]).astype(BF)
    n_ref[...] = n
    q_ref[...] = (nn(n, wq_ref[...]) * QSCALE).astype(BF)

    @pl.when(pl.program_id(0) == 0)
    def _():
        s_ref[...] = jnp.zeros_like(s_ref)

    s_ref[0:1, :] += jnp.sum(x * x, axis=0, keepdims=True)
    s_ref[1:2, :] += jnp.sum(a * a, axis=0, keepdims=True)


def after_self(x, o, wo, gain, w2):
    rows, dim = x.shape
    block = min(256, rows)
    line = lambda i: (i, 0)
    whole = lambda i: (0, 0)
    return pl.pallas_call(
        after_self_kernel,
        grid=(rows // block,),
        in_specs=[
            pl.BlockSpec((block, dim), line),
            pl.BlockSpec((block, o.shape[1]), line),
            pl.BlockSpec(wo.shape, whole),
            pl.BlockSpec((1, dim), whole),
            pl.BlockSpec((dim, dim), lambda i: (0, 1)),
        ],
        out_specs=[
            pl.BlockSpec((block, dim), line),
            pl.BlockSpec((block, dim), line),
            pl.BlockSpec((block, dim), line),
            pl.BlockSpec((8, dim), whole),
        ],
        out_shape=[
            jax.ShapeDtypeStruct((rows, dim), F32),
            jax.ShapeDtypeStruct((rows, dim), BF),
            jax.ShapeDtypeStruct((rows, dim), BF),
            jax.ShapeDtypeStruct((8, dim), F32),
        ],
        compiler_params=params(48),
        cost_estimate=cost(4 * rows * dim * dim, 14 * rows * dim),
        name="after_self",
    )(x, o, wo, gain, w2)


GELU_C = math.sqrt(2.0 / math.pi)
GELU_A = 0.044715


def mlp_kernel(
    o_ref, h1_ref, wc_ref, g_ref, t_ref, wg_ref, wu_ref, wd_ref,
    y_ref, dh_ref, do_ref, gu_ref, gd_ref, gc_ref, s_ref,
    n_scr, h_scr, m_scr, dn_scr, hid_scr, du_scr, dw_scr,
):
    j = pl.program_id(0)
    rows = o_ref.shape[0]
    step = min(256, rows)
    spans = [pl.ds(r, step) for r in range(0, rows, step)]
    gain = g_ref[...]

    @pl.when(j == 0)
    def _():
        total = None
        for at in spans:
            c = nn(o_ref[at, :], wc_ref[...])
            h = h1_ref[at, :] + c
            h_scr[at, :] = h
            n_scr[at, :] = (h * rms_scale(h) * gain).astype(BF)
            part = jnp.sum(c * c, axis=0, keepdims=True)
            total = part if total is None else total + part
        s_ref[...] = jnp.zeros_like(s_ref)
        s_ref[0:1, :] = total
        m_scr[...] = jnp.zeros_like(m_scr)
        dn_scr[...] = jnp.zeros_like(dn_scr)

    wg, wu, wd = wg_ref[...], wu_ref[...], wd_ref[...]
    width = wg.shape[1]
    for at in spans:
        n = n_scr[at, :]
        u = nn(n, wg)
        w = nn(n, wu)
        dhid = nt(t_ref[at, :], wd)
        square = u * u
        th = jnp.tanh(GELU_C * u * (1.0 + GELU_A * square))
        half = 0.5 * (1.0 + th)
        gel = u * half
        slope = half + 0.5 * u * (1.0 - th * th) * (GELU_C * (1.0 + 3.0 * GELU_A * square))
        hid = (gel * w).astype(BF)
        du = (dhid * w * slope).astype(BF)
        dw = (dhid * gel).astype(BF)
        hid_scr[at, :] = hid
        du_scr[at, :] = du
        dw_scr[at, :] = dw
        m_scr[at, :] += nn(hid, wd)
        dn_scr[at, :] += nt(du, wg) + nt(dw, wu)
    gd_ref[...] = tn(hid_scr[...], t_ref[...]).astype(BF)
    gu_ref[:, :width] = tn(n_scr[...], du_scr[...]).astype(BF)
    gu_ref[:, width:] = tn(n_scr[...], dw_scr[...]).astype(BF)

    @pl.when(j == pl.num_programs(0) - 1)
    def _():
        total = gains = None
        for at in spans:
            h = h_scr[at, :]
            y = h + m_scr[at, :]
            y_ref[at, :] = y.astype(BF)
            dh, dg = norm_back(h, gain, dn_scr[at, :])
            dh = dh + t_ref[at, :].astype(F32)
            dh_ref[at, :] = dh
            dc = dh.astype(BF)
            n_scr[at, :] = dc
            do_ref[at, :] = nt(dc, wc_ref[...]).astype(BF)
            part = jnp.sum(y * y, axis=0, keepdims=True)
            total = part if total is None else total + part
            gains = dg if gains is None else gains + dg
        gc_ref[...] = tn(o_ref[...], n_scr[...]).astype(BF)
        s_ref[1:2, :] = total
        s_ref[2:3, :] = gains


def feed_forward(o, h1, w2, gain, cot, w3, wd):
    rows, dim = o.shape
    hidden = wd.shape[0]
    width = 512
    steps = hidden // width
    whole = lambda j: (0, 0)
    once = pl.Buffered(1)
    full = pl.BlockSpec((rows, dim), whole, pipeline_mode=once)
    return pl.pallas_call(
        mlp_kernel,
        grid=(steps,),
        in_specs=[
            full,
            full,
            pl.BlockSpec((dim, dim), lambda j: (0, 4), pipeline_mode=once),
            pl.BlockSpec((1, dim), whole),
            full,
            pl.BlockSpec((dim, width), lambda j: (0, j)),
            pl.BlockSpec((dim, width), lambda j: (0, j + steps)),
            pl.BlockSpec((width, dim), lambda j: (j, 0)),
        ],
        out_specs=[
            full,
            full,
            full,
            pl.BlockSpec((dim, 2 * width), lambda j: (0, j)),
            pl.BlockSpec((width, dim), lambda j: (j, 0)),
            pl.BlockSpec((dim, dim), whole, pipeline_mode=once),
            pl.BlockSpec((8, dim), whole),
        ],
        out_shape=[
            jax.ShapeDtypeStruct((rows, dim), BF),
            jax.ShapeDtypeStruct((rows, dim), F32),
            jax.ShapeDtypeStruct((rows, dim), BF),
            jax.ShapeDtypeStruct((dim, 2 * hidden), BF),
            jax.ShapeDtypeStruct((hidden, dim), BF),
            jax.ShapeDtypeStruct((dim, dim), BF),
            jax.ShapeDtypeStruct((8, dim), F32),
        ],
        scratch_shapes=[
            pltpu.VMEM((rows, dim), BF),
            pltpu.VMEM((rows, dim), F32),
            pltpu.VMEM((rows, dim), F32),
            pltpu.VMEM((rows, dim), F32),
            pltpu.VMEM((rows, width), BF),
            pltpu.VMEM((rows, width), BF),
            pltpu.VMEM((rows, width), BF),
        ],
        compiler_params=params(60),
        cost_estimate=cost(18 * rows * dim * hidden + 6 * rows * dim * dim, 40 * MIB, rows * hidden),
        name="feed_forward",
    )(o, h1, w2, gain, cot, w3, w3, wd)


def before_self_kernel(
    dq_ref, wq_ref, h_ref, dh_ref, g_ref, wo_ref, d1_ref, da_ref, do_ref, s_ref
):
    dn = nt(dq_ref[...], wq_ref[...])
    dh, dg = norm_back(h_ref[...], g_ref[...], dn)
    d1 = dh_ref[...] + dh
    d1_ref[...] = d1
    da = d1.astype(BF)
    da_ref[...] = da
    do_ref[...] = nt(da, wo_ref[...]).astype(BF)

    @pl.when(pl.program_id(0) == 0)
    def _():
        s_ref[...] = jnp.zeros_like(s_ref)

    s_ref[0:1, :] += dg


def before_self(dq, w2, h1, dh2, gain, wo):
    rows, dim = dq.shape
    block = min(256, rows)
    line = lambda i: (i, 0)
    whole = lambda i: (0, 0)
    row = pl.BlockSpec((block, dim), line)
    return pl.pallas_call(
        before_self_kernel,
        grid=(rows // block,),
        in_specs=[
            row,
            pl.BlockSpec((dim, dim), lambda i: (0, 1)),
            row,
            row,
            pl.BlockSpec((1, dim), whole),
            pl.BlockSpec(wo.shape, whole),
        ],
        out_specs=[
            row,
            row,
            pl.BlockSpec((block, wo.shape[0]), line),
            pl.BlockSpec((8, dim), whole),
        ],
        out_shape=[
            jax.ShapeDtypeStruct((rows, dim), F32),
            jax.ShapeDtypeStruct((rows, dim), BF),
            jax.ShapeDtypeStruct((rows, wo.shape[0]), BF),
            jax.ShapeDtypeStruct((8, dim), F32),
        ],
        compiler_params=params(48),
        cost_estimate=cost(4 * rows * dim * dim, 18 * rows * dim),
        name="before_self",
    )(dq, w2, h1, dh2, gain, wo)


def qkv_back_kernel(slot_ref, dq_ref, dk_ref, dv_ref, w_ref, n_ref, x_ref, dn_ref, g_ref, acc, s_acc):
    i = pl.program_id(0)
    d = jnp.concatenate([dq_ref[...], dk_ref[...], dv_ref[...]], axis=1)
    dn = nt(d, w_ref[...])
    dn_ref[...] = dn.astype(BF)
    x = x_ref[...].astype(F32)
    dg = jnp.sum(dn * (x * rms_scale(x)), axis=0, keepdims=True)
    term = tn(n_ref[...], d)

    @pl.when(i == 0)
    def _():
        acc[...] = term
        s_acc[...] = jnp.zeros_like(s_acc)
        s_acc[0:1, :] = dg

    @pl.when(i > 0)
    def _():
        acc[...] += term
        s_acc[0:1, :] += dg

    @pl.when(i == pl.num_programs(0) - 1)
    def _():
        width = acc.shape[1]
        g_ref[:, :width] = acc[...].astype(BF)
        g_ref[:, width:] = jnp.broadcast_to(s_acc[0:1, :], (128, s_acc.shape[1])).T.astype(BF)


def qkv_backward(slots, dq, dk, dv, w, n, x, block):
    total, width = dq.shape
    dim = n.shape[1]
    row = pl.BlockSpec((block, width), lambda i, s: (i, 0))
    dealt = pl.BlockSpec((block, dim), lambda i, s: (s[i], 0))
    whole = lambda i, s: (0, 0)
    return pl.pallas_call(
        qkv_back_kernel,
        grid_spec=pltpu.PrefetchScalarGridSpec(
            num_scalar_prefetch=1,
            grid=(total // block,),
            in_specs=[
                row,
                row,
                row,
                pl.BlockSpec(w.shape, whole),
                pl.BlockSpec((block, dim), lambda i, s: (i, 0)),
                dealt,
            ],
            out_specs=[dealt, pl.BlockSpec((dim, 3 * width + 128), whole)],
            scratch_shapes=[pltpu.VMEM((dim, 3 * width), F32), pltpu.VMEM((8, dim), F32)],
        ),
        out_shape=[
            jax.ShapeDtypeStruct((total, dim), BF),
            jax.ShapeDtypeStruct((dim, 3 * width + 128), BF),
        ],
        compiler_params=params(48),
        cost_estimate=cost(12 * total * dim * width, 10 * total * dim),
        name="qkv_backward",
    )(slots, dq, dk, dv, w, n, x)


def turned(n, k):
    return [(i, (i + k) % n) for i in range(n)]


def rows_of(array, index, count):
    size = array.shape[0] // count
    return lax.dynamic_slice_in_dim(array, index * size, size, 0)


def assemble_kernel(place_ref, near_ref, far_ref, w_ref):
    z, core = place_ref[0], place_ref[1]
    count, size = near_ref.shape[0], near_ref.shape[1]
    for d in range(count):
        base = lax.rem(z - d + count, count) * (2 * size)
        w_ref[pl.ds(pl.multiple_of(base + core * size, 16), size), :] = near_ref[d]
        w_ref[pl.ds(pl.multiple_of(base + (1 - core) * size, 16), size), :] = far_ref[d]


def gather_first(own, z, part, n_fsdp, n_parts):
    size = own.shape[0] // 2
    if n_parts % 2 or size % 16:
        return lax.all_gather(own, "fsdp", axis=0, tiled=True)
    core = part % 2
    mine = lax.dynamic_slice_in_dim(own, core * size, size, 0)
    near = jnp.stack(
        [mine] + [lax.ppermute(mine, "fsdp", turned(n_fsdp, d)) for d in range(1, n_fsdp)]
    )
    far = lax.ppermute(near, "parts", [(i, i ^ 1) for i in range(n_parts)])
    return pl.pallas_call(
        assemble_kernel,
        in_specs=[
            pl.BlockSpec(memory_space=pltpu.SMEM),
            pl.BlockSpec(memory_space=pltpu.VMEM),
            pl.BlockSpec(memory_space=pltpu.VMEM),
        ],
        out_specs=pl.BlockSpec(memory_space=pltpu.VMEM),
        out_shape=jax.ShapeDtypeStruct((n_fsdp * own.shape[0], own.shape[1]), BF),
        compiler_params=params(32),
        name="assemble",
    )(jnp.stack([z, core]).astype(jnp.int32), near, far)


def sum_everywhere(value, sizes):
    for axis, size in sizes:
        bit = 1
        while bit < size:
            value = value + lax.ppermute(value, axis, [(i, i ^ bit) for i in range(size)])
            bit *= 2
    return value


def scatter_sum(grad):
    part = lax.psum_scatter(grad, ALL, scatter_dimension=0, tiled=True)
    return lax.all_gather(part, ("parts", "ctx"), axis=0, tiled=True)


def local(
    mesh_shape,
    decoder_in,
    encoder_out,
    segment_ids,
    block_order,
    prompt_len,
    self_query,
    self_key,
    self_value,
    self_output,
    cross_query,
    cross_key,
    cross_value,
    cross_output,
    gate_in,
    up_in,
    down_out,
    norm_self,
    norm_cross,
    norm_mlp,
    cotangent,
):
    n_parts, n_ctx, n_fsdp = mesh_shape
    part, place, z = lax.axis_index("parts"), lax.axis_index("ctx"), lax.axis_index("fsdp")
    plane, n_plane = part * n_ctx + place, n_parts * n_ctx
    x_own, enc_own = decoder_in[0], encoder_out[0]
    rows, dim = x_own.shape
    segs, order = segment_ids[0], block_order[0]
    total = segs.shape[0]
    slots_total = order.shape[0]
    block = total // slots_total
    per_dev = slots_total // n_ctx
    enc_rows = enc_own.shape[0]
    keys = enc_rows * n_ctx
    hidden = down_out.shape[0] * n_fsdp
    heads_here = 2 * -(-HEADS // (2 * n_ctx))
    width = heads_here * HEAD
    padded = width * n_ctx

    ring = (place + jnp.arange(n_ctx, dtype=jnp.int32)) % n_ctx
    order_here = jnp.roll(order, -per_dev * place)
    slots = jnp.argsort(order_here).astype(jnp.int32)
    counts = needed_blocks(segs, block)

    def gather_ctx(value):
        pieces = [value] + [lax.ppermute(value, "ctx", turned(n_ctx, -k)) for k in range(1, n_ctx)]
        return jnp.concatenate(pieces, axis=0)

    x_all = gather_ctx(x_own)

    def own_heads(w):
        w = jnp.pad(w, ((0, 0), (0, padded - dim)))
        return lax.dynamic_slice_in_dim(w, place * width, width, 1)

    w1 = gather_first(
        jnp.concatenate([own_heads(self_query), own_heads(self_key), own_heads(self_value)], axis=1),
        z, part, n_fsdp, n_parts,
    )
    gains = lax.all_gather(
        jnp.stack([norm_self, norm_cross, norm_mlp], axis=1), "fsdp", axis=0, tiled=True
    ).astype(F32)
    gain_self, gain_cross, gain_mlp = (gains[:, i][None] for i in range(3))
    w2 = lax.all_gather(
        jnp.concatenate(
            [
                rows_of(w, plane, n_plane)
                for w in (self_output, cross_query, cross_key, cross_value, cross_output)
            ],
            axis=1,
        ),
        ALL, axis=0, tiled=True,
    )
    enc_all = gather_ctx(enc_own)
    w3 = lax.all_gather(
        jnp.concatenate([rows_of(gate_in, plane, n_plane), rows_of(up_in, plane, n_plane)], axis=1),
        ALL, axis=0, tiled=True,
    )
    wd = lax.all_gather(rows_of(down_out, plane, n_plane), ALL, axis=0, tiled=True)

    n1, q, k, v = qkv_forward(order_here, x_all, gain_self, w1, block)
    spot = jnp.arange(128, dtype=jnp.int32)[None, :] % HEAD
    minus = jnp.where((spot >= PART0) & (spot < PART0 + 3), -1.0, 0.0)
    seg_q = jnp.where(spot == segs[:, None], 1.0, 0.0).astype(BF)
    seg_k = jnp.where((spot < SEGS) & (spot != segs[:, None]), -BIG, minus).astype(BF)
    o1, lse1 = self_forward(counts, slots, q, k, v, seg_q, seg_k, block)
    pieces = [
        lax.ppermute(o1[i * rows : (i + 1) * rows], "ctx", turned(n_ctx, i)) if i else o1[:rows]
        for i in range(n_ctx)
    ]
    o_cat = jnp.concatenate(pieces, axis=1)
    turn = (place - jnp.arange(n_ctx, dtype=jnp.int32)) % n_ctx
    wo = jnp.pad(w2[:, :dim], ((0, padded - dim), (0, 0))).reshape(n_ctx, width, dim)
    wo = jnp.take(wo, turn, axis=0).reshape(padded, dim)
    h1, n2, q2, stat1 = after_self(x_own, o_cat, wo, gain_cross, w2)

    w_kv = w2[:, 2 * dim : 4 * dim]
    kv2 = nn(enc_all, w_kv).astype(BF)
    where_key = (ring[:, None] * enc_rows + jnp.arange(enc_rows, dtype=jnp.int32)).reshape(-1, 1)
    len_q = jnp.where(spot == 0, jnp.ones((rows, 1), F32), 0.0).astype(BF)
    len_k = jnp.where((spot == 0) & (where_key >= prompt_len[0]), -BIG, minus).astype(BF)
    o2, lse2 = cross_forward(q2, kv2, len_q, len_k)

    layer_out, dh2, do2, g_gu, g_down, g_co, stat2 = feed_forward(
        o2, h1, w2, gain_mlp, cotangent[0], w3, wd
    )
    sum_gu = scatter_sum(g_gu)
    sum_down = scatter_sum(g_down)

    dq2, dk2, dv2 = cross_backward(q2, kv2, do2, o2, lse2, len_q, len_k)
    dh1, da, do1, stat3 = before_self(dq2, w2, h1, dh2, gain_cross, wo)
    do_pieces = [
        lax.ppermute(do1[:, i * width : (i + 1) * width], "ctx", turned(n_ctx, -i))
        if i
        else do1[:, :width]
        for i in range(n_ctx)
    ]
    do_all = jnp.concatenate(do_pieces, axis=0)
    g_cq = tn(n2, dq2)
    g_wo = tn(o_cat, da).reshape(n_ctx, width, dim)
    g_wo = jnp.take(g_wo, turn, axis=0).reshape(padded, dim)[:dim]
    g_ck, g_cv = tn(enc_all, dk2), tn(enc_all, dv2)
    sum_mid = scatter_sum(
        jnp.concatenate([g.astype(BF) for g in (g_wo, g_cq, g_ck, g_cv, g_co)], axis=1)
    )
    d_enc = nt(dk2, w2[:, 2 * dim : 3 * dim]) + nt(dv2, w2[:, 3 * dim : 4 * dim])
    enc_grad = d_enc[:enc_rows]
    for i in range(1, n_ctx):
        piece = d_enc[i * enc_rows : (i + 1) * enc_rows].astype(BF)
        enc_grad = enc_grad + lax.ppermute(piece, "ctx", turned(n_ctx, i)).astype(F32)

    small = jnp.concatenate([stat1[:2], stat2[:3], stat3[:1], jnp.zeros((2, dim), F32)], axis=0)
    small = sum_everywhere(small, (("parts", n_parts), ("ctx", n_ctx), ("fsdp", n_fsdp)))
    entries = float(n_parts * n_ctx * n_fsdp * rows * dim)
    rms_values = jnp.sqrt(jnp.sum(small[:4], axis=1) / entries)
    shard = dim // n_fsdp
    grad_gmlp = lax.dynamic_slice_in_dim(small[4], z * shard, shard)
    grad_gcross = lax.dynamic_slice_in_dim(small[5], z * shard, shard)

    dq, dk, dv = self_backward(counts, slots, q, k, v, do_all, o1, lse1, seg_q, seg_k, block)
    dn1, g_qkv = qkv_backward(slots, dq, dk, dv, w1, n1, x_all, block)
    dn_own = dn1[:rows].astype(F32)
    for i in range(1, n_ctx):
        piece = lax.ppermute(dn1[i * rows : (i + 1) * rows], "ctx", turned(n_ctx, i))
        dn_own = dn_own + piece.astype(F32)
    x32 = x_own.astype(F32)
    d_in, _ = norm_back(x32, gain_self, dn_own)
    decoder_grad = dh1 + d_in
    part_qkv = lax.psum_scatter(g_qkv, ("fsdp", "parts"), scatter_dimension=0, tiled=True)
    sum_qkv = lax.all_gather(part_qkv, "parts", axis=0, tiled=True)
    every = lax.all_gather(sum_qkv, "ctx", axis=0).astype(F32)
    grads_qkv = [
        jnp.concatenate([every[c, :, i * width : (i + 1) * width] for c in range(n_ctx)], axis=1)[:, :dim]
        for i in range(3)
    ]
    grad_gself = jnp.sum(every[:, :, 3 * width], axis=0)

    mids = [sum_mid[:, i * dim : (i + 1) * dim].astype(F32) for i in range(5)]
    steps = sum_gu.reshape(sum_gu.shape[0], hidden // 512, 2, 512).astype(F32)
    grad_gate = steps[:, :, 0].reshape(-1, hidden)
    grad_up = steps[:, :, 1].reshape(-1, hidden)
    return (
        layer_out[None],
        decoder_grad[None],
        enc_grad[None],
        *grads_qkv,
        mids[0],
        mids[1],
        mids[2],
        mids[3],
        mids[4],
        grad_gate,
        grad_up,
        sum_down.astype(F32),
        grad_gself,
        grad_gcross,
        grad_gmlp,
        rms_values,
    )


def solution(mesh):
    rows3 = P(("parts", "fsdp"), "ctx", None)
    group = P(("parts", "fsdp"), None)
    matrix, vector = P("fsdp", None), P("fsdp")
    shape = tuple(mesh.shape[a] for a in ("parts", "ctx", "fsdp"))
    return jax.shard_map(
        functools.partial(local, shape),
        mesh=mesh,
        in_specs=(rows3, rows3, group, group, P(("parts", "fsdp")))
        + (matrix,) * 11
        + (vector,) * 3
        + (rows3,),
        out_specs=(rows3,) * 3 + (matrix,) * 11 + (vector,) * 3 + (P(),),
        check_vma=False,
    )
```

time: 1950 us -> 902 us (0.46)
  matrix products: 788 us -> 42.1 us
  blocking collectives: 453 us -> 68.4 us
  Pallas kernels: 0 us -> 298 us
  other arithmetic: 144 us -> 34.7 us
  local copies, waits for them, and re-layouts: 158 us -> 51.7 us
  starting transfers between devices: 1.76 us -> 30.1 us
    dot_general x61 -> x7, matrix products: 788 us -> 42.1 us  [the longest x4 17.7 us: tn(): lax.dot_general(a, b, (((0,), (0,)), ((), ())), preferred_element_type=F32)]
    psum x2 -> x0, blocking collectives: 430 us -> none  [the longest x1 383 us: local(): lax.psum((shares[0], shares[1], shares[2], shares[3], shares[4], shares[5...]
    pallas_call x0 -> x10, Pallas kernels: none -> 298 us  [the longest x1 80.3 us: cross_backward(): pl.pallas_call(cross_backward_kernel, grid=(pairs, rows // block), in_spe...]
    all_gather x17 -> x5, waiting for transfers between devices: 192 us -> 43.6 us  [the longest x2 31.7 us: scatter_sum(): return lax.all_gather(part, ('parts', 'ctx'), axis=0, tiled=True)]
    ppermute x0 -> x15, waiting for transfers between devices: none -> 117 us  [the longest x2 49.5 us: gather_ctx(): lax.ppermute(value, 'ctx', turned(n_ctx, -k))]
    reduce_sum x7 -> x5, other arithmetic: 97.7 us -> 4.45 us  [the longest x1 3.08 us: norm_back(): dh = r * (t - hr * jnp.mean(t * hr, axis=-1, keepdims=True))]
    reduce_scatter x11 -> x4, waiting for transfers between devices: 109 us -> 194 us  [the longest x3 137 us: scatter_sum(): part = lax.psum_scatter(grad, ALL, scatter_dimension=0, tiled=True)]
    all_gather x2 -> x4, blocking collectives: 6.87 us -> 68.4 us  [the longest x1 23.1 us: local(): lax.all_gather(jnp.stack([norm_self, norm_cross, norm_mlp], axis=1), 'fsd...]
  transfers between devices with their start and end apart: 30 -> 24, of which waited for: 12 -> 13; matrix products, arithmetic and copies ran while one was open for 55% -> 8% of each run, Pallas kernels for 0% -> 18%
where the time goes in v1:
time: 902 us; the launch traced here: 897 us
  waiting for transfers between devices  356 us (39%)
  Pallas kernels  298 us (33%)
  blocking collectives  68.4 us (8%)
  local copies, waits for them, and re-layouts  51.7 us (6%)
  matrix products  42.1 us (5%)
  other arithmetic  34.7 us (4%)
  starting transfers between devices  30.1 us (3%)
  between operations  15.5 us (2%)
    reduce_scatter x3, waiting for transfers between devices, scatter_sum(): part = lax.psum_scatter(grad, ALL, scatter_dimension=0, tiled=True)  137 us
    pallas_call x1, Pallas kernels, cross_backward(): pl.pallas_call(cross_backward_kernel, grid=(pairs, rows // block), in_spe...  80.3 us
    pallas_call x1, Pallas kernels, self_backward(): pl.pallas_call(self_backward_kernel, grid_spec=pltpu.PrefetchScalarGridSp...  74.3 us
    reduce_scatter x1, waiting for transfers between devices, local(): lax.psum_scatter(g_qkv, ('fsdp', 'parts'), scatter_dimension=0, tiled=True)  56.8 us
    ppermute x2, waiting for transfers between devices, gather_ctx(): lax.ppermute(value, 'ctx', turned(n_ctx, -k))  49.5 us
    pallas_call x1, Pallas kernels, feed_forward(): pl.pallas_call(mlp_kernel, grid=(steps,), in_specs=[full, full, pl.BlockS...  45.4 us
    pallas_call x1, Pallas kernels, cross_forward(): pl.pallas_call(cross_forward_kernel, grid=(pairs, rows // block), in_spec...  36.1 us
    all_gather x2, waiting for transfers between devices, scatter_sum(): return lax.all_gather(part, ('parts', 'ctx'), axis=0, tiled=True)  31.7 us
  transfers between devices with their start and end apart: 24, of which 13 were waited for; matrix products, arithmetic and copies ran while one was open for 8% of the time, Pallas kernels for 18%

profile of v1, /device:TPU:9, one launch (start us, length us, event | category | flops | bytes accessed | tf_op | source)
XLA Modules:
  0.0 896.6 jit_solution(6124438820392743101)
XLA Ops:
  16.6 2.4 collective-permute-start.2
  22.6 23.1 %all-gather.1 = bf16[4,192,3]{1,2,0:T(4,128)(2,1)S(1)} all-gather(bf16[1,192,3]{1,2,0:T(4,128)(2,1)S(1)} %maximum_bitcast_fusion), channel_id=1, replica_groups=mesh['parts'=4,'ctx'=2,'fsdp'=4] {'fsdp'}, dimensions={0}, use_global_device_ids=true | all-gather | bytes 5760 | tf_op jit(solution)/shard_map/all_gather | solution.py:809
  51.1 2.3 select_convert_fusion
  54.2 49.5 %collective-permute-done = bf16[1024,768]{1,0:T(8,128)(2,1)} collective-permute-done((bf16[1024,768]{1,0:T(8,128)(2,1)S(1)}, bf16[1024,768]{1,0:T(8,128)(2,1)}, u32[]{:S(2)}, u32[]{:S(2)}) %collective-permute-start) | collective-permute-done | bytes 1572896 | tf_op jit(solution)/shard_map/ppermute | solution.py:796
  103.7 3.3 pad_maximum_fusion.x_ref
  107.0 8.1 qkv_forward.1
  116.3 21.9 %self_forward.1 = (bf16[2048,384]{1,0:T(8,128)(2,1)S(1)}, f32[2048,384]{1,0:T(8,128)}) custom-call(s32[4]{0:T(128)S(1)} %fusion.24.count_ref, s32[4]{0:T(128)S(1)} %get-tuple-element.50.slot_ref, bf16[2048,384]{1,0:T(8,128)(2,1)S(1)} %get-tuple-element.51.q_ref, bf16[2048,384]{1,0:T(8,128)(2,1)S(1)} %get-tuple-element.52.k_ref, ...), custom_call_target="tpu_custom_call" | custom-call | flops 12884901888 | bytes 6291456 | tf_op jit(solution)/shard_map/self_forward/pallas_call | solution.py:300
  140.4 1.9 collective-permute-start.5
  142.4 21.7 %collective-permute-done.5 = bf16[1024,384]{1,0:T(8,128)(2,1)S(1)} collective-permute-done((bf16[1024,384]{1,0:T(8,128)(2,1)}, bf16[1024,384]{1,0:T(8,128)(2,1)S(1)}, u32[]{:S(2)}, u32[]{:S(2)}) %collective-permute-start.5) | collective-permute-done | bytes 786464 | tf_op jit(solution)/shard_map/ppermute | solution.py:837
  166.9 1.6 gather_fusion
  170.2 7.5 after_self.1
  178.3 9.6 %convolution_convert_fusion.k_ref.v_ref = bf16[2048,1536]{1,0:T(8,128)(2,1)} fusion(bf16[768,3840]{1,0:T(8,128)(2,1)S(1)} %bitcast.73, bf16[1024,768]{1,0:T(8,128)(2,1)} %collective-permute-done.6, bf16[1024,768]{1,0:T(8,128)(2,1)S(1)} %bitcast.93), kind=kOutput, calls=%fused_computation.2 | convolution fusion | flops 4841275392 | bytes 11796480 | tf_op jit(solution)/shard_map/dot_general | solution.py:27
  188.0 36.1 %cross_forward.1 = (bf16[1024,768]{1,0:T(8,128)(2,1)S(1)}, f32[1024,768]{1,0:T(8,128)}) custom-call(bf16[1024,768]{1,0:T(8,128)(2,1)S(1)} %get-tuple-element.55.q_ref, bf16[2048,1536]{1,0:T(8,128)(2,1)} %convolution_convert_fusion.k_ref.v_ref, bf16[2048,1536]{1,0:T(8,128)(2,1)} %convolution_convert_fusion.k_ref.v_ref, ...), custom_call_target="tpu_custom_call" | custom-call | flops 25769803776 | bytes 6291456 | tf_op jit(solution)/shard_map/cross_forward/pallas_call | solution.py:176
  225.3 11.9 %all-gather.10.cloned.1.call-done.wg_ref.wu_ref = bf16[768,4096]{1,0:T(8,128)(2,1)} async-done(((bf16[24,4096]{1,0:T(8,128)(2,1)}), bf16[768,4096]{1,0:T(8,128)(2,1)}) %all-gather.10.cloned.1.call-update) | async-done | bytes 6291472 | tf_op jit(solution)/shard_map/all_gather | solution.py:824
  237.2 45.4 %feed_forward.1 = (bf16[1024,768]{1,0:T(8,128)(2,1)}, f32[1024,768]{1,0:T(8,128)}, bf16[1024,768]{1,0:T(8,128)(2,1)}, bf16[768,4096]{1,0:T(8,128)(2,1)}, bf16[20...) custom-call(bf16[1024,768]{1,0:T(8,128)(2,1)} %copy-done.23, ...), custom_call_target="tpu_custom_call" | custom-call | flops 32614907904 | bytes 41943040 | tf_op jit(solution)/shard_map/feed_forward/pallas_call | solution.py:536
  285.4 80.3 %cross_backward.1 = (bf16[1024,768]{1,0:T(8,128)(2,1)S(1)}, bf16[2048,768]{1,0:T(8,128)(2,1)}, bf16[2048,768]{1,0:T(8,128)(2,1)}) custom-call(bf16[1024,768]{1,0:T(8,128)(2,1)S(1)} %copy-done.15, bf16[2048,1536]{1,0:T(8,128)(2,1)} %convolution_convert_fusion.k_ref.v_ref, bf16[2048,1536]{1,0:T(8,128)(2,1)} %convolution_convert_fusion.k_ref.v_ref, ...), custom_call_target="tpu_custom_call" | custom-call | flops 64424509440 | bytes 9437184 | tf_op jit(solution)/shard_map/cross_backward/pallas_call | solution.py:225
  365.7 9.2 %before_self.1 = (f32[1024,768]{1,0:T(8,128)}, bf16[1024,768]{1,0:T(8,128)(2,1)S(1)}, bf16[1024,768]{1,0:T(8,128)(2,1)S(1)}, f32[8,768]{1,0:T(8,128)S(1)}) custom-call(bf16[1024,768]{1,0:T(8,128)(2,1)S(1)} %get-tuple-element.61.dq_ref, bf16[768,3840]{1,0:T(8,128)(2,1)} %all-gather.8.cloned.1.call-done.wq_ref.wc_ref, ...), custom_call_target="tpu_custom_call" | custom-call | flops 2415919104 | bytes 14155776 | tf_op jit(solution)/shard_map/before_self/pallas_call | solution.py:606
  375.0 2.5 fusion.29
  377.5 1.9 gather_fusion.1
  380.7 4.6 fusion.13
  385.3 5.4 fusion.12
  390.7 5.3 fusion.11
  400.8 17.7 %collective-permute-done.7 = bf16[1024,384]{1,0:T(8,128)(2,1)S(1)} collective-permute-done((bf16[1024,384]{1,0:T(8,128)(2,1)S(1)}, bf16[1024,384]{1,0:T(8,128)(2,1)S(1)}, u32[]{:S(2)}, u32[]{:S(2)}) %collective-permute-start.7) | collective-permute-done | bytes 786464 | tf_op jit(solution)/shard_map/ppermute | solution.py:862
  419.8 74.3 %self_backward.1 = (bf16[2048,384]{1,0:T(8,128)(2,1)S(1)}, bf16[2048,384]{1,0:T(8,128)(2,1)S(1)}, bf16[2048,384]{1,0:T(8,128)(2,1)S(1)}) custom-call(s32[4]{0:T(128)S(1)} %copy-done.19, s32[4]{0:T(128)S(1)} %copy-done.17, bf16[2048,384]{1,0:T(8,128)(2,1)} %copy-done.20, bf16[2048,384]{1,0:T(8,128)(2,1)} %copy-done.21, bf16[2048,384]{1,0:T(8,128)(2,1)} %copy-done.22, ...), custom_call_target="tpu_custom_call" | custom-call | flops 32212254720 | bytes 9437184 | tf_op jit(solution)/shard_map/self_backward/pallas_call | solution.py:350
  494.1 14.8 %qkv_backward.1 = (bf16[2048,768]{1,0:T(8,128)(2,1)}, bf16[768,1280]{1,0:T(8,128)(2,1)}) custom-call(s32[4]{0:T(128)S(1)} %copy-done.17, bf16[2048,384]{1,0:T(8,128)(2,1)S(1)} %get-tuple-element.66.dq_ref, bf16[2048,384]{1,0:T(8,128)(2,1)S(1)} %get-tuple-element.67.dk_ref, bf16[2048,384]{1,0:T(8,128)(2,1)S(1)} %get-tuple-element.68.dv_ref, ...), custom_call_target="tpu_custom_call" | custom-call | flops 7247757312 | bytes 15728640 | tf_op jit(solution)/shard_map/qkv_backward/pallas_call | solution.py:668
  510.6 7.4 fusion.15
  518.2 7.3 convolution_add_fusion
  530.4 5.4 collective-permute-start.11
  535.8 1.6 collective-permute-done.11
  538.6 23.9 %collective-permute-done.12 = f32[8,768]{1,0:T(8,128)S(1)} collective-permute-done((f32[8,768]{1,0:T(8,128)S(1)}, f32[8,768]{1,0:T(8,128)S(1)}, u32[]{:S(2)}, u32[]{:S(2)}) %collective-permute-start.12) | collective-permute-done | bytes 24608 | tf_op jit(solution)/shard_map/ppermute | solution.py:740
  563.8 1.8 collective-permute-start.8
  566.0 9.3 %collective-permute-start.14 = (f32[8,768]{1,0:T(8,128)S(1)}, f32[8,768]{1,0:T(8,128)S(1)}, u32[]{:S(2)}, u32[]{:S(2)}) collective-permute-start(f32[8,768]{1,0:T(8,128)S(1)} %add.223), channel_id=1, source_target_pairs={{0,2},{1,3},{2,0},{3,1},{4,6},{5,7},{6,4},{7,5},{8,10},{9,11},{10,... | collective-permute-start | bytes 73736 | tf_op jit(solution)/shard_map/ppermute | solution.py:740
  578.5 4.3 fusion.8
  582.8 56.7 %reduce-scatter.9.cloned.1.call-done = bf16[24,4096]{1,0:T(8,128)(2,1)} async-done(((bf16[768,4096]{1,0:T(8,128)(2,1)}), bf16[24,4096]{1,0:T(8,128)(2,1)}) %reduce-scatter.9.cloned.1.call-update) | async-done | bytes 196624 | tf_op jit(solution)/shard_map/reduce_scatter | solution.py:746
  639.6 3.1 fusion.2
  642.7 4.1 fusion.6
  646.8 56.8 %reduce-scatter.5.cloned.1.call-done = bf16[48,1280]{1,0:T(8,128)(2,1)} async-done(((bf16[768,1280]{1,0:T(8,128)(2,1)}), bf16[48,1280]{1,0:T(8,128)(2,1)}) %reduce-scatter.5.cloned.1.call-update) | async-done | bytes 122896 | tf_op jit(solution)/shard_map/reduce_scatter | solution.py:898
  703.6 9.6 %all_gather.34 = bf16[192,1280]{1,0:T(8,128)(2,1)S(1)} all-gather(bf16[48,1280]{1,0:T(8,128)(2,1)} %reduce-scatter.5.cloned.1.call-done), channel_id=1, replica_groups=mesh['parts'=4,'ctx'=2,'fsdp'=4] {'parts'}, dimensions={0}, use_global_device_ids=true | all-gather | bytes 614400 | tf_op jit(solution)/shard_map/all_gather | solution.py:899
  713.2 13.3 %all-gather = bf16[384,1280]{1,0:T(8,128)(2,1)S(1)} all-gather(bf16[192,1280]{1,0:T(8,128)(2,1)S(1)} %all_gather.34), channel_id=2, replica_groups=mesh['parts'=4,'ctx'=2,'fsdp'=4] {'ctx'}, dimensions={0}, use_global_device_ids=true | all-gather | bytes 1474560 | tf_op jit(solution)/shard_map/all_gather | solution.py:900
  730.0 80.6 %reduce-scatter.11.cloned.1.call-done = bf16[64,768]{1,0:T(8,128)(2,1)} async-done(((bf16[2048,768]{1,0:T(8,128)(2,1)}), bf16[64,768]{1,0:T(8,128)(2,1)}) %reduce-scatter.11.cloned.1.call-update) | async-done | bytes 98320 | tf_op jit(solution)/shard_map/reduce_scatter | solution.py:746
  810.7 22.3 %all_gather.39 = bf16[512,768]{1,0:T(8,128)(2,1)S(1)} all-gather(bf16[64,768]{1,0:T(8,128)(2,1)} %reduce-scatter.11.cloned.1.call-done), channel_id=1, replica_groups=mesh['parts'=4,'ctx'=2,'fsdp'=4] {'parts','ctx'}, dimensions={0}, use_global_device_ids=true | all-gather | bytes 884736 | tf_op jit(solution)/shard_map/all_gather | solution.py:747
  834.3 6.9 all-gather.14.cloned.1.call-done
  841.2 3.0 slice_convert_fusion.1
  844.1 24.8 %all-gather.16.cloned.1.call-done = bf16[192,4096]{1,0:T(8,128)(2,1)} async-done(((bf16[24,4096]{1,0:T(8,128)(2,1)}), bf16[192,4096]{1,0:T(8,128)(2,1)}) %all-gather.16.cloned.1.call-update) | async-done | bytes 1572880 | tf_op jit(solution)/shard_map/all_gather | solution.py:747
  868.9 5.5 reshape.188
  874.4 11.9 %slice_reduce_fusion = (f32[192,4,512]{2,1,0:T(4,128)S(1)}, f32[192,4,512]{2,1,0:T(4,128)S(1)}) fusion(f32[192,4,2,512]{3,2,1,0:T(2,128)} %reshape.188), kind=kLoop, calls=%fused_computation.23 | loop fusion | bytes 6291456 | tf_op jit(solution)/shard_map/slice | solution.py:910
  886.3 1.7 copy.71
  888.0 1.7 copy.70
  (219 shorter events, 55.5 us)
Async XLA Ops:
  7.2 14.4 %copy-start.2 = (bf16[1,1024,768]{2,1,0:T(8,128)(2,1)S(1)}, bf16[1,1024,768]{2,1,0:T(8,128)(2,1)}, u32[]{:S(2)}) copy-start(bf16[1,1024,768]{2,1,0:T(8,128)(2,1)} %param.20) | copy-start | bytes 4718596
  7.2 15.3 %copy-start.39 = (bf16[192]{0:T(256)(128)(2,1)S(1)}, bf16[192]{0:T(256)(128)(2,1)}, u32[]{:S(2)}) copy-start(bf16[192]{0:T(256)(128)(2,1)} %param.36) | copy-start | bytes 1156
  7.2 15.3 %copy-start.40 = (bf16[192]{0:T(256)(128)(2,1)S(1)}, bf16[192]{0:T(256)(128)(2,1)}, u32[]{:S(2)}) copy-start(bf16[192]{0:T(256)(128)(2,1)} %param.37) | copy-start | bytes 1156
  7.2 15.3 %copy-start.41 = (bf16[192]{0:T(256)(128)(2,1)S(1)}, bf16[192]{0:T(256)(128)(2,1)}, u32[]{:S(2)}) copy-start(bf16[192]{0:T(256)(128)(2,1)} %param.38) | copy-start | bytes 1156
  7.2 38.6 %copy-start.42 = (s32[1,4]{1,0:T(1,128)S(1)}, s32[1,4]{1,0:T(1,128)}, u32[]{:S(2)}) copy-start(s32[1,4]{1,0:T(1,128)} %param.23) | copy-start | bytes 52
  7.3 40.5 %copy-start.34 = (s32[1,2048]{1,0:T(1,128)S(1)}, s32[1,2048]{1,0:T(1,128)}, u32[]{:S(2)}) copy-start(s32[1,2048]{1,0:T(1,128)} %param.22) | copy-start | bytes 24580
  7.3 158.4 %all-gather.8.cloned.1.call-start = ((), (), s32[]{:S(2)}) async-start(), calls=%async_computation.4 | async-start | bytes 6082560 | tf_op jit(solution)/shard_map/all_gather | solution.py:813
  12.0 213.2 %all-gather.12.cloned.1.call-start = ((), (), s32[]{:S(2)}) async-start(), calls=%async_computation.6 | async-start | bytes 3244032 | tf_op jit(solution)/shard_map/all_gather | solution.py:828
  12.8 224.4 %all-gather.10.cloned.1.call-start = ((), (), s32[]{:S(2)}) async-start(), calls=%async_computation.5 | async-start | bytes 6488064 | tf_op jit(solution)/shard_map/all_gather | solution.py:824
  14.5 503.6 %reduce-scatter.7.cloned.1.call-start = ((), (), s32[]{:S(2)}) async-start(), calls=%async_computation.8 | async-start | bytes 6082560 | tf_op jit(solution)/shard_map/reduce_scatter | solution.py:746
  16.6 33.0 %collective-permute-start.2 = (bf16[96,1152]{1,0:T(8,128)(2,1)S(1)}, bf16[96,1152]{1,0:T(8,128)(2,1)S(1)}, u32[]{:S(2)}, u32[]{:S(2)}) collective-permute-start(bf16[96,1152]{1,0:T(8,128)(2,1)S(1)} %fusion.18), channel_id=1, source_target_pairs={{0,2},{1,3},{2,0},{3,1},{4,6},{5,7},{6,4},{7,5},{8,10},{9,11},{10,... | collective-permute-start | bytes 663560 | tf_op jit(solution)/shard_map/ppermute | solution.py:719
  18.9 30.7 %collective-permute-start.1 = (bf16[96,1152]{1,0:T(8,128)(2,1)S(1)}, bf16[96,1152]{1,0:T(8,128)(2,1)S(1)}, u32[]{:S(2)}, u32[]{:S(2)}) collective-permute-start(bf16[96,1152]{1,0:T(8,128)(2,1)S(1)} %fusion.18), channel_id=1, source_target_pairs={{0,1},{1,2},{2,3},{3,0},{4,5},{5,6},{6,7},{7,4},{8,9},{9,10},{10,1... | collective-permute-start | bytes 663560 | tf_op jit(solution)/shard_map/ppermute | solution.py:719
  18.9 30.7 %collective-permute-start.3 = (bf16[96,1152]{1,0:T(8,128)(2,1)S(1)}, bf16[96,1152]{1,0:T(8,128)(2,1)S(1)}, u32[]{:S(2)}, u32[]{:S(2)}) collective-permute-start(bf16[96,1152]{1,0:T(8,128)(2,1)S(1)} %fusion.18), channel_id=1, source_target_pairs={{0,3},{1,0},{2,1},{3,2},{4,7},{5,4},{6,5},{7,6},{8,11},{9,8},{10,9... | collective-permute-start | bytes 663560 | tf_op jit(solution)/shard_map/ppermute | solution.py:719
  20.4 157.9 %collective-permute-start.6 = (bf16[1024,768]{1,0:T(8,128)(2,1)}, bf16[1024,768]{1,0:T(8,128)(2,1)}, u32[]{:S(2)}, u32[]{:S(2)}) collective-permute-start(bf16[1024,768]{1,0:T(8,128)(2,1)} %bitcast.92), channel_id=1, source_target_pairs={{0,4},{4,0},{1,5},{5,1},{2,6},{6,2},{3,7},{7,3},{8,12},{12,8},{9,1... | collective-permute-start | bytes 4718600 | tf_op jit(solution)/shard_map/ppermute | solution.py:796
  21.7 82.1 %collective-permute-start = (bf16[1024,768]{1,0:T(8,128)(2,1)S(1)}, bf16[1024,768]{1,0:T(8,128)(2,1)}, u32[]{:S(2)}, u32[]{:S(2)}) collective-permute-start(bf16[1024,768]{1,0:T(8,128)(2,1)S(1)} %bitcast.69), channel_id=1, source_target_pairs={{0,4},{4,0},{1,5},{5,1},{2,6},{6,2},{3,7},{7,3},{8,12},{12,8},{9,1... | collective-permute-start | bytes 4718600 | tf_op jit(solution)/shard_map/ppermute | solution.py:796
  49.4 66.9 %copy-start.16 = (s32[4]{0:T(128)}, s32[4]{0:T(128)S(1)}, u32[]{:S(2)}) copy-start(s32[4]{0:T(128)S(1)} %get-tuple-element.50.slot_ref) | copy-start | bytes 52
  49.6 66.7 %copy-start.18 = (s32[4]{0:T(128)}, s32[4]{0:T(128)S(1)}, u32[]{:S(2)}) copy-start(s32[4]{0:T(128)S(1)} %fusion.24.count_ref) | copy-start | bytes 52
  49.8 3.7 collective-permute-start.4
  51.1 65.1 %copy-start.7 = (bf16[2048,128]{1,0:T(8,128)(2,1)}, bf16[2048,128]{1,0:T(8,128)(2,1)S(1)}, u32[]{:S(2)}) copy-start(bf16[2048,128]{1,0:T(8,128)(2,1)S(1)} %select_convert_fusion.2.qa_ref) | copy-start | bytes 1572868
  53.5 62.8 %copy-start.9 = (bf16[2048,128]{1,0:T(8,128)(2,1)}, bf16[2048,128]{1,0:T(8,128)(2,1)S(1)}, u32[]{:S(2)}) copy-start(bf16[2048,128]{1,0:T(8,128)(2,1)S(1)} %get-tuple-element.106.ka_ref) | copy-start | bytes 1572868
  54.2 52.8 %copy-start.3 = (bf16[768,1152]{1,0:T(8,128)(2,1)}, bf16[768,1152]{1,0:T(8,128)(2,1)S(1)}, u32[]{:S(2)}) copy-start(bf16[768,1152]{1,0:T(8,128)(2,1)S(1)} %assemble.1.w_ref) | copy-start | bytes 5308420
  116.2 21.9 %copy-start.20 = (bf16[2048,384]{1,0:T(8,128)(2,1)}, bf16[2048,384]{1,0:T(8,128)(2,1)S(1)}, u32[]{:S(2)}) copy-start(bf16[2048,384]{1,0:T(8,128)(2,1)S(1)} %get-tuple-element.51.q_ref) | copy-start | bytes 4718596
  116.2 21.9 %copy-start.21 = (bf16[2048,384]{1,0:T(8,128)(2,1)}, bf16[2048,384]{1,0:T(8,128)(2,1)S(1)}, u32[]{:S(2)}) copy-start(bf16[2048,384]{1,0:T(8,128)(2,1)S(1)} %get-tuple-element.52.k_ref) | copy-start | bytes 4718596
  140.4 28.2 %copy-start.28 = (bf16[1024,384]{1,0:T(8,128)(2,1)}, bf16[1024,384]{1,0:T(8,128)(2,1)S(1)}, u32[]{:S(2)}) copy-start(bf16[1024,384]{1,0:T(8,128)(2,1)S(1)} %get-tuple-element.92) | copy-start | bytes 2359300
  140.4 23.8 %collective-permute-start.5 = (bf16[1024,384]{1,0:T(8,128)(2,1)}, bf16[1024,384]{1,0:T(8,128)(2,1)S(1)}, u32[]{:S(2)}, u32[]{:S(2)}) collective-permute-start(bf16[1024,384]{1,0:T(8,128)(2,1)} %get-tuple-element.93), channel_id=1, source_target_pairs={{0,4},{4,0},{1,5},{5,1},{2,6},{6,2},{3,7},{7,3},{8,12},{12,8},{9,1... | collective-permute-start | bytes 2359304 | tf_op jit(solution)/shard_map/ppermute | solution.py:837
  168.5 9.7 %slice-start = ((s8[5898240]{0:T(1024)(128)(4,1)}), s8[4194304]{0:T(1024)(128)(4,1)S(1)}, s32[]{:S(2)}) async-start(s8[5898240]{0:T(1024)(128)(4,1)} %bitcast.72), calls=%async_computation.13 | async-start | bytes 8388608
  178.3 9.7 %copy-start.14 = (bf16[1024,768]{1,0:T(8,128)(2,1)}, bf16[1024,768]{1,0:T(8,128)(2,1)S(1)}, u32[]{:S(2)}) copy-start(bf16[1024,768]{1,0:T(8,128)(2,1)S(1)} %get-tuple-element.55.q_ref) | copy-start | bytes 4718596
  178.3 9.7 %copy-start.11 = (bf16[2048,128]{1,0:T(8,128)(2,1)S(1)}, bf16[2048,128]{1,0:T(8,128)(2,1)}, u32[]{:S(2)}) copy-start(bf16[2048,128]{1,0:T(8,128)(2,1)} %get-tuple-element.105.ka_ref) | copy-start | bytes 1572868
  397.2 242.3 %reduce-scatter.9.cloned.1.call-start = ((), (), s32[]{:S(2)}) async-start(), calls=%async_computation.10 | async-start | bytes 6488064 | tf_op jit(solution)/shard_map/reduce_scatter | solution.py:746
  397.8 305.7 %reduce-scatter.5.cloned.1.call-start = ((), (), s32[]{:S(2)}) async-start(), calls=%async_computation.7 | async-start | bytes 2088960 | tf_op jit(solution)/shard_map/reduce_scatter | solution.py:898
  397.9 21.9 %copy-start.8 = (bf16[2048,128]{1,0:T(8,128)(2,1)S(1)}, bf16[2048,128]{1,0:T(8,128)(2,1)}, u32[]{:S(2)}) copy-start(bf16[2048,128]{1,0:T(8,128)(2,1)} %copy-done.7) | copy-start | bytes 1572868
  397.9 21.9 %copy-start.10 = (bf16[2048,128]{1,0:T(8,128)(2,1)S(1)}, bf16[2048,128]{1,0:T(8,128)(2,1)}, u32[]{:S(2)}) copy-start(bf16[2048,128]{1,0:T(8,128)(2,1)} %copy-done.9) | copy-start | bytes 1572868
  397.9 21.9 %copy-start.17 = (s32[4]{0:T(128)S(1)}, s32[4]{0:T(128)}, u32[]{:S(2)}) copy-start(s32[4]{0:T(128)} %copy-done.16) | copy-start | bytes 52
  397.9 21.9 %copy-start.19 = (s32[4]{0:T(128)S(1)}, s32[4]{0:T(128)}, u32[]{:S(2)}) copy-start(s32[4]{0:T(128)} %copy-done.18) | copy-start | bytes 52
  399.5 18.9 %collective-permute-start.7 = (bf16[1024,384]{1,0:T(8,128)(2,1)S(1)}, bf16[1024,384]{1,0:T(8,128)(2,1)S(1)}, u32[]{:S(2)}, u32[]{:S(2)}) collective-permute-start(bf16[1024,384]{1,0:T(8,128)(2,1)S(1)} %get-tuple-element.91), channel_id=1, source_target_pairs={{0,4},{4,0},{1,5},{5,1},{2,6},{6,2},{3,7},{7,3},{8,12},{12,8},{9,1... | collective-permute-start | bytes 2359304 | tf_op jit(solution)/shard_map/ppermute | solution.py:862
  509.0 301.7 %reduce-scatter.11.cloned.1.call-start = ((), (), s32[]{:S(2)}) async-start(), calls=%async_computation.12 | async-start | bytes 3244032 | tf_op jit(solution)/shard_map/reduce_scatter | solution.py:746
  509.8 331.4 %all-gather.14.cloned.1.call-start = ((), (), s32[]{:S(2)}) async-start(), calls=%async_computation.9 | async-start | bytes 1658880 | tf_op jit(solution)/shard_map/all_gather | solution.py:747
  518.1 350.8 %all-gather.16.cloned.1.call-start = ((), (), s32[]{:S(2)}) async-start(), calls=%async_computation.11 | async-start | bytes 1769472 | tf_op jit(solution)/shard_map/all_gather | solution.py:747
  525.5 38.3 %copy-start.27 = (f32[2048,768]{1,0:T(8,128)}, f32[2048,768]{1,0:T(8,128)S(1)}, u32[]{:S(2)}) copy-start(f32[2048,768]{1,0:T(8,128)S(1)} %convolution_add_fusion) | copy-start | bytes 18874372
  525.5 37.1 %copy-start.25 = (bf16[2048,768]{1,0:T(8,128)(2,1)S(1)}, bf16[2048,768]{1,0:T(8,128)(2,1)}, u32[]{:S(2)}) copy-start(bf16[2048,768]{1,0:T(8,128)(2,1)} %get-tuple-element.70) | copy-start | bytes 9437188
  526.9 51.7 %collective-permute-start.9 = (bf16[1024,768]{1,0:T(8,128)(2,1)}, bf16[1024,768]{1,0:T(8,128)(2,1)}, u32[]{:S(2)}, u32[]{:S(2)}) collective-permute-start(bf16[1024,768]{1,0:T(8,128)(2,1)} %slice.207), channel_id=1, source_target_pairs={{0,4},{4,0},{1,5},{5,1},{2,6},{6,2},{3,7},{7,3},{8,12},{12,8},{9,1... | collective-permute-start | bytes 4718600 | tf_op jit(solution)/shard_map/ppermute | solution.py:879
  528.2 2.1 collective-permute-start.10
  530.4 7.0 collective-permute-start.11
  537.4 25.2 %collective-permute-start.12 = (f32[8,768]{1,0:T(8,128)S(1)}, f32[8,768]{1,0:T(8,128)S(1)}, u32[]{:S(2)}, u32[]{:S(2)}) collective-permute-start(f32[8,768]{1,0:T(8,128)S(1)} %add.221), channel_id=1, source_target_pairs={{0,4},{4,0},{1,5},{5,1},{2,6},{6,2},{3,7},{7,3},{8,12},{12,8},{9,1... | collective-permute-start | bytes 73736 | tf_op jit(solution)/shard_map/ppermute | solution.py:740
  562.5 3.5 collective-permute-start.13
  563.8 75.7 %collective-permute-start.8 = (bf16[1024,768]{1,0:T(8,128)(2,1)}, bf16[1024,768]{1,0:T(8,128)(2,1)}, u32[]{:S(2)}, u32[]{:S(2)}) collective-permute-start(bf16[1024,768]{1,0:T(8,128)(2,1)} %slice.120), channel_id=1, source_target_pairs={{0,4},{4,0},{1,5},{5,1},{2,6},{6,2},{3,7},{7,3},{8,12},{12,8},{9,1... | collective-permute-start | bytes 4718600 | tf_op jit(solution)/shard_map/ppermute | solution.py:893
  566.0 10.5 %collective-permute-start.14 = (f32[8,768]{1,0:T(8,128)S(1)}, f32[8,768]{1,0:T(8,128)S(1)}, u32[]{:S(2)}, u32[]{:S(2)}) collective-permute-start(f32[8,768]{1,0:T(8,128)S(1)} %add.223), channel_id=1, source_target_pairs={{0,2},{1,3},{2,0},{3,1},{4,6},{5,7},{6,4},{7,5},{8,10},{9,11},{10,... | collective-permute-start | bytes 73736 | tf_op jit(solution)/shard_map/ppermute | solution.py:740
  578.5 61.1 %copy-start.35 = (f32[768]{0:T(1024)S(1)}, f32[768]{0:T(1024)}, u32[]{:S(2)}) copy-start(f32[768]{0:T(1024)} %get-tuple-element.101) | copy-start | bytes 9220
  (24 other events, 105.3 us)
Sparse Core Ops, SparseCore 0:
  12.1 87.8 all-gather.7
  103.5 62.5 all-gather.11
  169.6 67.5 all-gather.9
  397.4 109.0 reduce-scatter.6
  511.9 127.5 reduce-scatter.8
  643.6 59.9 reduce-scatter.4
  709.9 100.7 reduce-scatter.10
  812.7 28.4 all-gather.13
  843.2 25.6 all-gather.15

commit v2 on v1

--- a/solution.py
+++ b/solution.py
@@ -75,27 +75,34 @@
     return jnp.where(left, own, other), jnp.where(left, other, own)
 
 
-def forward_block(lo, n, diag, q_ref, qa_ref, kx, vx, o_ref, lse_ref, chunk):
+def chunks_of(n, diag, rows):
+    size = rows if diag else math.gcd(512, n)
+    first = n % size
+    return ([(0, first)] if first else []) + [(c, size) for c in range(first, n, size)]
+
+
+def forward_block(lo, n, diag, q_ref, qa_ref, kx, vx, o_ref, lse_ref):
     q = q_ref[...]
     rows = q.shape[0]
     left = lanes(q.shape) < HEAD
     sides = pair_of(q, qa_ref[...])
+    pieces = chunks_of(n, diag, rows)
     scores, tops, accs = [], [], []
     for h in range(2):
         found = []
-        for c in range(0, n, chunk):
-            s = nt(sides[h], kx[h, pl.ds(lo + c, chunk), :])
-            if diag and c + chunk > n - rows:
-                r = lax.broadcasted_iota(jnp.int32, s.shape, 0) + (n - rows - c)
+        for c, size in pieces:
+            s = nt(sides[h], kx[h, pl.ds(lo + c, size), :])
+            if diag and c + size == n:
+                r = lax.broadcasted_iota(jnp.int32, s.shape, 0)
                 s = jnp.where(lanes(s.shape) <= r, s, -BIG)
             found.append(s)
         scores.append(found)
     for h in range(2):
         top = functools.reduce(jnp.maximum, [jnp.max(s, axis=1, keepdims=True) for s in scores[h]])
         acc = None
-        for i, s in enumerate(scores[h]):
+        for s, (c, size) in zip(scores[h], pieces):
             p = jnp.exp2(s - top).astype(BF)
-            term = nn(p, vx[h, pl.ds(lo + i * chunk, chunk), :])
+            term = nn(p, vx[h, pl.ds(lo + c, size), :])
             acc = term if acc is None else acc + term
         accs.append(acc)
         tops.append(top)
@@ -123,7 +130,7 @@
 
 
 def backward_block(
-    lo, n, diag, q_ref, do_ref, o_ref, lse_ref, qa_ref, kx, vx, km, dq_ref, dk_acc, dv_acc, chunk
+    lo, n, diag, q_ref, do_ref, o_ref, lse_ref, qa_ref, kx, vx, km, dq_ref, dk_acc, dv_acc
 ):
     q, do = q_ref[...], do_ref[...]
     rows = q.shape[0]
@@ -138,13 +145,13 @@
     qm = pair_of(q, zero)
     dm = pair_of(do, zero)
     dq = None
-    for c in range(0, n, chunk):
-        at = pl.ds(lo + c, chunk)
+    for c, size in chunks_of(n, diag, rows):
+        at = pl.ds(lo + c, size)
         dk = dv = None
         for h in range(2):
             st = nt(kx[h, at, :], qx[h])
-            if diag and c + chunk > n - rows:
-                r = lax.broadcasted_iota(jnp.int32, st.shape, 0) + (c - (n - rows))
+            if diag and c + size == n:
+                r = lax.broadcasted_iota(jnp.int32, st.shape, 0)
                 st = jnp.where(r <= lanes(st.shape), st, -BIG)
             pt = jnp.exp2(st)
             dp = nt(vx[h, at, :], dx[h])
@@ -164,7 +171,7 @@
         forward_prep(k_ref, v_ref, ka_ref, kx, vx)
 
     keys = k_ref.shape[0]
-    forward_block(0, keys, False, q_ref, qa_ref, kx, vx, o_ref, lse_ref, math.gcd(512, keys))
+    forward_block(0, keys, False, q_ref, qa_ref, kx, vx, o_ref, lse_ref)
 
 
 def cross_forward(q, kv, qa, ka):
@@ -206,7 +213,7 @@
     keys = k_ref.shape[0]
     backward_block(
         0, keys, False, q_ref, do_ref, o_ref, lse_ref, qa_ref, kx, vx, km,
-        dq_ref, dk_acc, dv_acc, math.gcd(512, keys),
+        dq_ref, dk_acc, dv_acc,
     )
 
     @pl.when(pl.program_id(1) == pl.num_programs(1) - 1)
@@ -282,7 +289,7 @@
         @pl.when(count_ref[i] == n)
         def _():
             lo = pl.multiple_of((i + 1) * block - n * grain, grain)
-            forward_block(lo, n * grain, True, q_ref, qa_ref, kx, vx, o_ref, lse_ref, grain)
+            forward_block(lo, n * grain, True, q_ref, qa_ref, kx, vx, o_ref, lse_ref)
 
 
 def self_specs(block, total):
@@ -317,12 +324,13 @@
 
 
 def self_backward_kernel(
-    count_ref, slot_ref, q_ref, k_ref, v_ref, do_ref, o_ref, lse_ref, qa_ref, ka_ref,
-    dq_ref, dk_ref, dv_ref, kx, vx, km, dk_acc, dv_acc,
+    count_ref, slot_ref, q_ref, k_ref, v_ref, own_ref, far_ref, o_ref, lse_ref, qa_ref, ka_ref,
+    dq_ref, dk_ref, dv_ref, kx, vx, km, dk_acc, dv_acc, do_ref, *, per_dev,
 ):
     i = pl.program_id(1)
     block = q_ref.shape[0]
     grain = grain_of(block)
+    do_ref[...] = jnp.where(slot_ref[i] < per_dev, own_ref[...], far_ref[...])
 
     @pl.when(i == 0)
     def _():
@@ -335,7 +343,7 @@
             lo = pl.multiple_of((i + 1) * block - n * grain, grain)
             backward_block(
                 lo, n * grain, True, q_ref, do_ref, o_ref, lse_ref, qa_ref, kx, vx, km,
-                dq_ref, dk_acc, dv_acc, grain,
+                dq_ref, dk_acc, dv_acc,
             )
 
     @pl.when(i == pl.num_programs(1) - 1)
@@ -344,28 +352,40 @@
         dv_ref[...] = dv_acc[...].astype(BF)
 
 
-def self_backward(counts, slots, q, k, v, do, o, lse, qa, ka, block):
+def self_backward(counts, slots, q, k, v, own, far, o, lse, qa, ka, block):
     total, width = q.shape
+    per_dev = own.shape[0] // block
     row, col, dealt, qas, kas = self_specs(block, total)
     return pl.pallas_call(
-        self_backward_kernel,
+        functools.partial(self_backward_kernel, per_dev=per_dev),
         grid_spec=pltpu.PrefetchScalarGridSpec(
             num_scalar_prefetch=2,
             grid=(width // 128, total // block),
-            in_specs=[row, col, col, dealt, dealt, row, qas, kas],
+            in_specs=[
+                row,
+                col,
+                col,
+                pl.BlockSpec((block, 128), lambda h, i, n, s: (jnp.minimum(s[i], per_dev - 1), h)),
+                pl.BlockSpec((block, 128), lambda h, i, n, s: (jnp.maximum(s[i] - per_dev, 0), h)),
+                dealt,
+                row,
+                qas,
+                kas,
+            ],
             out_specs=[row, col, col],
             scratch_shapes=[pltpu.VMEM((2, total, 128), BF)] * 3
-            + [pltpu.VMEM((total, 128), F32)] * 2,
+            + [pltpu.VMEM((total, 128), F32)] * 2
+            + [pltpu.VMEM((block, 128), BF)],
         ),
         out_shape=[jax.ShapeDtypeStruct((total, width), BF)] * 3,
         compiler_params=params(48),
         cost_estimate=cost(20 * total * total * width, 12 * total * width, total * total * 3),
         name="self_backward",
-    )(counts, slots, q, k, v, do, o, lse, qa, ka)
-
-
-def qkv_kernel(order_ref, x_ref, g_ref, w_ref, n_ref, q_ref, k_ref, v_ref):
-    x = x_ref[...].astype(F32)
+    )(counts, slots, q, k, v, own, far, o, lse, qa, ka)
+
+
+def qkv_kernel(order_ref, own_ref, far_ref, g_ref, w_ref, n_ref, q_ref, k_ref, v_ref, *, per_dev):
+    x = jnp.where(pl.program_id(0) < per_dev, own_ref[...], far_ref[...]).astype(F32)
     n = (x * rms_scale(x) * g_ref[...]).astype(BF)
     n_ref[...] = n
     width = q_ref.shape[1]
@@ -375,18 +395,21 @@
     v_ref[...] = out[:, 2 * width :].astype(BF)
 
 
-def qkv_forward(order, x, gain, w, block):
-    total, dim = x.shape
+def qkv_forward(order, own, far, gain, w, block):
+    dim = own.shape[1]
+    total = own.shape[0] + far.shape[0]
     width = w.shape[1] // 3
+    per_dev = own.shape[0] // block
     here = lambda i, o: (o[i], 0)
     whole = lambda i, o: (0, 0)
     return pl.pallas_call(
-        qkv_kernel,
+        functools.partial(qkv_kernel, per_dev=per_dev),
         grid_spec=pltpu.PrefetchScalarGridSpec(
             num_scalar_prefetch=1,
             grid=(total // block,),
             in_specs=[
-                pl.BlockSpec((block, dim), lambda i, o: (i, 0)),
+                pl.BlockSpec((block, dim), lambda i, o: (jnp.minimum(i, per_dev - 1), 0)),
+                pl.BlockSpec((block, dim), lambda i, o: (jnp.maximum(i - per_dev, 0), 0)),
                 pl.BlockSpec((1, dim), whole),
                 pl.BlockSpec(w.shape, whole),
             ],
@@ -397,12 +420,45 @@
         compiler_params=params(48),
         cost_estimate=cost(6 * total * dim * width, 8 * total * dim),
         name="qkv_forward",
-    )(order, x, gain, w)
-
-
-def after_self_kernel(x_ref, o_ref, wo_ref, g_ref, wq_ref, h_ref, n_ref, q_ref, s_ref):
+    )(order, own, far, gain, w)
+
+
+def enc_kv_kernel(own_ref, far_ref, w_ref, kv_ref, *, own_blocks):
+    enc = jnp.where(pl.program_id(0) < own_blocks, own_ref[...], far_ref[...])
+    half = w_ref.shape[1] // 2
+    for c in range(2):
+        at = slice(c * half, (c + 1) * half)
+        kv_ref[:, at] = nn(enc, w_ref[:, at]).astype(BF)
+
+
+def enc_forward(own, far, w2):
+    rows, dim = own.shape
+    block = min(512, rows)
+    keys = rows + far.shape[0]
+    ours = rows // block
+    return pl.pallas_call(
+        functools.partial(enc_kv_kernel, own_blocks=ours),
+        grid=(keys // block,),
+        in_specs=[
+            pl.BlockSpec((block, dim), lambda i: (jnp.minimum(i, ours - 1), 0)),
+            pl.BlockSpec((block, dim), lambda i: (jnp.maximum(i - ours, 0), 0)),
+            pl.BlockSpec((dim, 2 * dim), lambda i: (0, 1)),
+        ],
+        out_specs=pl.BlockSpec((block, 2 * dim), lambda i: (i, 0)),
+        out_shape=jax.ShapeDtypeStruct((keys, 2 * dim), BF),
+        compiler_params=params(48),
+        cost_estimate=cost(4 * keys * dim * dim, 8 * keys * dim),
+        name="enc_forward",
+    )(own, far, w2)
+
+
+def after_self_kernel(turn_ref, x_ref, *refs, count):
+    o_refs, w_refs = refs[:count], refs[count : 2 * count]
+    g_ref, wq_ref, h_ref, n_ref, q_ref, s_ref = refs[2 * count :]
     x = x_ref[...].astype(F32)
-    a = nn(o_ref[...], wo_ref[...])
+    a = nn(o_refs[0][...], w_refs[0][...])
+    for o_ref, w_ref in zip(o_refs[1:], w_refs[1:]):
+        a = a + nn(o_ref[...], w_ref[...])
     h = x + a
     h_ref[...] = h
     n = (h * rms_scale(h) * g_ref[...]).astype(BF)
@@ -417,53 +473,61 @@
     s_ref[1:2, :] += jnp.sum(a * a, axis=0, keepdims=True)
 
 
-def after_self(x, o, wo, gain, w2):
+def turn_specs(count, width, dim):
+    return [pl.BlockSpec((width, dim), lambda i, t, k=k: (t[k], 0)) for k in range(count)]
+
+
+def after_self(turn, x, pieces, wo, gain, w2):
     rows, dim = x.shape
-    block = min(256, rows)
-    line = lambda i: (i, 0)
-    whole = lambda i: (0, 0)
-    return pl.pallas_call(
-        after_self_kernel,
-        grid=(rows // block,),
-        in_specs=[
-            pl.BlockSpec((block, dim), line),
-            pl.BlockSpec((block, o.shape[1]), line),
-            pl.BlockSpec(wo.shape, whole),
-            pl.BlockSpec((1, dim), whole),
-            pl.BlockSpec((dim, dim), lambda i: (0, 1)),
-        ],
-        out_specs=[
-            pl.BlockSpec((block, dim), line),
-            pl.BlockSpec((block, dim), line),
-            pl.BlockSpec((block, dim), line),
-            pl.BlockSpec((8, dim), whole),
-        ],
+    count, width = len(pieces), pieces[0].shape[1]
+    block = min(512, rows)
+    line = lambda i, t: (i, 0)
+    whole = lambda i, t: (0, 0)
+    row = pl.BlockSpec((block, dim), line)
+    return pl.pallas_call(
+        functools.partial(after_self_kernel, count=count),
+        grid_spec=pltpu.PrefetchScalarGridSpec(
+            num_scalar_prefetch=1,
+            grid=(rows // block,),
+            in_specs=[row]
+            + [pl.BlockSpec((block, width), line)] * count
+            + turn_specs(count, width, dim)
+            + [pl.BlockSpec((1, dim), whole), pl.BlockSpec((dim, dim), lambda i, t: (0, 1))],
+            out_specs=[row, row, row, pl.BlockSpec((8, dim), whole)],
+        ),
         out_shape=[
             jax.ShapeDtypeStruct((rows, dim), F32),
             jax.ShapeDtypeStruct((rows, dim), BF),
             jax.ShapeDtypeStruct((rows, dim), BF),
             jax.ShapeDtypeStruct((8, dim), F32),
         ],
-        compiler_params=params(48),
+        compiler_params=params(56),
         cost_estimate=cost(4 * rows * dim * dim, 14 * rows * dim),
         name="after_self",
-    )(x, o, wo, gain, w2)
+    )(turn, x, *pieces, *([wo] * count), gain, w2)
 
 
 GELU_C = math.sqrt(2.0 / math.pi)
 GELU_A = 0.044715
 
 
+PIECES = (4, 8, 3, 64)
+
+
 def mlp_kernel(
-    o_ref, h1_ref, wc_ref, g_ref, t_ref, wg_ref, wu_ref, wd_ref,
-    y_ref, dh_ref, do_ref, gu_ref, gd_ref, gc_ref, s_ref,
-    n_scr, h_scr, m_scr, dn_scr, hid_scr, du_scr, dw_scr,
+    o_ref, h1_ref, wc_ref, g_ref, t_ref, gu_ref, wd_ref,
+    y_ref, dh_ref, dc_ref, do_ref, s_ref, g_out,
+    n_scr, h_scr, m_scr, dn_scr, hid_scr, du_scr, dw_scr, wg_scr, wu_scr, gu_out, d_out, sems,
 ):
     j = pl.program_id(0)
+    last = pl.num_programs(0) - 1
     rows = o_ref.shape[0]
     step = min(256, rows)
     spans = [pl.ds(r, step) for r in range(0, rows, step)]
     gain = g_ref[...]
+    n_fsdp, n_two, _, tall, _ = gu_ref.shape
+    third = 256
+    high = 3 * tall
 
     @pl.when(j == 0)
     def _():
@@ -480,8 +544,14 @@
         m_scr[...] = jnp.zeros_like(m_scr)
         dn_scr[...] = jnp.zeros_like(dn_scr)
 
-    wg, wu, wd = wg_ref[...], wu_ref[...], wd_ref[...]
-    width = wg.shape[1]
+    for z in range(n_fsdp):
+        for p in range(n_two):
+            for t in range(3):
+                at, to = pl.ds(z * high + t * tall, tall), pl.ds(p * third, third)
+                wg_scr[at, to] = gu_ref[z, p, 0, :, t * third : (t + 1) * third]
+                wu_scr[at, to] = gu_ref[z, p, 1, :, t * third : (t + 1) * third]
+    wg, wu = wg_scr[...], wu_scr[...]
+    wd = wd_ref[...].reshape(-1, wd_ref.shape[-1])
     for at in spans:
         n = n_scr[at, :]
         u = nn(n, wg)
@@ -500,11 +570,38 @@
         dw_scr[at, :] = dw
         m_scr[at, :] += nn(hid, wd)
         dn_scr[at, :] += nt(du, wg) + nt(dw, wu)
-    gd_ref[...] = tn(hid_scr[...], t_ref[...]).astype(BF)
-    gu_ref[:, :width] = tn(n_scr[...], du_scr[...]).astype(BF)
-    gu_ref[:, width:] = tn(n_scr[...], dw_scr[...]).astype(BF)
-
-    @pl.when(j == pl.num_programs(0) - 1)
+
+    slot = lax.rem(j, 2)
+
+    def copies(step_of, slot_of):
+        return (
+            pltpu.make_async_copy(
+                gu_out.at[slot_of],
+                g_out.at[:, pl.ds(step_of * n_two, n_two), pl.ds(0, 2)],
+                sems.at[slot_of, 0],
+            ),
+            pltpu.make_async_copy(d_out.at[slot_of], g_out.at[step_of, :, 2], sems.at[slot_of, 1]),
+        )
+
+    @pl.when(j >= 2)
+    def _():
+        for copy in copies(j - 2, slot):
+            copy.wait()
+
+    d_out[slot] = tn(hid_scr[...], t_ref[...]).astype(BF).reshape(d_out.shape[1:])
+    for side, source in ((0, du_scr), (1, dw_scr)):
+        grad = tn(n_scr[...], source[...]).astype(BF)
+        for z in range(n_fsdp):
+            for p in range(n_two):
+                for t in range(3):
+                    gu_out[slot, z, p, side, :, t * third : (t + 1) * third] = grad[
+                        z * high + t * tall : z * high + (t + 1) * tall,
+                        p * third : (p + 1) * third,
+                    ]
+    for copy in copies(j, slot):
+        copy.start()
+
+    @pl.when(j == last)
     def _():
         total = gains = None
         for at in spans:
@@ -515,24 +612,27 @@
             dh = dh + t_ref[at, :].astype(F32)
             dh_ref[at, :] = dh
             dc = dh.astype(BF)
-            n_scr[at, :] = dc
+            dc_ref[at, :] = dc
             do_ref[at, :] = nt(dc, wc_ref[...]).astype(BF)
             part = jnp.sum(y * y, axis=0, keepdims=True)
             total = part if total is None else total + part
             gains = dg if gains is None else gains + dg
-        gc_ref[...] = tn(o_ref[...], n_scr[...]).astype(BF)
         s_ref[1:2, :] = total
         s_ref[2:3, :] = gains
-
-
-def feed_forward(o, h1, w2, gain, cot, w3, wd):
+        for copy in copies(j - 1, 1 - slot) + copies(j, slot):
+            copy.wait()
+
+
+def feed_forward(o, h1, w2, gain, cot, w3):
     rows, dim = o.shape
-    hidden = wd.shape[0]
-    width = 512
-    steps = hidden // width
+    n_fsdp, n_plane, _, tall, _ = w3.shape
+    steps = n_fsdp
+    two = n_plane // steps
+    width = two * 256
     whole = lambda j: (0, 0)
     once = pl.Buffered(1)
     full = pl.BlockSpec((rows, dim), whole, pipeline_mode=once)
+    flops = 18 * rows * dim * width * steps + 6 * rows * dim * dim
     return pl.pallas_call(
         mlp_kernel,
         grid=(steps,),
@@ -542,27 +642,24 @@
             pl.BlockSpec((dim, dim), lambda j: (0, 4), pipeline_mode=once),
             pl.BlockSpec((1, dim), whole),
             full,
-            pl.BlockSpec((dim, width), lambda j: (0, j)),
-            pl.BlockSpec((dim, width), lambda j: (0, j + steps)),
-            pl.BlockSpec((width, dim), lambda j: (j, 0)),
+            pl.BlockSpec((n_fsdp, two, 2, tall, dim), lambda j: (0, j, 0, 0, 0)),
+            pl.BlockSpec((1, n_plane, 1, tall, dim), lambda j: (j, 0, 2, 0, 0)),
         ],
         out_specs=[
             full,
             full,
             full,
-            pl.BlockSpec((dim, 2 * width), lambda j: (0, j)),
-            pl.BlockSpec((width, dim), lambda j: (j, 0)),
-            pl.BlockSpec((dim, dim), whole, pipeline_mode=once),
+            full,
             pl.BlockSpec((8, dim), whole),
+            pl.BlockSpec(memory_space=pl.ANY),
         ],
         out_shape=[
             jax.ShapeDtypeStruct((rows, dim), BF),
             jax.ShapeDtypeStruct((rows, dim), F32),
             jax.ShapeDtypeStruct((rows, dim), BF),
-            jax.ShapeDtypeStruct((dim, 2 * hidden), BF),
-            jax.ShapeDtypeStruct((hidden, dim), BF),
-            jax.ShapeDtypeStruct((dim, dim), BF),
+            jax.ShapeDtypeStruct((rows, dim), BF),
             jax.ShapeDtypeStruct((8, dim), F32),
+            jax.ShapeDtypeStruct(w3.shape, BF),
         ],
         scratch_shapes=[
             pltpu.VMEM((rows, dim), BF),
@@ -572,23 +669,158 @@
             pltpu.VMEM((rows, width), BF),
             pltpu.VMEM((rows, width), BF),
             pltpu.VMEM((rows, width), BF),
+            pltpu.VMEM((dim, width), BF),
+            pltpu.VMEM((dim, width), BF),
+            pltpu.VMEM((2, n_fsdp, two, 2, tall, dim), BF),
+            pltpu.VMEM((2, n_plane, tall, dim), BF),
+            pltpu.SemaphoreType.DMA((2, 2)),
         ],
         compiler_params=params(60),
-        cost_estimate=cost(18 * rows * dim * hidden + 6 * rows * dim * dim, 40 * MIB, rows * hidden),
+        cost_estimate=cost(flops, 40 * MIB, rows * width * steps),
         name="feed_forward",
-    )(o, h1, w2, gain, cot, w3, w3, wd)
-
-
-def before_self_kernel(
-    dq_ref, wq_ref, h_ref, dh_ref, g_ref, wo_ref, d1_ref, da_ref, do_ref, s_ref
-):
+    )(o, h1, w2, gain, cot, w3, w3)
+
+
+def unpack_kernel(me_ref, p_ref, gate_ref, up_ref, down_ref):
+    core, x, place = me_ref[0], me_ref[1], me_ref[2]
+    tall = p_ref.shape[4]
+    third = 256
+    for p in range(8):
+        near = (core ^ ((p // 2) % 2), x ^ (p // 4), place ^ (p % 2))
+        for t in range(3):
+            at, to = pl.ds(t * tall, tall), pl.ds(p * third, third)
+            lane = slice(t * third, (t + 1) * third)
+            gate_ref[at, to] = p_ref[near + (0, slice(None), lane)].astype(F32)
+            up_ref[at, to] = p_ref[near + (1, slice(None), lane)].astype(F32)
+        down_ref[pl.ds(p * tall, tall), :] = p_ref[near + (2,)].astype(F32)
+
+
+def unpack(me, pieces):
+    tall, dim = pieces.shape[-2:]
+    vmem = pl.BlockSpec(memory_space=pltpu.VMEM)
+    return pl.pallas_call(
+        unpack_kernel,
+        in_specs=[pl.BlockSpec(memory_space=pltpu.SMEM), vmem],
+        out_specs=[vmem] * 3,
+        out_shape=[
+            jax.ShapeDtypeStruct((3 * tall, 8 * 256), F32),
+            jax.ShapeDtypeStruct((3 * tall, 8 * 256), F32),
+            jax.ShapeDtypeStruct((8 * tall, dim), F32),
+        ],
+        compiler_params=params(32),
+        name="unpack",
+    )(me, pieces)
+
+
+def mid_grads_kernel(turn_ref, *refs, count):
+    o_refs = refs[:count]
+    da_ref, n2_ref, dq_ref, own_ref, far_ref, dk_ref, dv_ref, o2_ref, dc_ref, g_ref = refs[count:]
+    m = pl.program_id(0)
+    dim = g_ref.shape[0]
+    width = o_refs[0].shape[1]
+    ours = own_ref.shape[0]
+
+    @pl.when(m == 0)
+    def _():
+        for i in range(count):
+            base = pl.multiple_of(turn_ref[i] * width, width)
+            term = tn(o_refs[i][...], da_ref[...]).astype(BF)
+
+            @pl.when(base < dim)
+            def _():
+                g_ref[pl.ds(base, width), :] = term
+
+    for at, right in ((2, dk_ref), (3, dv_ref)):
+
+        @pl.when(m == at)
+        def _():
+            total = tn(own_ref[...], right[:ours, :]) + tn(far_ref[...], right[ours:, :])
+            g_ref[...] = total.astype(BF)
+
+    for at, left, right in ((1, n2_ref, dq_ref), (4, o2_ref, dc_ref)):
+
+        @pl.when(m == at)
+        def _():
+            g_ref[...] = tn(left[...], right[...]).astype(BF)
+
+
+def mid_grads(turn, pieces, da, n2, dq2, own, far, dk2, dv2, o2, dc):
+    dim = n2.shape[1]
+    rows = n2.shape[0]
+    args = (*pieces, da, n2, dq2, own, far, dk2, dv2, o2, dc)
+    shapes = [(rows, a.shape[1]) for a in pieces] + [a.shape for a in args[len(pieces) :]]
+    flops = 2 * dim * dim * (3 * rows + 2 * dk2.shape[0])
+    return pl.pallas_call(
+        functools.partial(mid_grads_kernel, count=len(pieces)),
+        grid_spec=pltpu.PrefetchScalarGridSpec(
+            num_scalar_prefetch=1,
+            grid=(5,),
+            in_specs=[
+                pl.BlockSpec(shape, lambda m, t: (0, 0), pipeline_mode=pl.Buffered(1))
+                for shape in shapes
+            ],
+            out_specs=pl.BlockSpec((dim, dim), lambda m, t: (0, m)),
+        ),
+        out_shape=jax.ShapeDtypeStruct((dim, 5 * dim), BF),
+        compiler_params=params(48),
+        cost_estimate=cost(flops, 24 * MIB),
+        name="mid_grads",
+    )(turn, *args)
+
+
+def enc_back_kernel(dk_ref, dv_ref, wk_ref, wv_ref, far_ref, own_ref, *, far_blocks):
+    d = nt(dk_ref[...], wk_ref[...]) + nt(dv_ref[...], wv_ref[...])
+
+    @pl.when(pl.program_id(0) < far_blocks)
+    def _():
+        far_ref[...] = d.astype(BF)
+
+    @pl.when(pl.program_id(0) >= far_blocks)
+    def _():
+        own_ref[...] = d
+
+
+def enc_backward(dk, dv, w2, own_rows):
+    keys, dim = dk.shape
+    block = min(512, own_rows)
+    blocks, own = keys // block, own_rows // block
+    far = blocks - own
+    row = pl.BlockSpec((block, dim), lambda i: ((i + own) % blocks, 0))
+    return pl.pallas_call(
+        functools.partial(enc_back_kernel, far_blocks=far),
+        grid=(blocks,),
+        in_specs=[
+            row,
+            row,
+            pl.BlockSpec((dim, dim), lambda i: (0, 2)),
+            pl.BlockSpec((dim, dim), lambda i: (0, 3)),
+        ],
+        out_specs=[
+            pl.BlockSpec((block, dim), lambda i: (jnp.minimum(i, far - 1), 0)),
+            pl.BlockSpec((block, dim), lambda i: (jnp.maximum(i - far, 0), 0)),
+        ],
+        out_shape=[
+            jax.ShapeDtypeStruct((keys - own_rows, dim), BF),
+            jax.ShapeDtypeStruct((own_rows, dim), F32),
+        ],
+        compiler_params=params(48),
+        cost_estimate=cost(4 * keys * dim * dim, 8 * keys * dim),
+        name="enc_backward",
+    )(dk, dv, w2, w2)
+
+
+def before_self_kernel(turn_ref, dq_ref, wq_ref, h_ref, dh_ref, g_ref, *refs, count):
+    w_refs = refs[:count]
+    d1_ref, da_ref, s_ref = refs[count : count + 3]
+    do_refs = refs[count + 3 :]
     dn = nt(dq_ref[...], wq_ref[...])
     dh, dg = norm_back(h_ref[...], g_ref[...], dn)
     d1 = dh_ref[...] + dh
     d1_ref[...] = d1
     da = d1.astype(BF)
     da_ref[...] = da
-    do_ref[...] = nt(da, wo_ref[...]).astype(BF)
+    for do_ref, w_ref in zip(do_refs, w_refs):
+        do_ref[...] = nt(da, w_ref[...]).astype(BF)
 
     @pl.when(pl.program_id(0) == 0)
     def _():
@@ -597,60 +829,102 @@
     s_ref[0:1, :] += dg
 
 
-def before_self(dq, w2, h1, dh2, gain, wo):
+def before_self(turn, dq, w2, h1, dh2, gain, wo, width):
     rows, dim = dq.shape
-    block = min(256, rows)
-    line = lambda i: (i, 0)
-    whole = lambda i: (0, 0)
+    count = turn.shape[0]
+    block = min(512, rows)
+    line = lambda i, t: (i, 0)
+    whole = lambda i, t: (0, 0)
     row = pl.BlockSpec((block, dim), line)
     return pl.pallas_call(
-        before_self_kernel,
-        grid=(rows // block,),
-        in_specs=[
-            row,
-            pl.BlockSpec((dim, dim), lambda i: (0, 1)),
-            row,
-            row,
-            pl.BlockSpec((1, dim), whole),
-            pl.BlockSpec(wo.shape, whole),
-        ],
-        out_specs=[
-            row,
-            row,
-            pl.BlockSpec((block, wo.shape[0]), line),
-            pl.BlockSpec((8, dim), whole),
-        ],
+        functools.partial(before_self_kernel, count=count),
+        grid_spec=pltpu.PrefetchScalarGridSpec(
+            num_scalar_prefetch=1,
+            grid=(rows // block,),
+            in_specs=[
+                row,
+                pl.BlockSpec((dim, dim), lambda i, t: (0, 1)),
+                row,
+                row,
+                pl.BlockSpec((1, dim), whole),
+            ]
+            + turn_specs(count, width, dim),
+            out_specs=[row, row, pl.BlockSpec((8, dim), whole)]
+            + [pl.BlockSpec((block, width), line)] * count,
+        ),
         out_shape=[
             jax.ShapeDtypeStruct((rows, dim), F32),
             jax.ShapeDtypeStruct((rows, dim), BF),
-            jax.ShapeDtypeStruct((rows, wo.shape[0]), BF),
             jax.ShapeDtypeStruct((8, dim), F32),
-        ],
-        compiler_params=params(48),
+        ]
+        + [jax.ShapeDtypeStruct((rows, width), BF)] * count,
+        compiler_params=params(56),
         cost_estimate=cost(4 * rows * dim * dim, 18 * rows * dim),
         name="before_self",
-    )(dq, w2, h1, dh2, gain, wo)
-
-
-def qkv_back_kernel(slot_ref, dq_ref, dk_ref, dv_ref, w_ref, n_ref, x_ref, dn_ref, g_ref, acc, s_acc):
-    i = pl.program_id(0)
+    )(turn, dq, w2, h1, dh2, gain, *([wo] * count))
+
+
+def normed_sum(dn, x):
+    return jnp.sum(dn * (x * rms_scale(x)), axis=0, keepdims=True)
+
+
+def qkv_far_kernel(order_ref, dq_ref, dk_ref, dv_ref, w_ref, x_ref, dn_ref, s_ref):
     d = jnp.concatenate([dq_ref[...], dk_ref[...], dv_ref[...]], axis=1)
     dn = nt(d, w_ref[...])
     dn_ref[...] = dn.astype(BF)
-    x = x_ref[...].astype(F32)
-    dg = jnp.sum(dn * (x * rms_scale(x)), axis=0, keepdims=True)
+
+    @pl.when(pl.program_id(0) == 0)
+    def _():
+        s_ref[...] = jnp.zeros_like(s_ref)
+
+    s_ref[0:1, :] += normed_sum(dn, x_ref[...].astype(F32))
+
+
+def qkv_back_far(order, dq, dk, dv, w, x_far, block):
+    width, dim = dq.shape[1], x_far.shape[1]
+    first = order.shape[0] - x_far.shape[0] // block
+    row = pl.BlockSpec((block, width), lambda i, o: (o[i + first], 0))
+    line = pl.BlockSpec((block, dim), lambda i, o: (i, 0))
+    whole = lambda i, o: (0, 0)
+    return pl.pallas_call(
+        qkv_far_kernel,
+        grid_spec=pltpu.PrefetchScalarGridSpec(
+            num_scalar_prefetch=1,
+            grid=(x_far.shape[0] // block,),
+            in_specs=[row, row, row, pl.BlockSpec(w.shape, whole), line],
+            out_specs=[line, pl.BlockSpec((8, dim), whole)],
+        ),
+        out_shape=[
+            jax.ShapeDtypeStruct(x_far.shape, BF),
+            jax.ShapeDtypeStruct((8, dim), F32),
+        ],
+        compiler_params=params(48),
+        cost_estimate=cost(6 * x_far.shape[0] * dim * width, 10 * x_far.shape[0] * dim),
+        name="qkv_back_far",
+    )(order, dq, dk, dv, w, x_far)
+
+
+def qkv_own_kernel(
+    order_ref, dq_ref, dk_ref, dv_ref, w_ref, n_ref, x_ref, far_ref, dn_ref, g_ref, acc, s_acc, *, per_dev
+):
+    i = pl.program_id(0)
+    d = jnp.concatenate([dq_ref[...], dk_ref[...], dv_ref[...]], axis=1)
     term = tn(n_ref[...], d)
 
     @pl.when(i == 0)
     def _():
         acc[...] = term
-        s_acc[...] = jnp.zeros_like(s_acc)
-        s_acc[0:1, :] = dg
+        s_acc[...] = far_ref[...]
 
     @pl.when(i > 0)
     def _():
         acc[...] += term
-        s_acc[0:1, :] += dg
+
+    @pl.when(i < per_dev)
+    def _():
+        dn = nt(d, w_ref[...])
+        dn_ref[...] = dn
+        s_acc[0:1, :] += normed_sum(dn, x_ref[...].astype(F32))
 
     @pl.when(i == pl.num_programs(0) - 1)
     def _():
@@ -659,14 +933,15 @@
         g_ref[:, width:] = jnp.broadcast_to(s_acc[0:1, :], (128, s_acc.shape[1])).T.astype(BF)
 
 
-def qkv_backward(slots, dq, dk, dv, w, n, x, block):
+def qkv_back_own(order, dq, dk, dv, w, n, x_own, far_sum, block):
     total, width = dq.shape
     dim = n.shape[1]
-    row = pl.BlockSpec((block, width), lambda i, s: (i, 0))
-    dealt = pl.BlockSpec((block, dim), lambda i, s: (s[i], 0))
-    whole = lambda i, s: (0, 0)
-    return pl.pallas_call(
-        qkv_back_kernel,
+    per_dev = x_own.shape[0] // block
+    row = pl.BlockSpec((block, width), lambda i, o: (o[i], 0))
+    ours = pl.BlockSpec((block, dim), lambda i, o: (jnp.minimum(i, per_dev - 1), 0))
+    whole = lambda i, o: (0, 0)
+    return pl.pallas_call(
+        functools.partial(qkv_own_kernel, per_dev=per_dev),
         grid_spec=pltpu.PrefetchScalarGridSpec(
             num_scalar_prefetch=1,
             grid=(total // block,),
@@ -675,20 +950,21 @@
                 row,
                 row,
                 pl.BlockSpec(w.shape, whole),
-                pl.BlockSpec((block, dim), lambda i, s: (i, 0)),
-                dealt,
+                pl.BlockSpec((block, dim), lambda i, o: (o[i], 0)),
+                ours,
+                pl.BlockSpec((8, dim), whole),
             ],
-            out_specs=[dealt, pl.BlockSpec((dim, 3 * width + 128), whole)],
+            out_specs=[ours, pl.BlockSpec((dim, 3 * width + 128), whole)],
             scratch_shapes=[pltpu.VMEM((dim, 3 * width), F32), pltpu.VMEM((8, dim), F32)],
         ),
         out_shape=[
-            jax.ShapeDtypeStruct((total, dim), BF),
+            jax.ShapeDtypeStruct(x_own.shape, F32),
             jax.ShapeDtypeStruct((dim, 3 * width + 128), BF),
         ],
         compiler_params=params(48),
-        cost_estimate=cost(12 * total * dim * width, 10 * total * dim),
-        name="qkv_backward",
-    )(slots, dq, dk, dv, w, n, x)
+        cost_estimate=cost(9 * total * dim * width, 10 * total * dim),
+        name="qkv_back_own",
+    )(order, dq, dk, dv, w, n, x_own, far_sum)
 
 
 def turned(n, k):
@@ -700,37 +976,95 @@
     return lax.dynamic_slice_in_dim(array, index * size, size, 0)
 
 
-def assemble_kernel(place_ref, near_ref, far_ref, w_ref):
+def assemble_kernel(place_ref, near_ref, far_ref, w_ref, g_ref):
     z, core = place_ref[0], place_ref[1]
     count, size = near_ref.shape[0], near_ref.shape[1]
+    width = w_ref.shape[1]
     for d in range(count):
         base = lax.rem(z - d + count, count) * (2 * size)
-        w_ref[pl.ds(pl.multiple_of(base + core * size, 16), size), :] = near_ref[d]
-        w_ref[pl.ds(pl.multiple_of(base + (1 - core) * size, 16), size), :] = far_ref[d]
+        for ref, half in ((near_ref, core), (far_ref, 1 - core)):
+            at = pl.ds(pl.multiple_of(base + half * size, 16), size)
+            w_ref[at, :] = ref[d, :, :width]
+            g_ref[at, :] = ref[d, :, width:]
 
 
 def gather_first(own, z, part, n_fsdp, n_parts):
     size = own.shape[0] // 2
+    width = own.shape[1] - 128
     if n_parts % 2 or size % 16:
-        return lax.all_gather(own, "fsdp", axis=0, tiled=True)
+        full = lax.all_gather(own, "fsdp", axis=0, tiled=True)
+        return full[:, :width], full[:, width:]
     core = part % 2
     mine = lax.dynamic_slice_in_dim(own, core * size, size, 0)
     near = jnp.stack(
         [mine] + [lax.ppermute(mine, "fsdp", turned(n_fsdp, d)) for d in range(1, n_fsdp)]
     )
     far = lax.ppermute(near, "parts", [(i, i ^ 1) for i in range(n_parts)])
+    vmem = pl.BlockSpec(memory_space=pltpu.VMEM)
+    total = n_fsdp * own.shape[0]
     return pl.pallas_call(
         assemble_kernel,
-        in_specs=[
-            pl.BlockSpec(memory_space=pltpu.SMEM),
-            pl.BlockSpec(memory_space=pltpu.VMEM),
-            pl.BlockSpec(memory_space=pltpu.VMEM),
-        ],
-        out_specs=pl.BlockSpec(memory_space=pltpu.VMEM),
-        out_shape=jax.ShapeDtypeStruct((n_fsdp * own.shape[0], own.shape[1]), BF),
+        in_specs=[pl.BlockSpec(memory_space=pltpu.SMEM), vmem, vmem],
+        out_specs=[vmem, vmem],
+        out_shape=[
+            jax.ShapeDtypeStruct((total, width), BF),
+            jax.ShapeDtypeStruct((total, 128), BF),
+        ],
         compiler_params=params(32),
         name="assemble",
     )(jnp.stack([z, core]).astype(jnp.int32), near, far)
+
+
+def pick(array, index, axis):
+    return lax.dynamic_index_in_dim(array, index, axis, keepdims=False)
+
+
+class Plane:
+    def __init__(self, part, place, z, n_parts, n_fsdp):
+        self.core, self.x, self.place, self.z = part % 2, part // 2, place, z
+        self.n_fsdp = n_fsdp
+        self.swap_core = [(i, i ^ 1) for i in range(n_parts)]
+        self.swap_x = [(i, i ^ 2) for i in range(n_parts)]
+
+    def over_core(self, grad):
+        rows = grad.shape[0] // (4 * self.n_fsdp)
+        g = grad.reshape(self.n_fsdp, 2, 2, rows, grad.shape[1])
+        got = lax.ppermute(pick(g, 1 - self.core, 2), "parts", self.swap_core).astype(F32)
+        g = pick(g, self.core, 2).astype(F32)
+        send = (pick(g, 1 - self.x, 1) + pick(got, 1 - self.x, 1)).astype(BF)
+        keep = (pick(g, self.x, 1) + pick(got, self.x, 1)).astype(BF)
+        return send, keep
+
+    def over_x(self, send, keep):
+        got = lax.ppermute(send, "parts", self.swap_x)
+        return (keep.astype(F32) + got.astype(F32)).astype(BF)
+
+    def over_fsdp(self, g):
+        total = pick(g, self.z, 0).astype(F32)
+        for d in range(1, self.n_fsdp):
+            piece = pick(g, (self.z + d) % self.n_fsdp, 0)
+            total = total + lax.ppermute(piece, "fsdp", turned(self.n_fsdp, d)).astype(F32)
+        return total.astype(BF)
+
+    def over_ctx(self, g):
+        return (g.astype(F32) + lax.ppermute(g, "ctx", turned(2, 1)).astype(F32)).astype(BF)
+
+    def widen_ctx(self, g):
+        return jnp.stack([g, lax.ppermute(g, "ctx", turned(2, 1))])
+
+    def widen(self, g):
+        g = jnp.stack([g, lax.ppermute(g, "parts", self.swap_x)])
+        return jnp.stack([g, lax.ppermute(g, "parts", self.swap_core)])
+
+    def rows(self, wide):
+        pieces = [
+            lax.dynamic_slice(
+                wide, (c ^ self.core, a ^ self.x, 0, 0), (1, 1) + wide.shape[2:]
+            )[0, 0]
+            for a in range(2)
+            for c in range(2)
+        ]
+        return jnp.concatenate(pieces).astype(F32)
 
 
 def sum_everywhere(value, sizes):
@@ -740,11 +1074,6 @@
             value = value + lax.ppermute(value, axis, [(i, i ^ bit) for i in range(size)])
             bit *= 2
     return value
-
-
-def scatter_sum(grad):
-    part = lax.psum_scatter(grad, ALL, scatter_dimension=0, tiled=True)
-    return lax.all_gather(part, ("parts", "ctx"), axis=0, tiled=True)
 
 
 def local(
@@ -792,135 +1121,160 @@
     slots = jnp.argsort(order_here).astype(jnp.int32)
     counts = needed_blocks(segs, block)
 
-    def gather_ctx(value):
-        pieces = [value] + [lax.ppermute(value, "ctx", turned(n_ctx, -k)) for k in range(1, n_ctx)]
-        return jnp.concatenate(pieces, axis=0)
-
-    x_all = gather_ctx(x_own)
+    def from_ctx(value):
+        pieces = [lax.ppermute(value, "ctx", turned(n_ctx, -k)) for k in range(1, n_ctx)]
+        return pieces[0] if n_ctx == 2 else jnp.concatenate(pieces, axis=0)
+
+    x_far = from_ctx(x_own)
+
+    fast = (n_parts, n_ctx, n_fsdp) == (4, 2, 4)
+    shard = dim // n_fsdp
 
     def own_heads(w):
         w = jnp.pad(w, ((0, 0), (0, padded - dim)))
         return lax.dynamic_slice_in_dim(w, place * width, width, 1)
 
-    w1 = gather_first(
-        jnp.concatenate([own_heads(self_query), own_heads(self_key), own_heads(self_value)], axis=1),
+    gain_cols = jnp.pad(jnp.stack([norm_self, norm_cross, norm_mlp], axis=1), ((0, 0), (0, 125)))
+    w1, gains = gather_first(
+        jnp.concatenate(
+            [own_heads(self_query), own_heads(self_key), own_heads(self_value), gain_cols], axis=1
+        ),
         z, part, n_fsdp, n_parts,
     )
-    gains = lax.all_gather(
-        jnp.stack([norm_self, norm_cross, norm_mlp], axis=1), "fsdp", axis=0, tiled=True
-    ).astype(F32)
-    gain_self, gain_cross, gain_mlp = (gains[:, i][None] for i in range(3))
-    w2 = lax.all_gather(
-        jnp.concatenate(
-            [
-                rows_of(w, plane, n_plane)
-                for w in (self_output, cross_query, cross_key, cross_value, cross_output)
-            ],
-            axis=1,
-        ),
-        ALL, axis=0, tiled=True,
-    )
-    enc_all = gather_ctx(enc_own)
-    w3 = lax.all_gather(
-        jnp.concatenate([rows_of(gate_in, plane, n_plane), rows_of(up_in, plane, n_plane)], axis=1),
-        ALL, axis=0, tiled=True,
-    )
-    wd = lax.all_gather(rows_of(down_out, plane, n_plane), ALL, axis=0, tiled=True)
-
-    n1, q, k, v = qkv_forward(order_here, x_all, gain_self, w1, block)
+    gains = gains[:, :8].astype(F32).T
+    gain_self, gain_cross, gain_mlp = (gains[i : i + 1] for i in range(3))
+    mats = (self_output, cross_query, cross_key, cross_value, cross_output)
+    if fast:
+        w2 = lax.all_gather(
+            jnp.concatenate([rows_of(w, plane, n_plane) for w in mats], axis=1),
+            ALL, axis=0, tiled=True,
+        )
+
+        def column_piece(w):
+            cut = lax.dynamic_slice_in_dim(w, plane * 256, 256, 1)
+            return jnp.concatenate([cut[t * 64 : (t + 1) * 64] for t in range(3)], axis=1)
+
+        w3 = lax.all_gather(
+            jnp.stack(
+                [column_piece(gate_in), column_piece(up_in), rows_of(down_out, plane, n_plane)]
+            ),
+            ALL, axis=0,
+        ).reshape(PIECES + (dim,))
+    else:
+        w2 = lax.all_gather(jnp.concatenate(mats, axis=1), "fsdp", axis=0, tiled=True)
+
+        def packed(w):
+            w = lax.all_gather(w, "fsdp", axis=0, tiled=True).reshape(4, 3, 64, 8, 256)
+            return w.transpose(0, 3, 2, 1, 4).reshape(4, 8, 64, dim)
+
+        w_down = lax.all_gather(down_out, "fsdp", axis=0, tiled=True).reshape(4, 8, 64, dim)
+        w3 = jnp.stack([packed(gate_in), packed(up_in), w_down], axis=2)
+    enc_far = from_ctx(enc_own)
+
+    n1, q, k, v = qkv_forward(order_here, x_own, x_far, gain_self, w1, block)
     spot = jnp.arange(128, dtype=jnp.int32)[None, :] % HEAD
     minus = jnp.where((spot >= PART0) & (spot < PART0 + 3), -1.0, 0.0)
     seg_q = jnp.where(spot == segs[:, None], 1.0, 0.0).astype(BF)
     seg_k = jnp.where((spot < SEGS) & (spot != segs[:, None]), -BIG, minus).astype(BF)
     o1, lse1 = self_forward(counts, slots, q, k, v, seg_q, seg_k, block)
-    pieces = [
-        lax.ppermute(o1[i * rows : (i + 1) * rows], "ctx", turned(n_ctx, i)) if i else o1[:rows]
-        for i in range(n_ctx)
+    pieces = [o1] + [
+        lax.ppermute(o1[i * rows : (i + 1) * rows], "ctx", turned(n_ctx, i)) for i in range(1, n_ctx)
     ]
-    o_cat = jnp.concatenate(pieces, axis=1)
     turn = (place - jnp.arange(n_ctx, dtype=jnp.int32)) % n_ctx
-    wo = jnp.pad(w2[:, :dim], ((0, padded - dim), (0, 0))).reshape(n_ctx, width, dim)
-    wo = jnp.take(wo, turn, axis=0).reshape(padded, dim)
-    h1, n2, q2, stat1 = after_self(x_own, o_cat, wo, gain_cross, w2)
-
-    w_kv = w2[:, 2 * dim : 4 * dim]
-    kv2 = nn(enc_all, w_kv).astype(BF)
+    wo = w2 if padded == dim else jnp.pad(w2[:, :dim], ((0, padded - dim), (0, 0)))
+    kv2 = enc_forward(enc_own, enc_far, w2)
+    pieces[1], kv2 = lax.optimization_barrier((pieces[1], kv2))
+    h1, n2, q2, stat1 = after_self(turn, x_own, pieces, wo, gain_cross, w2)
+
     where_key = (ring[:, None] * enc_rows + jnp.arange(enc_rows, dtype=jnp.int32)).reshape(-1, 1)
     len_q = jnp.where(spot == 0, jnp.ones((rows, 1), F32), 0.0).astype(BF)
     len_k = jnp.where((spot == 0) & (where_key >= prompt_len[0]), -BIG, minus).astype(BF)
     o2, lse2 = cross_forward(q2, kv2, len_q, len_k)
 
-    layer_out, dh2, do2, g_gu, g_down, g_co, stat2 = feed_forward(
-        o2, h1, w2, gain_mlp, cotangent[0], w3, wd
-    )
-    sum_gu = scatter_sum(g_gu)
-    sum_down = scatter_sum(g_down)
+    layer_out, dh2, dc, do2, stat2, g_ff = feed_forward(o2, h1, w2, gain_mlp, cotangent[0], w3)
+    if fast:
+        part_ff = lax.psum_scatter(g_ff.reshape(32, 3, 64, dim), ALL, scatter_dimension=0)
 
     dq2, dk2, dv2 = cross_backward(q2, kv2, do2, o2, lse2, len_q, len_k)
-    dh1, da, do1, stat3 = before_self(dq2, w2, h1, dh2, gain_cross, wo)
-    do_pieces = [
-        lax.ppermute(do1[:, i * width : (i + 1) * width], "ctx", turned(n_ctx, -i))
-        if i
-        else do1[:, :width]
-        for i in range(n_ctx)
+    dh1, da, stat3, *do1 = before_self(turn, dq2, w2, h1, dh2, gain_cross, wo, width)
+    do_far = [lax.ppermute(do1[i], "ctx", turned(n_ctx, -i)) for i in range(1, n_ctx)]
+    do_far = do_far[0] if n_ctx == 2 else jnp.concatenate(do_far, axis=0)
+    g_mid = mid_grads(turn, pieces, da, n2, dq2, enc_own, enc_far, dk2, dv2, o2, dc)
+    d_far, enc_grad = enc_backward(dk2, dv2, w2, enc_rows)
+    enc_got = [
+        lax.ppermute(d_far[(i - 1) * enc_rows : i * enc_rows], "ctx", turned(n_ctx, i))
+        for i in range(1, n_ctx)
     ]
-    do_all = jnp.concatenate(do_pieces, axis=0)
-    g_cq = tn(n2, dq2)
-    g_wo = tn(o_cat, da).reshape(n_ctx, width, dim)
-    g_wo = jnp.take(g_wo, turn, axis=0).reshape(padded, dim)[:dim]
-    g_ck, g_cv = tn(enc_all, dk2), tn(enc_all, dv2)
-    sum_mid = scatter_sum(
-        jnp.concatenate([g.astype(BF) for g in (g_wo, g_cq, g_ck, g_cv, g_co)], axis=1)
-    )
-    d_enc = nt(dk2, w2[:, 2 * dim : 3 * dim]) + nt(dv2, w2[:, 3 * dim : 4 * dim])
-    enc_grad = d_enc[:enc_rows]
-    for i in range(1, n_ctx):
-        piece = d_enc[i * enc_rows : (i + 1) * enc_rows].astype(BF)
-        enc_grad = enc_grad + lax.ppermute(piece, "ctx", turned(n_ctx, i)).astype(F32)
+    for piece in enc_got:
+        enc_grad = enc_grad + piece.astype(F32)
 
     small = jnp.concatenate([stat1[:2], stat2[:3], stat3[:1], jnp.zeros((2, dim), F32)], axis=0)
     small = sum_everywhere(small, (("parts", n_parts), ("ctx", n_ctx), ("fsdp", n_fsdp)))
     entries = float(n_parts * n_ctx * n_fsdp * rows * dim)
     rms_values = jnp.sqrt(jnp.sum(small[:4], axis=1) / entries)
-    shard = dim // n_fsdp
     grad_gmlp = lax.dynamic_slice_in_dim(small[4], z * shard, shard)
     grad_gcross = lax.dynamic_slice_in_dim(small[5], z * shard, shard)
 
-    dq, dk, dv = self_backward(counts, slots, q, k, v, do_all, o1, lse1, seg_q, seg_k, block)
-    dn1, g_qkv = qkv_backward(slots, dq, dk, dv, w1, n1, x_all, block)
-    dn_own = dn1[:rows].astype(F32)
-    for i in range(1, n_ctx):
-        piece = lax.ppermute(dn1[i * rows : (i + 1) * rows], "ctx", turned(n_ctx, i))
+    do_own = do1[0]
+    if fast:
+        net = Plane(part, place, z, n_parts, n_fsdp)
+        send, keep = net.over_core(g_mid)
+        do_own, do_far, send, keep, d_far = lax.optimization_barrier(
+            (do_own, do_far, send, keep, d_far)
+        )
+        g_mid = net.over_x(send, keep)
+
+    dq, dk, dv = self_backward(counts, slots, q, k, v, do_own, do_far, o1, lse1, seg_q, seg_k, block)
+    if fast:
+        dq, dk, dv, part_ff, g_mid = lax.optimization_barrier((dq, dk, dv, part_ff, g_mid))
+    dn_far, far_sum = qkv_back_far(order_here, dq, dk, dv, w1, x_far, block)
+    dn_got = [
+        lax.ppermute(dn_far[(i - 1) * rows : i * rows], "ctx", turned(n_ctx, i))
+        for i in range(1, n_ctx)
+    ]
+    dn_own, g_qkv = qkv_back_own(order_here, dq, dk, dv, w1, n1, x_own, far_sum, block)
+    for piece in dn_got:
         dn_own = dn_own + piece.astype(F32)
-    x32 = x_own.astype(F32)
-    d_in, _ = norm_back(x32, gain_self, dn_own)
+    d_in, _ = norm_back(x_own.astype(F32), gain_self, dn_own)
     decoder_grad = dh1 + d_in
-    part_qkv = lax.psum_scatter(g_qkv, ("fsdp", "parts"), scatter_dimension=0, tiled=True)
-    sum_qkv = lax.all_gather(part_qkv, "parts", axis=0, tiled=True)
-    every = lax.all_gather(sum_qkv, "ctx", axis=0).astype(F32)
+
+    if fast:
+        send, keep = net.over_core(g_qkv)
+        sum_mid = net.rows(net.widen(net.over_ctx(net.over_fsdp(g_mid))))
+        me = jnp.stack([net.core, net.x, place]).astype(jnp.int32)
+        grad_gate, grad_up, grad_down = unpack(me, net.widen(net.widen_ctx(part_ff)))
+        wide = net.widen(net.widen_ctx(net.over_fsdp(net.over_x(send, keep))))
+        every = jnp.stack([net.rows(pick(wide, i ^ place, 2)) for i in range(2)])
+    else:
+
+        def total(g):
+            g = lax.psum_scatter(g, "fsdp", scatter_dimension=0, tiled=True).astype(F32)
+            return lax.psum(g, ("parts", "ctx"))
+
+        sum_mid = total(g_mid)
+        flat = [
+            g_ff[:, :, i].reshape(4, 8, 64, 3, 256).transpose(0, 3, 2, 1, 4).reshape(dim, hidden)
+            for i in range(2)
+        ]
+        grad_gate, grad_up = total(flat[0]), total(flat[1])
+        grad_down = total(g_ff[:, :, 2].reshape(hidden, dim))
+        sum_qkv = lax.psum_scatter(g_qkv, "fsdp", scatter_dimension=0, tiled=True).astype(F32)
+        every = lax.all_gather(lax.psum(sum_qkv, "parts"), "ctx", axis=0)
     grads_qkv = [
         jnp.concatenate([every[c, :, i * width : (i + 1) * width] for c in range(n_ctx)], axis=1)[:, :dim]
         for i in range(3)
     ]
     grad_gself = jnp.sum(every[:, :, 3 * width], axis=0)
-
-    mids = [sum_mid[:, i * dim : (i + 1) * dim].astype(F32) for i in range(5)]
-    steps = sum_gu.reshape(sum_gu.shape[0], hidden // 512, 2, 512).astype(F32)
-    grad_gate = steps[:, :, 0].reshape(-1, hidden)
-    grad_up = steps[:, :, 1].reshape(-1, hidden)
+    mids = [sum_mid[:, i * dim : (i + 1) * dim] for i in range(5)]
     return (
         layer_out[None],
         decoder_grad[None],
         enc_grad[None],
         *grads_qkv,
-        mids[0],
-        mids[1],
-        mids[2],
-        mids[3],
-        mids[4],
+        *mids,
         grad_gate,
         grad_up,
-        sum_down.astype(F32),
+        grad_down,
         grad_gself,
         grad_gcross,
         grad_gmlp,

time: 902 us -> 668 us (0.74)
  waiting for transfers between devices: 356 us -> 169 us
  blocking collectives: 68.4 us -> 0 us
  Pallas kernels: 298 us -> 353 us
  matrix products: 42.1 us -> 0 us
  starting transfers between devices: 30.1 us -> 53.8 us
  local copies, waits for them, and re-layouts: 51.7 us -> 28.4 us
    reduce_scatter x4 -> x1, waiting for transfers between devices: 194 us -> 0.01 us  [local(): lax.psum_scatter(g_ff.reshape(32, 3, 64, dim), ALL, scatter_dimension=0)]
    all_gather x4 -> x0, blocking collectives: 68.4 us -> none  [the longest x1 23.1 us: local(): lax.all_gather(jnp.stack([norm_self, norm_cross, norm_mlp], axis=1), 'fsd...]
    all_gather x5 -> x2, waiting for transfers between devices: 43.6 us -> 0.01 us  [the longest x1 0.01 us: local(): lax.all_gather(jnp.concatenate([rows_of(w, plane, n_plane) for w in mats]...]
    dot_general x7 -> x0, matrix products: 42.1 us -> none  [the longest x4 17.7 us: tn(): lax.dot_general(a, b, (((0,), (0,)), ((), ())), preferred_element_type=F32)]
    pallas_call x5 -> x10, Pallas kernels: 114 us -> 155 us  [the longest x1 68.5 us: self_backward(): pl.pallas_call(functools.partial(self_backward_kernel, per_dev=per_dev),...]
    ppermute x5 -> x24, starting transfers between devices: 5.82 us -> 42.5 us  [the longest x6 12.9 us: over_fsdp(): lax.ppermute(piece, 'fsdp', turned(self.n_fsdp, d)).astype(F32)]
    ppermute x5 -> x24, waiting for transfers between devices: 67.2 us -> 100 us  [the longest x2 49 us: from_ctx(): lax.ppermute(value, 'ctx', turned(n_ctx, -k))]
    ppermute x3, waiting for transfers between devices: 0.01 us -> 19 us  [gather_first(): lax.ppermute(mine, 'fsdp', turned(n_fsdp, d))]
  transfers between devices with their start and end apart: 24 -> 37, of which waited for: 13 -> 18; matrix products, arithmetic and copies ran while one was open for 8% -> 7% of each run, Pallas kernels for 18% -> 46%
where the time goes in v2:
time: 668 us; the launch traced here: 661 us
  Pallas kernels  353 us (53%)
  waiting for transfers between devices  169 us (25%)
  starting transfers between devices  53.8 us (8%)
  other arithmetic  41.7 us (6%)
  local copies, waits for them, and re-layouts  28.4 us (4%)
  between operations  15.5 us (2%)
    pallas_call x1, Pallas kernels, cross_backward(): pl.pallas_call(cross_backward_kernel, grid=(pairs, rows // block), in_spe...  80.3 us
    pallas_call x1, Pallas kernels, self_backward(): pl.pallas_call(functools.partial(self_backward_kernel, per_dev=per_dev),...  68.5 us
    ppermute x2, waiting for transfers between devices, from_ctx(): lax.ppermute(value, 'ctx', turned(n_ctx, -k))  49 us
    pallas_call x1, Pallas kernels, feed_forward(): pl.pallas_call(mlp_kernel, grid=(steps,), in_specs=[full, full, pl.BlockS...  46.2 us
    pallas_call x1, Pallas kernels, cross_forward(): pl.pallas_call(cross_forward_kernel, grid=(pairs, rows // block), in_spec...  36.2 us
    pallas_call x1, Pallas kernels, self_forward(): pl.pallas_call(self_forward_kernel, grid_spec=pltpu.PrefetchScalarGridSpe...  34.4 us
    ppermute x5, waiting for transfers between devices, sum_everywhere(): lax.ppermute(value, axis, [(i, i ^ bit) for i in range(size)])  33.9 us
    ppermute x3, waiting for transfers between devices, gather_first(): lax.ppermute(mine, 'fsdp', turned(n_fsdp, d))  19 us
  transfers between devices with their start and end apart: 37, of which 18 were waited for; matrix products, arithmetic and copies ran while one was open for 7% of the time, Pallas kernels for 46%

profile of v2, /device:TPU:9, one launch (start us, length us, event | category | flops | bytes accessed | tf_op | source)
XLA Modules:
  0.0 661.3 jit_solution(2715706867647091603)
XLA Ops:
  14.2 2.4 collective-permute-start.2
  22.9 7.7 %collective-permute-done.2 = bf16[96,1280]{1,0:T(8,128)(2,1)S(1)} collective-permute-done((bf16[96,1280]{1,0:T(8,128)(2,1)S(1)}, bf16[96,1280]{1,0:T(8,128)(2,1)S(1)}, u32[]{:S(2)}, u32[]{:S(2)}) %collective-permute-start.2) | collective-permute-done | bytes 245792 | tf_op jit(solution)/shard_map/ppermute | solution.py:1000
  30.7 11.2 %collective-permute-done.1 = bf16[96,1280]{1,0:T(8,128)(2,1)S(1)} collective-permute-done((bf16[96,1280]{1,0:T(8,128)(2,1)S(1)}, bf16[96,1280]{1,0:T(8,128)(2,1)S(1)}, u32[]{:S(2)}, u32[]{:S(2)}) %collective-permute-start.1) | collective-permute-done | bytes 245792 | tf_op jit(solution)/shard_map/ppermute | solution.py:1000
  44.5 2.6 select_convert_fusion
  51.9 49.0 %collective-permute-done.far_ref.x_ref = bf16[1024,768]{1,0:T(8,128)(2,1)} collective-permute-done((bf16[1024,768]{1,0:T(8,128)(2,1)}, bf16[1024,768]{1,0:T(8,128)(2,1)}, u32[]{:S(2)}, u32[]{:S(2)}) %collective-permute-start) | collective-permute-done | bytes 1572896 | tf_op jit(solution)/shard_map/ppermute | solution.py:1125
  100.9 8.5 %qkv_forward.1 = (bf16[2048,768]{1,0:T(8,128)(2,1)}, bf16[2048,384]{1,0:T(8,128)(2,1)S(1)}, bf16[2048,384]{1,0:T(8,128)(2,1)S(1)}, bf16[2048,384]{1,0:T(8,128)(2,1)S(1)}) custom-call(s32[4]{0:T(128)S(1)} %dynamic_slice.163.order_ref, bf16[1024,768]{1,0:T(8,128)(2,1)} %bitcast.own_ref.x_ref, bf16[1024,768]{1,0:T(8,128)(2,1)} %collective-permute-done.far_ref.x_ref, ...), custom_call_target="tpu_custom_call" | custom-call | flops 3623878656 | bytes 12582912 | tf_op jit(solution)/shard_map/qkv_forward/pallas_call | solution.py:405
  110.6 34.4 %self_forward.1 = (bf16[2048,384]{1,0:T(8,128)(2,1)S(1)}, f32[2048,384]{1,0:T(8,128)}) custom-call(s32[4]{0:T(128)S(1)} %fusion.55.count_ref, s32[4]{0:T(128)S(1)} %get-tuple-element.70.slot_ref, bf16[2048,384]{1,0:T(8,128)(2,1)S(1)} %get-tuple-element.73.q_ref, bf16[2048,384]{1,0:T(8,128)(2,1)S(1)} %get-tuple-element.74.k_ref, ...), custom_call_target="tpu_custom_call" | custom-call | flops 12884901888 | bytes 6291456 | tf_op jit(solution)/shard_map/self_forward/pallas_call | solution.py:307
  147.9 9.4 %enc_forward.1.k_ref.v_ref = bf16[2048,1536]{1,0:T(8,128)(2,1)} custom-call(bf16[1024,768]{1,0:T(8,128)(2,1)} %bitcast.11.own_ref.refs_5_, bf16[1024,768]{1,0:T(8,128)(2,1)} %collective-permute-done.6.far_ref.refs_6_, bf16[768,3840]{1,0:T(8,128)(2,1)} %all-gather.4.cloned.1.call-done.w_ref.refs_2_.refs_3_.refs_5_.wc_ref.wq_ref.refs_0_.refs_1_.wk_ref.wv_ref), custom_call_target="tpu_custom_call" | custom-call | flops 4831838208 | bytes 12582912 | tf_op jit(solution)/shard_map/enc_forward/pallas_call | solution.py:439
  157.3 16.1 %collective-permute-done.5.refs_1_ = bf16[1024,384]{1,0:T(8,128)(2,1)S(1)} collective-permute-done((bf16[1024,384]{1,0:T(8,128)(2,1)}, bf16[1024,384]{1,0:T(8,128)(2,1)S(1)}, u32[]{:S(2)}, u32[]{:S(2)}) %collective-permute-start.5) | collective-permute-done | bytes 786464 | tf_op jit(solution)/shard_map/ppermute | solution.py:1181
  174.3 9.1 %after_self.1 = (f32[1024,768]{1,0:T(8,128)}, bf16[1024,768]{1,0:T(8,128)(2,1)}, bf16[1024,768]{1,0:T(8,128)(2,1)}, f32[8,768]{1,0:T(8,128)}) custom-call(s32[2]{0:T(128)} %and_select_fusion.5.turn_ref, bf16[1024,768]{1,0:T(8,128)(2,1)} %bitcast.own_ref.x_ref, bf16[2048,384]{1,0:T(8,128)(2,1)} %copy-done.2, bf16[1024,384]{1,0:T(8,128)(2,1)} %copy-done.7, ...), custom_call_target="tpu_custom_call" | custom-call | flops 2415919104 | bytes 11010048 | tf_op jit(solution)/shard_map/after_self/pallas_call | solution.py:487
  185.0 36.2 %cross_forward.1 = (bf16[1024,768]{1,0:T(8,128)(2,1)S(1)}, f32[1024,768]{1,0:T(8,128)}) custom-call(bf16[1024,768]{1,0:T(8,128)(2,1)S(1)} %copy-done.16, bf16[2048,1536]{1,0:T(8,128)(2,1)} %enc_forward.1.k_ref.v_ref, bf16[2048,1536]{1,0:T(8,128)(2,1)} %enc_forward.1.k_ref.v_ref, bf16[1024,128]{1,0:T(8,128)(2,1)S(1)} %broadcast_in_dim.79.qa_ref, ...), custom_call_target="tpu_custom_call" | custom-call | flops 25769803776 | bytes 6291456 | tf_op jit(solution)/shard_map/cross_forward/pallas_call | solution.py:183
  222.3 46.2 %feed_forward.1 = (bf16[1024,768]{1,0:T(8,128)(2,1)}, f32[1024,768]{1,0:T(8,128)}, bf16[1024,768]{1,0:T(8,128)(2,1)}, bf16[1024,768]{1,0:T(8,128)(2,1)}, f32[8,7...) custom-call(bf16[1024,768]{1,0:T(8,128)(2,1)} %copy-done.20, f32[1024,768]{1,0:T(8,128)} %get-tuple-element.81.h1_ref.h_ref, ...), custom_call_target="tpu_custom_call" | custom-call | flops 32614907904 | bytes 41943040 | tf_op jit(solution)/shard_map/feed_forward/pallas_call | solution.py:636
  271.3 80.3 %cross_backward.1 = (bf16[1024,768]{1,0:T(8,128)(2,1)S(1)}, bf16[2048,768]{1,0:T(8,128)(2,1)}, bf16[2048,768]{1,0:T(8,128)(2,1)}) custom-call(bf16[1024,768]{1,0:T(8,128)(2,1)S(1)} %copy-done.17, bf16[2048,1536]{1,0:T(8,128)(2,1)} %enc_forward.1.k_ref.v_ref, bf16[2048,1536]{1,0:T(8,128)(2,1)} %enc_forward.1.k_ref.v_ref, bf16[1024,768]{1,0:T(8,128)(2,1)S(1)} %copy-done.24, ...), custom_call_target="tpu_custom_call" | custom-call | flops 64424509440 | bytes 9437184 | tf_op jit(solution)/shard_map/cross_backward/pallas_call | solution.py:232
  352.8 10.8 %before_self.1 = (f32[1024,768]{1,0:T(8,128)}, bf16[1024,768]{1,0:T(8,128)(2,1)}, f32[8,768]{1,0:T(8,128)}, bf16[1024,384]{1,0:T(8,128)(2,1)}, bf16[1024,384]{1,0:T(8,128)(2,1)}) custom-call(s32[2]{0:T(128)} %and_select_fusion.5.turn_ref, bf16[1024,768]{1,0:T(8,128)(2,1)} %copy-done.5, ...), custom_call_target="tpu_custom_call" | custom-call | flops 2415919104 | bytes 14155776 | tf_op jit(solution)/shard_map/before_self/pallas_call | solution.py:839
  365.1 17.5 %mid_grads.1 = bf16[768,3840]{1,0:T(8,128)(2,1)} custom-call(s32[2]{0:T(128)S(1)} %copy-done.14, bf16[2048,384]{1,0:T(8,128)(2,1)S(1)} %copy-done.3, bf16[1024,384]{1,0:T(8,128)(2,1)S(1)} %copy-done.8, bf16[1024,768]{1,0:T(8,128)(2,1)S(1)} %copy-done.18, bf16[1024,768]{1,0:T(8,128)(2,1)S(1)} %copy-done.15, bf16[1024,768]{1,0:T(8,128)(2,1)} %copy-done.5, ...), custom_call_target="tpu_custom_call" | custom-call | flops 8455716864 | bytes 25165824 | tf_op jit(solution)/shard_map/mid_grads/pallas_call | solution.py:753
  382.5 6.8 %dynamic-slice_convert_fusion = (f32[4,2,1,48,3840]{4,3,2,1,0:T(8,128)}, bf16[4,2,48,3840]{3,2,1,0:T(8,128)(2,1)}) fusion(bf16[4,2,2,48,3840]{4,3,2,1,0:T(8,128)(2,1)} %bitcast.172, s32[]{:T(128)S(6)} %select_n.261, s32[]{:T(128)S(6)} %select_n.264), kind=kLoop, calls=%fused_computation.18 | loop fusion | flops 1474560 | bytes 14745608 | tf_op jit(solution)/shard_map/convert_element_type | solution.py:1033
  389.3 10.0 %collective-permute-start.8 = (bf16[4,2,48,3840]{3,2,1,0:T(8,128)(2,1)}, bf16[4,2,48,3840]{3,2,1,0:T(8,128)(2,1)}, u32[]{:S(2)}, u32[]{:S(2)}) collective-permute-start(bf16[4,2,48,3840]{3,2,1,0:T(8,128)(2,1)} %get-tuple-element.123), channel_id=1, source_target_pairs={{0,8},{8,0},{16,24},{24,16},{1,9},{9,1},{17,25},{25,17},{2,10},{10... | collective-permute-start | bytes 8847368 | tf_op jit(solution)/shard_map/ppermute | solution.py:1032
  401.0 9.3 %enc_backward.1 = (bf16[1024,768]{1,0:T(8,128)(2,1)}, f32[1024,768]{1,0:T(8,128)S(1)}) custom-call(bf16[2048,768]{1,0:T(8,128)(2,1)} %get-tuple-element.92.refs_7_.dk_ref, bf16[2048,768]{1,0:T(8,128)(2,1)} %get-tuple-element.93.refs_8_.dv_ref, ...), custom_call_target="tpu_custom_call" | custom-call | flops 4831838208 | bytes 12582912 | tf_op jit(solution)/shard_map/enc_backward/pallas_call | solution.py:789
  411.5 2.8 collective-permute-start.30
  415.9 1.8 fusion.7
  417.7 28.9 %collective-permute-done.31 = f32[8,768]{1,0:T(8,128)S(1)} collective-permute-done((f32[8,768]{1,0:T(8,128)S(1)}, f32[8,768]{1,0:T(8,128)S(1)}, u32[]{:S(2)}, u32[]{:S(2)}) %collective-permute-start.31) | collective-permute-done | bytes 24608 | tf_op jit(solution)/shard_map/ppermute | solution.py:1074
  446.6 2.7 collective-permute-start.32
  452.0 2.2 collective-permute-done.33
  456.1 3.5 add_bitcast_fusion
  459.6 2.5 convert_element_type.161
  464.3 3.7 collective-permute-done.7.far_ref
  469.7 68.5 %self_backward.1 = (bf16[2048,384]{1,0:T(8,128)(2,1)S(1)}, bf16[2048,384]{1,0:T(8,128)(2,1)S(1)}, bf16[2048,384]{1,0:T(8,128)(2,1)}) custom-call(s32[4]{0:T(128)S(1)} %fusion.55.count_ref, s32[4]{0:T(128)S(1)} %get-tuple-element.70.slot_ref, bf16[2048,384]{1,0:T(8,128)(2,1)} %copy-done.21, bf16[2048,384]{1,0:T(8,128)(2,1)} %copy-done.22, ...), custom_call_target="tpu_custom_call" | custom-call | flops 32212254720 | bytes 9437184 | tf_op jit(solution)/shard_map/self_backward/pallas_call | solution.py:359
  541.8 5.8 collective-permute-start.20
  548.8 5.6 qkv_back_far.1
  554.4 13.5 %qkv_back_own.1 = (f32[1024,768]{1,0:T(8,128)}, bf16[768,1280]{1,0:T(8,128)(2,1)}) custom-call(s32[4]{0:T(128)S(1)} %dynamic_slice.163.order_ref, bf16[2048,384]{1,0:T(8,128)(2,1)S(1)} %get-tuple-element.105.dq_ref, bf16[2048,384]{1,0:T(8,128)(2,1)S(1)} %get-tuple-element.106.dk_ref, bf16[2048,384]{1,0:T(8,128)(2,1)S(1)} %copy-done.6, ...), custom_call_target="tpu_custom_call" | custom-call | flops 5435817984 | bytes 15728640 | tf_op jit(solution)/shard_map/qkv_back_own/pallas_call | solution.py:943
  567.9 3.2 collective-permute-done.20
  571.1 7.9 %collective-permute-done.21 = bf16[48,3840]{1,0:T(8,128)(2,1)S(1)} collective-permute-done((bf16[48,3840]{1,0:T(8,128)(2,1)S(1)}, bf16[48,3840]{1,0:T(8,128)(2,1)S(1)}, u32[]{:S(2)}, u32[]{:S(2)}) %collective-permute-start.21) | collective-permute-done | bytes 368672 | tf_op jit(solution)/shard_map/ppermute | solution.py:1046
  580.9 1.7 dynamic-slice_convert_fusion.1
  585.4 4.5 collective-permute-done.23
  591.9 7.2 %collective-permute-done.27 = bf16[2,3,64,768]{3,2,1,0:T(8,128)(2,1)S(1)} collective-permute-done((bf16[2,3,64,768]{3,2,1,0:T(8,128)(2,1)S(1)}, bf16[2,3,64,768]{3,2,1,0:T(8,128)(2,1)S(1)}, u32[]{:S(2)}, u32[]{:S(2)}) %collective-permute-start.27) | collective-permute-done | bytes 589856 | tf_op jit(solution)/shard_map/ppermute | solution.py:1056
  599.2 2.0 collective-permute-start.28
  601.3 5.7 collective-permute-done.24
  607.1 2.0 collective-permute-start.25
  609.1 8.4 %collective-permute-done.13 = bf16[4,48,1280]{2,1,0:T(8,128)(2,1)S(1)} collective-permute-done((bf16[4,48,1280]{2,1,0:T(8,128)(2,1)S(1)}, bf16[4,48,1280]{2,1,0:T(8,128)(2,1)S(1)}, u32[]{:S(2)}, u32[]{:S(2)}) %collective-permute-start.13) | collective-permute-done | bytes 491552 | tf_op jit(solution)/shard_map/ppermute | solution.py:1039
  618.5 2.0 collective-permute-start.16
  620.5 3.2 collective-permute-done.10
  623.7 3.1 collective-permute-start.15
  626.8 2.6 fusion.2
  629.4 2.3 collective-permute-done.15
  632.7 4.1 fusion.6
  636.8 1.8 collective-permute-start.18
  639.2 5.0 collective-permute-done.18
  647.7 2.9 unpack.1
  (231 shorter events, 67.4 us)
Async XLA Ops:
  7.3 12.8 %copy-start.29 = (s32[1,2048]{1,0:T(1,128)S(1)}, s32[1,2048]{1,0:T(1,128)}, u32[]{:S(2)}) copy-start(s32[1,2048]{1,0:T(1,128)} %param.22) | copy-start | bytes 24580
  7.3 14.8 %copy-start.39 = (s32[1,4]{1,0:T(1,128)S(1)}, s32[1,4]{1,0:T(1,128)}, u32[]{:S(2)}) copy-start(s32[1,4]{1,0:T(1,128)} %param.23) | copy-start | bytes 52
  7.3 140.6 %all-gather.4.cloned.1.call-start = ((), (), s32[]{:S(2)}) async-start(), calls=%async_computation.1 | async-start | bytes 6082560 | tf_op jit(solution)/shard_map/all_gather | solution.py:1148
  12.0 210.3 %all-gather.6.cloned.1.call-start = ((), (), s32[]{:S(2)}) async-start(), calls=%async_computation.3 | async-start | bytes 9732096 | tf_op jit(solution)/shard_map/all_gather | solution.py:1157
  13.8 525.8 %reduce-scatter.2.cloned.1.call-start = ((), (), s32[]{:S(2)}) async-start(), calls=%async_computation.2 | async-start | bytes 9732096 | tf_op jit(solution)/shard_map/reduce_scatter | solution.py:1196
  14.2 16.4 %collective-permute-start.2 = (bf16[96,1280]{1,0:T(8,128)(2,1)S(1)}, bf16[96,1280]{1,0:T(8,128)(2,1)S(1)}, u32[]{:S(2)}, u32[]{:S(2)}) collective-permute-start(bf16[96,1280]{1,0:T(8,128)(2,1)S(1)} %fusion.29), channel_id=1, source_target_pairs={{0,2},{1,3},{2,0},{3,1},{4,6},{5,7},{6,4},{7,5},{8,10},{9,11},{10,... | collective-permute-start | bytes 737288 | tf_op jit(solution)/shard_map/ppermute | solution.py:1000
  16.6 25.3 %collective-permute-start.1 = (bf16[96,1280]{1,0:T(8,128)(2,1)S(1)}, bf16[96,1280]{1,0:T(8,128)(2,1)S(1)}, u32[]{:S(2)}, u32[]{:S(2)}) collective-permute-start(bf16[96,1280]{1,0:T(8,128)(2,1)S(1)} %fusion.29), channel_id=1, source_target_pairs={{0,1},{1,2},{2,3},{3,0},{4,5},{5,6},{6,7},{7,4},{8,9},{9,10},{10,1... | collective-permute-start | bytes 737288 | tf_op jit(solution)/shard_map/ppermute | solution.py:1000
  16.6 25.3 %collective-permute-start.3 = (bf16[96,1280]{1,0:T(8,128)(2,1)S(1)}, bf16[96,1280]{1,0:T(8,128)(2,1)S(1)}, u32[]{:S(2)}, u32[]{:S(2)}) collective-permute-start(bf16[96,1280]{1,0:T(8,128)(2,1)S(1)} %fusion.29), channel_id=1, source_target_pairs={{0,3},{1,0},{2,1},{3,2},{4,7},{5,4},{6,5},{7,6},{8,11},{9,8},{10,9... | collective-permute-start | bytes 737288 | tf_op jit(solution)/shard_map/ppermute | solution.py:1000
  18.1 129.9 %collective-permute-start.6 = (bf16[1024,768]{1,0:T(8,128)(2,1)}, bf16[1024,768]{1,0:T(8,128)(2,1)}, u32[]{:S(2)}, u32[]{:S(2)}) collective-permute-start(bf16[1024,768]{1,0:T(8,128)(2,1)} %bitcast.11.own_ref.refs_5_), channel_id=1, source_target_pairs={{0,4},{4,0},{1,5},{5,1},{2,6},{6,2},{3,7},{7,3},{8,12},{12,8},{9,1... | collective-permute-start | bytes 4718600 | tf_op jit(solution)/shard_map/ppermute | solution.py:1125
  19.3 81.6 %collective-permute-start = (bf16[1024,768]{1,0:T(8,128)(2,1)}, bf16[1024,768]{1,0:T(8,128)(2,1)}, u32[]{:S(2)}, u32[]{:S(2)}) collective-permute-start(bf16[1024,768]{1,0:T(8,128)(2,1)} %bitcast.own_ref.x_ref), channel_id=1, source_target_pairs={{0,4},{4,0},{1,5},{5,1},{2,6},{6,2},{3,7},{7,3},{8,12},{12,8},{9,1... | collective-permute-start | bytes 4718600 | tf_op jit(solution)/shard_map/ppermute | solution.py:1125
  20.9 23.6 %copy-start.35 = (s32[128]{0:T(128)}, s32[128]{0:T(128)S(1)}, u32[]{:S(2)}) copy-start(s32[128]{0:T(128)S(1)} %and_select_fusion.2) | copy-start | bytes 1540
  42.0 5.0 collective-permute-start.4
  44.4 66.2 %copy-start.9 = (bf16[2048,128]{1,0:T(8,128)(2,1)}, bf16[2048,128]{1,0:T(8,128)(2,1)S(1)}, u32[]{:S(2)}) copy-start(bf16[2048,128]{1,0:T(8,128)(2,1)S(1)} %select_convert_fusion.2.qa_ref) | copy-start | bytes 1572868
  47.0 63.6 %copy-start.11 = (bf16[2048,128]{1,0:T(8,128)(2,1)}, bf16[2048,128]{1,0:T(8,128)(2,1)S(1)}, u32[]{:S(2)}) copy-start(bf16[2048,128]{1,0:T(8,128)(2,1)S(1)} %get-tuple-element.178.ka_ref) | copy-start | bytes 1572868
  110.6 34.5 %copy-start.21 = (bf16[2048,384]{1,0:T(8,128)(2,1)}, bf16[2048,384]{1,0:T(8,128)(2,1)S(1)}, u32[]{:S(2)}) copy-start(bf16[2048,384]{1,0:T(8,128)(2,1)S(1)} %get-tuple-element.73.q_ref) | copy-start | bytes 4718596
  110.6 34.5 %copy-start.22 = (bf16[2048,384]{1,0:T(8,128)(2,1)}, bf16[2048,384]{1,0:T(8,128)(2,1)S(1)}, u32[]{:S(2)}) copy-start(bf16[2048,384]{1,0:T(8,128)(2,1)S(1)} %get-tuple-element.74.k_ref) | copy-start | bytes 4718596
  145.1 12.2 %copy-start.2 = (bf16[2048,384]{1,0:T(8,128)(2,1)}, bf16[2048,384]{1,0:T(8,128)(2,1)S(1)}, u32[]{:S(2)}) copy-start(bf16[2048,384]{1,0:T(8,128)(2,1)S(1)} %get-tuple-element.76.refs_0_.o_ref) | copy-start | bytes 4718596
  146.2 27.2 %collective-permute-start.5 = (bf16[1024,384]{1,0:T(8,128)(2,1)}, bf16[1024,384]{1,0:T(8,128)(2,1)S(1)}, u32[]{:S(2)}, u32[]{:S(2)}) collective-permute-start(bf16[1024,384]{1,0:T(8,128)(2,1)} %slice.93), channel_id=1, source_target_pairs={{0,4},{4,0},{1,5},{5,1},{2,6},{6,2},{3,7},{7,3},{8,12},{12,8},{9,1... | collective-permute-start | bytes 2359304 | tf_op jit(solution)/shard_map/ppermute | solution.py:1181
  382.5 17.6 %copy-start.34 = (f32[8,768]{1,0:T(8,128)S(1)}, f32[8,768]{1,0:T(8,128)}, u32[]{:S(2)}) copy-start(f32[8,768]{1,0:T(8,128)} %get-tuple-element.120) | copy-start | bytes 73732
  389.3 70.3 %collective-permute-start.8 = (bf16[4,2,48,3840]{3,2,1,0:T(8,128)(2,1)}, bf16[4,2,48,3840]{3,2,1,0:T(8,128)(2,1)}, u32[]{:S(2)}, u32[]{:S(2)}) collective-permute-start(bf16[4,2,48,3840]{3,2,1,0:T(8,128)(2,1)} %get-tuple-element.123), channel_id=1, source_target_pairs={{0,8},{8,0},{16,24},{24,16},{1,9},{9,1},{17,25},{25,17},{2,10},{10... | collective-permute-start | bytes 8847368 | tf_op jit(solution)/shard_map/ppermute | solution.py:1032
  401.0 10.4 %collective-permute-start.29 = (f32[8,768]{1,0:T(8,128)S(1)}, f32[8,768]{1,0:T(8,128)S(1)}, u32[]{:S(2)}, u32[]{:S(2)}) collective-permute-start(f32[8,768]{1,0:T(8,128)S(1)} %maximum_maximum_fusion), channel_id=1, source_target_pairs={{0,8},{8,0},{16,24},{24,16},{1,9},{9,1},{17,25},{25,17},{2,10},{10... | collective-permute-start | bytes 73736 | tf_op jit(solution)/shard_map/ppermute | solution.py:1074
  410.3 45.8 %collective-permute-start.11 = (bf16[1024,768]{1,0:T(8,128)(2,1)}, bf16[1024,768]{1,0:T(8,128)(2,1)}, u32[]{:S(2)}, u32[]{:S(2)}) collective-permute-start(bf16[1024,768]{1,0:T(8,128)(2,1)} %get-tuple-element.95), channel_id=1, source_target_pairs={{0,4},{4,0},{1,5},{5,1},{2,6},{6,2},{3,7},{7,3},{8,12},{12,8},{9,1... | collective-permute-start | bytes 4718600 | tf_op jit(solution)/shard_map/ppermute | solution.py:1205
  411.5 4.4 collective-permute-start.30
  415.9 30.7 %collective-permute-start.31 = (f32[8,768]{1,0:T(8,128)S(1)}, f32[8,768]{1,0:T(8,128)S(1)}, u32[]{:S(2)}, u32[]{:S(2)}) collective-permute-start(f32[8,768]{1,0:T(8,128)S(1)} %add.404), channel_id=1, source_target_pairs={{0,4},{4,0},{1,5},{5,1},{2,6},{6,2},{3,7},{7,3},{8,12},{12,8},{9,1... | collective-permute-start | bytes 73736 | tf_op jit(solution)/shard_map/ppermute | solution.py:1074
  446.6 3.9 collective-permute-start.32
  450.6 3.6 collective-permute-start.33
  450.7 17.2 %collective-permute-start.7 = (bf16[1024,384]{1,0:T(8,128)(2,1)}, bf16[1024,384]{1,0:T(8,128)(2,1)S(1)}, u32[]{:S(2)}, u32[]{:S(2)}) collective-permute-start(bf16[1024,384]{1,0:T(8,128)(2,1)} %get-tuple-element.89), channel_id=1, source_target_pairs={{0,4},{4,0},{1,5},{5,1},{2,6},{6,2},{3,7},{7,3},{8,12},{12,8},{9,1... | collective-permute-start | bytes 2359304 | tf_op jit(solution)/shard_map/ppermute | solution.py:1200
  467.9 70.2 %collective-permute-start.9 = (bf16[4,48,3840]{2,1,0:T(8,128)(2,1)}, bf16[4,48,3840]{2,1,0:T(8,128)(2,1)S(1)}, u32[]{:S(2)}, u32[]{:S(2)}) collective-permute-start(bf16[4,48,3840]{2,1,0:T(8,128)(2,1)} %fusion.11), channel_id=1, source_target_pairs={{0,16},{8,24},{16,0},{24,8},{1,17},{9,25},{17,1},{25,9},{2,18},{10... | collective-permute-start | bytes 4423688 | tf_op jit(solution)/shard_map/ppermute | solution.py:1039
  539.6 44.8 %collective-permute-start.26 = (bf16[3,64,768]{2,1,0:T(8,128)(2,1)}, bf16[3,64,768]{2,1,0:T(8,128)(2,1)S(1)}, u32[]{:S(2)}, u32[]{:S(2)}) collective-permute-start(bf16[3,64,768]{2,1,0:T(8,128)(2,1)} %bitcast.183), channel_id=1, source_target_pairs={{0,4},{4,0},{1,5},{5,1},{2,6},{6,2},{3,7},{7,3},{8,12},{12,8},{9,1... | collective-permute-start | bytes 884744 | tf_op jit(solution)/shard_map/ppermute | solution.py:1053
  541.8 29.3 %collective-permute-start.20 = (bf16[48,3840]{1,0:T(8,128)(2,1)S(1)}, bf16[48,3840]{1,0:T(8,128)(2,1)S(1)}, u32[]{:S(2)}, u32[]{:S(2)}) collective-permute-start(bf16[48,3840]{1,0:T(8,128)(2,1)S(1)} %get-tuple-element.135), channel_id=1, source_target_pairs={{0,1},{1,2},{2,3},{3,0},{4,5},{5,6},{6,7},{7,4},{8,9},{9,10},{10,1... | collective-permute-start | bytes 1105928 | tf_op jit(solution)/shard_map/ppermute | solution.py:1046
  547.6 23.5 %collective-permute-start.22 = (bf16[48,3840]{1,0:T(8,128)(2,1)S(1)}, bf16[48,3840]{1,0:T(8,128)(2,1)S(1)}, u32[]{:S(2)}, u32[]{:S(2)}) collective-permute-start(bf16[48,3840]{1,0:T(8,128)(2,1)S(1)} %get-tuple-element.136), channel_id=1, source_target_pairs={{0,3},{1,0},{2,1},{3,2},{4,7},{5,4},{6,5},{7,6},{8,11},{9,8},{10,9... | collective-permute-start | bytes 1105928 | tf_op jit(solution)/shard_map/ppermute | solution.py:1046
  547.6 31.4 %collective-permute-start.21 = (bf16[48,3840]{1,0:T(8,128)(2,1)S(1)}, bf16[48,3840]{1,0:T(8,128)(2,1)S(1)}, u32[]{:S(2)}, u32[]{:S(2)}) collective-permute-start(bf16[48,3840]{1,0:T(8,128)(2,1)S(1)} %get-tuple-element.137), channel_id=1, source_target_pairs={{0,2},{1,3},{2,0},{3,1},{4,6},{5,7},{6,4},{7,5},{8,10},{9,11},{10,... | collective-permute-start | bytes 1105928 | tf_op jit(solution)/shard_map/ppermute | solution.py:1046
  580.2 9.7 %collective-permute-start.23 = (bf16[48,3840]{1,0:T(8,128)(2,1)S(1)}, bf16[48,3840]{1,0:T(8,128)(2,1)S(1)}, u32[]{:S(2)}, u32[]{:S(2)}) collective-permute-start(bf16[48,3840]{1,0:T(8,128)(2,1)S(1)} %fusion.17), channel_id=1, source_target_pairs={{0,4},{4,0},{1,5},{5,1},{2,6},{6,2},{3,7},{7,3},{8,12},{12,8},{9,1... | collective-permute-start | bytes 1105928 | tf_op jit(solution)/shard_map/ppermute | solution.py:1050
  582.6 7.5 %collective-permute-start.12 = (bf16[4,2,48,1280]{3,2,1,0:T(8,128)(2,1)S(1)}, bf16[4,2,48,1280]{3,2,1,0:T(8,128)(2,1)S(1)}, u32[]{:S(2)}, u32[]{:S(2)}) collective-permute-start(bf16[4,2,48,1280]{3,2,1,0:T(8,128)(2,1)S(1)} %get-tuple-element.130), channel_id=1, source_target_pairs={{0,8},{8,0},{16,24},{24,16},{1,9},{9,1},{17,25},{25,17},{2,10},{10... | collective-permute-start | bytes 2949128 | tf_op jit(solution)/shard_map/ppermute | solution.py:1032
  583.5 40.1 %collective-permute-start.10 = (bf16[1024,768]{1,0:T(8,128)(2,1)S(1)}, bf16[1024,768]{1,0:T(8,128)(2,1)S(1)}, u32[]{:S(2)}, u32[]{:S(2)}) collective-permute-start(bf16[1024,768]{1,0:T(8,128)(2,1)S(1)} %get-tuple-element.111), channel_id=1, source_target_pairs={{0,4},{4,0},{1,5},{5,1},{2,6},{6,2},{3,7},{7,3},{8,12},{12,8},{9,1... | collective-permute-start | bytes 4718600 | tf_op jit(solution)/shard_map/ppermute | solution.py:1232
  584.4 14.6 %collective-permute-start.27 = (bf16[2,3,64,768]{3,2,1,0:T(8,128)(2,1)S(1)}, bf16[2,3,64,768]{3,2,1,0:T(8,128)(2,1)S(1)}, u32[]{:S(2)}, u32[]{:S(2)}) collective-permute-start(bf16[2,3,64,768]{3,2,1,0:T(8,128)(2,1)S(1)} %get-tuple-element.163), channel_id=1, source_target_pairs={{0,16},{8,24},{16,0},{24,8},{1,17},{9,25},{17,1},{25,9},{2,18},{10... | collective-permute-start | bytes 1769480 | tf_op jit(solution)/shard_map/ppermute | solution.py:1056
  590.0 16.9 %collective-permute-start.24 = (bf16[48,3840]{1,0:T(8,128)(2,1)S(1)}, bf16[48,3840]{1,0:T(8,128)(2,1)S(1)}, u32[]{:S(2)}, u32[]{:S(2)}) collective-permute-start(bf16[48,3840]{1,0:T(8,128)(2,1)S(1)} %add_convert_fusion.1), channel_id=1, source_target_pairs={{0,16},{8,24},{16,0},{24,8},{1,17},{9,25},{17,1},{25,9},{2,18},{10... | collective-permute-start | bytes 1105928 | tf_op jit(solution)/shard_map/ppermute | solution.py:1056
  590.4 27.1 %collective-permute-start.13 = (bf16[4,48,1280]{2,1,0:T(8,128)(2,1)S(1)}, bf16[4,48,1280]{2,1,0:T(8,128)(2,1)S(1)}, u32[]{:S(2)}, u32[]{:S(2)}) collective-permute-start(bf16[4,48,1280]{2,1,0:T(8,128)(2,1)S(1)} %fusion.18), channel_id=1, source_target_pairs={{0,16},{8,24},{16,0},{24,8},{1,17},{9,25},{17,1},{25,9},{2,18},{10... | collective-permute-start | bytes 1474568 | tf_op jit(solution)/shard_map/ppermute | solution.py:1039
  599.2 48.3 %collective-permute-start.28 = (bf16[2,2,3,64,768]{4,3,2,1,0:T(8,128)(2,1)S(1)}, bf16[2,2,3,64,768]{4,3,2,1,0:T(8,128)(2,1)S(1)}, u32[]{:S(2)}, u32[]{:S(2)}) collective-permute-start(bf16[2,2,3,64,768]{4,3,2,1,0:T(8,128)(2,1)S(1)} %get-tuple-element.139), channel_id=1, source_target_pairs={{0,8},{8,0},{16,24},{24,16},{1,9},{9,1},{17,25},{25,17},{2,10},{10... | collective-permute-start | bytes 3538952 | tf_op jit(solution)/shard_map/ppermute | solution.py:1057
  607.1 19.7 %copy-start.25 = (f32[1024,768]{1,0:T(8,128)S(1)}, f32[1024,768]{1,0:T(8,128)}, u32[]{:S(2)}) copy-start(f32[1024,768]{1,0:T(8,128)} %get-tuple-element.110) | copy-start | bytes 9437188
  607.1 19.7 %copy-start.33 = (f32[768]{0:T(1024)S(1)}, f32[768]{0:T(1024)}, u32[]{:S(2)}) copy-start(f32[768]{0:T(1024)} %get-tuple-element.173) | copy-start | bytes 9220
  607.1 31.5 %collective-permute-start.25 = (bf16[2,48,3840]{2,1,0:T(8,128)(2,1)S(1)}, bf16[2,48,3840]{2,1,0:T(8,128)(2,1)S(1)}, u32[]{:S(2)}, u32[]{:S(2)}) collective-permute-start(bf16[2,48,3840]{2,1,0:T(8,128)(2,1)S(1)} %get-tuple-element.160), channel_id=1, source_target_pairs={{0,8},{8,0},{16,24},{24,16},{1,9},{9,1},{17,25},{25,17},{2,10},{10... | collective-permute-start | bytes 2211848 | tf_op jit(solution)/shard_map/ppermute | solution.py:1057
  617.7 11.7 %collective-permute-start.14 = (bf16[48,1280]{1,0:T(8,128)(2,1)S(1)}, bf16[48,1280]{1,0:T(8,128)(2,1)S(1)}, u32[]{:S(2)}, u32[]{:S(2)}) collective-permute-start(bf16[48,1280]{1,0:T(8,128)(2,1)S(1)} %get-tuple-element.166), channel_id=1, source_target_pairs={{0,1},{1,2},{2,3},{3,0},{4,5},{5,6},{6,7},{7,4},{8,9},{9,10},{10,1... | collective-permute-start | bytes 368648 | tf_op jit(solution)/shard_map/ppermute | solution.py:1046
  618.5 10.9 %collective-permute-start.16 = (bf16[48,1280]{1,0:T(8,128)(2,1)S(1)}, bf16[48,1280]{1,0:T(8,128)(2,1)S(1)}, u32[]{:S(2)}, u32[]{:S(2)}) collective-permute-start(bf16[48,1280]{1,0:T(8,128)(2,1)S(1)} %get-tuple-element.167), channel_id=1, source_target_pairs={{0,3},{1,0},{2,1},{3,2},{4,7},{5,4},{6,5},{7,6},{8,11},{9,8},{10,9... | collective-permute-start | bytes 368648 | tf_op jit(solution)/shard_map/ppermute | solution.py:1046
  623.7 8.0 %collective-permute-start.15 = (bf16[48,1280]{1,0:T(8,128)(2,1)S(1)}, bf16[48,1280]{1,0:T(8,128)(2,1)S(1)}, u32[]{:S(2)}, u32[]{:S(2)}) collective-permute-start(bf16[48,1280]{1,0:T(8,128)(2,1)S(1)} %get-tuple-element.168), channel_id=1, source_target_pairs={{0,2},{1,3},{2,0},{3,1},{4,6},{5,7},{6,4},{7,5},{8,10},{9,11},{10,... | collective-permute-start | bytes 368648 | tf_op jit(solution)/shard_map/ppermute | solution.py:1046
  631.8 5.0 collective-permute-start.17
  636.8 7.3 %collective-permute-start.18 = (bf16[2,48,1280]{2,1,0:T(8,128)(2,1)S(1)}, bf16[2,48,1280]{2,1,0:T(8,128)(2,1)S(1)}, u32[]{:S(2)}, u32[]{:S(2)}) collective-permute-start(bf16[2,48,1280]{2,1,0:T(8,128)(2,1)S(1)} %get-tuple-element.170), channel_id=1, source_target_pairs={{0,16},{8,24},{16,0},{24,8},{1,17},{9,25},{17,1},{25,9},{2,18},{10... | collective-permute-start | bytes 737288 | tf_op jit(solution)/shard_map/ppermute | solution.py:1056
  644.2 6.4 collective-permute-start.19
  (31 other events, 150.3 us)
Sparse Core Ops, SparseCore 0:
  12.1 87.4 all-gather.3
  103.1 94.5 all-gather.5
  268.7 143.3 reduce-scatter.1

commit v3 on v2

--- a/solution.py
+++ b/solution.py
@@ -75,41 +75,90 @@
     return jnp.where(left, own, other), jnp.where(left, other, own)
 
 
-def chunks_of(n, diag, rows):
-    size = rows if diag else math.gcd(512, n)
-    first = n % size
-    return ([(0, first)] if first else []) + [(c, size) for c in range(first, n, size)]
-
-
-def forward_block(lo, n, diag, q_ref, qa_ref, kx, vx, o_ref, lse_ref):
+CHUNK = 512
+
+
+def below(s, rows_first):
+    r = lax.broadcasted_iota(jnp.int32, s.shape, 0)
+    c = lanes(s.shape)
+    return jnp.where(c <= r if rows_first else r <= c, s, -BIG)
+
+
+def lane_max(s):
+    return functools.reduce(jnp.maximum, [s[:, c : c + 128] for c in range(0, s.shape[1], 128)])
+
+
+def sweep(step, lo, full, odd, grain, unroll):
+    base = lo
+    if odd is not None:
+
+        @pl.when(odd == 1)
+        def _():
+            step(lo, 0, grain)
+
+        base = lo + odd * grain
+
+    def body(c, carry):
+        step(pl.multiple_of(base + c * CHUNK, grain), pl.multiple_of(grain + c * CHUNK, 128), CHUNK)
+        return carry
+
+    lax.fori_loop(0, full, body, 0, unroll=unroll)
+    return pl.multiple_of(base + full * CHUNK, grain)
+
+
+def forward_block(
+    lo, full, odd, grain, diag, q_ref, qa_ref, kx, vx, o_ref, lse_ref, s_scr, m_scr, a_scr, unroll
+):
     q = q_ref[...]
     rows = q.shape[0]
     left = lanes(q.shape) < HEAD
     sides = pair_of(q, qa_ref[...])
-    pieces = chunks_of(n, diag, rows)
-    scores, tops, accs = [], [], []
-    for h in range(2):
-        found = []
-        for c, size in pieces:
-            s = nt(sides[h], kx[h, pl.ds(lo + c, size), :])
-            if diag and c + size == n:
-                r = lax.broadcasted_iota(jnp.int32, s.shape, 0)
-                s = jnp.where(lanes(s.shape) <= r, s, -BIG)
-            found.append(s)
-        scores.append(found)
-    for h in range(2):
-        top = functools.reduce(jnp.maximum, [jnp.max(s, axis=1, keepdims=True) for s in scores[h]])
-        acc = None
-        for s, (c, size) in zip(scores[h], pieces):
-            p = jnp.exp2(s - top).astype(BF)
-            term = nn(p, vx[h, pl.ds(lo + c, size), :])
-            acc = term if acc is None else acc + term
-        accs.append(acc)
-        tops.append(top)
-    wide = jnp.where(left, accs[0], accs[1])
-    total = jnp.where(left, accs[1], accs[0])
+    m_scr[...] = jnp.full_like(m_scr, -BIG)
+    a_scr[...] = jnp.zeros_like(a_scr)
+    last = s_scr.shape[2] - rows
+
+    def scores(key, at, size, masked=False):
+        for h in range(2):
+            s = nt(sides[h], kx[h, pl.ds(key, size), :])
+            s = below(s, True) if masked else s
+            s_scr[h, :, pl.ds(at, size)] = s
+            m_scr[h] = jnp.maximum(m_scr[h], lane_max(s))
+
+    end = sweep(scores, lo, full, odd, grain, unroll)
+    if diag:
+        scores(end, last, rows, True)
+    tops = [jnp.max(m_scr[h], axis=1, keepdims=True) for h in range(2)]
+
+    def values(key, at, size):
+        for h in range(2):
+            p = jnp.exp2(s_scr[h, :, pl.ds(at, size)] - tops[h]).astype(BF)
+            a_scr[h] += nn(p, vx[h, pl.ds(key, size), :])
+
+    end = sweep(values, lo, full, odd, grain, unroll)
+    if diag:
+        values(end, last, rows)
+    wide = jnp.where(left, a_scr[0], a_scr[1])
+    total = jnp.where(left, a_scr[1], a_scr[0])
     o_ref[...] = (wide / pltpu.roll(total, HEAD, 1)).astype(o_ref.dtype)
     lse_ref[...] = jnp.where(left, tops[1], tops[0]) + jnp.log2(total)
+
+
+def forward_scratch(block, keys):
+    return [
+        pltpu.VMEM((2, keys, 128), BF),
+        pltpu.VMEM((2, keys, 128), BF),
+        pltpu.VMEM((2, block, keys + CHUNK), F32),
+        pltpu.VMEM((2, block, 128), F32),
+        pltpu.VMEM((2, block, 128), F32),
+    ]
+
+
+def backward_scratch(block, keys):
+    return (
+        [pltpu.VMEM((2, keys, 128), BF)] * 3
+        + [pltpu.VMEM((keys, 128), F32)] * 2
+        + [pltpu.VMEM((block, 128), F32)]
+    )
 
 
 def forward_prep(k_ref, v_ref, ka_ref, kx, vx):
@@ -130,11 +179,11 @@
 
 
 def backward_block(
-    lo, n, diag, q_ref, do_ref, o_ref, lse_ref, qa_ref, kx, vx, km, dq_ref, dk_acc, dv_acc
+    lo, full, odd, grain, diag, q, do, o_ref, lse_ref, qa_ref, kx, vx, km,
+    dq_ref, dk_acc, dv_acc, dq_acc, unroll,
 ):
-    q, do = q_ref[...], do_ref[...]
+    left = lanes(q.shape) < HEAD
     rows = q.shape[0]
-    left = lanes(q.shape) < HEAD
     product = do.astype(F32) * o_ref[...].astype(F32)
     first = jnp.sum(jnp.where(left, product, 0.0), axis=1, keepdims=True)
     second = jnp.sum(jnp.where(left, 0.0, product), axis=1, keepdims=True)
@@ -144,16 +193,14 @@
     dx = pair_of(do, with_parts(zero, delta))
     qm = pair_of(q, zero)
     dm = pair_of(do, zero)
-    dq = None
-    for c, size in chunks_of(n, diag, rows):
-        at = pl.ds(lo + c, size)
-        dk = dv = None
+    dq_acc[...] = jnp.zeros_like(dq_acc)
+
+    def step(key, _, size, masked=False):
+        at = pl.ds(key, size)
+        dq = dk = dv = None
         for h in range(2):
             st = nt(kx[h, at, :], qx[h])
-            if diag and c + size == n:
-                r = lax.broadcasted_iota(jnp.int32, st.shape, 0)
-                st = jnp.where(r <= lanes(st.shape), st, -BIG)
-            pt = jnp.exp2(st)
+            pt = jnp.exp2(below(st, False) if masked else st)
             dp = nt(vx[h, at, :], dx[h])
             ds = (pt * dp).astype(BF)
             tv, tk, tq = nn(pt.astype(BF), dm[h]), nn(ds, qm[h]), tn(ds, km[h, at, :])
@@ -162,16 +209,25 @@
             dq = tq if dq is None else dq + tq
         dv_acc[at, :] += dv
         dk_acc[at, :] += dk
-    dq_ref[...] = (dq * SCALE).astype(dq_ref.dtype)
-
-
-def cross_forward_kernel(q_ref, k_ref, v_ref, qa_ref, ka_ref, o_ref, lse_ref, kx, vx):
+        dq_acc[...] += dq
+
+    end = sweep(step, lo, full, odd, grain, unroll)
+    if diag:
+        step(end, 0, rows, True)
+    dq_ref[...] = (dq_acc[...] * SCALE).astype(dq_ref.dtype)
+
+
+def cross_forward_kernel(
+    q_ref, k_ref, v_ref, qa_ref, ka_ref, o_ref, lse_ref, kx, vx, s_scr, m_scr, a_scr
+):
     @pl.when(pl.program_id(1) == 0)
     def _():
         forward_prep(k_ref, v_ref, ka_ref, kx, vx)
 
-    keys = k_ref.shape[0]
-    forward_block(0, keys, False, q_ref, qa_ref, kx, vx, o_ref, lse_ref)
+    full = k_ref.shape[0] // CHUNK
+    forward_block(
+        0, full, None, CHUNK, False, q_ref, qa_ref, kx, vx, o_ref, lse_ref, s_scr, m_scr, a_scr, full
+    )
 
 
 def cross_forward(q, kv, qa, ka):
@@ -195,7 +251,7 @@
             jax.ShapeDtypeStruct((rows, width), BF),
             jax.ShapeDtypeStruct((rows, width), F32),
         ],
-        scratch_shapes=[pltpu.VMEM((2, keys, 128), BF)] * 2,
+        scratch_shapes=forward_scratch(block, keys),
         compiler_params=params(48),
         cost_estimate=cost(16 * rows * keys * width, 8 * rows * width, rows * keys * 12),
         name="cross_forward",
@@ -204,16 +260,15 @@
 
 def cross_backward_kernel(
     q_ref, k_ref, v_ref, do_ref, o_ref, lse_ref, qa_ref, ka_ref,
-    dq_ref, dk_ref, dv_ref, kx, vx, km, dk_acc, dv_acc,
+    dq_ref, dk_ref, dv_ref, kx, vx, km, dk_acc, dv_acc, dq_acc,
 ):
     @pl.when(pl.program_id(1) == 0)
     def _():
         backward_prep(k_ref, v_ref, ka_ref, kx, vx, km, dk_acc, dv_acc)
 
-    keys = k_ref.shape[0]
     backward_block(
-        0, keys, False, q_ref, do_ref, o_ref, lse_ref, qa_ref, kx, vx, km,
-        dq_ref, dk_acc, dv_acc,
+        0, k_ref.shape[0] // CHUNK, None, CHUNK, False, q_ref[...], do_ref[...], o_ref, lse_ref,
+        qa_ref, kx, vx, km, dq_ref, dk_acc, dv_acc, dq_acc, 2,
     )
 
     @pl.when(pl.program_id(1) == pl.num_programs(1) - 1)
@@ -248,15 +303,11 @@
             jax.ShapeDtypeStruct((keys, width), BF),
             jax.ShapeDtypeStruct((keys, width), BF),
         ],
-        scratch_shapes=[pltpu.VMEM((2, keys, 128), BF)] * 3 + [pltpu.VMEM((keys, 128), F32)] * 2,
+        scratch_shapes=backward_scratch(block, keys),
         compiler_params=params(48),
         cost_estimate=cost(40 * rows * keys * width, 12 * rows * width, rows * keys * 12),
         name="cross_backward",
     )(q, kv, kv, do, o, lse, qa, ka)
-
-
-def counts_for(blocks, least):
-    return list(range(least, min(blocks, 8) + 1))
 
 
 def grain_of(block):
@@ -269,95 +320,39 @@
     first = segs.reshape(total // block, block)[:, 0]
     start = jnp.sum((segs[None, :] < first[:, None]).astype(jnp.int32), axis=1)
     ends = (jnp.arange(total // block, dtype=jnp.int32) + 1) * block
-    need = (ends - start // grain * grain) // grain
-    return jnp.minimum(need, counts_for(total // grain, block // grain)[-1])
+    return (ends - start // grain * grain) // grain
+
+
+def self_range(count, i, block):
+    grain = grain_of(block)
+    before = count - block // grain
+    per = CHUNK // grain
+    lo = pl.multiple_of((i + 1) * block - count * grain, grain)
+    return lo, before // per, before % per, grain
 
 
 def self_forward_kernel(
-    count_ref, slot_ref, q_ref, k_ref, v_ref, qa_ref, ka_ref, o_ref, lse_ref, kx, vx
+    count_ref, slot_ref, q_ref, k_ref, v_ref, qa_ref, ka_ref, o_ref, lse_ref,
+    kx, vx, s_scr, m_scr, a_scr,
 ):
     i = pl.program_id(1)
-    block = q_ref.shape[0]
-    grain = grain_of(block)
 
     @pl.when(i == 0)
     def _():
         forward_prep(k_ref, v_ref, ka_ref, kx, vx)
 
-    for n in counts_for(k_ref.shape[0] // grain, block // grain):
-
-        @pl.when(count_ref[i] == n)
-        def _():
-            lo = pl.multiple_of((i + 1) * block - n * grain, grain)
-            forward_block(lo, n * grain, True, q_ref, qa_ref, kx, vx, o_ref, lse_ref)
-
-
-def self_specs(block, total):
+    forward_block(
+        *self_range(count_ref[i], i, q_ref.shape[0]), True, q_ref, qa_ref, kx, vx, o_ref, lse_ref,
+        s_scr, m_scr, a_scr, 1,
+    )
+
+
+def self_forward(counts, slots, q, k, v, qa, ka, block):
+    total, width = q.shape
     row = pl.BlockSpec((block, 128), lambda h, i, n, s: (i, h))
     col = pl.BlockSpec((total, 128), lambda h, i, n, s: (0, h))
-    dealt = pl.BlockSpec((block, 128), lambda h, i, n, s: (s[i], h))
-    qa = pl.BlockSpec((block, 128), lambda h, i, n, s: (i, 0))
-    ka = pl.BlockSpec((total, 128), lambda h, i, n, s: (0, 0))
-    return row, col, dealt, qa, ka
-
-
-def self_forward(counts, slots, q, k, v, qa, ka, block):
-    total, width = q.shape
-    row, col, dealt, qas, kas = self_specs(block, total)
     return pl.pallas_call(
         self_forward_kernel,
-        grid_spec=pltpu.PrefetchScalarGridSpec(
-            num_scalar_prefetch=2,
-            grid=(width // 128, total // block),
-            in_specs=[row, col, col, qas, kas],
-            out_specs=[dealt, row],
-            scratch_shapes=[pltpu.VMEM((2, total, 128), BF)] * 2,
-        ),
-        out_shape=[
-            jax.ShapeDtypeStruct((total, width), BF),
-            jax.ShapeDtypeStruct((total, width), F32),
-        ],
-        compiler_params=params(48),
-        cost_estimate=cost(8 * total * total * width, 8 * total * width, total * total * 3),
-        name="self_forward",
-    )(counts, slots, q, k, v, qa, ka)
-
-
-def self_backward_kernel(
-    count_ref, slot_ref, q_ref, k_ref, v_ref, own_ref, far_ref, o_ref, lse_ref, qa_ref, ka_ref,
-    dq_ref, dk_ref, dv_ref, kx, vx, km, dk_acc, dv_acc, do_ref, *, per_dev,
-):
-    i = pl.program_id(1)
-    block = q_ref.shape[0]
-    grain = grain_of(block)
-    do_ref[...] = jnp.where(slot_ref[i] < per_dev, own_ref[...], far_ref[...])
-
-    @pl.when(i == 0)
-    def _():
-        backward_prep(k_ref, v_ref, ka_ref, kx, vx, km, dk_acc, dv_acc)
-
-    for n in counts_for(k_ref.shape[0] // grain, block // grain):
-
-        @pl.when(count_ref[i] == n)
-        def _():
-            lo = pl.multiple_of((i + 1) * block - n * grain, grain)
-            backward_block(
-                lo, n * grain, True, q_ref, do_ref, o_ref, lse_ref, qa_ref, kx, vx, km,
-                dq_ref, dk_acc, dv_acc,
-            )
-
-    @pl.when(i == pl.num_programs(1) - 1)
-    def _():
-        dk_ref[...] = (dk_acc[...] * LN2).astype(BF)
-        dv_ref[...] = dv_acc[...].astype(BF)
-
-
-def self_backward(counts, slots, q, k, v, own, far, o, lse, qa, ka, block):
-    total, width = q.shape
-    per_dev = own.shape[0] // block
-    row, col, dealt, qas, kas = self_specs(block, total)
-    return pl.pallas_call(
-        functools.partial(self_backward_kernel, per_dev=per_dev),
         grid_spec=pltpu.PrefetchScalarGridSpec(
             num_scalar_prefetch=2,
             grid=(width // 128, total // block),
@@ -365,21 +360,72 @@
                 row,
                 col,
                 col,
-                pl.BlockSpec((block, 128), lambda h, i, n, s: (jnp.minimum(s[i], per_dev - 1), h)),
-                pl.BlockSpec((block, 128), lambda h, i, n, s: (jnp.maximum(s[i] - per_dev, 0), h)),
-                dealt,
+                pl.BlockSpec((block, 128), lambda h, i, n, s: (i, 0)),
+                pl.BlockSpec((total, 128), lambda h, i, n, s: (0, 0)),
+            ],
+            out_specs=[pl.BlockSpec((block, 128), lambda h, i, n, s: (s[i], h)), row],
+            scratch_shapes=forward_scratch(block, total),
+        ),
+        out_shape=[
+            jax.ShapeDtypeStruct((total, width), BF),
+            jax.ShapeDtypeStruct((total, width), F32),
+        ],
+        compiler_params=params(48),
+        cost_estimate=cost(8 * total * total * width, 8 * total * width, total * total * 3),
+        name="self_forward",
+    )(counts, slots, q, k, v, qa, ka)
+
+
+def self_backward_kernel(
+    count_ref, slot_ref, q_ref, k_ref, v_ref, own_ref, far_ref, o_ref, lse_ref, qa_ref, ka_ref,
+    dq_ref, dk_ref, dv_ref, kx, vx, km, dk_acc, dv_acc, dq_acc, *, per_dev,
+):
+    i = pl.program_id(0)
+    do = jnp.where(slot_ref[i] < per_dev, own_ref[...], far_ref[...])
+
+    @pl.when(i == 0)
+    def _():
+        backward_prep(k_ref, v_ref, ka_ref, kx, vx, km, dk_acc, dv_acc)
+
+    backward_block(
+        *self_range(count_ref[i], i, q_ref.shape[0]), True, q_ref[...], do, o_ref, lse_ref, qa_ref,
+        kx, vx, km, dq_ref, dk_acc, dv_acc, dq_acc, 1,
+    )
+
+    @pl.when(i == pl.num_programs(0) - 1)
+    def _():
+        dk_ref[...] = (dk_acc[...] * LN2).astype(BF)
+        dv_ref[...] = dv_acc[...].astype(BF)
+
+
+def self_backward(pair, counts, slots, q, k, v, own, far, o, lse, qa, ka, block):
+    total = q.shape[0]
+    per_dev = own.shape[0] // block
+    row = pl.BlockSpec((block, 128), lambda i, n, s: (i, pair))
+    col = pl.BlockSpec((total, 128), lambda i, n, s: (0, pair))
+    whole = pl.BlockSpec((total, 128), lambda i, n, s: (0, 0))
+    return pl.pallas_call(
+        functools.partial(self_backward_kernel, per_dev=per_dev),
+        grid_spec=pltpu.PrefetchScalarGridSpec(
+            num_scalar_prefetch=2,
+            grid=(total // block,),
+            in_specs=[
                 row,
-                qas,
-                kas,
+                col,
+                col,
+                pl.BlockSpec((block, 128), lambda i, n, s: (jnp.minimum(s[i], per_dev - 1), pair)),
+                pl.BlockSpec((block, 128), lambda i, n, s: (jnp.maximum(s[i] - per_dev, 0), pair)),
+                pl.BlockSpec((block, 128), lambda i, n, s: (s[i], pair)),
+                row,
+                pl.BlockSpec((block, 128), lambda i, n, s: (i, 0)),
+                whole,
             ],
-            out_specs=[row, col, col],
-            scratch_shapes=[pltpu.VMEM((2, total, 128), BF)] * 3
-            + [pltpu.VMEM((total, 128), F32)] * 2
-            + [pltpu.VMEM((block, 128), BF)],
+            out_specs=[pl.BlockSpec((block, 128), lambda i, n, s: (i, 0)), whole, whole],
+            scratch_shapes=backward_scratch(block, total),
         ),
-        out_shape=[jax.ShapeDtypeStruct((total, width), BF)] * 3,
+        out_shape=[jax.ShapeDtypeStruct((total, 128), BF)] * 3,
         compiler_params=params(48),
-        cost_estimate=cost(20 * total * total * width, 12 * total * width, total * total * 3),
+        cost_estimate=cost(20 * total * total * 128, 12 * total * 128, total * total),
         name="self_backward",
     )(counts, slots, q, k, v, own, far, o, lse, qa, ka)
 
@@ -712,11 +758,20 @@
     )(me, pieces)
 
 
-def mid_grads_kernel(turn_ref, *refs, count):
+def deal_rows(core, full, send_ref, keep_ref):
+    count, size = send_ref.shape[:2]
+    for i in range(count):
+        for ref, c in ((send_ref, 1 - core), (keep_ref, core)):
+            ref[i] = full[pl.ds(pl.multiple_of((2 * i + c) * size, 16), size), :]
+
+
+def mid_grads_kernel(turn_ref, core_ref, *refs, count, deal):
     o_refs = refs[:count]
-    da_ref, n2_ref, dq_ref, own_ref, far_ref, dk_ref, dv_ref, o2_ref, dc_ref, g_ref = refs[count:]
+    da_ref, n2_ref, dq_ref, own_ref, far_ref, dk_ref, dv_ref, o2_ref, dc_ref = refs[count : count + 9]
+    outs = refs[count + 9 :]
+    full = outs[-1]
     m = pl.program_id(0)
-    dim = g_ref.shape[0]
+    dim = full.shape[0]
     width = o_refs[0].shape[1]
     ours = own_ref.shape[0]
 
@@ -728,44 +783,59 @@
 
             @pl.when(base < dim)
             def _():
-                g_ref[pl.ds(base, width), :] = term
+                full[pl.ds(base, width), :] = term
 
     for at, right in ((2, dk_ref), (3, dv_ref)):
 
         @pl.when(m == at)
         def _():
             total = tn(own_ref[...], right[:ours, :]) + tn(far_ref[...], right[ours:, :])
-            g_ref[...] = total.astype(BF)
+            full[...] = total.astype(BF)
 
     for at, left, right in ((1, n2_ref, dq_ref), (4, o2_ref, dc_ref)):
 
         @pl.when(m == at)
         def _():
-            g_ref[...] = tn(left[...], right[...]).astype(BF)
-
-
-def mid_grads(turn, pieces, da, n2, dq2, own, far, dk2, dv2, o2, dc):
-    dim = n2.shape[1]
-    rows = n2.shape[0]
+            full[...] = tn(left[...], right[...]).astype(BF)
+
+    if deal:
+        deal_rows(core_ref[0], full, outs[0], outs[1])
+    else:
+        outs[0][...] = full[...]
+
+
+def dealt_out(dim, block, total, index, deal):
+    if not deal:
+        return [pl.BlockSpec((dim, block), lambda *a: (0, index(*a)))], [
+            jax.ShapeDtypeStruct((dim, total), BF)
+        ]
+    spec = pl.BlockSpec((8, dim // 16, block), lambda *a: (0, 0, index(*a)))
+    return [spec] * 2, [jax.ShapeDtypeStruct((8, dim // 16, total), BF)] * 2
+
+
+def mid_grads(turn, core, pieces, da, n2, dq2, own, far, dk2, dv2, o2, dc, deal):
+    rows, dim = n2.shape
     args = (*pieces, da, n2, dq2, own, far, dk2, dv2, o2, dc)
     shapes = [(rows, a.shape[1]) for a in pieces] + [a.shape for a in args[len(pieces) :]]
     flops = 2 * dim * dim * (3 * rows + 2 * dk2.shape[0])
-    return pl.pallas_call(
-        functools.partial(mid_grads_kernel, count=len(pieces)),
+    specs, outs = dealt_out(dim, dim, 5 * dim, lambda m, t, c: m, deal)
+    return pl.pallas_call(
+        functools.partial(mid_grads_kernel, count=len(pieces), deal=deal),
         grid_spec=pltpu.PrefetchScalarGridSpec(
-            num_scalar_prefetch=1,
+            num_scalar_prefetch=2,
             grid=(5,),
             in_specs=[
-                pl.BlockSpec(shape, lambda m, t: (0, 0), pipeline_mode=pl.Buffered(1))
+                pl.BlockSpec(shape, lambda m, t, c: (0, 0), pipeline_mode=pl.Buffered(1))
                 for shape in shapes
             ],
-            out_specs=pl.BlockSpec((dim, dim), lambda m, t: (0, m)),
+            out_specs=specs,
+            scratch_shapes=[pltpu.VMEM((dim, dim), BF)],
         ),
-        out_shape=jax.ShapeDtypeStruct((dim, 5 * dim), BF),
+        out_shape=outs,
         compiler_params=params(48),
         cost_estimate=cost(flops, 24 * MIB),
         name="mid_grads",
-    )(turn, *args)
+    )(turn, core, *args)
 
 
 def enc_back_kernel(dk_ref, dv_ref, wk_ref, wv_ref, far_ref, own_ref, *, far_blocks):
@@ -804,7 +874,7 @@
             jax.ShapeDtypeStruct((own_rows, dim), F32),
         ],
         compiler_params=params(48),
-        cost_estimate=cost(4 * keys * dim * dim, 8 * keys * dim),
+        cost_estimate=cost(keys * dim, keys),
         name="enc_backward",
     )(dk, dv, w2, w2)
 
@@ -864,107 +934,113 @@
     )(turn, dq, w2, h1, dh2, gain, *([wo] * count))
 
 
-def normed_sum(dn, x):
-    return jnp.sum(dn * (x * rms_scale(x)), axis=0, keepdims=True)
-
-
-def qkv_far_kernel(order_ref, dq_ref, dk_ref, dv_ref, w_ref, x_ref, dn_ref, s_ref):
-    d = jnp.concatenate([dq_ref[...], dk_ref[...], dv_ref[...]], axis=1)
-    dn = nt(d, w_ref[...])
-    dn_ref[...] = dn.astype(BF)
-
-    @pl.when(pl.program_id(0) == 0)
-    def _():
-        s_ref[...] = jnp.zeros_like(s_ref)
-
-    s_ref[0:1, :] += normed_sum(dn, x_ref[...].astype(F32))
-
-
-def qkv_back_far(order, dq, dk, dv, w, x_far, block):
-    width, dim = dq.shape[1], x_far.shape[1]
-    first = order.shape[0] - x_far.shape[0] // block
-    row = pl.BlockSpec((block, width), lambda i, o: (o[i + first], 0))
-    line = pl.BlockSpec((block, dim), lambda i, o: (i, 0))
-    whole = lambda i, o: (0, 0)
-    return pl.pallas_call(
-        qkv_far_kernel,
-        grid_spec=pltpu.PrefetchScalarGridSpec(
-            num_scalar_prefetch=1,
-            grid=(x_far.shape[0] // block,),
-            in_specs=[row, row, row, pl.BlockSpec(w.shape, whole), line],
-            out_specs=[line, pl.BlockSpec((8, dim), whole)],
-        ),
-        out_shape=[
-            jax.ShapeDtypeStruct(x_far.shape, BF),
-            jax.ShapeDtypeStruct((8, dim), F32),
-        ],
-        compiler_params=params(48),
-        cost_estimate=cost(6 * x_far.shape[0] * dim * width, 10 * x_far.shape[0] * dim),
-        name="qkv_back_far",
-    )(order, dq, dk, dv, w, x_far)
-
-
-def qkv_own_kernel(
-    order_ref, dq_ref, dk_ref, dv_ref, w_ref, n_ref, x_ref, far_ref, dn_ref, g_ref, acc, s_acc, *, per_dev
-):
+def joined(refs):
+    return jnp.concatenate([r[...] for r in refs], axis=1)
+
+
+def qkv_grads_kernel(core_ref, *refs, count, deal):
+    d_refs = refs[:count]
+    n_ref, w_ref, gain_ref, extra_ref = refs[count : count + 4]
+    outs = refs[count + 4 :]
+    acc, full = outs[-2:]
     i = pl.program_id(0)
-    d = jnp.concatenate([dq_ref[...], dk_ref[...], dv_ref[...]], axis=1)
-    term = tn(n_ref[...], d)
+    term = tn(n_ref[...], joined(d_refs))
 
     @pl.when(i == 0)
     def _():
         acc[...] = term
-        s_acc[...] = far_ref[...]
 
     @pl.when(i > 0)
     def _():
         acc[...] += term
 
-    @pl.when(i < per_dev)
-    def _():
-        dn = nt(d, w_ref[...])
-        dn_ref[...] = dn
-        s_acc[0:1, :] += normed_sum(dn, x_ref[...].astype(F32))
-
     @pl.when(i == pl.num_programs(0) - 1)
     def _():
         width = acc.shape[1]
-        g_ref[:, :width] = acc[...].astype(BF)
-        g_ref[:, width:] = jnp.broadcast_to(s_acc[0:1, :], (128, s_acc.shape[1])).T.astype(BF)
-
-
-def qkv_back_own(order, dq, dk, dv, w, n, x_own, far_sum, block):
-    total, width = dq.shape
-    dim = n.shape[1]
-    per_dev = x_own.shape[0] // block
-    row = pl.BlockSpec((block, width), lambda i, o: (o[i], 0))
-    ours = pl.BlockSpec((block, dim), lambda i, o: (jnp.minimum(i, per_dev - 1), 0))
-    whole = lambda i, o: (0, 0)
-    return pl.pallas_call(
-        functools.partial(qkv_own_kernel, per_dev=per_dev),
+        grad = acc[...]
+        gains = jnp.sum(grad * w_ref[...].astype(F32), axis=1, keepdims=True) / gain_ref[:, :1]
+        extra = extra_ref[...]
+        full[:, :width] = grad.astype(BF)
+        full[:, width:] = jnp.where(lanes(extra.shape) == 0, gains, extra).astype(BF)
+        if deal:
+            deal_rows(core_ref[0], full, outs[0], outs[1])
+        else:
+            outs[0][...] = full[...]
+
+
+def qkv_grads(core, ds, n, w, gain, extra, deal):
+    total, dim = n.shape
+    block = min(512, total)
+    width = w.shape[1]
+    specs, outs = dealt_out(dim, width + 128, width + 128, lambda i, c: 0, deal)
+    whole = lambda i, c: (0, 0)
+    return pl.pallas_call(
+        functools.partial(qkv_grads_kernel, count=len(ds), deal=deal),
         grid_spec=pltpu.PrefetchScalarGridSpec(
             num_scalar_prefetch=1,
             grid=(total // block,),
-            in_specs=[
-                row,
-                row,
-                row,
+            in_specs=[pl.BlockSpec((block, 128), lambda i, c: (i, 0))] * len(ds)
+            + [
+                pl.BlockSpec((block, dim), lambda i, c: (i, 0)),
                 pl.BlockSpec(w.shape, whole),
-                pl.BlockSpec((block, dim), lambda i, o: (o[i], 0)),
-                ours,
-                pl.BlockSpec((8, dim), whole),
+                pl.BlockSpec((dim, 128), whole),
+                pl.BlockSpec((dim, 128), whole),
             ],
-            out_specs=[ours, pl.BlockSpec((dim, 3 * width + 128), whole)],
-            scratch_shapes=[pltpu.VMEM((dim, 3 * width), F32), pltpu.VMEM((8, dim), F32)],
+            out_specs=specs,
+            scratch_shapes=[pltpu.VMEM((dim, width), F32), pltpu.VMEM((dim, width + 128), BF)],
         ),
-        out_shape=[
-            jax.ShapeDtypeStruct(x_own.shape, F32),
-            jax.ShapeDtypeStruct((dim, 3 * width + 128), BF),
-        ],
+        out_shape=outs,
         compiler_params=params(48),
-        cost_estimate=cost(9 * total * dim * width, 10 * total * dim),
-        name="qkv_back_own",
-    )(order, dq, dk, dv, w, n, x_own, far_sum)
+        cost_estimate=cost(2 * total * dim * width, 6 * total * dim),
+        name="qkv_grads",
+    )(core, *ds, n, w, gain, extra)
+
+
+def qkv_back_kernel(order_ref, *refs, count):
+    dn_ref = refs[count + 1]
+    dn_ref[...] = nt(joined(refs[:count]), refs[count][...]).astype(dn_ref.dtype)
+
+
+def qkv_back(order, first, ds, w, rows, dtype, block):
+    dim = w.shape[0]
+    return pl.pallas_call(
+        functools.partial(qkv_back_kernel, count=len(ds)),
+        grid_spec=pltpu.PrefetchScalarGridSpec(
+            num_scalar_prefetch=1,
+            grid=(rows // block,),
+            in_specs=[pl.BlockSpec((block, 128), lambda i, o: (o[i + first], 0))] * len(ds)
+            + [pl.BlockSpec(w.shape, lambda i, o: (0, 0))],
+            out_specs=pl.BlockSpec((block, dim), lambda i, o: (i, 0)),
+        ),
+        out_shape=jax.ShapeDtypeStruct((rows, dim), dtype),
+        compiler_params=params(48),
+        cost_estimate=cost(2 * rows * dim * w.shape[1], 10 * rows * dim),
+        name="qkv_back",
+    )(order, *ds, w)
+
+
+def finish_kernel(x_ref, dh_ref, g_ref, own_ref, *refs):
+    dn = own_ref[...]
+    for ref in refs[:-1]:
+        dn = dn + ref[...].astype(F32)
+    dh, _ = norm_back(x_ref[...].astype(F32), g_ref[...], dn)
+    refs[-1][...] = dh_ref[...] + dh
+
+
+def finish(x, dh1, gain, own, got):
+    rows, dim = x.shape
+    block = min(256, rows)
+    row = pl.BlockSpec((block, dim), lambda i: (i, 0))
+    return pl.pallas_call(
+        finish_kernel,
+        grid=(rows // block,),
+        in_specs=[row, row, pl.BlockSpec((1, dim), lambda i: (0, 0)), row] + [row] * len(got),
+        out_specs=row,
+        out_shape=jax.ShapeDtypeStruct((rows, dim), F32),
+        compiler_params=params(32),
+        cost_estimate=cost(10 * rows * dim, 16 * rows * dim),
+        name="finish",
+    )(x, dh1, gain, own, *got)
 
 
 def turned(n, k):
@@ -1026,14 +1102,12 @@
         self.swap_core = [(i, i ^ 1) for i in range(n_parts)]
         self.swap_x = [(i, i ^ 2) for i in range(n_parts)]
 
-    def over_core(self, grad):
-        rows = grad.shape[0] // (4 * self.n_fsdp)
-        g = grad.reshape(self.n_fsdp, 2, 2, rows, grad.shape[1])
-        got = lax.ppermute(pick(g, 1 - self.core, 2), "parts", self.swap_core).astype(F32)
-        g = pick(g, self.core, 2).astype(F32)
-        send = (pick(g, 1 - self.x, 1) + pick(got, 1 - self.x, 1)).astype(BF)
-        keep = (pick(g, self.x, 1) + pick(got, self.x, 1)).astype(BF)
-        return send, keep
+    def over_core(self, send, keep):
+        shape = (self.n_fsdp, 2) + send.shape[1:]
+        got = lax.ppermute(send, "parts", self.swap_core).reshape(shape)
+        keep = keep.reshape(shape)
+        add = lambda i: (pick(keep, i, 1).astype(F32) + pick(got, i, 1).astype(F32)).astype(BF)
+        return add(1 - self.x), add(self.x)
 
     def over_x(self, send, keep):
         got = lax.ppermute(send, "parts", self.swap_x)
@@ -1065,15 +1139,6 @@
             for c in range(2)
         ]
         return jnp.concatenate(pieces).astype(F32)
-
-
-def sum_everywhere(value, sizes):
-    for axis, size in sizes:
-        bit = 1
-        while bit < size:
-            value = value + lax.ppermute(value, axis, [(i, i ^ bit) for i in range(size)])
-            bit *= 2
-    return value
 
 
 def local(
@@ -1169,7 +1234,8 @@
 
         w_down = lax.all_gather(down_out, "fsdp", axis=0, tiled=True).reshape(4, 8, 64, dim)
         w3 = jnp.stack([packed(gate_in), packed(up_in), w_down], axis=2)
-    enc_far = from_ctx(enc_own)
+    x_far, enc_sent = lax.optimization_barrier((x_far, enc_own))
+    enc_far = from_ctx(enc_sent)
 
     n1, q, k, v = qkv_forward(order_here, x_own, x_far, gain_self, w1, block)
     spot = jnp.arange(128, dtype=jnp.int32)[None, :] % HEAD
@@ -1199,72 +1265,100 @@
     dh1, da, stat3, *do1 = before_self(turn, dq2, w2, h1, dh2, gain_cross, wo, width)
     do_far = [lax.ppermute(do1[i], "ctx", turned(n_ctx, -i)) for i in range(1, n_ctx)]
     do_far = do_far[0] if n_ctx == 2 else jnp.concatenate(do_far, axis=0)
-    g_mid = mid_grads(turn, pieces, da, n2, dq2, enc_own, enc_far, dk2, dv2, o2, dc)
+    do_own = do1[0]
+    core = jnp.reshape(part % 2, (1,)).astype(jnp.int32)
+    g_mid = mid_grads(
+        turn, core, pieces, da, n2, dq2, enc_own, enc_far, dk2, dv2, o2, dc, fast
+    )
     d_far, enc_grad = enc_backward(dk2, dv2, w2, enc_rows)
+
+    sums = jnp.sum(jnp.concatenate([stat1[:2], stat2[:2]], axis=0), axis=1)
+    extra = jnp.concatenate(
+        [
+            jnp.zeros((dim, 1), F32),
+            stat2[2][:, None],
+            stat3[0][:, None],
+            jnp.broadcast_to(sums[None], (dim, 4)),
+            jnp.zeros((dim, 121), F32),
+        ],
+        axis=1,
+    )
+    gain_wide = jnp.broadcast_to(gain_self.reshape(dim, 1), (dim, 128))
+
+    def self_pair(pair, own, far):
+        return self_backward(
+            pair, counts, slots, q, k, v, own, far, o1, lse1, seg_q, seg_k, block
+        )
+
+    pairs = width // 128
+    if fast:
+        net = Plane(part, place, z, n_parts, n_fsdp)
+        send, keep = net.over_core(*g_mid)
+        do_own, do_far, send, d_far, extra = lax.optimization_barrier(
+            (do_own, do_far, send, d_far, extra)
+        )
     enc_got = [
         lax.ppermute(d_far[(i - 1) * enc_rows : i * enc_rows], "ctx", turned(n_ctx, i))
         for i in range(1, n_ctx)
     ]
+    if fast:
+        by_pair = [self_pair(0, do_own, do_far)]
+        g_mid = net.over_x(send, keep)
+        g_mid, do_far = lax.optimization_barrier((g_mid, by_pair[0][0], do_far))[::2]
+        by_pair.append(self_pair(1, do_own, do_far))
+        g_mid = net.over_fsdp(g_mid)
+        g_mid, part_ff, enc_got, do_far = lax.optimization_barrier(
+            (g_mid, part_ff, enc_got, do_far, by_pair[1][0])
+        )[:4]
+        by_pair.append(self_pair(2, do_own, do_far))
+        wide_ff = net.widen_ctx(part_ff)
+        g_mid = net.over_ctx(g_mid)
+        by_pair[2], wide_ff, g_mid = lax.optimization_barrier((by_pair[2], wide_ff, g_mid))
+    else:
+        by_pair = [self_pair(i, do_own, do_far) for i in range(pairs)]
     for piece in enc_got:
         enc_grad = enc_grad + piece.astype(F32)
-
-    small = jnp.concatenate([stat1[:2], stat2[:3], stat3[:1], jnp.zeros((2, dim), F32)], axis=0)
-    small = sum_everywhere(small, (("parts", n_parts), ("ctx", n_ctx), ("fsdp", n_fsdp)))
-    entries = float(n_parts * n_ctx * n_fsdp * rows * dim)
-    rms_values = jnp.sqrt(jnp.sum(small[:4], axis=1) / entries)
-    grad_gmlp = lax.dynamic_slice_in_dim(small[4], z * shard, shard)
-    grad_gcross = lax.dynamic_slice_in_dim(small[5], z * shard, shard)
-
-    do_own = do1[0]
-    if fast:
-        net = Plane(part, place, z, n_parts, n_fsdp)
-        send, keep = net.over_core(g_mid)
-        do_own, do_far, send, keep, d_far = lax.optimization_barrier(
-            (do_own, do_far, send, keep, d_far)
-        )
-        g_mid = net.over_x(send, keep)
-
-    dq, dk, dv = self_backward(counts, slots, q, k, v, do_own, do_far, o1, lse1, seg_q, seg_k, block)
-    if fast:
-        dq, dk, dv, part_ff, g_mid = lax.optimization_barrier((dq, dk, dv, part_ff, g_mid))
-    dn_far, far_sum = qkv_back_far(order_here, dq, dk, dv, w1, x_far, block)
+    ds = [d[i] for i in range(3) for d in by_pair]
+    g_qkv = qkv_grads(core, ds, n1, w1, gain_wide, extra, fast)
+    dn_far = qkv_back(order_here, per_dev, ds, w1, total - rows, BF, block)
     dn_got = [
         lax.ppermute(dn_far[(i - 1) * rows : i * rows], "ctx", turned(n_ctx, i))
         for i in range(1, n_ctx)
     ]
-    dn_own, g_qkv = qkv_back_own(order_here, dq, dk, dv, w1, n1, x_own, far_sum, block)
-    for piece in dn_got:
-        dn_own = dn_own + piece.astype(F32)
-    d_in, _ = norm_back(x_own.astype(F32), gain_self, dn_own)
-    decoder_grad = dh1 + d_in
+    dn_own = qkv_back(order_here, 0, ds, w1, rows, F32, block)
+    decoder_grad = finish(x_own, dh1, gain_self, dn_own, dn_got)
 
     if fast:
-        send, keep = net.over_core(g_qkv)
-        sum_mid = net.rows(net.widen(net.over_ctx(net.over_fsdp(g_mid))))
+        send, keep = net.over_core(*g_qkv)
+        sum_mid = net.rows(net.widen(g_mid))
         me = jnp.stack([net.core, net.x, place]).astype(jnp.int32)
-        grad_gate, grad_up, grad_down = unpack(me, net.widen(net.widen_ctx(part_ff)))
+        grad_gate, grad_up, grad_down = unpack(me, net.widen(wide_ff))
         wide = net.widen(net.widen_ctx(net.over_fsdp(net.over_x(send, keep))))
         every = jnp.stack([net.rows(pick(wide, i ^ place, 2)) for i in range(2)])
     else:
 
-        def total(g):
+        def total_of(g):
             g = lax.psum_scatter(g, "fsdp", scatter_dimension=0, tiled=True).astype(F32)
             return lax.psum(g, ("parts", "ctx"))
 
-        sum_mid = total(g_mid)
+        (g_mid,), (g_qkv,) = g_mid, g_qkv
+        sum_mid = total_of(g_mid)
         flat = [
             g_ff[:, :, i].reshape(4, 8, 64, 3, 256).transpose(0, 3, 2, 1, 4).reshape(dim, hidden)
             for i in range(2)
         ]
-        grad_gate, grad_up = total(flat[0]), total(flat[1])
-        grad_down = total(g_ff[:, :, 2].reshape(hidden, dim))
+        grad_gate, grad_up = total_of(flat[0]), total_of(flat[1])
+        grad_down = total_of(g_ff[:, :, 2].reshape(hidden, dim))
         sum_qkv = lax.psum_scatter(g_qkv, "fsdp", scatter_dimension=0, tiled=True).astype(F32)
         every = lax.all_gather(lax.psum(sum_qkv, "parts"), "ctx", axis=0)
     grads_qkv = [
         jnp.concatenate([every[c, :, i * width : (i + 1) * width] for c in range(n_ctx)], axis=1)[:, :dim]
         for i in range(3)
     ]
-    grad_gself = jnp.sum(every[:, :, 3 * width], axis=0)
+    tail = jnp.sum(every[:, :, 3 * width : 3 * width + 8], axis=0)
+    grad_gself, grad_gmlp, grad_gcross = tail[:, 0], tail[:, 1], tail[:, 2]
+    entries = float(n_parts * n_ctx * n_fsdp * rows * dim)
+    rms_values = jnp.sqrt(tail[0, jnp.array([3, 4, 5, 6])] / entries)
     mids = [sum_mid[:, i * dim : (i + 1) * dim] for i in range(5)]
     return (
         layer_out[None],

time: 668 us -> 579 us (0.87)
  waiting for transfers between devices: 169 us -> 103 us
  starting transfers between devices: 53.8 us -> 30.4 us
  local copies, waits for them, and re-layouts: 28.4 us -> 49.7 us
  Pallas kernels: 353 us -> 340 us
  other arithmetic: 41.7 us -> 29.9 us
    ppermute x2, waiting for transfers between devices: 49 us -> 6.04 us  [from_ctx(): lax.ppermute(value, 'ctx', turned(n_ctx, -k))]
    ppermute x7 -> x2, waiting for transfers between devices: 33.9 us -> 2.77 us  [over_core(): got = lax.ppermute(send, 'parts', self.swap_core).reshape(shape)]
    unnamed x90 -> x170, local copies, waits for them, and re-layouts: 16.6 us -> 36.6 us
    all_gather x1, waiting for transfers between devices: 0.01 us -> 17 us  [local(): lax.all_gather(jnp.stack([column_piece(gate_in), column_piece(up_in), row...]
    ppermute x7 -> x2, starting transfers between devices: 16.4 us -> 0.31 us  [over_core(): got = lax.ppermute(send, 'parts', self.swap_core).reshape(shape)]
    pallas_call x1 -> x3, Pallas kernels: 68.5 us -> 52.6 us  [self_backward(): pl.pallas_call(functools.partial(self_backward_kernel, per_dev=per_dev),...]
    ppermute x1, waiting for transfers between devices: 16.1 us -> 6.58 us  [local(): lax.ppermute(o1[i * rows:(i + 1) * rows], 'ctx', turned(n_ctx, i))]
    ppermute x2, waiting for transfers between devices: 0.01 us -> 9.41 us  [widen_ctx(): return jnp.stack([g, lax.ppermute(g, 'ctx', turned(2, 1))])]
  transfers between devices with their start and end apart: 37 -> 32, of which waited for: 18 -> 15; matrix products, arithmetic and copies ran while one was open for 7% -> 6% of each run, Pallas kernels for 46% -> 50%
where the time goes in v3:
time: 579 us; the launch traced here: 568 us
  Pallas kernels  340 us (59%)
  waiting for transfers between devices  103 us (18%)
  local copies, waits for them, and re-layouts  49.7 us (9%)
  starting transfers between devices  30.4 us (5%)
  other arithmetic  29.9 us (5%)
  between operations  15.7 us (3%)
    pallas_call x1, Pallas kernels, cross_backward(): pl.pallas_call(cross_backward_kernel, grid=(pairs, rows // block), in_spe...  84.1 us
    pallas_call x3, Pallas kernels, self_backward(): pl.pallas_call(functools.partial(self_backward_kernel, per_dev=per_dev),...  52.6 us
    pallas_call x1, Pallas kernels, feed_forward(): pl.pallas_call(mlp_kernel, grid=(steps,), in_specs=[full, full, pl.BlockS...  46.3 us
    unnamed x170, local copies, waits for them, and re-layouts  36.6 us
    pallas_call x1, Pallas kernels, cross_forward(): pl.pallas_call(cross_forward_kernel, grid=(pairs, rows // block), in_spec...  35.7 us
    pallas_call x1, Pallas kernels, self_forward(): pl.pallas_call(self_forward_kernel, grid_spec=pltpu.PrefetchScalarGridSpe...  30.4 us
    pallas_call x1, Pallas kernels, mid_grads(): pl.pallas_call(functools.partial(mid_grads_kernel, count=len(pieces), dea...  17.7 us
    all_gather x1, waiting for transfers between devices, local(): lax.all_gather(jnp.stack([column_piece(gate_in), column_piece(up_in), row...  17 us
  transfers between devices with their start and end apart: 32, of which 15 were waited for; matrix products, arithmetic and copies ran while one was open for 6% of the time, Pallas kernels for 50%

profile of v3, /device:TPU:9, one launch (start us, length us, event | category | flops | bytes accessed | tf_op | source)
XLA Modules:
  0.0 568.1 jit_solution(14462682658011544553)
XLA Ops:
  14.3 1.5 collective-permute-start.1
  15.8 4.1 collective-permute-start.2
  25.0 5.1 collective-permute-done.1
  30.1 9.4 %collective-permute-done.2 = bf16[96,1280]{1,0:T(8,128)(2,1)S(1)} collective-permute-done((bf16[96,1280]{1,0:T(8,128)(2,1)S(1)}, bf16[96,1280]{1,0:T(8,128)(2,1)S(1)}, u32[]{:S(2)}, u32[]{:S(2)}) %collective-permute-start.2) | collective-permute-done | bytes 245792 | tf_op jit(solution)/shard_map/ppermute | solution.py:1076
  39.6 2.3 collective-permute-start.4
  44.6 1.8 select_convert_fusion.2.qa_ref
  46.4 3.2 select_convert_fusion
  54.5 3.8 collective-permute-done.far_ref
  58.3 1.9 collective-permute-start.6
  60.2 8.5 %qkv_forward.1 = (bf16[2048,768]{1,0:T(8,128)(2,1)}, bf16[2048,384]{1,0:T(8,128)(2,1)S(1)}, bf16[2048,384]{1,0:T(8,128)(2,1)S(1)}, bf16[2048,384]{1,0:T(8,128)(2,1)S(1)}) custom-call(s32[4]{0:T(128)S(1)} %dynamic_slice.131.order_ref, bf16[1024,768]{1,0:T(8,128)(2,1)} %bitcast.135, bf16[1024,768]{1,0:T(8,128)(2,1)} %collective-permute-done.far_ref, ...), custom_call_target="tpu_custom_call" | custom-call | flops 3623878656 | bytes 12582912 | tf_op jit(solution)/shard_map/qkv_forward/pallas_call | solution.py:451
  69.8 30.4 %self_forward.1 = (bf16[2048,384]{1,0:T(8,128)(2,1)S(1)}, f32[2048,384]{1,0:T(8,128)}) custom-call(s32[4]{0:T(128)S(1)} %and_select_fusion.3.count_ref, s32[4]{0:T(128)S(1)} %get-tuple-element.85.slot_ref, bf16[2048,384]{1,0:T(8,128)(2,1)S(1)} %get-tuple-element.89.q_ref, bf16[2048,384]{1,0:T(8,128)(2,1)S(1)} %get-tuple-element.90.k_ref, ...), custom_call_target="tpu_custom_call" | custom-call | flops 12884901888 | bytes 6291456 | tf_op jit(solution)/shard_map/self_forward/pallas_call | solution.py:354
  101.0 2.2 collective-permute-done.6.far_ref.refs_6_
  107.3 8.5 %enc_forward.1.k_ref.v_ref = bf16[2048,1536]{1,0:T(8,128)(2,1)} custom-call(bf16[1024,768]{1,0:T(8,128)(2,1)S(1)} %bitcast.141, bf16[1024,768]{1,0:T(8,128)(2,1)S(1)} %copy-done.50, bf16[768,3840]{1,0:T(8,128)(2,1)} %all-gather.4.cloned.1.call-done.w_ref.refs_2_.refs_3_.refs_5_.wc_ref.wq_ref.refs_0_.refs_1_.wk_ref.wv_ref), custom_call_target="tpu_custom_call" | custom-call | flops 4831838208 | bytes 12582912 | tf_op jit(solution)/shard_map/enc_forward/pallas_call | solution.py:485
  115.7 6.6 %collective-permute-done.5.refs_1_ = bf16[1024,384]{1,0:T(8,128)(2,1)S(1)} collective-permute-done((bf16[1024,384]{1,0:T(8,128)(2,1)S(1)}, bf16[1024,384]{1,0:T(8,128)(2,1)S(1)}, u32[]{:S(2)}, u32[]{:S(2)}) %collective-permute-start.5) | collective-permute-done | bytes 786464 | tf_op jit(solution)/shard_map/ppermute | solution.py:1247
  123.2 9.2 %after_self.1 = (f32[1024,768]{1,0:T(8,128)}, bf16[1024,768]{1,0:T(8,128)(2,1)}, bf16[1024,768]{1,0:T(8,128)(2,1)}, f32[8,768]{1,0:T(8,128)}) custom-call(s32[2]{0:T(128)} %and_select_fusion.5.turn_ref, bf16[1024,768]{1,0:T(8,128)(2,1)} %bitcast.136, bf16[2048,384]{1,0:T(8,128)(2,1)} %copy-done.6, bf16[1024,384]{1,0:T(8,128)(2,1)} %copy-done.34, ...), custom_call_target="tpu_custom_call" | custom-call | flops 2415919104 | bytes 11010048 | tf_op jit(solution)/shard_map/after_self/pallas_call | solution.py:533
  132.5 1.5 copy-done.52
  134.1 35.7 %cross_forward.1 = (bf16[1024,768]{1,0:T(8,128)(2,1)S(1)}, f32[1024,768]{1,0:T(8,128)}) custom-call(bf16[1024,768]{1,0:T(8,128)(2,1)S(1)} %copy-done.52, bf16[2048,1536]{1,0:T(8,128)(2,1)} %enc_forward.1.k_ref.v_ref, bf16[2048,1536]{1,0:T(8,128)(2,1)} %enc_forward.1.k_ref.v_ref, bf16[1024,128]{1,0:T(8,128)(2,1)S(1)} %broadcast_in_dim.96.qa_ref, ...), custom_call_target="tpu_custom_call" | custom-call | flops 25769803776 | bytes 6291456 | tf_op jit(solution)/shard_map/cross_forward/pallas_call | solution.py:239
  170.9 17.0 %all-gather.6.cloned.1.call-done = bf16[96,64,768]{2,1,0:T(8,128)(2,1)} async-done(((bf16[3,64,768]{2,1,0:T(8,128)(2,1)}), bf16[96,64,768]{2,1,0:T(8,128)(2,1)}) %all-gather.6.cloned.1.call-update) | async-done | bytes 9437200 | tf_op jit(solution)/shard_map/all_gather | solution.py:1222
  187.9 46.3 %feed_forward.1 = (bf16[1024,768]{1,0:T(8,128)(2,1)}, f32[1024,768]{1,0:T(8,128)}, bf16[1024,768]{1,0:T(8,128)(2,1)}, bf16[1024,768]{1,0:T(8,128)(2,1)}, f32[8,7...) custom-call(bf16[1024,768]{1,0:T(8,128)(2,1)} %copy-done.62, f32[1024,768]{1,0:T(8,128)} %get-tuple-element.98.h1_ref.h_ref, ...), custom_call_target="tpu_custom_call" | custom-call | flops 32614907904 | bytes 41943040 | tf_op jit(solution)/shard_map/feed_forward/pallas_call | solution.py:682
  237.0 84.1 %cross_backward.1 = (bf16[1024,768]{1,0:T(8,128)(2,1)S(1)}, bf16[2048,768]{1,0:T(8,128)(2,1)}, bf16[2048,768]{1,0:T(8,128)(2,1)}) custom-call(bf16[1024,768]{1,0:T(8,128)(2,1)S(1)} %copy-done.53, bf16[2048,1536]{1,0:T(8,128)(2,1)} %enc_forward.1.k_ref.v_ref, bf16[2048,1536]{1,0:T(8,128)(2,1)} %enc_forward.1.k_ref.v_ref, bf16[1024,768]{1,0:T(8,128)(2,1)S(1)} %copy-done.63, ...), custom_call_target="tpu_custom_call" | custom-call | flops 64424509440 | bytes 9437184 | tf_op jit(solution)/shard_map/cross_backward/pallas_call | solution.py:287
  322.3 10.4 %before_self.1 = (f32[1024,768]{1,0:T(8,128)}, bf16[1024,768]{1,0:T(8,128)(2,1)}, f32[8,768]{1,0:T(8,128)}, bf16[1024,384]{1,0:T(8,128)(2,1)}, bf16[1024,384]{1,0:T(8,128)(2,1)}) custom-call(s32[2]{0:T(128)} %and_select_fusion.5.turn_ref, bf16[1024,768]{1,0:T(8,128)(2,1)} %copy-done.33, ...), custom_call_target="tpu_custom_call" | custom-call | flops 2415919104 | bytes 14155776 | tf_op jit(solution)/shard_map/before_self/pallas_call | solution.py:909
  334.2 17.7 %mid_grads.1 = (bf16[8,48,3840]{2,1,0:T(8,128)(2,1)}, bf16[8,48,3840]{2,1,0:T(8,128)(2,1)}) custom-call(s32[2]{0:T(128)S(1)} %copy-done.46, s32[1]{0:T(128)} %bitcast.6.core_ref, bf16[2048,384]{1,0:T(8,128)(2,1)S(1)} %copy-done.7, bf16[1024,384]{1,0:T(8,128)(2,1)S(1)} %copy-done.35, bf16[1024,768]{1,0:T(8,128)(2,1)S(1)} %copy-done.54, ...), custom_call_target="tpu_custom_call" | custom-call | flops 8455716864 | bytes 25165824 | tf_op jit(solution)/shard_map/mid_grads/pallas_call | solution.py:822
  357.7 8.4 %enc_backward.1 = (bf16[1024,768]{1,0:T(8,128)(2,1)S(1)}, f32[1024,768]{1,0:T(8,128)S(1)}) custom-call(bf16[2048,768]{1,0:T(8,128)(2,1)} %get-tuple-element.109.refs_7_.dk_ref, bf16[2048,768]{1,0:T(8,128)(2,1)} %get-tuple-element.110.refs_8_.dv_ref, ...), custom_call_target="tpu_custom_call" | custom-call | flops 1572864 | bytes 2048 | tf_op jit(solution)/shard_map/enc_backward/pallas_call | solution.py:859
  367.3 2.9 fusion.1
  370.2 4.3 collective-permute-done.7.far_ref
  380.7 17.6 %self_backward.3 = (bf16[2048,128]{1,0:T(8,128)(2,1)S(1)}, bf16[2048,128]{1,0:T(8,128)(2,1)S(1)}, bf16[2048,128]{1,0:T(8,128)(2,1)S(1)}) custom-call(s32[4]{0:T(128)S(1)} %and_select_fusion.3.count_ref, s32[4]{0:T(128)S(1)} %get-tuple-element.85.slot_ref, bf16[2048,384]{1,0:T(8,128)(2,1)S(1)} %copy-done.58, bf16[2048,384]{1,0:T(8,128)(2,1)} %copy-done.60, ...), custom_call_target="tpu_custom_call" | custom-call | flops 10737418240 | bytes 3145728 | tf_op jit(solution)/shard_map/self_backward/pallas_call | solution.py:407
  398.2 9.6 %collective-permute-done.9 = bf16[4,48,3840]{2,1,0:T(8,128)(2,1)} collective-permute-done((bf16[4,48,3840]{2,1,0:T(8,128)(2,1)}, bf16[4,48,3840]{2,1,0:T(8,128)(2,1)}, u32[]{:S(2)}, u32[]{:S(2)}) %collective-permute-start.9) | collective-permute-done | bytes 1474592 | tf_op jit(solution)/shard_map/ppermute | solution.py:1113
  407.9 2.4 fusion
  410.5 2.4 collective-permute-start.11
  412.9 17.7 %self_backward.4 = (bf16[2048,128]{1,0:T(8,128)(2,1)S(1)}, bf16[2048,128]{1,0:T(8,128)(2,1)S(1)}, bf16[2048,128]{1,0:T(8,128)(2,1)S(1)}) custom-call(s32[4]{0:T(128)S(1)} %and_select_fusion.3.count_ref, s32[4]{0:T(128)S(1)} %get-tuple-element.85.slot_ref, bf16[2048,384]{1,0:T(8,128)(2,1)S(1)} %copy-done.58, bf16[2048,384]{1,0:T(8,128)(2,1)} %copy-done.60, ...), custom_call_target="tpu_custom_call" | custom-call | flops 10737418240 | bytes 3145728 | tf_op jit(solution)/shard_map/self_backward/pallas_call | solution.py:407
  433.0 7.0 %collective-permute-done.11 = bf16[48,3840]{1,0:T(8,128)(2,1)S(1)} collective-permute-done((bf16[48,3840]{1,0:T(8,128)(2,1)S(1)}, bf16[48,3840]{1,0:T(8,128)(2,1)S(1)}, u32[]{:S(2)}, u32[]{:S(2)}) %collective-permute-start.11) | collective-permute-done | bytes 368672 | tf_op jit(solution)/shard_map/ppermute | solution.py:1120
  440.1 5.6 collective-permute-done.12
  452.8 17.3 %self_backward.5 = (bf16[2048,128]{1,0:T(8,128)(2,1)S(1)}, bf16[2048,128]{1,0:T(8,128)(2,1)S(1)}, bf16[2048,128]{1,0:T(8,128)(2,1)S(1)}) custom-call(s32[4]{0:T(128)S(1)} %and_select_fusion.3.count_ref, s32[4]{0:T(128)S(1)} %get-tuple-element.85.slot_ref, bf16[2048,384]{1,0:T(8,128)(2,1)S(1)} %copy-done.59, bf16[2048,384]{1,0:T(8,128)(2,1)} %copy-done.60, ...), custom_call_target="tpu_custom_call" | custom-call | flops 10737418240 | bytes 3145728 | tf_op jit(solution)/shard_map/self_backward/pallas_call | solution.py:407
  472.7 10.1 %qkv_grads.1 = (bf16[8,48,1280]{2,1,0:T(8,128)(2,1)}, bf16[8,48,1280]{2,1,0:T(8,128)(2,1)}) custom-call(s32[1]{0:T(128)} %bitcast.6.core_ref, bf16[2048,128]{1,0:T(8,128)(2,1)S(1)} %copy-done.10, bf16[2048,128]{1,0:T(8,128)(2,1)S(1)} %copy-done.19, bf16[2048,128]{1,0:T(8,128)(2,1)S(1)} %get-tuple-element.134.refs_2_, bf16[2048,128]{1,0:T(8,128)(2,1)S(1)} %copy-done.13, ...), custom_call_target="tpu_custom_call" | custom-call | flops 3623878656 | bytes 9437184 | tf_op jit(solution)/shard_map/qkv_grads/pallas_call | solution.py:977
  483.0 2.8 collective-permute-done.17
  487.1 1.8 collective-permute-start.18
  489.0 3.5 add_bitcast_fusion
  494.0 5.4 qkv_back.3
  499.9 5.7 qkv_back.2.own_ref
  508.0 12.7 %collective-permute-done.25 = bf16[48,3840]{1,0:T(8,128)(2,1)S(1)} collective-permute-done((bf16[48,3840]{1,0:T(8,128)(2,1)S(1)}, bf16[48,3840]{1,0:T(8,128)(2,1)S(1)}, u32[]{:S(2)}, u32[]{:S(2)}) %collective-permute-start.25) | collective-permute-done | bytes 368672 | tf_op jit(solution)/shard_map/ppermute | solution.py:1130
  521.8 3.0 collective-permute-done.21
  525.5 2.1 collective-permute-start.28
  527.6 9.4 %collective-permute-done.22 = bf16[48,1280]{1,0:T(8,128)(2,1)S(1)} collective-permute-done((bf16[48,1280]{1,0:T(8,128)(2,1)S(1)}, bf16[48,1280]{1,0:T(8,128)(2,1)S(1)}, u32[]{:S(2)}, u32[]{:S(2)}) %collective-permute-start.22) | collective-permute-done | bytes 122912 | tf_op jit(solution)/shard_map/ppermute | solution.py:1127
  538.0 4.2 collective-permute-done.23
  542.2 3.4 collective-permute-start.24
  545.8 1.6 fusion.48
  550.0 3.0 finish.1
  553.2 2.9 unpack.1
  (293 shorter events, 74.4 us)
Async XLA Ops:
  7.3 97.2 %all-gather.4.cloned.1.call-start = ((), (), s32[]{:S(2)}) async-start(), calls=%async_computation.1 | async-start | bytes 6082560 | tf_op jit(solution)/shard_map/all_gather | solution.py:1213
  12.0 175.9 %all-gather.6.cloned.1.call-start = ((), (), s32[]{:S(2)}) async-start(), calls=%async_computation.3 | async-start | bytes 9732096 | tf_op jit(solution)/shard_map/all_gather | solution.py:1222
  13.0 11.2 %copy-start.81 = (s32[1,4]{1,0:T(1,128)S(1)}, s32[1,4]{1,0:T(1,128)}, u32[]{:S(2)}) copy-start(s32[1,4]{1,0:T(1,128)} %param.24) | copy-start | bytes 52
  13.8 432.9 %reduce-scatter.2.cloned.1.call-start = ((), (), s32[]{:S(2)}) async-start(), calls=%async_computation.2 | async-start | bytes 9732096 | tf_op jit(solution)/shard_map/reduce_scatter | solution.py:1262
  14.2 10.8 %collective-permute-start.3 = (bf16[96,1280]{1,0:T(8,128)(2,1)S(1)}, bf16[96,1280]{1,0:T(8,128)(2,1)S(1)}, u32[]{:S(2)}, u32[]{:S(2)}) collective-permute-start(bf16[96,1280]{1,0:T(8,128)(2,1)S(1)} %fusion.18), channel_id=1, source_target_pairs={{0,3},{1,0},{2,1},{3,2},{4,7},{5,4},{6,5},{7,6},{8,11},{9,8},{10,9... | collective-permute-start | bytes 737288 | tf_op jit(solution)/shard_map/ppermute | solution.py:1076
  14.3 15.8 %collective-permute-start.1 = (bf16[96,1280]{1,0:T(8,128)(2,1)S(1)}, bf16[96,1280]{1,0:T(8,128)(2,1)S(1)}, u32[]{:S(2)}, u32[]{:S(2)}) collective-permute-start(bf16[96,1280]{1,0:T(8,128)(2,1)S(1)} %fusion.18), channel_id=1, source_target_pairs={{0,1},{1,2},{2,3},{3,0},{4,5},{5,6},{6,7},{7,4},{8,9},{9,10},{10,1... | collective-permute-start | bytes 737288 | tf_op jit(solution)/shard_map/ppermute | solution.py:1076
  15.8 23.7 %collective-permute-start.2 = (bf16[96,1280]{1,0:T(8,128)(2,1)S(1)}, bf16[96,1280]{1,0:T(8,128)(2,1)S(1)}, u32[]{:S(2)}, u32[]{:S(2)}) collective-permute-start(bf16[96,1280]{1,0:T(8,128)(2,1)S(1)} %fusion.18), channel_id=1, source_target_pairs={{0,2},{1,3},{2,0},{3,1},{4,6},{5,7},{6,4},{7,5},{8,10},{9,11},{10,... | collective-permute-start | bytes 737288 | tf_op jit(solution)/shard_map/ppermute | solution.py:1076
  19.9 38.4 %collective-permute-start = (bf16[1024,768]{1,0:T(8,128)(2,1)S(1)}, bf16[1024,768]{1,0:T(8,128)(2,1)}, u32[]{:S(2)}, u32[]{:S(2)}) collective-permute-start(bf16[1024,768]{1,0:T(8,128)(2,1)S(1)} %bitcast.137), channel_id=1, source_target_pairs={{0,4},{4,0},{1,5},{5,1},{2,6},{6,2},{3,7},{7,3},{8,12},{12,8},{9,1... | collective-permute-start | bytes 4718600 | tf_op jit(solution)/shard_map/ppermute | solution.py:1190
  39.6 10.0 %collective-permute-start.4 = (bf16[4,96,1280]{2,1,0:T(8,128)(2,1)S(1)}, bf16[4,96,1280]{2,1,0:T(8,128)(2,1)S(1)}, u32[]{:S(2)}, u32[]{:S(2)}) collective-permute-start(bf16[4,96,1280]{2,1,0:T(8,128)(2,1)S(1)} %pad_maximum_fusion.2.near_ref), channel_id=1, source_target_pairs={{0,8},{8,0},{16,24},{24,16},{1,9},{9,1},{17,25},{25,17},{2,10},{10... | collective-permute-start | bytes 2949128 | tf_op jit(solution)/shard_map/ppermute | solution.py:1078
  54.5 14.2 %copy-start.44 = (f32[1,768]{1,0:T(1,128)}, f32[1,768]{1,0:T(1,128)S(1)}, u32[]{:S(2)}) copy-start(f32[1,768]{1,0:T(1,128)S(1)} %get-tuple-element.201.g_ref) | copy-start | bytes 9220
  58.3 45.0 %collective-permute-start.6 = (bf16[1024,768]{1,0:T(8,128)(2,1)}, bf16[1024,768]{1,0:T(8,128)(2,1)S(1)}, u32[]{:S(2)}, u32[]{:S(2)}) collective-permute-start(bf16[1024,768]{1,0:T(8,128)(2,1)} %bitcast.139), channel_id=1, source_target_pairs={{0,4},{4,0},{1,5},{5,1},{2,6},{6,2},{3,7},{7,3},{8,12},{12,8},{9,1... | collective-permute-start | bytes 4718600 | tf_op jit(solution)/shard_map/ppermute | solution.py:1190
  69.8 30.4 %copy-start.57 = (bf16[2048,384]{1,0:T(8,128)(2,1)}, bf16[2048,384]{1,0:T(8,128)(2,1)S(1)}, u32[]{:S(2)}) copy-start(bf16[2048,384]{1,0:T(8,128)(2,1)S(1)} %get-tuple-element.89.q_ref) | copy-start | bytes 4718596
  69.8 30.4 %copy-start.60 = (bf16[2048,384]{1,0:T(8,128)(2,1)}, bf16[2048,384]{1,0:T(8,128)(2,1)S(1)}, u32[]{:S(2)}) copy-start(bf16[2048,384]{1,0:T(8,128)(2,1)S(1)} %get-tuple-element.90.k_ref) | copy-start | bytes 4718596
  100.2 15.5 %copy-start.6 = (bf16[2048,384]{1,0:T(8,128)(2,1)}, bf16[2048,384]{1,0:T(8,128)(2,1)S(1)}, u32[]{:S(2)}) copy-start(bf16[2048,384]{1,0:T(8,128)(2,1)S(1)} %get-tuple-element.92.refs_0_.o_ref) | copy-start | bytes 4718596
  100.3 22.0 %collective-permute-start.5 = (bf16[1024,384]{1,0:T(8,128)(2,1)S(1)}, bf16[1024,384]{1,0:T(8,128)(2,1)S(1)}, u32[]{:S(2)}, u32[]{:S(2)}) collective-permute-start(bf16[1024,384]{1,0:T(8,128)(2,1)S(1)} %slice.96), channel_id=1, source_target_pairs={{0,4},{4,0},{1,5},{5,1},{2,6},{6,2},{3,7},{7,3},{8,12},{12,8},{9,1... | collective-permute-start | bytes 2359304 | tf_op jit(solution)/shard_map/ppermute | solution.py:1247
  351.9 15.4 %collective-permute-start.8 = (bf16[8,48,3840]{2,1,0:T(8,128)(2,1)}, bf16[8,48,3840]{2,1,0:T(8,128)(2,1)}, u32[]{:S(2)}, u32[]{:S(2)}) collective-permute-start(bf16[8,48,3840]{2,1,0:T(8,128)(2,1)} %get-tuple-element.113), channel_id=1, source_target_pairs={{0,8},{8,0},{16,24},{24,16},{1,9},{9,1},{17,25},{25,17},{2,10},{10... | collective-permute-start | bytes 8847368 | tf_op jit(solution)/shard_map/ppermute | solution.py:1107
  352.9 21.6 %collective-permute-start.7 = (bf16[1024,384]{1,0:T(8,128)(2,1)}, bf16[1024,384]{1,0:T(8,128)(2,1)}, u32[]{:S(2)}, u32[]{:S(2)}) collective-permute-start(bf16[1024,384]{1,0:T(8,128)(2,1)} %get-tuple-element.106), channel_id=1, source_target_pairs={{0,4},{4,0},{1,5},{5,1},{2,6},{6,2},{3,7},{7,3},{8,12},{12,8},{9,1... | collective-permute-start | bytes 2359304 | tf_op jit(solution)/shard_map/ppermute | solution.py:1266
  374.5 33.4 %collective-permute-start.9 = (bf16[4,48,3840]{2,1,0:T(8,128)(2,1)}, bf16[4,48,3840]{2,1,0:T(8,128)(2,1)}, u32[]{:S(2)}, u32[]{:S(2)}) collective-permute-start(bf16[4,48,3840]{2,1,0:T(8,128)(2,1)} %fusion.1), channel_id=1, source_target_pairs={{0,16},{8,24},{16,0},{24,8},{1,17},{9,25},{17,1},{25,9},{2,18},{10... | collective-permute-start | bytes 4423688 | tf_op jit(solution)/shard_map/ppermute | solution.py:1113
  375.6 71.0 %collective-permute-start.13 = (bf16[1024,768]{1,0:T(8,128)(2,1)}, bf16[1024,768]{1,0:T(8,128)(2,1)}, u32[]{:S(2)}, u32[]{:S(2)}) collective-permute-start(bf16[1024,768]{1,0:T(8,128)(2,1)} %copy-done.48), channel_id=1, source_target_pairs={{0,4},{4,0},{1,5},{5,1},{2,6},{6,2},{3,7},{7,3},{8,12},{12,8},{9,1... | collective-permute-start | bytes 4718600 | tf_op jit(solution)/shard_map/ppermute | solution.py:1301
  380.7 27.2 %copy-start.65 = (bf16[8,48,3840]{2,1,0:T(8,128)(2,1)S(1)}, bf16[8,48,3840]{2,1,0:T(8,128)(2,1)}, u32[]{:S(2)}) copy-start(bf16[8,48,3840]{2,1,0:T(8,128)(2,1)} %get-tuple-element.112) | copy-start | bytes 8847364
  398.2 12.1 %copy-start.9 = (bf16[2048,128]{1,0:T(8,128)(2,1)}, bf16[2048,128]{1,0:T(8,128)(2,1)S(1)}, u32[]{:S(2)}) copy-start(bf16[2048,128]{1,0:T(8,128)(2,1)S(1)} %get-tuple-element.121.refs_0_) | copy-start | bytes 1572868
  398.2 12.1 %copy-start.12 = (bf16[2048,128]{1,0:T(8,128)(2,1)}, bf16[2048,128]{1,0:T(8,128)(2,1)S(1)}, u32[]{:S(2)}) copy-start(bf16[2048,128]{1,0:T(8,128)(2,1)S(1)} %get-tuple-element.135.refs_3_) | copy-start | bytes 1572868
  398.2 12.1 %copy-start.15 = (bf16[2048,128]{1,0:T(8,128)(2,1)}, bf16[2048,128]{1,0:T(8,128)(2,1)S(1)}, u32[]{:S(2)}) copy-start(bf16[2048,128]{1,0:T(8,128)(2,1)S(1)} %get-tuple-element.138.refs_6_) | copy-start | bytes 1572868
  410.5 22.6 %collective-permute-start.10 = (bf16[48,3840]{1,0:T(8,128)(2,1)S(1)}, bf16[48,3840]{1,0:T(8,128)(2,1)S(1)}, u32[]{:S(2)}, u32[]{:S(2)}) collective-permute-start(bf16[48,3840]{1,0:T(8,128)(2,1)S(1)} %get-tuple-element.164), channel_id=1, source_target_pairs={{0,1},{1,2},{2,3},{3,0},{4,5},{5,6},{6,7},{7,4},{8,9},{9,10},{10,1... | collective-permute-start | bytes 1105928 | tf_op jit(solution)/shard_map/ppermute | solution.py:1120
  410.5 29.6 %collective-permute-start.11 = (bf16[48,3840]{1,0:T(8,128)(2,1)S(1)}, bf16[48,3840]{1,0:T(8,128)(2,1)S(1)}, u32[]{:S(2)}, u32[]{:S(2)}) collective-permute-start(bf16[48,3840]{1,0:T(8,128)(2,1)S(1)} %get-tuple-element.166), channel_id=1, source_target_pairs={{0,2},{1,3},{2,0},{3,1},{4,6},{5,7},{6,4},{7,5},{8,10},{9,11},{10,... | collective-permute-start | bytes 1105928 | tf_op jit(solution)/shard_map/ppermute | solution.py:1120
  412.9 32.8 %collective-permute-start.12 = (bf16[48,3840]{1,0:T(8,128)(2,1)S(1)}, bf16[48,3840]{1,0:T(8,128)(2,1)S(1)}, u32[]{:S(2)}, u32[]{:S(2)}) collective-permute-start(bf16[48,3840]{1,0:T(8,128)(2,1)S(1)} %get-tuple-element.165), channel_id=1, source_target_pairs={{0,3},{1,0},{2,1},{3,2},{4,7},{5,4},{6,5},{7,6},{8,11},{9,8},{10,9... | collective-permute-start | bytes 1105928 | tf_op jit(solution)/shard_map/ppermute | solution.py:1120
  446.7 24.4 %collective-permute-start.15 = (bf16[48,3840]{1,0:T(8,128)(2,1)}, bf16[48,3840]{1,0:T(8,128)(2,1)S(1)}, u32[]{:S(2)}, u32[]{:S(2)}) collective-permute-start(bf16[48,3840]{1,0:T(8,128)(2,1)} %fusion.6), channel_id=1, source_target_pairs={{0,4},{4,0},{1,5},{5,1},{2,6},{6,2},{3,7},{7,3},{8,12},{12,8},{9,1... | collective-permute-start | bytes 1105928 | tf_op jit(solution)/shard_map/ppermute | solution.py:1124
  447.2 23.0 %collective-permute-start.14 = (bf16[3,64,768]{2,1,0:T(8,128)(2,1)}, bf16[3,64,768]{2,1,0:T(8,128)(2,1)S(1)}, u32[]{:S(2)}, u32[]{:S(2)}) collective-permute-start(bf16[3,64,768]{2,1,0:T(8,128)(2,1)} %bitcast.158), channel_id=1, source_target_pairs={{0,4},{4,0},{1,5},{5,1},{2,6},{6,2},{3,7},{7,3},{8,12},{12,8},{9,1... | collective-permute-start | bytes 884744 | tf_op jit(solution)/shard_map/ppermute | solution.py:1127
  452.8 17.4 %copy-start.70 = (bf16[1,3,64,768]{3,2,1,0:T(8,128)(2,1)S(1)}, bf16[1,3,64,768]{3,2,1,0:T(8,128)(2,1)}, u32[]{:S(2)}) copy-start(bf16[1,3,64,768]{3,2,1,0:T(8,128)(2,1)} %reduce-scatter.2.cloned.1.call-done) | copy-start | bytes 884740
  452.8 18.3 %copy-start.68 = (bf16[48,3840]{1,0:T(8,128)(2,1)S(1)}, bf16[48,3840]{1,0:T(8,128)(2,1)}, u32[]{:S(2)}) copy-start(bf16[48,3840]{1,0:T(8,128)(2,1)} %fusion.6) | copy-start | bytes 1105924
  452.8 19.2 %copy-start.76 = (f32[768]{0:T(1024)S(1)}, f32[768]{0:T(1024)}, u32[]{:S(2)}) copy-start(f32[768]{0:T(1024)} %get-tuple-element.198) | copy-start | bytes 9220
  452.8 19.3 %copy-start.25 = (bf16[2048,128]{1,0:T(8,128)(2,1)S(1)}, bf16[2048,128]{1,0:T(8,128)(2,1)}, u32[]{:S(2)}) copy-start(bf16[2048,128]{1,0:T(8,128)(2,1)} %copy-done.24) | copy-start | bytes 1572868
  470.1 12.7 %copy-start.27 = (bf16[2048,128]{1,0:T(8,128)(2,1)}, bf16[2048,128]{1,0:T(8,128)(2,1)S(1)}, u32[]{:S(2)}) copy-start(bf16[2048,128]{1,0:T(8,128)(2,1)S(1)} %get-tuple-element.134.refs_2_) | copy-start | bytes 1572868
  470.1 12.7 %copy-start.29 = (bf16[2048,128]{1,0:T(8,128)(2,1)}, bf16[2048,128]{1,0:T(8,128)(2,1)S(1)}, u32[]{:S(2)}) copy-start(bf16[2048,128]{1,0:T(8,128)(2,1)S(1)} %get-tuple-element.137.refs_5_) | copy-start | bytes 1572868
  470.1 12.7 %copy-start.31 = (bf16[2048,128]{1,0:T(8,128)(2,1)}, bf16[2048,128]{1,0:T(8,128)(2,1)S(1)}, u32[]{:S(2)}) copy-start(bf16[2048,128]{1,0:T(8,128)(2,1)S(1)} %get-tuple-element.140.refs_8_) | copy-start | bytes 1572868
  482.8 3.0 collective-permute-start.17
  487.1 18.5 %collective-permute-start.18 = (bf16[4,48,1280]{2,1,0:T(8,128)(2,1)S(1)}, bf16[4,48,1280]{2,1,0:T(8,128)(2,1)S(1)}, u32[]{:S(2)}, u32[]{:S(2)}) collective-permute-start(bf16[4,48,1280]{2,1,0:T(8,128)(2,1)S(1)} %fusion.8), channel_id=1, source_target_pairs={{0,16},{8,24},{16,0},{24,8},{1,17},{9,25},{17,1},{25,9},{2,18},{10... | collective-permute-start | bytes 1474568 | tf_op jit(solution)/shard_map/ppermute | solution.py:1113
  492.5 32.8 %collective-permute-start.27 = (bf16[2,3,64,768]{3,2,1,0:T(8,128)(2,1)S(1)}, bf16[2,3,64,768]{3,2,1,0:T(8,128)(2,1)S(1)}, u32[]{:S(2)}, u32[]{:S(2)}) collective-permute-start(bf16[2,3,64,768]{3,2,1,0:T(8,128)(2,1)S(1)} %copy-done.66), channel_id=1, source_target_pairs={{0,16},{8,24},{16,0},{24,8},{1,17},{9,25},{17,1},{25,9},{2,18},{10... | collective-permute-start | bytes 1769480 | tf_op jit(solution)/shard_map/ppermute | solution.py:1130
  492.6 28.2 %collective-permute-start.25 = (bf16[48,3840]{1,0:T(8,128)(2,1)S(1)}, bf16[48,3840]{1,0:T(8,128)(2,1)S(1)}, u32[]{:S(2)}, u32[]{:S(2)}) collective-permute-start(bf16[48,3840]{1,0:T(8,128)(2,1)S(1)} %copy-done.67), channel_id=1, source_target_pairs={{0,16},{8,24},{16,0},{24,8},{1,17},{9,25},{17,1},{25,9},{2,18},{10... | collective-permute-start | bytes 1105928 | tf_op jit(solution)/shard_map/ppermute | solution.py:1130
  499.5 48.0 %collective-permute-start.16 = (bf16[1024,768]{1,0:T(8,128)(2,1)}, bf16[1024,768]{1,0:T(8,128)(2,1)S(1)}, u32[]{:S(2)}, u32[]{:S(2)}) collective-permute-start(bf16[1024,768]{1,0:T(8,128)(2,1)} %qkv_back.3), channel_id=1, source_target_pairs={{0,4},{4,0},{1,5},{5,1},{2,6},{6,2},{3,7},{7,3},{8,12},{12,8},{9,1... | collective-permute-start | bytes 4718600 | tf_op jit(solution)/shard_map/ppermute | solution.py:1325
  506.8 14.0 %collective-permute-start.19 = (bf16[48,1280]{1,0:T(8,128)(2,1)S(1)}, bf16[48,1280]{1,0:T(8,128)(2,1)S(1)}, u32[]{:S(2)}, u32[]{:S(2)}) collective-permute-start(bf16[48,1280]{1,0:T(8,128)(2,1)S(1)} %get-tuple-element.193), channel_id=1, source_target_pairs={{0,1},{1,2},{2,3},{3,0},{4,5},{5,6},{6,7},{7,4},{8,9},{9,10},{10,1... | collective-permute-start | bytes 368648 | tf_op jit(solution)/shard_map/ppermute | solution.py:1120
  506.9 14.9 %collective-permute-start.20 = (bf16[48,1280]{1,0:T(8,128)(2,1)S(1)}, bf16[48,1280]{1,0:T(8,128)(2,1)S(1)}, u32[]{:S(2)}, u32[]{:S(2)}) collective-permute-start(bf16[48,1280]{1,0:T(8,128)(2,1)S(1)} %get-tuple-element.195), channel_id=1, source_target_pairs={{0,2},{1,3},{2,0},{3,1},{4,6},{5,7},{6,4},{7,5},{8,10},{9,11},{10,... | collective-permute-start | bytes 368648 | tf_op jit(solution)/shard_map/ppermute | solution.py:1120
  520.7 4.0 collective-permute-start.21
  520.8 16.6 %collective-permute-start.26 = (bf16[2,48,3840]{2,1,0:T(8,128)(2,1)S(1)}, bf16[2,48,3840]{2,1,0:T(8,128)(2,1)S(1)}, u32[]{:S(2)}, u32[]{:S(2)}) collective-permute-start(bf16[2,48,3840]{2,1,0:T(8,128)(2,1)S(1)} %get-tuple-element.189), channel_id=1, source_target_pairs={{0,8},{8,0},{16,24},{24,16},{1,9},{9,1},{17,25},{25,17},{2,10},{10... | collective-permute-start | bytes 2211848 | tf_op jit(solution)/shard_map/ppermute | solution.py:1131
  524.8 12.2 %collective-permute-start.22 = (bf16[48,1280]{1,0:T(8,128)(2,1)S(1)}, bf16[48,1280]{1,0:T(8,128)(2,1)S(1)}, u32[]{:S(2)}, u32[]{:S(2)}) collective-permute-start(bf16[48,1280]{1,0:T(8,128)(2,1)S(1)} %fusion.23), channel_id=1, source_target_pairs={{0,4},{4,0},{1,5},{5,1},{2,6},{6,2},{3,7},{7,3},{8,12},{12,8},{9,1... | collective-permute-start | bytes 368648 | tf_op jit(solution)/shard_map/ppermute | solution.py:1127
  525.5 27.5 %collective-permute-start.28 = (bf16[2,2,3,64,768]{4,3,2,1,0:T(8,128)(2,1)S(1)}, bf16[2,2,3,64,768]{4,3,2,1,0:T(8,128)(2,1)S(1)}, u32[]{:S(2)}, u32[]{:S(2)}) collective-permute-start(bf16[2,2,3,64,768]{4,3,2,1,0:T(8,128)(2,1)S(1)} %get-tuple-element.168), channel_id=1, source_target_pairs={{0,8},{8,0},{16,24},{24,16},{1,9},{9,1},{17,25},{25,17},{2,10},{10... | collective-permute-start | bytes 3538952 | tf_op jit(solution)/shard_map/ppermute | solution.py:1131
  537.0 5.1 collective-permute-start.23
  542.2 13.9 %collective-permute-start.24 = (bf16[2,2,48,1280]{3,2,1,0:T(8,128)(2,1)S(1)}, bf16[2,2,48,1280]{3,2,1,0:T(8,128)(2,1)S(1)}, u32[]{:S(2)}, u32[]{:S(2)}) collective-permute-start(bf16[2,2,48,1280]{3,2,1,0:T(8,128)(2,1)S(1)} %get-tuple-element.192), channel_id=1, source_target_pairs={{0,8},{8,0},{16,24},{24,16},{1,9},{9,1},{17,25},{25,17},{2,10},{10... | collective-permute-start | bytes 1474568 | tf_op jit(solution)/shard_map/ppermute | solution.py:1131
  (66 other events, 259.3 us)
Sparse Core Ops, SparseCore 0:
  12.1 90.1 all-gather.3
  105.8 82.0 all-gather.5
  234.3 133.6 reduce-scatter.1

commit v4 on v3

--- a/solution.py
+++ b/solution.py
@@ -20,7 +20,7 @@
 BF = jnp.bfloat16
 F32 = jnp.float32
 MIB = 1 << 20
-ALL = ("fsdp", "parts", "ctx")
+AROUND = ("fsdp", "parts")
 
 
 def nn(a, b):
@@ -39,7 +39,7 @@
     return lax.broadcasted_iota(jnp.int32, shape, len(shape) - 1)
 
 
-def params(mib):
+def params(mib=60):
     return pltpu.CompilerParams(vmem_limit_bytes=mib * MIB)
 
 
@@ -117,26 +117,29 @@
     a_scr[...] = jnp.zeros_like(a_scr)
     last = s_scr.shape[2] - rows
 
-    def scores(key, at, size, masked=False):
+    def scores(key, at, size, start=None):
+        live = pl.ds(start or 0, rows - (start or 0))
         for h in range(2):
-            s = nt(sides[h], kx[h, pl.ds(key, size), :])
-            s = below(s, True) if masked else s
-            s_scr[h, :, pl.ds(at, size)] = s
-            m_scr[h] = jnp.maximum(m_scr[h], lane_max(s))
-
+            s = nt(sides[h][start or 0 :], kx[h, pl.ds(key, size), :])
+            s = s if start is None else below(s, True)
+            s_scr[h, live, pl.ds(at, size)] = s
+            m_scr[h, live, :] = jnp.maximum(m_scr[h, live, :], lane_max(s))
+
+    steps = range(0, rows, grain) if diag else ()
     end = sweep(scores, lo, full, odd, grain, unroll)
-    if diag:
-        scores(end, last, rows, True)
+    for start in steps:
+        scores(end + start, last + start, grain, start)
     tops = [jnp.max(m_scr[h], axis=1, keepdims=True) for h in range(2)]
 
-    def values(key, at, size):
+    def values(key, at, size, start=0):
+        live = pl.ds(start, rows - start)
         for h in range(2):
-            p = jnp.exp2(s_scr[h, :, pl.ds(at, size)] - tops[h]).astype(BF)
-            a_scr[h] += nn(p, vx[h, pl.ds(key, size), :])
+            p = jnp.exp2(s_scr[h, live, pl.ds(at, size)] - tops[h][start:]).astype(BF)
+            a_scr[h, live, :] += nn(p, vx[h, pl.ds(key, size), :])
 
     end = sweep(values, lo, full, odd, grain, unroll)
-    if diag:
-        values(end, last, rows)
+    for start in steps:
+        values(end + start, last + start, grain, start)
     wide = jnp.where(left, a_scr[0], a_scr[1])
     total = jnp.where(left, a_scr[1], a_scr[0])
     o_ref[...] = (wide / pltpu.roll(total, HEAD, 1)).astype(o_ref.dtype)
@@ -195,25 +198,26 @@
     dm = pair_of(do, zero)
     dq_acc[...] = jnp.zeros_like(dq_acc)
 
-    def step(key, _, size, masked=False):
+    def step(key, _, size, start=None):
         at = pl.ds(key, size)
+        live = slice(start or 0, rows)
         dq = dk = dv = None
         for h in range(2):
-            st = nt(kx[h, at, :], qx[h])
-            pt = jnp.exp2(below(st, False) if masked else st)
-            dp = nt(vx[h, at, :], dx[h])
+            st = nt(kx[h, at, :], qx[h][live])
+            pt = jnp.exp2(st if start is None else below(st, False))
+            dp = nt(vx[h, at, :], dx[h][live])
             ds = (pt * dp).astype(BF)
-            tv, tk, tq = nn(pt.astype(BF), dm[h]), nn(ds, qm[h]), tn(ds, km[h, at, :])
+            tv, tk, tq = nn(pt.astype(BF), dm[h][live]), nn(ds, qm[h][live]), tn(ds, km[h, at, :])
             dv = tv if dv is None else dv + tv
             dk = tk if dk is None else dk + tk
             dq = tq if dq is None else dq + tq
         dv_acc[at, :] += dv
         dk_acc[at, :] += dk
-        dq_acc[...] += dq
+        dq_acc[live, :] += dq
 
     end = sweep(step, lo, full, odd, grain, unroll)
-    if diag:
-        step(end, 0, rows, True)
+    for start in range(0, rows, grain) if diag else ():
+        step(end + start, 0, grain, start)
     dq_ref[...] = (dq_acc[...] * SCALE).astype(dq_ref.dtype)
 
 
@@ -252,7 +256,7 @@
             jax.ShapeDtypeStruct((rows, width), F32),
         ],
         scratch_shapes=forward_scratch(block, keys),
-        compiler_params=params(48),
+        compiler_params=params(),
         cost_estimate=cost(16 * rows * keys * width, 8 * rows * width, rows * keys * 12),
         name="cross_forward",
     )(q, kv, kv, qa, ka)
@@ -268,7 +272,7 @@
 
     backward_block(
         0, k_ref.shape[0] // CHUNK, None, CHUNK, False, q_ref[...], do_ref[...], o_ref, lse_ref,
-        qa_ref, kx, vx, km, dq_ref, dk_acc, dv_acc, dq_acc, 2,
+        qa_ref, kx, vx, km, dq_ref, dk_acc, dv_acc, dq_acc, k_ref.shape[0] // CHUNK,
     )
 
     @pl.when(pl.program_id(1) == pl.num_programs(1) - 1)
@@ -304,7 +308,7 @@
             jax.ShapeDtypeStruct((keys, width), BF),
         ],
         scratch_shapes=backward_scratch(block, keys),
-        compiler_params=params(48),
+        compiler_params=params(),
         cost_estimate=cost(40 * rows * keys * width, 12 * rows * width, rows * keys * 12),
         name="cross_backward",
     )(q, kv, kv, do, o, lse, qa, ka)
@@ -370,7 +374,7 @@
             jax.ShapeDtypeStruct((total, width), BF),
             jax.ShapeDtypeStruct((total, width), F32),
         ],
-        compiler_params=params(48),
+        compiler_params=params(),
         cost_estimate=cost(8 * total * total * width, 8 * total * width, total * total * 3),
         name="self_forward",
     )(counts, slots, q, k, v, qa, ka)
@@ -424,7 +428,7 @@
             scratch_shapes=backward_scratch(block, total),
         ),
         out_shape=[jax.ShapeDtypeStruct((total, 128), BF)] * 3,
-        compiler_params=params(48),
+        compiler_params=params(),
         cost_estimate=cost(20 * total * total * 128, 12 * total * 128, total * total),
         name="self_backward",
     )(counts, slots, q, k, v, own, far, o, lse, qa, ka)
@@ -463,7 +467,7 @@
         ),
         out_shape=[jax.ShapeDtypeStruct((total, dim), BF)]
         + [jax.ShapeDtypeStruct((total, width), BF)] * 3,
-        compiler_params=params(48),
+        compiler_params=params(),
         cost_estimate=cost(6 * total * dim * width, 8 * total * dim),
         name="qkv_forward",
     )(order, own, far, gain, w)
@@ -492,7 +496,7 @@
         ],
         out_specs=pl.BlockSpec((block, 2 * dim), lambda i: (i, 0)),
         out_shape=jax.ShapeDtypeStruct((keys, 2 * dim), BF),
-        compiler_params=params(48),
+        compiler_params=params(),
         cost_estimate=cost(4 * keys * dim * dim, 8 * keys * dim),
         name="enc_forward",
     )(own, far, w2)
@@ -547,7 +551,7 @@
             jax.ShapeDtypeStruct((rows, dim), BF),
             jax.ShapeDtypeStruct((8, dim), F32),
         ],
-        compiler_params=params(56),
+        compiler_params=params(),
         cost_estimate=cost(4 * rows * dim * dim, 14 * rows * dim),
         name="after_self",
     )(turn, x, *pieces, *([wo] * count), gain, w2)
@@ -721,18 +725,18 @@
             pltpu.VMEM((2, n_plane, tall, dim), BF),
             pltpu.SemaphoreType.DMA((2, 2)),
         ],
-        compiler_params=params(60),
+        compiler_params=params(),
         cost_estimate=cost(flops, 40 * MIB, rows * width * steps),
         name="feed_forward",
     )(o, h1, w2, gain, cot, w3, w3)
 
 
 def unpack_kernel(me_ref, p_ref, gate_ref, up_ref, down_ref):
-    core, x, place = me_ref[0], me_ref[1], me_ref[2]
+    core, x = me_ref[0], me_ref[1]
     tall = p_ref.shape[4]
     third = 256
     for p in range(8):
-        near = (core ^ ((p // 2) % 2), x ^ (p // 4), place ^ (p % 2))
+        near = (core ^ ((p // 2) % 2), x ^ (p // 4), p % 2)
         for t in range(3):
             at, to = pl.ds(t * tall, tall), pl.ds(p * third, third)
             lane = slice(t * third, (t + 1) * third)
@@ -753,7 +757,7 @@
             jax.ShapeDtypeStruct((3 * tall, 8 * 256), F32),
             jax.ShapeDtypeStruct((8 * tall, dim), F32),
         ],
-        compiler_params=params(32),
+        compiler_params=params(),
         name="unpack",
     )(me, pieces)
 
@@ -765,43 +769,74 @@
             ref[i] = full[pl.ds(pl.multiple_of((2 * i + c) * size, 16), size), :]
 
 
-def mid_grads_kernel(turn_ref, core_ref, *refs, count, deal):
-    o_refs = refs[:count]
-    da_ref, n2_ref, dq_ref, own_ref, far_ref, dk_ref, dv_ref, o2_ref, dc_ref = refs[count : count + 9]
-    outs = refs[count + 9 :]
-    full = outs[-1]
+def mid_grads_kernel(turn_ref, *refs, count, far_blocks):
+    n_in = count + 9
+    sources = refs[:n_in]
+    wk_ref, wv_ref, g_ref, far_out, own_out = refs[n_in : n_in + 5]
+    buffers = refs[n_in + 5 : 2 * n_in + 5]
+    sems = refs[-1]
     m = pl.program_id(0)
-    dim = full.shape[0]
-    width = o_refs[0].shape[1]
-    ours = own_ref.shape[0]
+    dim = g_ref.shape[0]
+    copies = [
+        pltpu.make_async_copy(
+            source.at[pl.ds(0, buffer.shape[0])] if source.shape != buffer.shape else source,
+            buffer,
+            sems.at[i],
+        )
+        for i, (source, buffer) in enumerate(zip(sources, buffers))
+    ]
+    n2, dq, da, *o_pieces, own, far, dk, dv, o2, dc = buffers
+    ours = own.shape[0]
+    width = o_pieces[0].shape[1]
 
     @pl.when(m == 0)
     def _():
+        for copy in copies:
+            copy.start()
+        for copy in copies[:2]:
+            copy.wait()
+        g_ref[...] = tn(n2[...], dq[...]).astype(BF)
+
+    @pl.when(m == 1)
+    def _():
+        for copy in copies[2 : 3 + count]:
+            copy.wait()
         for i in range(count):
             base = pl.multiple_of(turn_ref[i] * width, width)
-            term = tn(o_refs[i][...], da_ref[...]).astype(BF)
+            term = tn(o_pieces[i][...], da[...]).astype(BF)
 
             @pl.when(base < dim)
             def _():
-                full[pl.ds(base, width), :] = term
-
-    for at, right in ((2, dk_ref), (3, dv_ref)):
+                g_ref[pl.ds(base, width), :] = term
+
+    for at, right, first in ((2, dk, 3), (3, dv, 6)):
 
         @pl.when(m == at)
         def _():
-            total = tn(own_ref[...], right[:ours, :]) + tn(far_ref[...], right[ours:, :])
-            full[...] = total.astype(BF)
-
-    for at, left, right in ((1, n2_ref, dq_ref), (4, o2_ref, dc_ref)):
-
-        @pl.when(m == at)
-        def _():
-            full[...] = tn(left[...], right[...]).astype(BF)
-
-    if deal:
-        deal_rows(core_ref[0], full, outs[0], outs[1])
-    else:
-        outs[0][...] = full[...]
+            for copy in copies[count + first : count + 6 if at == 2 else count + 7]:
+                copy.wait()
+            g_ref[...] = (tn(own[...], right[:ours, :]) + tn(far[...], right[ours:, :])).astype(BF)
+
+    @pl.when(m == 4)
+    def _():
+        for copy in copies[count + 7 :]:
+            copy.wait()
+        g_ref[...] = tn(o2[...], dc[...]).astype(BF)
+
+    block = far_out.shape[0]
+    blocks = dk.shape[0] // block
+
+    def enc_rows(i):
+        at = pl.ds(pl.multiple_of(lax.rem(i + ours // block, blocks) * block, block), block)
+        return nt(dk[at, :], wk_ref[...]) + nt(dv[at, :], wv_ref[...])
+
+    @pl.when((m >= 5) & (m < 5 + far_blocks))
+    def _():
+        far_out[...] = enc_rows(m - 5).astype(BF)
+
+    @pl.when(m >= 5 + far_blocks)
+    def _():
+        own_out[...] = enc_rows(m - 5)
 
 
 def dealt_out(dim, block, total, index, deal):
@@ -813,70 +848,43 @@
     return [spec] * 2, [jax.ShapeDtypeStruct((8, dim // 16, total), BF)] * 2
 
 
-def mid_grads(turn, core, pieces, da, n2, dq2, own, far, dk2, dv2, o2, dc, deal):
+def mid_grads(turn, pieces, da, n2, dq2, own, far, dk2, dv2, o2, dc, w2):
     rows, dim = n2.shape
-    args = (*pieces, da, n2, dq2, own, far, dk2, dv2, o2, dc)
-    shapes = [(rows, a.shape[1]) for a in pieces] + [a.shape for a in args[len(pieces) :]]
-    flops = 2 * dim * dim * (3 * rows + 2 * dk2.shape[0])
-    specs, outs = dealt_out(dim, dim, 5 * dim, lambda m, t, c: m, deal)
+    args = (n2, dq2, da, *pieces, own, far, dk2, dv2, o2, dc)
+    shapes = [(rows, a.shape[1]) for a in args[: 3 + len(pieces)]]
+    shapes += [a.shape for a in args[3 + len(pieces) :]]
+    flops = 2 * dim * dim * (3 * rows + 4 * dk2.shape[0])
+    block = min(512, own.shape[0])
+    far_blocks, own_blocks = far.shape[0] // block, own.shape[0] // block
+    once = pl.Buffered(1)
+    column = lambda m, t: (0, jnp.where(m < 2, 1 - m, jnp.minimum(m, 4)))
     return pl.pallas_call(
-        functools.partial(mid_grads_kernel, count=len(pieces), deal=deal),
+        functools.partial(mid_grads_kernel, count=len(pieces), far_blocks=far_blocks),
         grid_spec=pltpu.PrefetchScalarGridSpec(
-            num_scalar_prefetch=2,
-            grid=(5,),
-            in_specs=[
-                pl.BlockSpec(shape, lambda m, t, c: (0, 0), pipeline_mode=pl.Buffered(1))
-                for shape in shapes
+            num_scalar_prefetch=1,
+            grid=(5 + far_blocks + own_blocks,),
+            in_specs=[pl.BlockSpec(memory_space=pl.ANY)] * len(args)
+            + [
+                pl.BlockSpec((dim, dim), lambda m, t: (0, 2), pipeline_mode=once),
+                pl.BlockSpec((dim, dim), lambda m, t: (0, 3), pipeline_mode=once),
             ],
-            out_specs=specs,
-            scratch_shapes=[pltpu.VMEM((dim, dim), BF)],
+            out_specs=[
+                pl.BlockSpec((dim, dim), column),
+                pl.BlockSpec((block, dim), lambda m, t: (jnp.clip(m - 5, 0, far_blocks - 1), 0)),
+                pl.BlockSpec((block, dim), lambda m, t: (jnp.maximum(m - 5 - far_blocks, 0), 0)),
+            ],
+            scratch_shapes=[pltpu.VMEM(shape, BF) for shape in shapes]
+            + [pltpu.SemaphoreType.DMA((len(args),))],
         ),
-        out_shape=outs,
-        compiler_params=params(48),
-        cost_estimate=cost(flops, 24 * MIB),
+        out_shape=[
+            jax.ShapeDtypeStruct((dim, 5 * dim), BF),
+            jax.ShapeDtypeStruct(far.shape, BF),
+            jax.ShapeDtypeStruct(own.shape, F32),
+        ],
+        compiler_params=params(),
+        cost_estimate=cost(flops, 30 * MIB),
         name="mid_grads",
-    )(turn, core, *args)
-
-
-def enc_back_kernel(dk_ref, dv_ref, wk_ref, wv_ref, far_ref, own_ref, *, far_blocks):
-    d = nt(dk_ref[...], wk_ref[...]) + nt(dv_ref[...], wv_ref[...])
-
-    @pl.when(pl.program_id(0) < far_blocks)
-    def _():
-        far_ref[...] = d.astype(BF)
-
-    @pl.when(pl.program_id(0) >= far_blocks)
-    def _():
-        own_ref[...] = d
-
-
-def enc_backward(dk, dv, w2, own_rows):
-    keys, dim = dk.shape
-    block = min(512, own_rows)
-    blocks, own = keys // block, own_rows // block
-    far = blocks - own
-    row = pl.BlockSpec((block, dim), lambda i: ((i + own) % blocks, 0))
-    return pl.pallas_call(
-        functools.partial(enc_back_kernel, far_blocks=far),
-        grid=(blocks,),
-        in_specs=[
-            row,
-            row,
-            pl.BlockSpec((dim, dim), lambda i: (0, 2)),
-            pl.BlockSpec((dim, dim), lambda i: (0, 3)),
-        ],
-        out_specs=[
-            pl.BlockSpec((block, dim), lambda i: (jnp.minimum(i, far - 1), 0)),
-            pl.BlockSpec((block, dim), lambda i: (jnp.maximum(i - far, 0), 0)),
-        ],
-        out_shape=[
-            jax.ShapeDtypeStruct((keys - own_rows, dim), BF),
-            jax.ShapeDtypeStruct((own_rows, dim), F32),
-        ],
-        compiler_params=params(48),
-        cost_estimate=cost(keys * dim, keys),
-        name="enc_backward",
-    )(dk, dv, w2, w2)
+    )(turn, *args, w2, w2)
 
 
 def before_self_kernel(turn_ref, dq_ref, wq_ref, h_ref, dh_ref, g_ref, *refs, count):
@@ -928,7 +936,7 @@
             jax.ShapeDtypeStruct((8, dim), F32),
         ]
         + [jax.ShapeDtypeStruct((rows, width), BF)] * count,
-        compiler_params=params(56),
+        compiler_params=params(),
         cost_estimate=cost(4 * rows * dim * dim, 18 * rows * dim),
         name="before_self",
     )(turn, dq, w2, h1, dh2, gain, *([wo] * count))
@@ -990,7 +998,7 @@
             scratch_shapes=[pltpu.VMEM((dim, width), F32), pltpu.VMEM((dim, width + 128), BF)],
         ),
         out_shape=outs,
-        compiler_params=params(48),
+        compiler_params=params(),
         cost_estimate=cost(2 * total * dim * width, 6 * total * dim),
         name="qkv_grads",
     )(core, *ds, n, w, gain, extra)
@@ -1013,7 +1021,7 @@
             out_specs=pl.BlockSpec((block, dim), lambda i, o: (i, 0)),
         ),
         out_shape=jax.ShapeDtypeStruct((rows, dim), dtype),
-        compiler_params=params(48),
+        compiler_params=params(),
         cost_estimate=cost(2 * rows * dim * w.shape[1], 10 * rows * dim),
         name="qkv_back",
     )(order, *ds, w)
@@ -1037,7 +1045,7 @@
         in_specs=[row, row, pl.BlockSpec((1, dim), lambda i: (0, 0)), row] + [row] * len(got),
         out_specs=row,
         out_shape=jax.ShapeDtypeStruct((rows, dim), F32),
-        compiler_params=params(32),
+        compiler_params=params(),
         cost_estimate=cost(10 * rows * dim, 16 * rows * dim),
         name="finish",
     )(x, dh1, gain, own, *got)
@@ -1086,7 +1094,7 @@
             jax.ShapeDtypeStruct((total, width), BF),
             jax.ShapeDtypeStruct((total, 128), BF),
         ],
-        compiler_params=params(32),
+        compiler_params=params(),
         name="assemble",
     )(jnp.stack([z, core]).astype(jnp.int32), near, far)
 
@@ -1126,9 +1134,14 @@
     def widen_ctx(self, g):
         return jnp.stack([g, lax.ppermute(g, "ctx", turned(2, 1))])
 
+    def widen_x(self, g):
+        return jnp.stack([g, lax.ppermute(g, "parts", self.swap_x)])
+
+    def widen_core(self, g):
+        return jnp.stack([g, lax.ppermute(g, "parts", self.swap_core)])
+
     def widen(self, g):
-        g = jnp.stack([g, lax.ppermute(g, "parts", self.swap_x)])
-        return jnp.stack([g, lax.ppermute(g, "parts", self.swap_core)])
+        return self.widen_core(self.widen_x(g))
 
     def rows(self, wide):
         pieces = [
@@ -1200,30 +1213,34 @@
         return lax.dynamic_slice_in_dim(w, place * width, width, 1)
 
     gain_cols = jnp.pad(jnp.stack([norm_self, norm_cross, norm_mlp], axis=1), ((0, 0), (0, 125)))
-    w1, gains = gather_first(
-        jnp.concatenate(
-            [own_heads(self_query), own_heads(self_key), own_heads(self_value), gain_cols], axis=1
-        ),
-        z, part, n_fsdp, n_parts,
+    first = jnp.concatenate(
+        [own_heads(self_query), own_heads(self_key), own_heads(self_value), gain_cols], axis=1
     )
+    first, self_output, gate_in = lax.optimization_barrier((first, self_output, gate_in))
+    w1, gains = gather_first(first, z, part, n_fsdp, n_parts)
     gains = gains[:, :8].astype(F32).T
     gain_self, gain_cross, gain_mlp = (gains[i : i + 1] for i in range(3))
     mats = (self_output, cross_query, cross_key, cross_value, cross_output)
     if fast:
         w2 = lax.all_gather(
-            jnp.concatenate([rows_of(w, plane, n_plane) for w in mats], axis=1),
-            ALL, axis=0, tiled=True,
+            jnp.concatenate([rows_of(w, part, n_parts) for w in mats], axis=1),
+            AROUND, axis=0, tiled=True,
         )
 
-        def column_piece(w):
-            cut = lax.dynamic_slice_in_dim(w, plane * 256, 256, 1)
-            return jnp.concatenate([cut[t * 64 : (t + 1) * 64] for t in range(3)], axis=1)
+        def column_pieces(w):
+            cut = lax.dynamic_slice_in_dim(w, part * 512, 512, 1).reshape(3, 64, 2, 256)
+            return cut.transpose(2, 1, 0, 3).reshape(2, 64, dim)
 
         w3 = lax.all_gather(
             jnp.stack(
-                [column_piece(gate_in), column_piece(up_in), rows_of(down_out, plane, n_plane)]
-            ),
-            ALL, axis=0,
+                [
+                    column_pieces(gate_in),
+                    column_pieces(up_in),
+                    rows_of(down_out, part, n_parts).reshape(2, 64, dim),
+                ],
+                axis=1,
+            ).reshape(-1, dim),
+            AROUND, axis=0, tiled=True,
         ).reshape(PIECES + (dim,))
     else:
         w2 = lax.all_gather(jnp.concatenate(mats, axis=1), "fsdp", axis=0, tiled=True)
@@ -1259,7 +1276,9 @@
 
     layer_out, dh2, dc, do2, stat2, g_ff = feed_forward(o2, h1, w2, gain_mlp, cotangent[0], w3)
     if fast:
-        part_ff = lax.psum_scatter(g_ff.reshape(32, 3, 64, dim), ALL, scatter_dimension=0)
+        part_ff = lax.psum_scatter(
+            g_ff.reshape(-1, dim), AROUND, scatter_dimension=0, tiled=True
+        ).reshape(2, 3, 64, dim)
 
     dq2, dk2, dv2 = cross_backward(q2, kv2, do2, o2, lse2, len_q, len_k)
     dh1, da, stat3, *do1 = before_self(turn, dq2, w2, h1, dh2, gain_cross, wo, width)
@@ -1267,10 +1286,9 @@
     do_far = do_far[0] if n_ctx == 2 else jnp.concatenate(do_far, axis=0)
     do_own = do1[0]
     core = jnp.reshape(part % 2, (1,)).astype(jnp.int32)
-    g_mid = mid_grads(
-        turn, core, pieces, da, n2, dq2, enc_own, enc_far, dk2, dv2, o2, dc, fast
+    g_mid, d_far, enc_grad = mid_grads(
+        turn, pieces, da, n2, dq2, enc_own, enc_far, dk2, dv2, o2, dc, w2
     )
-    d_far, enc_grad = enc_backward(dk2, dv2, w2, enc_rows)
 
     sums = jnp.sum(jnp.concatenate([stat1[:2], stat2[:2]], axis=0), axis=1)
     extra = jnp.concatenate(
@@ -1293,27 +1311,20 @@
     pairs = width // 128
     if fast:
         net = Plane(part, place, z, n_parts, n_fsdp)
-        send, keep = net.over_core(*g_mid)
-        do_own, do_far, send, d_far, extra = lax.optimization_barrier(
-            (do_own, do_far, send, d_far, extra)
+        do_own, do_far, d_far, extra, g_mid, part_ff = lax.optimization_barrier(
+            (do_own, do_far, d_far, extra, g_mid, part_ff)
         )
+        part_mid = lax.psum_scatter(g_mid, AROUND, scatter_dimension=0, tiled=True)
     enc_got = [
         lax.ppermute(d_far[(i - 1) * enc_rows : i * enc_rows], "ctx", turned(n_ctx, i))
         for i in range(1, n_ctx)
     ]
     if fast:
         by_pair = [self_pair(0, do_own, do_far)]
-        g_mid = net.over_x(send, keep)
-        g_mid, do_far = lax.optimization_barrier((g_mid, by_pair[0][0], do_far))[::2]
-        by_pair.append(self_pair(1, do_own, do_far))
-        g_mid = net.over_fsdp(g_mid)
-        g_mid, part_ff, enc_got, do_far = lax.optimization_barrier(
-            (g_mid, part_ff, enc_got, do_far, by_pair[1][0])
-        )[:4]
-        by_pair.append(self_pair(2, do_own, do_far))
-        wide_ff = net.widen_ctx(part_ff)
-        g_mid = net.over_ctx(g_mid)
-        by_pair[2], wide_ff, g_mid = lax.optimization_barrier((by_pair[2], wide_ff, g_mid))
+        part_ff, do_far = lax.optimization_barrier((part_ff, do_far, by_pair[0][0]))[:2]
+        by_pair += [self_pair(1, do_own, do_far), self_pair(2, do_own, do_far)]
+        sum_ff = net.over_ctx(part_ff)
+        by_pair, sum_ff, enc_got = lax.optimization_barrier((by_pair, sum_ff, enc_got))
     else:
         by_pair = [self_pair(i, do_own, do_far) for i in range(pairs)]
     for piece in enc_got:
@@ -1326,14 +1337,19 @@
         for i in range(1, n_ctx)
     ]
     dn_own = qkv_back(order_here, 0, ds, w1, rows, F32, block)
+    if fast:
+        send, keep, dn_far = lax.optimization_barrier((*net.over_core(*g_qkv), dn_far))
+        g_qkv = net.over_fsdp(net.over_x(send, keep))
+        dn_got, g_qkv, part_mid, sum_ff, dn_own = lax.optimization_barrier(
+            (dn_got, g_qkv, part_mid, net.widen_x(sum_ff), dn_own)
+        )
     decoder_grad = finish(x_own, dh1, gain_self, dn_own, dn_got)
 
     if fast:
-        send, keep = net.over_core(*g_qkv)
-        sum_mid = net.rows(net.widen(g_mid))
-        me = jnp.stack([net.core, net.x, place]).astype(jnp.int32)
-        grad_gate, grad_up, grad_down = unpack(me, net.widen(wide_ff))
-        wide = net.widen(net.widen_ctx(net.over_fsdp(net.over_x(send, keep))))
+        sum_mid = net.rows(net.widen(net.over_ctx(part_mid)))
+        me = jnp.stack([net.core, net.x]).astype(jnp.int32)
+        grad_gate, grad_up, grad_down = unpack(me, net.widen_core(sum_ff))
+        wide = net.widen(net.widen_ctx(g_qkv))
         every = jnp.stack([net.rows(pick(wide, i ^ place, 2)) for i in range(2)])
     else:
 
@@ -1341,7 +1357,7 @@
             g = lax.psum_scatter(g, "fsdp", scatter_dimension=0, tiled=True).astype(F32)
             return lax.psum(g, ("parts", "ctx"))
 
-        (g_mid,), (g_qkv,) = g_mid, g_qkv
+        (g_qkv,) = g_qkv
         sum_mid = total_of(g_mid)
         flat = [
             g_ff[:, :, i].reshape(4, 8, 64, 3, 256).transpose(0, 3, 2, 1, 4).reshape(dim, hidden)

time: 579 us -> 528 us (0.912)
  waiting for transfers between devices: 103 us -> 80.5 us
  local copies, waits for them, and re-layouts: 49.7 us -> 31.6 us
  Pallas kernels: 340 us -> 327 us
  starting transfers between devices: 30.4 us -> 38.5 us
    unnamed x170 -> x42, local copies, waits for them, and re-layouts: 36.6 us -> 8.21 us
    ppermute x1, waiting for transfers between devices: 0.01 us -> 14.4 us  [local(): lax.ppermute(d_far[(i - 1) * enc_rows:i * enc_rows], 'ctx', turned(n_ctx,...]
    ppermute x6 -> x3, waiting for transfers between devices: 15.6 us -> 2.76 us  [over_fsdp(): lax.ppermute(piece, 'fsdp', turned(self.n_fsdp, d)).astype(F32)]
    all_gather x2, waiting for transfers between devices: 17 us -> 7.95 us  [the longest x1 7.95 us: local(): lax.all_gather(jnp.stack([column_pieces(gate_in), column_pieces(up_in), r...]
    ppermute x1, waiting for transfers between devices: 0.01 us -> 8.46 us  [local(): lax.ppermute(dn_far[(i - 1) * rows:i * rows], 'ctx', turned(n_ctx, i))]
    ppermute x6, waiting for transfers between devices: 16.9 us -> 8.73 us  [the longest x3 8.72 us: widen_x(): return jnp.stack([g, lax.ppermute(g, 'parts', self.swap_x)])]
    pallas_call x3, Pallas kernels: 52.6 us -> 45.2 us  [self_backward(): pl.pallas_call(functools.partial(self_backward_kernel, per_dev=per_dev),...]
    pallas_call x1, Pallas kernels: 30.4 us -> 23 us  [self_forward(): pl.pallas_call(self_forward_kernel, grid_spec=pltpu.PrefetchScalarGridSpe...]
  transfers between devices with their start and end apart: 32 -> 28, of which waited for: 15 -> 12; matrix products, arithmetic and copies ran while one was open for 6% -> 8% of each run, Pallas kernels for 50% -> 54%
where the time goes in v4:
time: 528 us; the launch traced here: 522 us
  Pallas kernels  327 us (62%)
  waiting for transfers between devices  80.5 us (15%)
  starting transfers between devices  38.5 us (7%)
  local copies, waits for them, and re-layouts  31.6 us (6%)
  other arithmetic  28.3 us (5%)
  between operations  15.5 us (3%)
    pallas_call x1, Pallas kernels, cross_backward(): pl.pallas_call(cross_backward_kernel, grid=(pairs, rows // block), in_spe...  78.5 us
    pallas_call x1, Pallas kernels, feed_forward(): pl.pallas_call(mlp_kernel, grid=(steps,), in_specs=[full, full, pl.BlockS...  46.4 us
    pallas_call x3, Pallas kernels, self_backward(): pl.pallas_call(functools.partial(self_backward_kernel, per_dev=per_dev),...  45.2 us
    pallas_call x1, Pallas kernels, cross_forward(): pl.pallas_call(cross_forward_kernel, grid=(pairs, rows // block), in_spec...  35.9 us
    pallas_call x1, Pallas kernels, self_forward(): pl.pallas_call(self_forward_kernel, grid_spec=pltpu.PrefetchScalarGridSpe...  23 us
    pallas_call x1, Pallas kernels, mid_grads(): pl.pallas_call(functools.partial(mid_grads_kernel, count=len(pieces), far...  23 us
    ppermute x3, waiting for transfers between devices, gather_first(): lax.ppermute(mine, 'fsdp', turned(n_fsdp, d))  20.5 us
    ppermute x1, waiting for transfers between devices, local(): lax.ppermute(d_far[(i - 1) * enc_rows:i * enc_rows], 'ctx', turned(n_ctx,...  14.4 us
  transfers between devices with their start and end apart: 28, of which 12 were waited for; matrix products, arithmetic and copies ran while one was open for 8% of the time, Pallas kernels for 54%

profile of v4, /device:TPU:9, one launch (start us, length us, event | category | flops | bytes accessed | tf_op | source)
XLA Modules:
  0.0 521.5 jit_solution(10727212794261151200)
XLA Ops:
  20.8 1.5 collective-permute-start.1
  22.2 4.1 collective-permute-start.2
  32.5 9.0 %collective-permute-done.1 = bf16[96,1280]{1,0:T(8,128)(2,1)S(1)} collective-permute-done((bf16[96,1280]{1,0:T(8,128)(2,1)S(1)}, bf16[96,1280]{1,0:T(8,128)(2,1)S(1)}, u32[]{:S(2)}, u32[]{:S(2)}) %collective-permute-start.1) | collective-permute-done | bytes 245792 | tf_op jit(solution)/shard_map/ppermute | solution.py:1084
  41.5 11.6 %collective-permute-done.2 = bf16[96,1280]{1,0:T(8,128)(2,1)S(1)} collective-permute-done((bf16[96,1280]{1,0:T(8,128)(2,1)S(1)}, bf16[96,1280]{1,0:T(8,128)(2,1)S(1)}, u32[]{:S(2)}, u32[]{:S(2)}) %collective-permute-start.2) | collective-permute-done | bytes 245792 | tf_op jit(solution)/shard_map/ppermute | solution.py:1084
  53.2 3.0 collective-permute-start.4
  58.0 1.4 sort.17
  59.4 1.8 select_convert_fusion.2.qa_ref
  61.2 3.3 select_convert_fusion
  65.5 2.9 assemble.1
  70.7 1.3 collective-permute-start.6
  72.0 9.2 %qkv_forward.1 = (bf16[2048,768]{1,0:T(8,128)(2,1)}, bf16[2048,384]{1,0:T(8,128)(2,1)}, bf16[2048,384]{1,0:T(8,128)(2,1)}, bf16[2048,384]{1,0:T(8,128)(2,1)}) custom-call(s32[4]{0:T(128)} %copy-done.15, bf16[1024,768]{1,0:T(8,128)(2,1)} %bitcast.106, bf16[1024,768]{1,0:T(8,128)(2,1)} %collective-permute-done.far_ref, f32[1,768]{1,0:T(1,128)} %get-tuple-element.214.g_ref, ...), custom_call_target="tpu_custom_call" | custom-call | flops 3623878656 | bytes 12582912 | tf_op jit(solution)/shard_map/qkv_forward/pallas_call | solution.py:455
  81.2 23.0 %self_forward.1 = (bf16[2048,384]{1,0:T(8,128)(2,1)}, f32[2048,384]{1,0:T(8,128)}) custom-call(s32[4]{0:T(128)} %and_select_fusion.3.count_ref, s32[4]{0:T(128)} %get-tuple-element.97.slot_ref, bf16[2048,384]{1,0:T(8,128)(2,1)} %get-tuple-element.102.q_ref, bf16[2048,384]{1,0:T(8,128)(2,1)} %get-tuple-element.103.k_ref, ...), custom_call_target="tpu_custom_call" | custom-call | flops 12884901888 | bytes 6291456 | tf_op jit(solution)/shard_map/self_forward/pallas_call | solution.py:358
  106.8 9.2 %enc_forward.1.k_ref.v_ref = bf16[2048,1536]{1,0:T(8,128)(2,1)} custom-call(bf16[1024,768]{1,0:T(8,128)(2,1)} %bitcast.141, bf16[1024,768]{1,0:T(8,128)(2,1)} %collective-permute-done.6.far_ref.refs_6_, bf16[768,3840]{1,0:T(8,128)(2,1)} %all-gather.3.cloned.1.call-done.w_ref.refs_2_.refs_3_.refs_5_.wc_ref.wq_ref.refs_0_.refs_1_.refs_11_.refs_12_), custom_call_target="tpu_custom_call" | custom-call | flops 4831838208 | bytes 12582912 | tf_op jit(solution)/shard_map/enc_forward/pallas_call | solution.py:489
  116.1 4.5 collective-permute-done.5.refs_1_.refs_4_
  121.5 9.1 %after_self.1 = (f32[1024,768]{1,0:T(8,128)}, bf16[1024,768]{1,0:T(8,128)(2,1)}, bf16[1024,768]{1,0:T(8,128)(2,1)}, f32[8,768]{1,0:T(8,128)}) custom-call(s32[2]{0:T(128)} %and_select_fusion.5.turn_ref, bf16[1024,768]{1,0:T(8,128)(2,1)} %bitcast.107, bf16[2048,384]{1,0:T(8,128)(2,1)} %get-tuple-element.105.refs_0_.refs_3_.o_ref, ...), custom_call_target="tpu_custom_call" | custom-call | flops 2415919104 | bytes 11010048 | tf_op jit(solution)/shard_map/after_self/pallas_call | solution.py:537
  131.4 35.9 %cross_forward.1 = (bf16[1024,768]{1,0:T(8,128)(2,1)}, f32[1024,768]{1,0:T(8,128)}) custom-call(bf16[1024,768]{1,0:T(8,128)(2,1)} %get-tuple-element.109.q_ref, bf16[2048,1536]{1,0:T(8,128)(2,1)} %enc_forward.1.k_ref.v_ref, bf16[2048,1536]{1,0:T(8,128)(2,1)} %enc_forward.1.k_ref.v_ref, bf16[1024,128]{1,0:T(8,128)(2,1)} %broadcast_in_dim.96.qa_ref, ...), custom_call_target="tpu_custom_call" | custom-call | flops 25769803776 | bytes 6291456 | tf_op jit(solution)/shard_map/cross_forward/pallas_call | solution.py:243
  167.3 7.9 %all-gather.5.cloned.1.call-done = bf16[6144,768]{1,0:T(8,128)(2,1)} async-done(((bf16[384,768]{1,0:T(8,128)(2,1)}), bf16[6144,768]{1,0:T(8,128)(2,1)}) %all-gather.5.cloned.1.call-update) | async-done | bytes 9437200 | tf_op jit(solution)/shard_map/all_gather | solution.py:1234
  175.2 46.4 %feed_forward.1 = (bf16[1024,768]{1,0:T(8,128)(2,1)}, f32[1024,768]{1,0:T(8,128)}, bf16[1024,768]{1,0:T(8,128)(2,1)}, bf16[1024,768]{1,0:T(8,128)(2,1)}, f32[8,7...) custom-call(bf16[1024,768]{1,0:T(8,128)(2,1)} %get-tuple-element.111.o_ref.refs_9_, ...), custom_call_target="tpu_custom_call" | custom-call | flops 32614907904 | bytes 41943040 | tf_op jit(solution)/shard_map/feed_forward/pallas_call | solution.py:686
  223.2 78.5 %cross_backward.1 = (bf16[1024,768]{1,0:T(8,128)(2,1)}, bf16[2048,768]{1,0:T(8,128)(2,1)}, bf16[2048,768]{1,0:T(8,128)(2,1)}) custom-call(bf16[1024,768]{1,0:T(8,128)(2,1)} %get-tuple-element.109.q_ref, bf16[2048,1536]{1,0:T(8,128)(2,1)} %enc_forward.1.k_ref.v_ref, bf16[2048,1536]{1,0:T(8,128)(2,1)} %enc_forward.1.k_ref.v_ref, ...), custom_call_target="tpu_custom_call" | custom-call | flops 64424509440 | bytes 9437184 | tf_op jit(solution)/shard_map/cross_backward/pallas_call | solution.py:291
  301.7 10.1 %before_self.1 = (f32[1024,768]{1,0:T(8,128)}, bf16[1024,768]{1,0:T(8,128)(2,1)}, f32[8,768]{1,0:T(8,128)}, bf16[1024,384]{1,0:T(8,128)(2,1)}, bf16[1024,384]{1,0:T(8,128)(2,1)}) custom-call(s32[2]{0:T(128)} %and_select_fusion.5.turn_ref, bf16[1024,768]{1,0:T(8,128)(2,1)} %get-tuple-element.117.dq_ref.refs_1_, ...), custom_call_target="tpu_custom_call" | custom-call | flops 2415919104 | bytes 14155776 | tf_op jit(solution)/shard_map/before_self/pallas_call | solution.py:917
  315.2 1.4 concatenate.71.refs_12_
  316.6 23.0 %mid_grads.1 = (bf16[768,3840]{1,0:T(8,128)(2,1)}, bf16[1024,768]{1,0:T(8,128)(2,1)}, f32[1024,768]{1,0:T(8,128)}) custom-call(s32[2]{0:T(128)} %and_select_fusion.5.turn_ref, bf16[1024,768]{1,0:T(8,128)(2,1)} %get-tuple-element.122.refs_0_, bf16[1024,768]{1,0:T(8,128)(2,1)} %get-tuple-element.117.dq_ref.refs_1_, ...), custom_call_target="tpu_custom_call" | custom-call | flops 13287555072 | bytes 31457280 | tf_op jit(solution)/shard_map/mid_grads/pallas_call | solution.py:861
  340.6 15.1 %self_backward.3 = (bf16[2048,128]{1,0:T(8,128)(2,1)}, bf16[2048,128]{1,0:T(8,128)(2,1)}, bf16[2048,128]{1,0:T(8,128)(2,1)}) custom-call(s32[4]{0:T(128)} %and_select_fusion.3.count_ref, s32[4]{0:T(128)} %get-tuple-element.97.slot_ref, bf16[2048,384]{1,0:T(8,128)(2,1)} %get-tuple-element.102.q_ref, bf16[2048,384]{1,0:T(8,128)(2,1)} %get-tuple-element.103.k_ref, ...), custom_call_target="tpu_custom_call" | custom-call | flops 10737418240 | bytes 3145728 | tf_op jit(solution)/shard_map/self_backward/pallas_call | solution.py:411
  357.2 15.0 %self_backward.5 = (bf16[2048,128]{1,0:T(8,128)(2,1)}, bf16[2048,128]{1,0:T(8,128)(2,1)}, bf16[2048,128]{1,0:T(8,128)(2,1)}) custom-call(s32[4]{0:T(128)} %and_select_fusion.3.count_ref, s32[4]{0:T(128)} %get-tuple-element.97.slot_ref, bf16[2048,384]{1,0:T(8,128)(2,1)} %get-tuple-element.102.q_ref, bf16[2048,384]{1,0:T(8,128)(2,1)} %get-tuple-element.103.k_ref, ...), custom_call_target="tpu_custom_call" | custom-call | flops 10737418240 | bytes 3145728 | tf_op jit(solution)/shard_map/self_backward/pallas_call | solution.py:411
  372.2 15.1 %self_backward.4 = (bf16[2048,128]{1,0:T(8,128)(2,1)}, bf16[2048,128]{1,0:T(8,128)(2,1)}, bf16[2048,128]{1,0:T(8,128)(2,1)}) custom-call(s32[4]{0:T(128)} %and_select_fusion.3.count_ref, s32[4]{0:T(128)} %get-tuple-element.97.slot_ref, bf16[2048,384]{1,0:T(8,128)(2,1)} %get-tuple-element.102.q_ref, bf16[2048,384]{1,0:T(8,128)(2,1)} %get-tuple-element.103.k_ref, ...), custom_call_target="tpu_custom_call" | custom-call | flops 10737418240 | bytes 3145728 | tf_op jit(solution)/shard_map/self_backward/pallas_call | solution.py:411
  387.5 14.4 %collective-permute-done.9 = bf16[1024,768]{1,0:T(8,128)(2,1)S(1)} collective-permute-done((bf16[1024,768]{1,0:T(8,128)(2,1)}, bf16[1024,768]{1,0:T(8,128)(2,1)S(1)}, u32[]{:S(2)}, u32[]{:S(2)}) %collective-permute-start.9) | collective-permute-done | bytes 1572896 | tf_op jit(solution)/shard_map/ppermute | solution.py:1319
  403.0 10.9 %qkv_grads.1 = (bf16[8,48,1280]{2,1,0:T(8,128)(2,1)}, bf16[8,48,1280]{2,1,0:T(8,128)(2,1)}) custom-call(s32[1]{0:T(128)} %bitcast.6.core_ref, bf16[2048,128]{1,0:T(8,128)(2,1)} %get-tuple-element.149.refs_0_, bf16[2048,128]{1,0:T(8,128)(2,1)} %get-tuple-element.150.refs_1_, bf16[2048,128]{1,0:T(8,128)(2,1)} %get-tuple-element.151.refs_2_, ...), custom_call_target="tpu_custom_call" | custom-call | flops 3623878656 | bytes 9437184 | tf_op jit(solution)/shard_map/qkv_grads/pallas_call | solution.py:985
  413.8 3.4 collective-permute-start.11
  417.2 6.5 %qkv_back.2 = bf16[1024,768]{1,0:T(8,128)(2,1)} custom-call(s32[4]{0:T(128)} %copy-done.15, bf16[2048,128]{1,0:T(8,128)(2,1)} %get-tuple-element.149.refs_0_, bf16[2048,128]{1,0:T(8,128)(2,1)} %get-tuple-element.150.refs_1_, bf16[2048,128]{1,0:T(8,128)(2,1)} %get-tuple-element.151.refs_2_, bf16[2048,128]{1,0:T(8,128)(2,1)} %get-tuple-element.152.refs_3_, ...), custom_call_target="tpu_custom_call" | custom-call | flops 1811939328 | bytes 7864320 | tf_op jit(solution)/shard_map/qkv_back/pallas_call | solution.py:1014
  424.0 3.0 collective-permute-start.12
  427.0 1.9 collective-permute-start.10
  429.0 6.6 %qkv_back.3.own_ref = f32[1024,768]{1,0:T(8,128)} custom-call(s32[4]{0:T(128)} %copy-done.15, bf16[2048,128]{1,0:T(8,128)(2,1)} %get-tuple-element.149.refs_0_, bf16[2048,128]{1,0:T(8,128)(2,1)} %get-tuple-element.150.refs_1_, bf16[2048,128]{1,0:T(8,128)(2,1)} %get-tuple-element.151.refs_2_, bf16[2048,128]{1,0:T(8,128)(2,1)} %get-tuple-element.152.refs_3_, ...), custom_call_target="tpu_custom_call" | custom-call | flops 1811939328 | bytes 7864320 | tf_op jit(solution)/shard_map/qkv_back/pallas_call | solution.py:1014
  435.6 2.7 collective-permute-done.12
  438.5 2.3 collective-permute-start.13
  440.8 3.5 collective-permute-start.14
  444.9 6.1 %collective-permute-done.16 = bf16[2,3,64,768]{3,2,1,0:T(8,128)(2,1)} collective-permute-done((bf16[2,3,64,768]{3,2,1,0:T(8,128)(2,1)S(1)}, bf16[2,3,64,768]{3,2,1,0:T(8,128)(2,1)}, u32[]{:S(2)}, u32[]{:S(2)}) %collective-permute-start.16) | collective-permute-done | bytes 589856 | tf_op jit(solution)/shard_map/ppermute | solution.py:1138
  452.2 2.8 collective-permute-done.15
  455.0 8.5 %collective-permute-done.10.refs_0_ = bf16[1024,768]{1,0:T(8,128)(2,1)} collective-permute-done((bf16[1024,768]{1,0:T(8,128)(2,1)}, bf16[1024,768]{1,0:T(8,128)(2,1)}, u32[]{:S(2)}, u32[]{:S(2)}) %collective-permute-start.10) | collective-permute-done | bytes 1572896 | tf_op jit(solution)/shard_map/ppermute | solution.py:1336
  463.4 1.3 collective-permute-start.20
  465.5 9.8 %collective-permute-done.17 = bf16[48,1280]{1,0:T(8,128)(2,1)S(1)} collective-permute-done((bf16[48,1280]{1,0:T(8,128)(2,1)S(1)}, bf16[48,1280]{1,0:T(8,128)(2,1)S(1)}, u32[]{:S(2)}, u32[]{:S(2)}) %collective-permute-start.17) | collective-permute-done | bytes 122912 | tf_op jit(solution)/shard_map/ppermute | solution.py:1135
  478.1 2.7 collective-permute-done.18
  480.8 5.6 %collective-permute-start.19 = (bf16[2,2,48,1280]{3,2,1,0:T(8,128)(2,1)S(1)}, bf16[2,2,48,1280]{3,2,1,0:T(8,128)(2,1)S(1)}, u32[]{:S(2)}, u32[]{:S(2)}) collective-permute-start(bf16[2,2,48,1280]{3,2,1,0:T(8,128)(2,1)S(1)} %get-tuple-element.205), channel_id=1, source_target_pairs={{0,8},{8,0},{16,24},{24,16},{1,9},{9,1},{17,25},{25,17},{2,10},{10... | collective-permute-start | bytes 1474568 | tf_op jit(solution)/shard_map/ppermute | solution.py:1141
  486.4 3.5 add_bitcast_fusion
  489.9 6.6 %finish.1 = f32[1024,768]{1,0:T(8,128)} custom-call(bf16[1024,768]{1,0:T(8,128)(2,1)} %bitcast.108, f32[1024,768]{1,0:T(8,128)} %get-tuple-element.119.dh_ref, f32[1,768]{1,0:T(1,128)} %get-tuple-element.214.g_ref, f32[1024,768]{1,0:T(8,128)} %qkv_back.3.own_ref, bf16[1024,768]{1,0:T(8,128)(2,1)} %collective-permute-done.10.refs_0_), custom_call_target="tpu_custom_call" | custom-call | flops 7864320 | bytes 12582912 | tf_op jit(solution)/shard_map/finish/pallas_call | solution.py:1042
  504.1 2.9 pad_maximum_fusion.p_ref
  507.0 4.0 unpack.1
  511.0 1.6 fusion.7
  512.9 1.6 fusion.38
  (162 shorter events, 50.6 us)
Async XLA Ops:
  7.2 9.6 %copy-start = (bf16[192,2048]{1,0:T(8,128)(2,1)S(1)}, bf16[192,2048]{1,0:T(8,128)(2,1)}, u32[]{:S(2)}) copy-start(bf16[192,2048]{1,0:T(8,128)(2,1)} %param.34) | copy-start | bytes 2359300
  7.2 99.6 %all-gather.3.cloned.1.call-start = ((), (), s32[]{:S(2)}) async-start(), calls=%async_computation.2 | async-start | bytes 6266880 | tf_op jit(solution)/shard_map/all_gather | solution.py:1225
  15.9 0.7 copy-start.11
  16.7 158.5 %all-gather.5.cloned.1.call-start = ((), (), s32[]{:S(2)}) async-start(), calls=%async_computation.3 | async-start | bytes 10027008 | tf_op jit(solution)/shard_map/all_gather | solution.py:1234
  19.6 6.7 %copy-start.2 = (bf16[1,1024,768]{2,1,0:T(8,128)(2,1)S(1)}, bf16[1,1024,768]{2,1,0:T(8,128)(2,1)}, u32[]{:S(2)}) copy-start(bf16[1,1024,768]{2,1,0:T(8,128)(2,1)} %param.21) | copy-start | bytes 4718596
  19.6 9.1 %copy-start.12 = (s32[1,2048]{1,0:T(1,128)S(1)}, s32[1,2048]{1,0:T(1,128)}, u32[]{:S(2)}) copy-start(s32[1,2048]{1,0:T(1,128)} %param.23) | copy-start | bytes 24580
  19.6 12.3 %copy-start.17 = (s32[1,4]{1,0:T(1,128)S(1)}, s32[1,4]{1,0:T(1,128)}, u32[]{:S(2)}) copy-start(s32[1,4]{1,0:T(1,128)} %param.24) | copy-start | bytes 52
  20.6 319.1 %reduce-scatter.3.cloned.1.call-start = ((), (), s32[]{:S(2)}) async-start(), calls=%async_computation.4 | async-start | bytes 10027008 | tf_op jit(solution)/shard_map/reduce_scatter | solution.py:1279
  20.7 11.8 %collective-permute-start.3 = (bf16[96,1280]{1,0:T(8,128)(2,1)S(1)}, bf16[96,1280]{1,0:T(8,128)(2,1)S(1)}, u32[]{:S(2)}, u32[]{:S(2)}) collective-permute-start(bf16[96,1280]{1,0:T(8,128)(2,1)S(1)} %constant_dynamic-slice_fusion.3), channel_id=1, source_target_pairs={{0,3},{1,0},{2,1},{3,2},{4,7},{5,4},{6,5},{7,6},{8,11},{9,8},{10,9... | collective-permute-start | bytes 737288 | tf_op jit(solution)/shard_map/ppermute | solution.py:1084
  20.8 20.7 %collective-permute-start.1 = (bf16[96,1280]{1,0:T(8,128)(2,1)S(1)}, bf16[96,1280]{1,0:T(8,128)(2,1)S(1)}, u32[]{:S(2)}, u32[]{:S(2)}) collective-permute-start(bf16[96,1280]{1,0:T(8,128)(2,1)S(1)} %constant_dynamic-slice_fusion.3), channel_id=1, source_target_pairs={{0,1},{1,2},{2,3},{3,0},{4,5},{5,6},{6,7},{7,4},{8,9},{9,10},{10,1... | collective-permute-start | bytes 737288 | tf_op jit(solution)/shard_map/ppermute | solution.py:1084
  22.2 30.8 %collective-permute-start.2 = (bf16[96,1280]{1,0:T(8,128)(2,1)S(1)}, bf16[96,1280]{1,0:T(8,128)(2,1)S(1)}, u32[]{:S(2)}, u32[]{:S(2)}) collective-permute-start(bf16[96,1280]{1,0:T(8,128)(2,1)S(1)} %constant_dynamic-slice_fusion.3), channel_id=1, source_target_pairs={{0,2},{1,3},{2,0},{3,1},{4,6},{5,7},{6,4},{7,5},{8,10},{9,11},{10,... | collective-permute-start | bytes 737288 | tf_op jit(solution)/shard_map/ppermute | solution.py:1084
  26.3 44.4 %collective-permute-start = (bf16[1024,768]{1,0:T(8,128)(2,1)S(1)}, bf16[1024,768]{1,0:T(8,128)(2,1)}, u32[]{:S(2)}, u32[]{:S(2)}) collective-permute-start(bf16[1024,768]{1,0:T(8,128)(2,1)S(1)} %bitcast.109), channel_id=1, source_target_pairs={{0,4},{4,0},{1,5},{5,1},{2,6},{6,2},{3,7},{7,3},{8,12},{12,8},{9,1... | collective-permute-start | bytes 4718600 | tf_op jit(solution)/shard_map/ppermute | solution.py:1203
  53.2 11.4 %copy-start.3 = (bf16[4,96,1280]{2,1,0:T(8,128)(2,1)}, bf16[4,96,1280]{2,1,0:T(8,128)(2,1)S(1)}, u32[]{:S(2)}) copy-start(bf16[4,96,1280]{2,1,0:T(8,128)(2,1)S(1)} %pad_maximum_fusion.2.near_ref) | copy-start | bytes 2949124
  53.2 11.4 %collective-permute-start.4 = (bf16[4,96,1280]{2,1,0:T(8,128)(2,1)S(1)}, bf16[4,96,1280]{2,1,0:T(8,128)(2,1)S(1)}, u32[]{:S(2)}, u32[]{:S(2)}) collective-permute-start(bf16[4,96,1280]{2,1,0:T(8,128)(2,1)S(1)} %pad_maximum_fusion.2.near_ref), channel_id=1, source_target_pairs={{0,8},{8,0},{16,24},{24,16},{1,9},{9,1},{17,25},{25,17},{2,10},{10... | collective-permute-start | bytes 2949128 | tf_op jit(solution)/shard_map/ppermute | solution.py:1086
  57.5 10.9 %copy-start.15 = (s32[4]{0:T(128)}, s32[4]{0:T(128)S(1)}, u32[]{:S(2)}) copy-start(s32[4]{0:T(128)S(1)} %dynamic_slice.105.order_ref) | copy-start | bytes 52
  64.6 0.9 copy-start.7
  70.7 36.2 %collective-permute-start.6 = (bf16[1024,768]{1,0:T(8,128)(2,1)}, bf16[1024,768]{1,0:T(8,128)(2,1)}, u32[]{:S(2)}, u32[]{:S(2)}) collective-permute-start(bf16[1024,768]{1,0:T(8,128)(2,1)} %bitcast.140), channel_id=1, source_target_pairs={{0,4},{4,0},{1,5},{5,1},{2,6},{6,2},{3,7},{7,3},{8,12},{12,8},{9,1... | collective-permute-start | bytes 4718600 | tf_op jit(solution)/shard_map/ppermute | solution.py:1203
  105.4 15.2 %collective-permute-start.5 = (bf16[1024,384]{1,0:T(8,128)(2,1)S(1)}, bf16[1024,384]{1,0:T(8,128)(2,1)S(1)}, u32[]{:S(2)}, u32[]{:S(2)}) collective-permute-start(bf16[1024,384]{1,0:T(8,128)(2,1)S(1)} %slice.78), channel_id=1, source_target_pairs={{0,4},{4,0},{1,5},{5,1},{2,6},{6,2},{3,7},{7,3},{8,12},{12,8},{9,1... | collective-permute-start | bytes 2359304 | tf_op jit(solution)/shard_map/ppermute | solution.py:1264
  120.6 0.9 copy-start.9
  221.7 241.8 %reduce-scatter.5.cloned.1.call-start = ((), (), s32[]{:S(2)}) async-start(), calls=%async_computation.5 | async-start | bytes 6266880 | tf_op jit(solution)/shard_map/reduce_scatter | solution.py:1317
  313.7 25.9 %collective-permute-start.7 = (bf16[1024,384]{1,0:T(8,128)(2,1)}, bf16[1024,384]{1,0:T(8,128)(2,1)S(1)}, u32[]{:S(2)}, u32[]{:S(2)}) collective-permute-start(bf16[1024,384]{1,0:T(8,128)(2,1)} %get-tuple-element.121), channel_id=1, source_target_pairs={{0,4},{4,0},{1,5},{5,1},{2,6},{6,2},{3,7},{7,3},{8,12},{12,8},{9,1... | collective-permute-start | bytes 2359304 | tf_op jit(solution)/shard_map/ppermute | solution.py:1285
  339.6 0.9 copy-start.16
  340.6 15.1 %copy-start.10 = (bf16[384,768]{1,0:T(8,128)(2,1)S(1)}, bf16[384,768]{1,0:T(8,128)(2,1)}, u32[]{:S(2)}) copy-start(bf16[384,768]{1,0:T(8,128)(2,1)} %reduce-scatter.3.cloned.1.call-done) | copy-start | bytes 1769476
  355.7 31.6 %collective-permute-start.8 = (bf16[2,3,64,768]{3,2,1,0:T(8,128)(2,1)S(1)}, bf16[2,3,64,768]{3,2,1,0:T(8,128)(2,1)S(1)}, u32[]{:S(2)}, u32[]{:S(2)}) collective-permute-start(bf16[2,3,64,768]{3,2,1,0:T(8,128)(2,1)S(1)} %bitcast.124), channel_id=1, source_target_pairs={{0,4},{4,0},{1,5},{5,1},{2,6},{6,2},{3,7},{7,3},{8,12},{12,8},{9,1... | collective-permute-start | bytes 1769480 | tf_op jit(solution)/shard_map/ppermute | solution.py:1132
  356.0 45.8 %collective-permute-start.9 = (bf16[1024,768]{1,0:T(8,128)(2,1)}, bf16[1024,768]{1,0:T(8,128)(2,1)S(1)}, u32[]{:S(2)}, u32[]{:S(2)}) collective-permute-start(bf16[1024,768]{1,0:T(8,128)(2,1)} %get-tuple-element.148), channel_id=1, source_target_pairs={{0,4},{4,0},{1,5},{5,1},{2,6},{6,2},{3,7},{7,3},{8,12},{12,8},{9,1... | collective-permute-start | bytes 4718600 | tf_op jit(solution)/shard_map/ppermute | solution.py:1319
  387.3 14.6 %copy-start.13 = (f32[768]{0:T(1024)S(1)}, f32[768]{0:T(1024)}, u32[]{:S(2)}) copy-start(f32[768]{0:T(1024)} %get-tuple-element.211) | copy-start | bytes 9220
  401.9 12.0 %copy-start.6 = (bf16[1024,768]{1,0:T(8,128)(2,1)}, bf16[1024,768]{1,0:T(8,128)(2,1)S(1)}, u32[]{:S(2)}) copy-start(bf16[1024,768]{1,0:T(8,128)(2,1)S(1)} %collective-permute-done.9) | copy-start | bytes 4718596
  413.8 9.9 %collective-permute-start.11 = (bf16[8,48,1280]{2,1,0:T(8,128)(2,1)}, bf16[8,48,1280]{2,1,0:T(8,128)(2,1)S(1)}, u32[]{:S(2)}, u32[]{:S(2)}) collective-permute-start(bf16[8,48,1280]{2,1,0:T(8,128)(2,1)} %get-tuple-element.161), channel_id=1, source_target_pairs={{0,8},{8,0},{16,24},{24,16},{1,9},{9,1},{17,25},{25,17},{2,10},{10... | collective-permute-start | bytes 2949128 | tf_op jit(solution)/shard_map/ppermute | solution.py:1115
  417.2 6.5 %copy-start.8 = (bf16[8,48,1280]{2,1,0:T(8,128)(2,1)S(1)}, bf16[8,48,1280]{2,1,0:T(8,128)(2,1)}, u32[]{:S(2)}) copy-start(bf16[8,48,1280]{2,1,0:T(8,128)(2,1)} %get-tuple-element.160) | copy-start | bytes 2949124
  424.0 14.3 %collective-permute-start.12 = (bf16[4,48,1280]{2,1,0:T(8,128)(2,1)S(1)}, bf16[4,48,1280]{2,1,0:T(8,128)(2,1)S(1)}, u32[]{:S(2)}, u32[]{:S(2)}) collective-permute-start(bf16[4,48,1280]{2,1,0:T(8,128)(2,1)S(1)} %fusion.2), channel_id=1, source_target_pairs={{0,16},{8,24},{16,0},{24,8},{1,17},{9,25},{17,1},{25,9},{2,18},{10... | collective-permute-start | bytes 1474568 | tf_op jit(solution)/shard_map/ppermute | solution.py:1121
  427.0 36.4 %collective-permute-start.10 = (bf16[1024,768]{1,0:T(8,128)(2,1)}, bf16[1024,768]{1,0:T(8,128)(2,1)}, u32[]{:S(2)}, u32[]{:S(2)}) collective-permute-start(bf16[1024,768]{1,0:T(8,128)(2,1)} %qkv_back.2), channel_id=1, source_target_pairs={{0,4},{4,0},{1,5},{5,1},{2,6},{6,2},{3,7},{7,3},{8,12},{12,8},{9,1... | collective-permute-start | bytes 4718600 | tf_op jit(solution)/shard_map/ppermute | solution.py:1336
  428.9 22.1 %collective-permute-start.16 = (bf16[2,3,64,768]{3,2,1,0:T(8,128)(2,1)S(1)}, bf16[2,3,64,768]{3,2,1,0:T(8,128)(2,1)}, u32[]{:S(2)}, u32[]{:S(2)}) collective-permute-start(bf16[2,3,64,768]{3,2,1,0:T(8,128)(2,1)S(1)} %add_convert_fusion), channel_id=1, source_target_pairs={{0,16},{8,24},{16,0},{24,8},{1,17},{9,25},{17,1},{25,9},{2,18},{10... | collective-permute-start | bytes 1769480 | tf_op jit(solution)/shard_map/ppermute | solution.py:1138
  438.5 13.7 %collective-permute-start.13 = (bf16[48,1280]{1,0:T(8,128)(2,1)S(1)}, bf16[48,1280]{1,0:T(8,128)(2,1)S(1)}, u32[]{:S(2)}, u32[]{:S(2)}) collective-permute-start(bf16[48,1280]{1,0:T(8,128)(2,1)S(1)} %get-tuple-element.206), channel_id=1, source_target_pairs={{0,1},{1,2},{2,3},{3,0},{4,5},{5,6},{6,7},{7,4},{8,9},{9,10},{10,1... | collective-permute-start | bytes 368648 | tf_op jit(solution)/shard_map/ppermute | solution.py:1128
  440.8 11.4 %collective-permute-start.14 = (bf16[48,1280]{1,0:T(8,128)(2,1)S(1)}, bf16[48,1280]{1,0:T(8,128)(2,1)S(1)}, u32[]{:S(2)}, u32[]{:S(2)}) collective-permute-start(bf16[48,1280]{1,0:T(8,128)(2,1)S(1)} %get-tuple-element.208), channel_id=1, source_target_pairs={{0,2},{1,3},{2,0},{3,1},{4,6},{5,7},{6,4},{7,5},{8,10},{9,11},{10,... | collective-permute-start | bytes 368648 | tf_op jit(solution)/shard_map/ppermute | solution.py:1128
  444.2 10.7 %collective-permute-start.15 = (bf16[48,1280]{1,0:T(8,128)(2,1)S(1)}, bf16[48,1280]{1,0:T(8,128)(2,1)S(1)}, u32[]{:S(2)}, u32[]{:S(2)}) collective-permute-start(bf16[48,1280]{1,0:T(8,128)(2,1)S(1)} %get-tuple-element.207), channel_id=1, source_target_pairs={{0,3},{1,0},{2,1},{3,2},{4,7},{5,4},{6,5},{7,6},{8,11},{9,8},{10,9... | collective-permute-start | bytes 368648 | tf_op jit(solution)/shard_map/ppermute | solution.py:1128
  463.4 12.7 %collective-permute-start.20 = (bf16[48,3840]{1,0:T(8,128)(2,1)}, bf16[48,3840]{1,0:T(8,128)(2,1)S(1)}, u32[]{:S(2)}, u32[]{:S(2)}) collective-permute-start(bf16[48,3840]{1,0:T(8,128)(2,1)} %reduce-scatter.5.cloned.1.call-done), channel_id=1, source_target_pairs={{0,4},{4,0},{1,5},{5,1},{2,6},{6,2},{3,7},{7,3},{8,12},{12,8},{9,1... | collective-permute-start | bytes 1105928 | tf_op jit(solution)/shard_map/ppermute | solution.py:1132
  464.8 10.5 %collective-permute-start.17 = (bf16[48,1280]{1,0:T(8,128)(2,1)S(1)}, bf16[48,1280]{1,0:T(8,128)(2,1)S(1)}, u32[]{:S(2)}, u32[]{:S(2)}) collective-permute-start(bf16[48,1280]{1,0:T(8,128)(2,1)S(1)} %fusion.14), channel_id=1, source_target_pairs={{0,4},{4,0},{1,5},{5,1},{2,6},{6,2},{3,7},{7,3},{8,12},{12,8},{9,1... | collective-permute-start | bytes 368648 | tf_op jit(solution)/shard_map/ppermute | solution.py:1135
  475.3 11.2 %copy-start.4 = (f32[1024,768]{1,0:T(8,128)S(1)}, f32[1024,768]{1,0:T(8,128)}, u32[]{:S(2)}) copy-start(f32[1024,768]{1,0:T(8,128)} %get-tuple-element.168) | copy-start | bytes 9437188
  475.3 5.5 %collective-permute-start.18 = (bf16[2,48,1280]{2,1,0:T(8,128)(2,1)S(1)}, bf16[2,48,1280]{2,1,0:T(8,128)(2,1)S(1)}, u32[]{:S(2)}, u32[]{:S(2)}) collective-permute-start(bf16[2,48,1280]{2,1,0:T(8,128)(2,1)S(1)} %get-tuple-element.210), channel_id=1, source_target_pairs={{0,16},{8,24},{16,0},{24,8},{1,17},{9,25},{17,1},{25,9},{2,18},{10... | collective-permute-start | bytes 737288 | tf_op jit(solution)/shard_map/ppermute | solution.py:1138
  477.3 19.2 %collective-permute-start.21 = (bf16[48,3840]{1,0:T(8,128)(2,1)S(1)}, bf16[48,3840]{1,0:T(8,128)(2,1)S(1)}, u32[]{:S(2)}, u32[]{:S(2)}) collective-permute-start(bf16[48,3840]{1,0:T(8,128)(2,1)S(1)} %add_convert_fusion.4), channel_id=1, source_target_pairs={{0,16},{8,24},{16,0},{24,8},{1,17},{9,25},{17,1},{25,9},{2,18},{10... | collective-permute-start | bytes 1105928 | tf_op jit(solution)/shard_map/ppermute | solution.py:1138
  480.8 17.4 %collective-permute-start.19 = (bf16[2,2,48,1280]{3,2,1,0:T(8,128)(2,1)S(1)}, bf16[2,2,48,1280]{3,2,1,0:T(8,128)(2,1)S(1)}, u32[]{:S(2)}, u32[]{:S(2)}) collective-permute-start(bf16[2,2,48,1280]{3,2,1,0:T(8,128)(2,1)S(1)} %get-tuple-element.205), channel_id=1, source_target_pairs={{0,8},{8,0},{16,24},{24,16},{1,9},{9,1},{17,25},{25,17},{2,10},{10... | collective-permute-start | bytes 1474568 | tf_op jit(solution)/shard_map/ppermute | solution.py:1141
  489.9 14.2 %collective-permute-start.23 = (bf16[2,2,3,64,768]{4,3,2,1,0:T(8,128)(2,1)S(1)}, bf16[2,2,3,64,768]{4,3,2,1,0:T(8,128)(2,1)}, u32[]{:S(2)}, u32[]{:S(2)}) collective-permute-start(bf16[2,2,3,64,768]{4,3,2,1,0:T(8,128)(2,1)S(1)} %pad_maximum_fusion.1), channel_id=1, source_target_pairs={{0,8},{8,0},{16,24},{24,16},{1,9},{9,1},{17,25},{25,17},{2,10},{10... | collective-permute-start | bytes 3538952 | tf_op jit(solution)/shard_map/ppermute | solution.py:1141
  497.7 13.3 %collective-permute-start.22 = (bf16[2,48,3840]{2,1,0:T(8,128)(2,1)}, bf16[2,48,3840]{2,1,0:T(8,128)(2,1)}, u32[]{:S(2)}, u32[]{:S(2)}) collective-permute-start(bf16[2,48,3840]{2,1,0:T(8,128)(2,1)} %get-tuple-element.202), channel_id=1, source_target_pairs={{0,8},{8,0},{16,24},{24,16},{1,9},{9,1},{17,25},{25,17},{2,10},{10... | collective-permute-start | bytes 2211848 | tf_op jit(solution)/shard_map/ppermute | solution.py:1141
  498.7 0.7 copy-start.14
  507.0 4.0 copy-start.5
  512.6 1.9 copy-start.1
Sparse Core Ops, SparseCore 0:
  16.8 76.3 all-gather.2
  96.0 79.1 all-gather.4
  221.8 113.0 reduce-scatter.2
  339.8 83.5 reduce-scatter.4

commit v5 on v4

--- a/solution.py
+++ b/solution.py
@@ -429,7 +429,7 @@
         ),
         out_shape=[jax.ShapeDtypeStruct((total, 128), BF)] * 3,
         compiler_params=params(),
-        cost_estimate=cost(20 * total * total * 128, 12 * total * 128, total * total),
+        cost_estimate=cost(4 * total * total * 128, 2 * total * 128),
         name="self_backward",
     )(counts, slots, q, k, v, own, far, o, lse, qa, ka)
 
@@ -731,35 +731,66 @@
     )(o, h1, w2, gain, cot, w3, w3)
 
 
-def unpack_kernel(me_ref, p_ref, gate_ref, up_ref, down_ref):
+def placed(me_ref, near_ref, far_ref, size):
     core, x = me_ref[0], me_ref[1]
-    tall = p_ref.shape[4]
+    for c, ref in enumerate((near_ref, far_ref)):
+        for a in range(2):
+            yield ref.at[a], pl.multiple_of(((a ^ x) * 2 + (c ^ core)) * size, 16)
+
+
+def unpack_kernel(me_ref, near_ref, far_ref, gate_ref, up_ref, down_ref):
+    core, x = me_ref[0], me_ref[1]
+    tall = near_ref.shape[3]
     third = 256
-    for p in range(8):
-        near = (core ^ ((p // 2) % 2), x ^ (p // 4), p % 2)
-        for t in range(3):
-            at, to = pl.ds(t * tall, tall), pl.ds(p * third, third)
-            lane = slice(t * third, (t + 1) * third)
-            gate_ref[at, to] = p_ref[near + (0, slice(None), lane)].astype(F32)
-            up_ref[at, to] = p_ref[near + (1, slice(None), lane)].astype(F32)
-        down_ref[pl.ds(p * tall, tall), :] = p_ref[near + (2,)].astype(F32)
-
-
-def unpack(me, pieces):
-    tall, dim = pieces.shape[-2:]
+    for c in range(2):
+        for a in range(2):
+            for i in range(2):
+                p = a * 4 + c * 2 + i
+                piece = lambda k: jnp.where(
+                    core == c, near_ref[a ^ x, i, k], far_ref[a ^ x, i, k]
+                ).astype(F32)
+                gate, up = piece(0), piece(1)
+                for t in range(3):
+                    at, to = pl.ds(t * tall, tall), pl.ds(p * third, third)
+                    gate_ref[at, to] = gate[:, t * third : (t + 1) * third]
+                    up_ref[at, to] = up[:, t * third : (t + 1) * third]
+                down_ref[pl.ds(p * tall, tall), :] = piece(2)
+
+
+def settle_mid_kernel(me_ref, near_ref, far_ref, *outs):
+    dim = outs[0].shape[1]
+    size = near_ref.shape[1]
+    for ref, row in placed(me_ref, near_ref, far_ref, size):
+        for m, out in enumerate(outs):
+            out[pl.ds(row, size), :] = ref[:, m * dim : (m + 1) * dim].astype(F32)
+
+
+def settle_qkv_kernel(me_ref, near_ref, far_ref, q_ref, k_ref, v_ref, tail_ref):
+    place = me_ref[2]
+    size = near_ref.shape[2]
+    width = q_ref.shape[1] // 2
+    for ref, row in placed(me_ref, near_ref, far_ref, size):
+        at = pl.ds(row, size)
+        tail = None
+        for i in range(2):
+            block = ref[i ^ place].astype(F32)
+            for t, out in enumerate((q_ref, k_ref, v_ref)):
+                out[at, i * width : (i + 1) * width] = block[:, t * width : (t + 1) * width]
+            part = block[:, 3 * width :]
+            tail = part if tail is None else tail + part
+        tail_ref[at, :] = tail
+
+
+def settle(kernel, me, near, far, shapes):
     vmem = pl.BlockSpec(memory_space=pltpu.VMEM)
     return pl.pallas_call(
-        unpack_kernel,
-        in_specs=[pl.BlockSpec(memory_space=pltpu.SMEM), vmem],
-        out_specs=[vmem] * 3,
-        out_shape=[
-            jax.ShapeDtypeStruct((3 * tall, 8 * 256), F32),
-            jax.ShapeDtypeStruct((3 * tall, 8 * 256), F32),
-            jax.ShapeDtypeStruct((8 * tall, dim), F32),
-        ],
-        compiler_params=params(),
-        name="unpack",
-    )(me, pieces)
+        kernel,
+        in_specs=[pl.BlockSpec(memory_space=pltpu.SMEM), vmem, vmem],
+        out_specs=[vmem] * len(shapes),
+        out_shape=[jax.ShapeDtypeStruct(shape, F32) for shape in shapes],
+        compiler_params=params(),
+        name=kernel.__name__[:-7],
+    )(me, near, far)
 
 
 def deal_rows(core, full, send_ref, keep_ref):
@@ -769,11 +800,11 @@
             ref[i] = full[pl.ds(pl.multiple_of((2 * i + c) * size, 16), size), :]
 
 
-def mid_grads_kernel(turn_ref, *refs, count, far_blocks):
+def mid_grads_kernel(turn_ref, *refs, count):
     n_in = count + 9
     sources = refs[:n_in]
-    wk_ref, wv_ref, g_ref, far_out, own_out = refs[n_in : n_in + 5]
-    buffers = refs[n_in + 5 : 2 * n_in + 5]
+    wk_ref, wv_ref, g_ref, far_out = refs[n_in : n_in + 4]
+    buffers = refs[n_in + 4 : 2 * n_in + 4]
     sems = refs[-1]
     m = pl.program_id(0)
     dim = g_ref.shape[0]
@@ -824,19 +855,11 @@
         g_ref[...] = tn(o2[...], dc[...]).astype(BF)
 
     block = far_out.shape[0]
-    blocks = dk.shape[0] // block
-
-    def enc_rows(i):
-        at = pl.ds(pl.multiple_of(lax.rem(i + ours // block, blocks) * block, block), block)
-        return nt(dk[at, :], wk_ref[...]) + nt(dv[at, :], wv_ref[...])
-
-    @pl.when((m >= 5) & (m < 5 + far_blocks))
-    def _():
-        far_out[...] = enc_rows(m - 5).astype(BF)
-
-    @pl.when(m >= 5 + far_blocks)
-    def _():
-        own_out[...] = enc_rows(m - 5)
+
+    @pl.when(m >= 5)
+    def _():
+        at = pl.ds(pl.multiple_of(ours + (m - 5) * block, block), block)
+        far_out[...] = (nt(dk[at, :], wk_ref[...]) + nt(dv[at, :], wv_ref[...])).astype(BF)
 
 
 def dealt_out(dim, block, total, index, deal):
@@ -853,16 +876,16 @@
     args = (n2, dq2, da, *pieces, own, far, dk2, dv2, o2, dc)
     shapes = [(rows, a.shape[1]) for a in args[: 3 + len(pieces)]]
     shapes += [a.shape for a in args[3 + len(pieces) :]]
-    flops = 2 * dim * dim * (3 * rows + 4 * dk2.shape[0])
+    flops = 2 * dim * dim * (3 * rows + 2 * dk2.shape[0] + 2 * far.shape[0])
     block = min(512, own.shape[0])
-    far_blocks, own_blocks = far.shape[0] // block, own.shape[0] // block
+    far_blocks = far.shape[0] // block
     once = pl.Buffered(1)
     column = lambda m, t: (0, jnp.where(m < 2, 1 - m, jnp.minimum(m, 4)))
     return pl.pallas_call(
-        functools.partial(mid_grads_kernel, count=len(pieces), far_blocks=far_blocks),
+        functools.partial(mid_grads_kernel, count=len(pieces)),
         grid_spec=pltpu.PrefetchScalarGridSpec(
             num_scalar_prefetch=1,
-            grid=(5 + far_blocks + own_blocks,),
+            grid=(5 + far_blocks,),
             in_specs=[pl.BlockSpec(memory_space=pl.ANY)] * len(args)
             + [
                 pl.BlockSpec((dim, dim), lambda m, t: (0, 2), pipeline_mode=once),
@@ -870,8 +893,7 @@
             ],
             out_specs=[
                 pl.BlockSpec((dim, dim), column),
-                pl.BlockSpec((block, dim), lambda m, t: (jnp.clip(m - 5, 0, far_blocks - 1), 0)),
-                pl.BlockSpec((block, dim), lambda m, t: (jnp.maximum(m - 5 - far_blocks, 0), 0)),
+                pl.BlockSpec((block, dim), lambda m, t: (jnp.maximum(m - 5, 0), 0)),
             ],
             scratch_shapes=[pltpu.VMEM(shape, BF) for shape in shapes]
             + [pltpu.SemaphoreType.DMA((len(args),))],
@@ -879,12 +901,40 @@
         out_shape=[
             jax.ShapeDtypeStruct((dim, 5 * dim), BF),
             jax.ShapeDtypeStruct(far.shape, BF),
-            jax.ShapeDtypeStruct(own.shape, F32),
         ],
         compiler_params=params(),
         cost_estimate=cost(flops, 30 * MIB),
         name="mid_grads",
     )(turn, *args, w2, w2)
+
+
+def enc_finish_kernel(dk_ref, dv_ref, wk_ref, wv_ref, *refs):
+    total = nt(dk_ref[...], wk_ref[...]) + nt(dv_ref[...], wv_ref[...])
+    for ref in refs[:-1]:
+        total = total + ref[...].astype(F32)
+    refs[-1][...] = total
+
+
+def enc_finish(dk, dv, w2, got):
+    rows, dim = got[0].shape
+    block = min(512, rows)
+    row = pl.BlockSpec((block, dim), lambda i: (i, 0))
+    return pl.pallas_call(
+        enc_finish_kernel,
+        grid=(rows // block,),
+        in_specs=[
+            row,
+            row,
+            pl.BlockSpec((dim, dim), lambda i: (0, 2)),
+            pl.BlockSpec((dim, dim), lambda i: (0, 3)),
+        ]
+        + [row] * len(got),
+        out_specs=row,
+        out_shape=jax.ShapeDtypeStruct((rows, dim), F32),
+        compiler_params=params(),
+        cost_estimate=cost(4 * rows * dim * dim, 12 * rows * dim),
+        name="enc_finish",
+    )(dk, dv, w2, w2, *got)
 
 
 def before_self_kernel(turn_ref, dq_ref, wq_ref, h_ref, dh_ref, g_ref, *refs, count):
@@ -999,7 +1049,7 @@
         ),
         out_shape=outs,
         compiler_params=params(),
-        cost_estimate=cost(2 * total * dim * width, 6 * total * dim),
+        cost_estimate=cost(total * dim, total),
         name="qkv_grads",
     )(core, *ds, n, w, gain, extra)
 
@@ -1022,7 +1072,7 @@
         ),
         out_shape=jax.ShapeDtypeStruct((rows, dim), dtype),
         compiler_params=params(),
-        cost_estimate=cost(2 * rows * dim * w.shape[1], 10 * rows * dim),
+        cost_estimate=cost(rows * dim, rows),
         name="qkv_back",
     )(order, *ds, w)
 
@@ -1137,21 +1187,8 @@
     def widen_x(self, g):
         return jnp.stack([g, lax.ppermute(g, "parts", self.swap_x)])
 
-    def widen_core(self, g):
-        return jnp.stack([g, lax.ppermute(g, "parts", self.swap_core)])
-
-    def widen(self, g):
-        return self.widen_core(self.widen_x(g))
-
-    def rows(self, wide):
-        pieces = [
-            lax.dynamic_slice(
-                wide, (c ^ self.core, a ^ self.x, 0, 0), (1, 1) + wide.shape[2:]
-            )[0, 0]
-            for a in range(2)
-            for c in range(2)
-        ]
-        return jnp.concatenate(pieces).astype(F32)
+    def from_core(self, g):
+        return lax.ppermute(g, "parts", self.swap_core)
 
 
 def local(
@@ -1216,7 +1253,6 @@
     first = jnp.concatenate(
         [own_heads(self_query), own_heads(self_key), own_heads(self_value), gain_cols], axis=1
     )
-    first, self_output, gate_in = lax.optimization_barrier((first, self_output, gate_in))
     w1, gains = gather_first(first, z, part, n_fsdp, n_parts)
     gains = gains[:, :8].astype(F32).T
     gain_self, gain_cross, gain_mlp = (gains[i : i + 1] for i in range(3))
@@ -1286,7 +1322,7 @@
     do_far = do_far[0] if n_ctx == 2 else jnp.concatenate(do_far, axis=0)
     do_own = do1[0]
     core = jnp.reshape(part % 2, (1,)).astype(jnp.int32)
-    g_mid, d_far, enc_grad = mid_grads(
+    g_mid, d_far = mid_grads(
         turn, pieces, da, n2, dq2, enc_own, enc_far, dk2, dv2, o2, dc, w2
     )
 
@@ -1327,30 +1363,35 @@
         by_pair, sum_ff, enc_got = lax.optimization_barrier((by_pair, sum_ff, enc_got))
     else:
         by_pair = [self_pair(i, do_own, do_far) for i in range(pairs)]
-    for piece in enc_got:
-        enc_grad = enc_grad + piece.astype(F32)
     ds = [d[i] for i in range(3) for d in by_pair]
-    g_qkv = qkv_grads(core, ds, n1, w1, gain_wide, extra, fast)
     dn_far = qkv_back(order_here, per_dev, ds, w1, total - rows, BF, block)
     dn_got = [
         lax.ppermute(dn_far[(i - 1) * rows : i * rows], "ctx", turned(n_ctx, i))
         for i in range(1, n_ctx)
     ]
+    ds, dn_far = lax.optimization_barrier((ds, dn_far))
+    g_qkv = qkv_grads(core, ds, n1, w1, gain_wide, extra, fast)
     dn_own = qkv_back(order_here, 0, ds, w1, rows, F32, block)
     if fast:
-        send, keep, dn_far = lax.optimization_barrier((*net.over_core(*g_qkv), dn_far))
-        g_qkv = net.over_fsdp(net.over_x(send, keep))
-        dn_got, g_qkv, part_mid, sum_ff, dn_own = lax.optimization_barrier(
-            (dn_got, g_qkv, part_mid, net.widen_x(sum_ff), dn_own)
+        sum_ff = net.widen_x(sum_ff)
+        g_qkv = net.over_fsdp(net.over_x(*net.over_core(*g_qkv)))
+        dn_got, part_mid, dn_own = lax.optimization_barrier((dn_got, part_mid, dn_own))
+    decoder_grad = finish(x_own, dh1, gain_self, dn_own, dn_got)
+    enc_grad = enc_finish(dk2, dv2, w2, enc_got)
+
+    if fast:
+        me = jnp.stack([net.core, net.x, place]).astype(jnp.int32)
+        g_qkv = net.widen_x(net.widen_ctx(g_qkv))
+        sum_mid = net.widen_x(net.over_ctx(part_mid))
+        square = (shard, dim)
+        *grads_qkv, tail = settle(
+            settle_qkv_kernel, me, g_qkv, net.from_core(g_qkv), [square] * 3 + [(shard, 128)]
         )
-    decoder_grad = finish(x_own, dh1, gain_self, dn_own, dn_got)
-
-    if fast:
-        sum_mid = net.rows(net.widen(net.over_ctx(part_mid)))
-        me = jnp.stack([net.core, net.x]).astype(jnp.int32)
-        grad_gate, grad_up, grad_down = unpack(me, net.widen_core(sum_ff))
-        wide = net.widen(net.widen_ctx(g_qkv))
-        every = jnp.stack([net.rows(pick(wide, i ^ place, 2)) for i in range(2)])
+        mids = settle(settle_mid_kernel, me, sum_mid, net.from_core(sum_mid), [square] * 5)
+        grad_gate, grad_up, grad_down = settle(
+            unpack_kernel, me, sum_ff, net.from_core(sum_ff),
+            [(shard, hidden), (shard, hidden), (hidden // n_fsdp, dim)],
+        )
     else:
 
         def total_of(g):
@@ -1367,15 +1408,17 @@
         grad_down = total_of(g_ff[:, :, 2].reshape(hidden, dim))
         sum_qkv = lax.psum_scatter(g_qkv, "fsdp", scatter_dimension=0, tiled=True).astype(F32)
         every = lax.all_gather(lax.psum(sum_qkv, "parts"), "ctx", axis=0)
-    grads_qkv = [
-        jnp.concatenate([every[c, :, i * width : (i + 1) * width] for c in range(n_ctx)], axis=1)[:, :dim]
-        for i in range(3)
-    ]
-    tail = jnp.sum(every[:, :, 3 * width : 3 * width + 8], axis=0)
+        grads_qkv = [
+            jnp.concatenate(
+                [every[c, :, i * width : (i + 1) * width] for c in range(n_ctx)], axis=1
+            )[:, :dim]
+            for i in range(3)
+        ]
+        tail = jnp.sum(every[:, :, 3 * width :], axis=0)
+        mids = [sum_mid[:, i * dim : (i + 1) * dim] for i in range(5)]
     grad_gself, grad_gmlp, grad_gcross = tail[:, 0], tail[:, 1], tail[:, 2]
     entries = float(n_parts * n_ctx * n_fsdp * rows * dim)
-    rms_values = jnp.sqrt(tail[0, jnp.array([3, 4, 5, 6])] / entries)
-    mids = [sum_mid[:, i * dim : (i + 1) * dim] for i in range(5)]
+    rms_values = jnp.sqrt(tail[0, 3:7] / entries)
     return (
         layer_out[None],
         decoder_grad[None],

time: 528 us -> 515 us (0.975)
  Pallas kernels: 327 us -> 347 us
  other arithmetic: 28.3 us -> 14.7 us
  waiting for transfers between devices: 80.5 us -> 70.8 us
  local copies, waits for them, and re-layouts: 31.6 us -> 26.2 us
    ppermute x1, waiting for transfers between devices: 14.4 us -> 0.01 us  [local(): lax.ppermute(d_far[(i - 1) * enc_rows:i * enc_rows], 'ctx', turned(n_ctx,...]
    ppermute x1, waiting for transfers between devices: 2.71 us -> 12.7 us  [over_x(): got = lax.ppermute(send, 'parts', self.swap_x)]
    pallas_call x2 -> x5, Pallas kernels: 27.1 us -> 35.7 us  [the longest x1 19.4 us: mid_grads(): pl.pallas_call(functools.partial(mid_grads_kernel, count=len(pieces)), gr...]
    pallas_call x3, Pallas kernels: 45.2 us -> 52.3 us  [self_backward(): pl.pallas_call(functools.partial(self_backward_kernel, per_dev=per_dev),...]
  transfers between devices with their start and end apart: 28 -> 28, of which waited for: 12 -> 11; matrix products, arithmetic and copies ran while one was open for 8% -> 6% of each run, Pallas kernels for 54% -> 59%
where the time goes in v5:
time: 515 us; the launch traced here: 509 us
  Pallas kernels  347 us (67%)
  waiting for transfers between devices  70.8 us (14%)
  starting transfers between devices  34.9 us (7%)
  local copies, waits for them, and re-layouts  26.2 us (5%)
  between operations  15.4 us (3%)
  other arithmetic  14.7 us (3%)
    pallas_call x1, Pallas kernels, cross_backward(): pl.pallas_call(cross_backward_kernel, grid=(pairs, rows // block), in_spe...  78.5 us
    pallas_call x3, Pallas kernels, self_backward(): pl.pallas_call(functools.partial(self_backward_kernel, per_dev=per_dev),...  52.3 us
    pallas_call x1, Pallas kernels, feed_forward(): pl.pallas_call(mlp_kernel, grid=(steps,), in_specs=[full, full, pl.BlockS...  46.3 us
    pallas_call x1, Pallas kernels, cross_forward(): pl.pallas_call(cross_forward_kernel, grid=(pairs, rows // block), in_spec...  35.9 us
    pallas_call x1, Pallas kernels, self_forward(): pl.pallas_call(self_forward_kernel, grid_spec=pltpu.PrefetchScalarGridSpe...  27.5 us
    ppermute x3, waiting for transfers between devices, gather_first(): lax.ppermute(mine, 'fsdp', turned(n_fsdp, d))  22.7 us
    pallas_call x1, Pallas kernels, mid_grads(): pl.pallas_call(functools.partial(mid_grads_kernel, count=len(pieces)), gr...  19.4 us
    pallas_call x2, Pallas kernels, qkv_back(): pl.pallas_call(functools.partial(qkv_back_kernel, count=len(ds)), grid_sp...  13.3 us
  transfers between devices with their start and end apart: 28, of which 11 were waited for; matrix products, arithmetic and copies ran while one was open for 6% of the time, Pallas kernels for 59%

profile of v5, /device:TPU:9, one launch (start us, length us, event | category | flops | bytes accessed | tf_op | source)
XLA Modules:
  0.0 509.4 jit_solution(5356684785827119432)
XLA Ops:
  16.2 1.5 collective-permute-start.1
  17.7 4.1 collective-permute-start.2
  25.9 10.0 %collective-permute-done.1 = bf16[96,1280]{1,0:T(8,128)(2,1)S(1)} collective-permute-done((bf16[96,1280]{1,0:T(8,128)(2,1)S(1)}, bf16[96,1280]{1,0:T(8,128)(2,1)S(1)}, u32[]{:S(2)}, u32[]{:S(2)}) %collective-permute-start.1) | collective-permute-done | bytes 245792 | tf_op jit(solution)/shard_map/ppermute | solution.py:1134
  35.9 12.7 %collective-permute-done.2 = bf16[96,1280]{1,0:T(8,128)(2,1)S(1)} collective-permute-done((bf16[96,1280]{1,0:T(8,128)(2,1)S(1)}, bf16[96,1280]{1,0:T(8,128)(2,1)S(1)}, u32[]{:S(2)}, u32[]{:S(2)}) %collective-permute-start.2) | collective-permute-done | bytes 245792 | tf_op jit(solution)/shard_map/ppermute | solution.py:1134
  50.4 2.7 collective-permute-start.4
  55.7 2.6 select_convert_fusion
  58.3 3.1 assemble.1
  64.8 9.2 %qkv_forward.1 = (bf16[2048,768]{1,0:T(8,128)(2,1)}, bf16[2048,384]{1,0:T(8,128)(2,1)}, bf16[2048,384]{1,0:T(8,128)(2,1)}, bf16[2048,384]{1,0:T(8,128)(2,1)}) custom-call(s32[4]{0:T(128)} %copy-done.23, bf16[1024,768]{1,0:T(8,128)(2,1)} %bitcast.70, bf16[1024,768]{1,0:T(8,128)(2,1)} %collective-permute-done.far_ref, f32[1,768]{1,0:T(1,128)} %get-tuple-element.207.g_ref, ...), custom_call_target="tpu_custom_call" | custom-call | flops 3623878656 | bytes 12582912 | tf_op jit(solution)/shard_map/qkv_forward/pallas_call | solution.py:455
  74.0 27.5 %self_forward.1 = (bf16[2048,384]{1,0:T(8,128)(2,1)}, f32[2048,384]{1,0:T(8,128)}) custom-call(s32[4]{0:T(128)} %and_select_fusion.3.count_ref, s32[4]{0:T(128)} %get-tuple-element.107.slot_ref, bf16[2048,384]{1,0:T(8,128)(2,1)} %get-tuple-element.111.q_ref, bf16[2048,384]{1,0:T(8,128)(2,1)} %get-tuple-element.112.k_ref, ...), custom_call_target="tpu_custom_call" | custom-call | flops 12884901888 | bytes 6291456 | tf_op jit(solution)/shard_map/self_forward/pallas_call | solution.py:358
  104.7 9.3 %enc_forward.1.k_ref.v_ref = bf16[2048,1536]{1,0:T(8,128)(2,1)} custom-call(bf16[1024,768]{1,0:T(8,128)(2,1)} %bitcast.105, bf16[1024,768]{1,0:T(8,128)(2,1)} %copy-done.24, bf16[768,3840]{1,0:T(8,128)(2,1)} %all-gather.3.cloned.1.call-done.w_ref.refs_2_.refs_3_.refs_5_.wc_ref.wq_ref.refs_0_.refs_1_.refs_11_.refs_12_.wk_ref.wv_ref), custom_call_target="tpu_custom_call" | custom-call | flops 4831838208 | bytes 12582912 | tf_op jit(solution)/shard_map/enc_forward/pallas_call | solution.py:489
  114.0 6.4 %collective-permute-done.5.refs_1_.refs_4_ = bf16[1024,384]{1,0:T(8,128)(2,1)S(1)} collective-permute-done((bf16[1024,384]{1,0:T(8,128)(2,1)S(1)}, bf16[1024,384]{1,0:T(8,128)(2,1)S(1)}, u32[]{:S(2)}, u32[]{:S(2)}) %collective-permute-start.5) | collective-permute-done | bytes 786464 | tf_op jit(solution)/shard_map/ppermute | solution.py:1300
  121.3 9.1 %after_self.1 = (f32[1024,768]{1,0:T(8,128)}, bf16[1024,768]{1,0:T(8,128)(2,1)}, bf16[1024,768]{1,0:T(8,128)(2,1)}, f32[8,768]{1,0:T(8,128)}) custom-call(s32[2]{0:T(128)} %and_select_fusion.5.turn_ref, bf16[1024,768]{1,0:T(8,128)(2,1)} %bitcast.71, bf16[2048,384]{1,0:T(8,128)(2,1)} %get-tuple-element.114.refs_0_.refs_3_.o_ref, ...), custom_call_target="tpu_custom_call" | custom-call | flops 2415919104 | bytes 11010048 | tf_op jit(solution)/shard_map/after_self/pallas_call | solution.py:537
  131.1 35.9 %cross_forward.1 = (bf16[1024,768]{1,0:T(8,128)(2,1)}, f32[1024,768]{1,0:T(8,128)}) custom-call(bf16[1024,768]{1,0:T(8,128)(2,1)} %get-tuple-element.117.q_ref, bf16[2048,1536]{1,0:T(8,128)(2,1)} %enc_forward.1.k_ref.v_ref, bf16[2048,1536]{1,0:T(8,128)(2,1)} %enc_forward.1.k_ref.v_ref, bf16[1024,128]{1,0:T(8,128)(2,1)} %broadcast_in_dim.93.qa_ref, ...), custom_call_target="tpu_custom_call" | custom-call | flops 25769803776 | bytes 6291456 | tf_op jit(solution)/shard_map/cross_forward/pallas_call | solution.py:243
  167.0 3.9 all-gather.5.cloned.1.call-done
  170.9 46.3 %feed_forward.1 = (bf16[1024,768]{1,0:T(8,128)(2,1)}, f32[1024,768]{1,0:T(8,128)}, bf16[1024,768]{1,0:T(8,128)(2,1)}, bf16[1024,768]{1,0:T(8,128)(2,1)}, f32[8,7...) custom-call(bf16[1024,768]{1,0:T(8,128)(2,1)} %get-tuple-element.119.o_ref.refs_9_, ...), custom_call_target="tpu_custom_call" | custom-call | flops 32614907904 | bytes 41943040 | tf_op jit(solution)/shard_map/feed_forward/pallas_call | solution.py:686
  218.8 78.5 %cross_backward.1 = (bf16[1024,768]{1,0:T(8,128)(2,1)}, bf16[2048,768]{1,0:T(8,128)(2,1)}, bf16[2048,768]{1,0:T(8,128)(2,1)}) custom-call(bf16[1024,768]{1,0:T(8,128)(2,1)} %get-tuple-element.117.q_ref, bf16[2048,1536]{1,0:T(8,128)(2,1)} %enc_forward.1.k_ref.v_ref, bf16[2048,1536]{1,0:T(8,128)(2,1)} %enc_forward.1.k_ref.v_ref, ...), custom_call_target="tpu_custom_call" | custom-call | flops 64424509440 | bytes 9437184 | tf_op jit(solution)/shard_map/cross_backward/pallas_call | solution.py:291
  297.2 9.9 %before_self.1 = (f32[1024,768]{1,0:T(8,128)}, bf16[1024,768]{1,0:T(8,128)(2,1)}, f32[8,768]{1,0:T(8,128)}, bf16[1024,384]{1,0:T(8,128)(2,1)}, bf16[1024,384]{1,0:T(8,128)(2,1)}) custom-call(s32[2]{0:T(128)} %and_select_fusion.5.turn_ref, bf16[1024,768]{1,0:T(8,128)(2,1)} %get-tuple-element.124.dq_ref.refs_1_, ...), custom_call_target="tpu_custom_call" | custom-call | flops 2415919104 | bytes 14155776 | tf_op jit(solution)/shard_map/before_self/pallas_call | solution.py:967
  309.0 1.3 collective-permute-start.7
  310.5 1.4 concatenate.20.refs_12_
  311.9 19.4 %mid_grads.1 = (bf16[768,3840]{1,0:T(8,128)(2,1)}, bf16[1024,768]{1,0:T(8,128)(2,1)}) custom-call(s32[2]{0:T(128)} %and_select_fusion.5.turn_ref, bf16[1024,768]{1,0:T(8,128)(2,1)} %get-tuple-element.129.refs_0_, bf16[1024,768]{1,0:T(8,128)(2,1)} %get-tuple-element.124.dq_ref.refs_1_, bf16[1024,768]{1,0:T(8,128)(2,1)} %get-tuple-element.130.refs_2_, ...), custom_call_target="tpu_custom_call" | custom-call | flops 10871635968 | bytes 31457280 | tf_op jit(solution)/shard_map/mid_grads/pallas_call | solution.py:884
  332.5 17.5 %self_backward.3 = (bf16[2048,128]{1,0:T(8,128)(2,1)}, bf16[2048,128]{1,0:T(8,128)(2,1)}, bf16[2048,128]{1,0:T(8,128)(2,1)}) custom-call(s32[4]{0:T(128)} %and_select_fusion.3.count_ref, s32[4]{0:T(128)} %get-tuple-element.107.slot_ref, bf16[2048,384]{1,0:T(8,128)(2,1)} %get-tuple-element.111.q_ref, bf16[2048,384]{1,0:T(8,128)(2,1)} %get-tuple-element.112.k_ref, ...), custom_call_target="tpu_custom_call" | custom-call | flops 2147483648 | bytes 524288 | tf_op jit(solution)/shard_map/self_backward/pallas_call | solution.py:411
  350.0 1.3 collective-permute-start.8
  351.3 17.3 %self_backward.5 = (bf16[2048,128]{1,0:T(8,128)(2,1)}, bf16[2048,128]{1,0:T(8,128)(2,1)}, bf16[2048,128]{1,0:T(8,128)(2,1)}) custom-call(s32[4]{0:T(128)} %and_select_fusion.3.count_ref, s32[4]{0:T(128)} %get-tuple-element.107.slot_ref, bf16[2048,384]{1,0:T(8,128)(2,1)} %get-tuple-element.111.q_ref, bf16[2048,384]{1,0:T(8,128)(2,1)} %get-tuple-element.112.k_ref, ...), custom_call_target="tpu_custom_call" | custom-call | flops 2147483648 | bytes 524288 | tf_op jit(solution)/shard_map/self_backward/pallas_call | solution.py:411
  368.6 17.5 %self_backward.4 = (bf16[2048,128]{1,0:T(8,128)(2,1)}, bf16[2048,128]{1,0:T(8,128)(2,1)}, bf16[2048,128]{1,0:T(8,128)(2,1)}) custom-call(s32[4]{0:T(128)} %and_select_fusion.3.count_ref, s32[4]{0:T(128)} %get-tuple-element.107.slot_ref, bf16[2048,384]{1,0:T(8,128)(2,1)} %get-tuple-element.111.q_ref, bf16[2048,384]{1,0:T(8,128)(2,1)} %get-tuple-element.112.k_ref, ...), custom_call_target="tpu_custom_call" | custom-call | flops 2147483648 | bytes 524288 | tf_op jit(solution)/shard_map/self_backward/pallas_call | solution.py:411
  386.3 6.3 %qkv_back.2 = bf16[1024,768]{1,0:T(8,128)(2,1)} custom-call(s32[4]{0:T(128)} %copy-done.23, bf16[2048,128]{1,0:T(8,128)(2,1)} %get-tuple-element.166.refs_0_, bf16[2048,128]{1,0:T(8,128)(2,1)} %get-tuple-element.167.refs_1_, bf16[2048,128]{1,0:T(8,128)(2,1)} %get-tuple-element.168.refs_2_, bf16[2048,128]{1,0:T(8,128)(2,1)} %get-tuple-element.169.refs_3_, ...), custom_call_target="tpu_custom_call" | custom-call | flops 786432 | bytes 1024 | tf_op jit(solution)/shard_map/qkv_back/pallas_call | solution.py:1064
  393.6 11.0 %qkv_grads.1 = (bf16[8,48,1280]{2,1,0:T(8,128)(2,1)}, bf16[8,48,1280]{2,1,0:T(8,128)(2,1)}) custom-call(s32[1]{0:T(128)} %bitcast.6.core_ref, bf16[2048,128]{1,0:T(8,128)(2,1)} %get-tuple-element.166.refs_0_, bf16[2048,128]{1,0:T(8,128)(2,1)} %get-tuple-element.167.refs_1_, bf16[2048,128]{1,0:T(8,128)(2,1)} %get-tuple-element.168.refs_2_, ...), custom_call_target="tpu_custom_call" | custom-call | flops 1572864 | bytes 2048 | tf_op jit(solution)/shard_map/qkv_grads/pallas_call | solution.py:1035
  404.6 2.9 collective-permute-start.11
  407.7 2.2 collective-permute-done.11
  409.9 2.3 fusion.2
  412.2 12.7 %collective-permute-done.12 = bf16[4,48,1280]{2,1,0:T(8,128)(2,1)} collective-permute-done((bf16[4,48,1280]{2,1,0:T(8,128)(2,1)}, bf16[4,48,1280]{2,1,0:T(8,128)(2,1)}, u32[]{:S(2)}, u32[]{:S(2)}) %collective-permute-start.12) | collective-permute-done | bytes 491552 | tf_op jit(solution)/shard_map/ppermute | solution.py:1171
  424.9 1.5 fusion
  427.1 2.9 collective-permute-start.14
  430.0 7.0 %qkv_back.3.own_ref = f32[1024,768]{1,0:T(8,128)} custom-call(s32[4]{0:T(128)} %copy-done.23, bf16[2048,128]{1,0:T(8,128)(2,1)} %get-tuple-element.166.refs_0_, bf16[2048,128]{1,0:T(8,128)(2,1)} %get-tuple-element.167.refs_1_, bf16[2048,128]{1,0:T(8,128)(2,1)} %get-tuple-element.168.refs_2_, bf16[2048,128]{1,0:T(8,128)(2,1)} %get-tuple-element.169.refs_3_, ...), custom_call_target="tpu_custom_call" | custom-call | flops 786432 | bytes 1024 | tf_op jit(solution)/shard_map/qkv_back/pallas_call | solution.py:1064
  436.9 6.8 %collective-permute-done.10.refs_0_ = bf16[1024,768]{1,0:T(8,128)(2,1)S(1)} collective-permute-done((bf16[1024,768]{1,0:T(8,128)(2,1)}, bf16[1024,768]{1,0:T(8,128)(2,1)S(1)}, u32[]{:S(2)}, u32[]{:S(2)}) %collective-permute-start.10) | collective-permute-done | bytes 1572896 | tf_op jit(solution)/shard_map/ppermute | solution.py:1369
  443.9 1.4 collective-permute-start.16
  445.3 10.4 %collective-permute-done.16 = bf16[48,1280]{1,0:T(8,128)(2,1)S(1)} collective-permute-done((bf16[48,1280]{1,0:T(8,128)(2,1)S(1)}, bf16[48,1280]{1,0:T(8,128)(2,1)S(1)}, u32[]{:S(2)}, u32[]{:S(2)}) %collective-permute-start.16) | collective-permute-done | bytes 122912 | tf_op jit(solution)/shard_map/ppermute | solution.py:1185
  456.0 1.5 collective-permute-start.20
  458.8 4.4 collective-permute-start.23
  464.0 4.4 collective-permute-start.18
  468.4 3.5 collective-permute-done.20
  471.9 2.4 collective-permute-start.21
  475.0 6.6 %enc_finish.1 = f32[1024,768]{1,0:T(8,128)} custom-call(bf16[2048,768]{1,0:T(8,128)(2,1)} %get-tuple-element.131.refs_7_.dk_ref, bf16[2048,768]{1,0:T(8,128)(2,1)} %get-tuple-element.132.refs_8_.dv_ref, bf16[768,3840]{1,0:T(8,128)(2,1)} %all-gather.3.cloned.1.call-done.w_ref.refs_2_.refs_3_.refs_5_.wc_ref.wq_ref.refs_0_.refs_1_.refs_11_.refs_12_.wk_ref.wv_ref, ...), custom_call_target="tpu_custom_call" | custom-call | flops 2415919104 | bytes 9437184 | tf_op jit(solution)/shard_map/enc_finish/pallas_call | solution.py:922
  481.7 4.1 unpack.1
  486.5 2.5 settle_qkv.1
  489.1 1.9 slice_reduce_fusion
  490.9 1.3 sqrt_bitcast_fusion
  492.2 6.4 %finish.1 = f32[1024,768]{1,0:T(8,128)} custom-call(bf16[1024,768]{1,0:T(8,128)(2,1)} %bitcast.72, f32[1024,768]{1,0:T(8,128)} %get-tuple-element.126.dh_ref, f32[1,768]{1,0:T(1,128)} %get-tuple-element.207.g_ref, f32[1024,768]{1,0:T(8,128)} %qkv_back.3.own_ref, bf16[1024,768]{1,0:T(8,128)(2,1)} %copy-done.9), custom_call_target="tpu_custom_call" | custom-call | flops 7864320 | bytes 12582912 | tf_op jit(solution)/shard_map/finish/pallas_call | solution.py:1092
  499.5 3.1 settle_mid.1
  (167 shorter events, 36.3 us)
Async XLA Ops:
  7.2 7.4 %copy-start = (bf16[512,768]{1,0:T(8,128)(2,1)S(1)}, bf16[512,768]{1,0:T(8,128)(2,1)}, u32[]{:S(2)}) copy-start(bf16[512,768]{1,0:T(8,128)(2,1)} %param.35) | copy-start | bytes 2359300
  7.2 96.3 %all-gather.3.cloned.1.call-start = ((), (), s32[]{:S(2)}) async-start(), calls=%async_computation.2 | async-start | bytes 6266880 | tf_op jit(solution)/shard_map/all_gather | solution.py:1261
  12.5 158.3 %all-gather.5.cloned.1.call-start = ((), (), s32[]{:S(2)}) async-start(), calls=%async_computation.3 | async-start | bytes 10027008 | tf_op jit(solution)/shard_map/all_gather | solution.py:1270
  14.6 1.3 copy-start.19
  14.7 1.4 copy-start.20
  14.7 1.4 copy-start.21
  14.8 7.0 %copy-start.3 = (bf16[1,1024,768]{2,1,0:T(8,128)(2,1)S(1)}, bf16[1,1024,768]{2,1,0:T(8,128)(2,1)}, u32[]{:S(2)}) copy-start(bf16[1,1024,768]{2,1,0:T(8,128)(2,1)} %param.20) | copy-start | bytes 4718596
  14.8 8.7 %copy-start.18 = (s32[1,2048]{1,0:T(1,128)S(1)}, s32[1,2048]{1,0:T(1,128)}, u32[]{:S(2)}) copy-start(s32[1,2048]{1,0:T(1,128)} %param.22) | copy-start | bytes 24580
  14.8 10.3 %copy-start.28 = (s32[1,4]{1,0:T(1,128)S(1)}, s32[1,4]{1,0:T(1,128)}, u32[]{:S(2)}) copy-start(s32[1,4]{1,0:T(1,128)} %param.23) | copy-start | bytes 52
  15.7 315.7 %reduce-scatter.3.cloned.1.call-start = ((), (), s32[]{:S(2)}) async-start(), calls=%async_computation.4 | async-start | bytes 10027008 | tf_op jit(solution)/shard_map/reduce_scatter | solution.py:1315
  16.1 9.8 %collective-permute-start.3 = (bf16[96,1280]{1,0:T(8,128)(2,1)S(1)}, bf16[96,1280]{1,0:T(8,128)(2,1)S(1)}, u32[]{:S(2)}, u32[]{:S(2)}) collective-permute-start(bf16[96,1280]{1,0:T(8,128)(2,1)S(1)} %fusion.4), channel_id=1, source_target_pairs={{0,3},{1,0},{2,1},{3,2},{4,7},{5,4},{6,5},{7,6},{8,11},{9,8},{10,9... | collective-permute-start | bytes 737288 | tf_op jit(solution)/shard_map/ppermute | solution.py:1134
  16.2 19.7 %collective-permute-start.1 = (bf16[96,1280]{1,0:T(8,128)(2,1)S(1)}, bf16[96,1280]{1,0:T(8,128)(2,1)S(1)}, u32[]{:S(2)}, u32[]{:S(2)}) collective-permute-start(bf16[96,1280]{1,0:T(8,128)(2,1)S(1)} %fusion.4), channel_id=1, source_target_pairs={{0,1},{1,2},{2,3},{3,0},{4,5},{5,6},{6,7},{7,4},{8,9},{9,10},{10,1... | collective-permute-start | bytes 737288 | tf_op jit(solution)/shard_map/ppermute | solution.py:1134
  17.7 31.0 %collective-permute-start.2 = (bf16[96,1280]{1,0:T(8,128)(2,1)S(1)}, bf16[96,1280]{1,0:T(8,128)(2,1)S(1)}, u32[]{:S(2)}, u32[]{:S(2)}) collective-permute-start(bf16[96,1280]{1,0:T(8,128)(2,1)S(1)} %fusion.4), channel_id=1, source_target_pairs={{0,2},{1,3},{2,0},{3,1},{4,6},{5,7},{6,4},{7,5},{8,10},{9,11},{10,... | collective-permute-start | bytes 737288 | tf_op jit(solution)/shard_map/ppermute | solution.py:1134
  21.8 41.8 %collective-permute-start = (bf16[1024,768]{1,0:T(8,128)(2,1)S(1)}, bf16[1024,768]{1,0:T(8,128)(2,1)}, u32[]{:S(2)}, u32[]{:S(2)}) collective-permute-start(bf16[1024,768]{1,0:T(8,128)(2,1)S(1)} %bitcast.73), channel_id=1, source_target_pairs={{0,4},{4,0},{1,5},{5,1},{2,6},{6,2},{3,7},{7,3},{8,12},{12,8},{9,1... | collective-permute-start | bytes 4718600 | tf_op jit(solution)/shard_map/ppermute | solution.py:1240
  50.4 7.9 %copy-start.5 = (bf16[4,96,1280]{2,1,0:T(8,128)(2,1)}, bf16[4,96,1280]{2,1,0:T(8,128)(2,1)S(1)}, u32[]{:S(2)}) copy-start(bf16[4,96,1280]{2,1,0:T(8,128)(2,1)S(1)} %pad_maximum_fusion.1.near_ref) | copy-start | bytes 2949124
  50.4 7.9 %collective-permute-start.4 = (bf16[4,96,1280]{2,1,0:T(8,128)(2,1)S(1)}, bf16[4,96,1280]{2,1,0:T(8,128)(2,1)}, u32[]{:S(2)}, u32[]{:S(2)}) collective-permute-start(bf16[4,96,1280]{2,1,0:T(8,128)(2,1)S(1)} %pad_maximum_fusion.1.near_ref), channel_id=1, source_target_pairs={{0,8},{8,0},{16,24},{24,16},{1,9},{9,1},{17,25},{25,17},{2,10},{10... | collective-permute-start | bytes 2949128 | tf_op jit(solution)/shard_map/ppermute | solution.py:1136
  53.8 7.5 %copy-start.23 = (s32[4]{0:T(128)}, s32[4]{0:T(128)S(1)}, u32[]{:S(2)}) copy-start(s32[4]{0:T(128)S(1)} %dynamic_slice.66.order_ref) | copy-start | bytes 52
  63.6 39.9 %collective-permute-start.6 = (bf16[1024,768]{1,0:T(8,128)(2,1)}, bf16[1024,768]{1,0:T(8,128)(2,1)S(1)}, u32[]{:S(2)}, u32[]{:S(2)}) collective-permute-start(bf16[1024,768]{1,0:T(8,128)(2,1)} %bitcast.104), channel_id=1, source_target_pairs={{0,4},{4,0},{1,5},{5,1},{2,6},{6,2},{3,7},{7,3},{8,12},{12,8},{9,1... | collective-permute-start | bytes 4718600 | tf_op jit(solution)/shard_map/ppermute | solution.py:1240
  102.7 17.7 %collective-permute-start.5 = (bf16[1024,384]{1,0:T(8,128)(2,1)S(1)}, bf16[1024,384]{1,0:T(8,128)(2,1)S(1)}, u32[]{:S(2)}, u32[]{:S(2)}) collective-permute-start(bf16[1024,384]{1,0:T(8,128)(2,1)S(1)} %slice.45), channel_id=1, source_target_pairs={{0,4},{4,0},{1,5},{5,1},{2,6},{6,2},{3,7},{7,3},{8,12},{12,8},{9,1... | collective-permute-start | bytes 2359304 | tf_op jit(solution)/shard_map/ppermute | solution.py:1300
  103.5 1.2 copy-start.24
  217.2 226.5 %reduce-scatter.5.cloned.1.call-start = ((), (), s32[]{:S(2)}) async-start(), calls=%async_computation.5 | async-start | bytes 6266880 | tf_op jit(solution)/shard_map/reduce_scatter | solution.py:1353
  309.0 22.3 %collective-permute-start.7 = (bf16[1024,384]{1,0:T(8,128)(2,1)}, bf16[1024,384]{1,0:T(8,128)(2,1)S(1)}, u32[]{:S(2)}, u32[]{:S(2)}) collective-permute-start(bf16[1024,384]{1,0:T(8,128)(2,1)} %get-tuple-element.128), channel_id=1, source_target_pairs={{0,4},{4,0},{1,5},{5,1},{2,6},{6,2},{3,7},{7,3},{8,12},{12,8},{9,1... | collective-permute-start | bytes 2359304 | tf_op jit(solution)/shard_map/ppermute | solution.py:1321
  332.2 54.0 %collective-permute-start.9 = (bf16[1024,768]{1,0:T(8,128)(2,1)}, bf16[1024,768]{1,0:T(8,128)(2,1)S(1)}, u32[]{:S(2)}, u32[]{:S(2)}) collective-permute-start(bf16[1024,768]{1,0:T(8,128)(2,1)} %get-tuple-element.155), channel_id=1, source_target_pairs={{0,4},{4,0},{1,5},{5,1},{2,6},{6,2},{3,7},{7,3},{8,12},{12,8},{9,1... | collective-permute-start | bytes 4718600 | tf_op jit(solution)/shard_map/ppermute | solution.py:1355
  332.5 17.5 %copy-start.13 = (bf16[384,768]{1,0:T(8,128)(2,1)S(1)}, bf16[384,768]{1,0:T(8,128)(2,1)}, u32[]{:S(2)}) copy-start(bf16[384,768]{1,0:T(8,128)(2,1)} %reduce-scatter.3.cloned.1.call-done) | copy-start | bytes 1769476
  350.0 36.1 %collective-permute-start.8 = (bf16[2,3,64,768]{3,2,1,0:T(8,128)(2,1)S(1)}, bf16[2,3,64,768]{3,2,1,0:T(8,128)(2,1)S(1)}, u32[]{:S(2)}, u32[]{:S(2)}) collective-permute-start(bf16[2,3,64,768]{3,2,1,0:T(8,128)(2,1)S(1)} %bitcast.87), channel_id=1, source_target_pairs={{0,4},{4,0},{1,5},{5,1},{2,6},{6,2},{3,7},{7,3},{8,12},{12,8},{9,1... | collective-permute-start | bytes 1769480 | tf_op jit(solution)/shard_map/ppermute | solution.py:1182
  386.3 6.4 %copy-start.8 = (bf16[1024,768]{1,0:T(8,128)(2,1)}, bf16[1024,768]{1,0:T(8,128)(2,1)S(1)}, u32[]{:S(2)}) copy-start(bf16[1024,768]{1,0:T(8,128)(2,1)S(1)} %collective-permute-done.9.refs_0_) | copy-start | bytes 4718596
  386.3 6.4 %copy-start.22 = (f32[768]{0:T(1024)S(1)}, f32[768]{0:T(1024)}, u32[]{:S(2)}) copy-start(f32[768]{0:T(1024)} %get-tuple-element.204) | copy-start | bytes 9220
  404.6 5.3 %collective-permute-start.11 = (bf16[8,48,1280]{2,1,0:T(8,128)(2,1)}, bf16[8,48,1280]{2,1,0:T(8,128)(2,1)S(1)}, u32[]{:S(2)}, u32[]{:S(2)}) collective-permute-start(bf16[8,48,1280]{2,1,0:T(8,128)(2,1)} %get-tuple-element.181), channel_id=1, source_target_pairs={{0,8},{8,0},{16,24},{24,16},{1,9},{9,1},{17,25},{25,17},{2,10},{10... | collective-permute-start | bytes 2949128 | tf_op jit(solution)/shard_map/ppermute | solution.py:1165
  407.5 36.2 %collective-permute-start.10 = (bf16[1024,768]{1,0:T(8,128)(2,1)}, bf16[1024,768]{1,0:T(8,128)(2,1)S(1)}, u32[]{:S(2)}, u32[]{:S(2)}) collective-permute-start(bf16[1024,768]{1,0:T(8,128)(2,1)} %qkv_back.2), channel_id=1, source_target_pairs={{0,4},{4,0},{1,5},{5,1},{2,6},{6,2},{3,7},{7,3},{8,12},{12,8},{9,1... | collective-permute-start | bytes 4718600 | tf_op jit(solution)/shard_map/ppermute | solution.py:1369
  409.9 2.3 copy-start.10
  412.2 12.7 %collective-permute-start.12 = (bf16[4,48,1280]{2,1,0:T(8,128)(2,1)}, bf16[4,48,1280]{2,1,0:T(8,128)(2,1)}, u32[]{:S(2)}, u32[]{:S(2)}) collective-permute-start(bf16[4,48,1280]{2,1,0:T(8,128)(2,1)} %fusion.2), channel_id=1, source_target_pairs={{0,16},{8,24},{16,0},{24,8},{1,17},{9,25},{17,1},{25,9},{2,18},{10... | collective-permute-start | bytes 1474568 | tf_op jit(solution)/shard_map/ppermute | solution.py:1171
  426.5 17.4 %collective-permute-start.13 = (bf16[48,1280]{1,0:T(8,128)(2,1)S(1)}, bf16[48,1280]{1,0:T(8,128)(2,1)S(1)}, u32[]{:S(2)}, u32[]{:S(2)}) collective-permute-start(bf16[48,1280]{1,0:T(8,128)(2,1)S(1)} %get-tuple-element.199), channel_id=1, source_target_pairs={{0,1},{1,2},{2,3},{3,0},{4,5},{5,6},{6,7},{7,4},{8,9},{9,10},{10,1... | collective-permute-start | bytes 368648 | tf_op jit(solution)/shard_map/ppermute | solution.py:1178
  427.1 16.8 %collective-permute-start.14 = (bf16[48,1280]{1,0:T(8,128)(2,1)S(1)}, bf16[48,1280]{1,0:T(8,128)(2,1)S(1)}, u32[]{:S(2)}, u32[]{:S(2)}) collective-permute-start(bf16[48,1280]{1,0:T(8,128)(2,1)S(1)} %get-tuple-element.201), channel_id=1, source_target_pairs={{0,2},{1,3},{2,0},{3,1},{4,6},{5,7},{6,4},{7,5},{8,10},{9,11},{10,... | collective-permute-start | bytes 368648 | tf_op jit(solution)/shard_map/ppermute | solution.py:1178
  430.0 13.9 %collective-permute-start.15 = (bf16[48,1280]{1,0:T(8,128)(2,1)S(1)}, bf16[48,1280]{1,0:T(8,128)(2,1)S(1)}, u32[]{:S(2)}, u32[]{:S(2)}) collective-permute-start(bf16[48,1280]{1,0:T(8,128)(2,1)S(1)} %get-tuple-element.200), channel_id=1, source_target_pairs={{0,3},{1,0},{2,1},{3,2},{4,7},{5,4},{6,5},{7,6},{8,11},{9,8},{10,9... | collective-permute-start | bytes 368648 | tf_op jit(solution)/shard_map/ppermute | solution.py:1178
  443.7 15.1 %copy-start.9 = (bf16[1024,768]{1,0:T(8,128)(2,1)}, bf16[1024,768]{1,0:T(8,128)(2,1)S(1)}, u32[]{:S(2)}) copy-start(bf16[1024,768]{1,0:T(8,128)(2,1)S(1)} %collective-permute-done.10.refs_0_) | copy-start | bytes 4718596
  443.7 12.2 %copy-start.16 = (bf16[48,3840]{1,0:T(8,128)(2,1)S(1)}, bf16[48,3840]{1,0:T(8,128)(2,1)}, u32[]{:S(2)}) copy-start(bf16[48,3840]{1,0:T(8,128)(2,1)} %reduce-scatter.5.cloned.1.call-done) | copy-start | bytes 1105924
  443.7 12.2 %collective-permute-start.19 = (bf16[48,3840]{1,0:T(8,128)(2,1)}, bf16[48,3840]{1,0:T(8,128)(2,1)S(1)}, u32[]{:S(2)}, u32[]{:S(2)}) collective-permute-start(bf16[48,3840]{1,0:T(8,128)(2,1)} %reduce-scatter.5.cloned.1.call-done), channel_id=1, source_target_pairs={{0,4},{4,0},{1,5},{5,1},{2,6},{6,2},{3,7},{7,3},{8,12},{12,8},{9,1... | collective-permute-start | bytes 1105928 | tf_op jit(solution)/shard_map/ppermute | solution.py:1182
  443.9 11.8 %collective-permute-start.16 = (bf16[48,1280]{1,0:T(8,128)(2,1)S(1)}, bf16[48,1280]{1,0:T(8,128)(2,1)S(1)}, u32[]{:S(2)}, u32[]{:S(2)}) collective-permute-start(bf16[48,1280]{1,0:T(8,128)(2,1)S(1)} %fusion.9), channel_id=1, source_target_pairs={{0,4},{4,0},{1,5},{5,1},{2,6},{6,2},{3,7},{7,3},{8,12},{12,8},{9,1... | collective-permute-start | bytes 368648 | tf_op jit(solution)/shard_map/ppermute | solution.py:1185
  445.3 13.4 %collective-permute-start.22 = (bf16[2,3,64,768]{3,2,1,0:T(8,128)(2,1)S(1)}, bf16[2,3,64,768]{3,2,1,0:T(8,128)(2,1)S(1)}, u32[]{:S(2)}, u32[]{:S(2)}) collective-permute-start(bf16[2,3,64,768]{3,2,1,0:T(8,128)(2,1)S(1)} %add_convert_fusion), channel_id=1, source_target_pairs={{0,16},{8,24},{16,0},{24,8},{1,17},{9,25},{17,1},{25,9},{2,18},{10... | collective-permute-start | bytes 1769480 | tf_op jit(solution)/shard_map/ppermute | solution.py:1188
  455.8 8.2 %collective-permute-start.17 = (bf16[2,48,1280]{2,1,0:T(8,128)(2,1)S(1)}, bf16[2,48,1280]{2,1,0:T(8,128)(2,1)S(1)}, u32[]{:S(2)}, u32[]{:S(2)}) collective-permute-start(bf16[2,48,1280]{2,1,0:T(8,128)(2,1)S(1)} %get-tuple-element.203), channel_id=1, source_target_pairs={{0,16},{8,24},{16,0},{24,8},{1,17},{9,25},{17,1},{25,9},{2,18},{10... | collective-permute-start | bytes 737288 | tf_op jit(solution)/shard_map/ppermute | solution.py:1188
  456.0 15.9 %collective-permute-start.20 = (bf16[48,3840]{1,0:T(8,128)(2,1)S(1)}, bf16[48,3840]{1,0:T(8,128)(2,1)S(1)}, u32[]{:S(2)}, u32[]{:S(2)}) collective-permute-start(bf16[48,3840]{1,0:T(8,128)(2,1)S(1)} %add_convert_fusion.3), channel_id=1, source_target_pairs={{0,16},{8,24},{16,0},{24,8},{1,17},{9,25},{17,1},{25,9},{2,18},{10... | collective-permute-start | bytes 1105928 | tf_op jit(solution)/shard_map/ppermute | solution.py:1188
  458.8 22.8 %copy-start.4 = (bf16[2,2,3,64,768]{4,3,2,1,0:T(8,128)(2,1)}, bf16[2,2,3,64,768]{4,3,2,1,0:T(8,128)(2,1)S(1)}, u32[]{:S(2)}) copy-start(bf16[2,2,3,64,768]{4,3,2,1,0:T(8,128)(2,1)S(1)} %pad_maximum_fusion.near_ref) | copy-start | bytes 3538948
  458.8 22.8 %collective-permute-start.23 = (bf16[2,2,3,64,768]{4,3,2,1,0:T(8,128)(2,1)S(1)}, bf16[2,2,3,64,768]{4,3,2,1,0:T(8,128)(2,1)}, u32[]{:S(2)}, u32[]{:S(2)}) collective-permute-start(bf16[2,2,3,64,768]{4,3,2,1,0:T(8,128)(2,1)S(1)} %pad_maximum_fusion.near_ref), channel_id=1, source_target_pairs={{0,8},{8,0},{16,24},{24,16},{1,9},{9,1},{17,25},{25,17},{2,10},{10... | collective-permute-start | bytes 3538952 | tf_op jit(solution)/shard_map/ppermute | solution.py:1191
  464.0 17.6 %copy-start.7 = (bf16[2,2,48,1280]{3,2,1,0:T(8,128)(2,1)}, bf16[2,2,48,1280]{3,2,1,0:T(8,128)(2,1)S(1)}, u32[]{:S(2)}) copy-start(bf16[2,2,48,1280]{3,2,1,0:T(8,128)(2,1)S(1)} %pad_maximum_fusion.4.near_ref) | copy-start | bytes 1474564
  464.0 21.7 %collective-permute-start.18 = (bf16[2,2,48,1280]{3,2,1,0:T(8,128)(2,1)S(1)}, bf16[2,2,48,1280]{3,2,1,0:T(8,128)(2,1)S(1)}, u32[]{:S(2)}, u32[]{:S(2)}) collective-permute-start(bf16[2,2,48,1280]{3,2,1,0:T(8,128)(2,1)S(1)} %pad_maximum_fusion.4.near_ref), channel_id=1, source_target_pairs={{0,8},{8,0},{16,24},{24,16},{1,9},{9,1},{17,25},{25,17},{2,10},{10... | collective-permute-start | bytes 1474568 | tf_op jit(solution)/shard_map/ppermute | solution.py:1191
  471.9 9.7 %copy-start.6 = (bf16[2,48,3840]{2,1,0:T(8,128)(2,1)}, bf16[2,48,3840]{2,1,0:T(8,128)(2,1)S(1)}, u32[]{:S(2)}) copy-start(bf16[2,48,3840]{2,1,0:T(8,128)(2,1)S(1)} %pad_maximum_fusion.2.near_ref) | copy-start | bytes 2211844
  471.9 26.7 %collective-permute-start.21 = (bf16[2,48,3840]{2,1,0:T(8,128)(2,1)S(1)}, bf16[2,48,3840]{2,1,0:T(8,128)(2,1)S(1)}, u32[]{:S(2)}, u32[]{:S(2)}) collective-permute-start(bf16[2,48,3840]{2,1,0:T(8,128)(2,1)S(1)} %pad_maximum_fusion.2.near_ref), channel_id=1, source_target_pairs={{0,8},{8,0},{16,24},{24,16},{1,9},{9,1},{17,25},{25,17},{2,10},{10... | collective-permute-start | bytes 2211848 | tf_op jit(solution)/shard_map/ppermute | solution.py:1191
  492.2 10.4 %copy-start.1 = (bf16[512,768]{1,0:T(8,128)(2,1)S(1)}, bf16[512,768]{1,0:T(8,128)(2,1)}, u32[]{:S(2)}) copy-start(bf16[512,768]{1,0:T(8,128)(2,1)} %param.35) | copy-start | bytes 2359300
  (9 other events, 8.3 us)
Sparse Core Ops, SparseCore 0:
  12.7 76.1 all-gather.2
  91.7 79.1 all-gather.4
  217.3 110.0 reduce-scatter.2
  331.7 81.4 reduce-scatter.4

commit v6 on v5

--- a/solution.py
+++ b/solution.py
@@ -384,7 +384,7 @@
     count_ref, slot_ref, q_ref, k_ref, v_ref, own_ref, far_ref, o_ref, lse_ref, qa_ref, ka_ref,
     dq_ref, dk_ref, dv_ref, kx, vx, km, dk_acc, dv_acc, dq_acc, *, per_dev,
 ):
-    i = pl.program_id(0)
+    i = pl.program_id(1)
     do = jnp.where(slot_ref[i] < per_dev, own_ref[...], far_ref[...])
 
     @pl.when(i == 0)
@@ -396,40 +396,39 @@
         kx, vx, km, dq_ref, dk_acc, dv_acc, dq_acc, 1,
     )
 
-    @pl.when(i == pl.num_programs(0) - 1)
+    @pl.when(i == pl.num_programs(1) - 1)
     def _():
         dk_ref[...] = (dk_acc[...] * LN2).astype(BF)
         dv_ref[...] = dv_acc[...].astype(BF)
 
 
-def self_backward(pair, counts, slots, q, k, v, own, far, o, lse, qa, ka, block):
-    total = q.shape[0]
+def self_backward(counts, slots, q, k, v, own, far, o, lse, qa, ka, block):
+    total, width = q.shape
     per_dev = own.shape[0] // block
-    row = pl.BlockSpec((block, 128), lambda i, n, s: (i, pair))
-    col = pl.BlockSpec((total, 128), lambda i, n, s: (0, pair))
-    whole = pl.BlockSpec((total, 128), lambda i, n, s: (0, 0))
+    row = pl.BlockSpec((block, 128), lambda h, i, n, s: (i, h))
+    col = pl.BlockSpec((total, 128), lambda h, i, n, s: (0, h))
     return pl.pallas_call(
         functools.partial(self_backward_kernel, per_dev=per_dev),
         grid_spec=pltpu.PrefetchScalarGridSpec(
             num_scalar_prefetch=2,
-            grid=(total // block,),
+            grid=(width // 128, total // block),
             in_specs=[
                 row,
                 col,
                 col,
-                pl.BlockSpec((block, 128), lambda i, n, s: (jnp.minimum(s[i], per_dev - 1), pair)),
-                pl.BlockSpec((block, 128), lambda i, n, s: (jnp.maximum(s[i] - per_dev, 0), pair)),
-                pl.BlockSpec((block, 128), lambda i, n, s: (s[i], pair)),
+                pl.BlockSpec((block, 128), lambda h, i, n, s: (jnp.minimum(s[i], per_dev - 1), h)),
+                pl.BlockSpec((block, 128), lambda h, i, n, s: (jnp.maximum(s[i] - per_dev, 0), h)),
+                pl.BlockSpec((block, 128), lambda h, i, n, s: (s[i], h)),
                 row,
-                pl.BlockSpec((block, 128), lambda i, n, s: (i, 0)),
-                whole,
+                pl.BlockSpec((block, 128), lambda h, i, n, s: (i, 0)),
+                pl.BlockSpec((total, 128), lambda h, i, n, s: (0, 0)),
             ],
-            out_specs=[pl.BlockSpec((block, 128), lambda i, n, s: (i, 0)), whole, whole],
+            out_specs=[row, col, col],
             scratch_shapes=backward_scratch(block, total),
         ),
-        out_shape=[jax.ShapeDtypeStruct((total, 128), BF)] * 3,
-        compiler_params=params(),
-        cost_estimate=cost(4 * total * total * 128, 2 * total * 128),
+        out_shape=[jax.ShapeDtypeStruct((total, width), BF)] * 3,
+        compiler_params=params(),
+        cost_estimate=cost(4 * total * total * width, 2 * total * width),
         name="self_backward",
     )(counts, slots, q, k, v, own, far, o, lse, qa, ka)
 
@@ -1037,7 +1036,7 @@
         grid_spec=pltpu.PrefetchScalarGridSpec(
             num_scalar_prefetch=1,
             grid=(total // block,),
-            in_specs=[pl.BlockSpec((block, 128), lambda i, c: (i, 0))] * len(ds)
+            in_specs=[pl.BlockSpec((block, width // 3), lambda i, c: (i, 0))] * len(ds)
             + [
                 pl.BlockSpec((block, dim), lambda i, c: (i, 0)),
                 pl.BlockSpec(w.shape, whole),
@@ -1066,7 +1065,7 @@
         grid_spec=pltpu.PrefetchScalarGridSpec(
             num_scalar_prefetch=1,
             grid=(rows // block,),
-            in_specs=[pl.BlockSpec((block, 128), lambda i, o: (o[i + first], 0))] * len(ds)
+            in_specs=[pl.BlockSpec((block, w.shape[1] // 3), lambda i, o: (o[i + first], 0))] * len(ds)
             + [pl.BlockSpec(w.shape, lambda i, o: (0, 0))],
             out_specs=pl.BlockSpec((block, dim), lambda i, o: (i, 0)),
         ),
@@ -1339,59 +1338,54 @@
     )
     gain_wide = jnp.broadcast_to(gain_self.reshape(dim, 1), (dim, 128))
 
-    def self_pair(pair, own, far):
-        return self_backward(
-            pair, counts, slots, q, k, v, own, far, o1, lse1, seg_q, seg_k, block
-        )
-
-    pairs = width // 128
     if fast:
         net = Plane(part, place, z, n_parts, n_fsdp)
-        do_own, do_far, d_far, extra, g_mid, part_ff = lax.optimization_barrier(
-            (do_own, do_far, d_far, extra, g_mid, part_ff)
+        do_own, do_far, d_far, extra, gain_wide, g_mid, part_ff = lax.optimization_barrier(
+            (do_own, do_far, d_far, extra, gain_wide, g_mid, part_ff)
         )
         part_mid = lax.psum_scatter(g_mid, AROUND, scatter_dimension=0, tiled=True)
+        sum_ff = net.over_ctx(part_ff)
     enc_got = [
         lax.ppermute(d_far[(i - 1) * enc_rows : i * enc_rows], "ctx", turned(n_ctx, i))
         for i in range(1, n_ctx)
     ]
+    ds = self_backward(counts, slots, q, k, v, do_own, do_far, o1, lse1, seg_q, seg_k, block)
     if fast:
-        by_pair = [self_pair(0, do_own, do_far)]
-        part_ff, do_far = lax.optimization_barrier((part_ff, do_far, by_pair[0][0]))[:2]
-        by_pair += [self_pair(1, do_own, do_far), self_pair(2, do_own, do_far)]
-        sum_ff = net.over_ctx(part_ff)
-        by_pair, sum_ff, enc_got = lax.optimization_barrier((by_pair, sum_ff, enc_got))
-    else:
-        by_pair = [self_pair(i, do_own, do_far) for i in range(pairs)]
-    ds = [d[i] for i in range(3) for d in by_pair]
+        ds, sum_ff, enc_got = lax.optimization_barrier((ds, sum_ff, enc_got))
+    g_qkv = qkv_grads(core, ds, n1, w1, gain_wide, extra, fast)
+    ds, g_qkv = lax.optimization_barrier((ds, g_qkv))
     dn_far = qkv_back(order_here, per_dev, ds, w1, total - rows, BF, block)
     dn_got = [
         lax.ppermute(dn_far[(i - 1) * rows : i * rows], "ctx", turned(n_ctx, i))
         for i in range(1, n_ctx)
     ]
-    ds, dn_far = lax.optimization_barrier((ds, dn_far))
-    g_qkv = qkv_grads(core, ds, n1, w1, gain_wide, extra, fast)
     dn_own = qkv_back(order_here, 0, ds, w1, rows, F32, block)
+    enc_grad = enc_finish(dk2, dv2, w2, enc_got)
     if fast:
+        send, keep = net.over_core(*g_qkv)
+        send, keep, dn_far = lax.optimization_barrier((send, keep, dn_far))
         sum_ff = net.widen_x(sum_ff)
-        g_qkv = net.over_fsdp(net.over_x(*net.over_core(*g_qkv)))
+        g_qkv, enc_grad = lax.optimization_barrier((net.over_x(send, keep), enc_grad))
+        g_qkv = net.over_fsdp(g_qkv)
         dn_got, part_mid, dn_own = lax.optimization_barrier((dn_got, part_mid, dn_own))
+        g_qkv, part_mid = lax.optimization_barrier((g_qkv, part_mid))
     decoder_grad = finish(x_own, dh1, gain_self, dn_own, dn_got)
-    enc_grad = enc_finish(dk2, dv2, w2, enc_got)
 
     if fast:
         me = jnp.stack([net.core, net.x, place]).astype(jnp.int32)
-        g_qkv = net.widen_x(net.widen_ctx(g_qkv))
+        square = (shard, dim)
+        ff = settle(
+            unpack_kernel, me, sum_ff, net.from_core(sum_ff),
+            [(shard, hidden), (shard, hidden), (hidden // n_fsdp, dim)],
+        )
+        g_qkv, decoder_grad = lax.optimization_barrier((net.widen_ctx(g_qkv), decoder_grad))
+        g_qkv, ff = lax.optimization_barrier((net.widen_x(g_qkv), ff))
+        grad_gate, grad_up, grad_down = ff
         sum_mid = net.widen_x(net.over_ctx(part_mid))
-        square = (shard, dim)
         *grads_qkv, tail = settle(
             settle_qkv_kernel, me, g_qkv, net.from_core(g_qkv), [square] * 3 + [(shard, 128)]
         )
         mids = settle(settle_mid_kernel, me, sum_mid, net.from_core(sum_mid), [square] * 5)
-        grad_gate, grad_up, grad_down = settle(
-            unpack_kernel, me, sum_ff, net.from_core(sum_ff),
-            [(shard, hidden), (shard, hidden), (hidden // n_fsdp, dim)],
-        )
     else:
 
         def total_of(g):

time: 515 us -> 491 us (0.953)
  waiting for transfers between devices: 70.8 us -> 49.6 us
    ppermute x1, waiting for transfers between devices: 10.4 us -> 1.04 us  [widen_ctx(): return jnp.stack([g, lax.ppermute(g, 'ctx', turned(2, 1))])]
    ppermute x1, waiting for transfers between devices: 12.7 us -> 6.58 us  [over_x(): got = lax.ppermute(send, 'parts', self.swap_x)]
    pallas_call x3 -> x1, Pallas kernels: 52.3 us -> 47.4 us  [self_backward(): pl.pallas_call(functools.partial(self_backward_kernel, per_dev=per_dev),...]
  transfers between devices with their start and end apart: 28 -> 28, of which waited for: 11 -> 9; matrix products, arithmetic and copies ran while one was open for 6% -> 7% of each run, Pallas kernels for 59% -> 61%
where the time goes in v6:
time: 491 us; the launch traced here: 486 us
  Pallas kernels  344 us (70%)
  waiting for transfers between devices  49.6 us (10%)
  starting transfers between devices  31 us (6%)
  local copies, waits for them, and re-layouts  26.4 us (5%)
  other arithmetic  19.4 us (4%)
  between operations  15.3 us (3%)
    pallas_call x1, Pallas kernels, cross_backward(): pl.pallas_call(cross_backward_kernel, grid=(pairs, rows // block), in_spe...  78.4 us
    pallas_call x1, Pallas kernels, self_backward(): pl.pallas_call(functools.partial(self_backward_kernel, per_dev=per_dev),...  47.4 us
    pallas_call x1, Pallas kernels, feed_forward(): pl.pallas_call(mlp_kernel, grid=(steps,), in_specs=[full, full, pl.BlockS...  46.3 us
    pallas_call x1, Pallas kernels, cross_forward(): pl.pallas_call(cross_forward_kernel, grid=(pairs, rows // block), in_spec...  35.9 us
    pallas_call x1, Pallas kernels, self_forward(): pl.pallas_call(self_forward_kernel, grid_spec=pltpu.PrefetchScalarGridSpe...  28.5 us
    ppermute x3, waiting for transfers between devices, gather_first(): lax.ppermute(mine, 'fsdp', turned(n_fsdp, d))  20.7 us
    pallas_call x1, Pallas kernels, mid_grads(): pl.pallas_call(functools.partial(mid_grads_kernel, count=len(pieces)), gr...  19.5 us
    pallas_call x2, Pallas kernels, qkv_back(): pl.pallas_call(functools.partial(qkv_back_kernel, count=len(ds)), grid_sp...  12.7 us
  transfers between devices with their start and end apart: 28, of which 9 were waited for; matrix products, arithmetic and copies ran while one was open for 7% of the time, Pallas kernels for 61%

profile of v6, /device:TPU:9, one launch (start us, length us, event | category | flops | bytes accessed | tf_op | source)
XLA Modules:
  0.0 485.7 jit_solution(5072754511441002951)
XLA Ops:
  16.2 1.5 collective-permute-start.1
  17.7 4.1 collective-permute-start.2
  21.8 1.2 collective-permute-start
  27.9 8.0 %collective-permute-done.1 = bf16[96,1280]{1,0:T(8,128)(2,1)S(1)} collective-permute-done((bf16[96,1280]{1,0:T(8,128)(2,1)S(1)}, bf16[96,1280]{1,0:T(8,128)(2,1)S(1)}, u32[]{:S(2)}, u32[]{:S(2)}) %collective-permute-start.1) | collective-permute-done | bytes 245792 | tf_op jit(solution)/shard_map/ppermute | solution.py:1133
  35.9 12.7 %collective-permute-done.2 = bf16[96,1280]{1,0:T(8,128)(2,1)S(1)} collective-permute-done((bf16[96,1280]{1,0:T(8,128)(2,1)S(1)}, bf16[96,1280]{1,0:T(8,128)(2,1)S(1)}, u32[]{:S(2)}, u32[]{:S(2)}) %collective-permute-start.2) | collective-permute-done | bytes 245792 | tf_op jit(solution)/shard_map/ppermute | solution.py:1133
  48.8 2.7 collective-permute-start.4
  53.3 1.5 sort.17
  54.8 1.8 select_convert_fusion.2.qa_ref
  56.6 3.3 select_convert_fusion
  60.8 2.9 assemble.1
  64.8 1.2 slice_reduce_fusion.3
  66.0 1.3 collective-permute-start.6
  67.3 9.2 %qkv_forward.1 = (bf16[2048,768]{1,0:T(8,128)(2,1)}, bf16[2048,384]{1,0:T(8,128)(2,1)}, bf16[2048,384]{1,0:T(8,128)(2,1)}, bf16[2048,384]{1,0:T(8,128)(2,1)}) custom-call(s32[4]{0:T(128)} %copy-done.21, bf16[1024,768]{1,0:T(8,128)(2,1)} %bitcast.66, bf16[1024,768]{1,0:T(8,128)(2,1)} %collective-permute-done.far_ref, f32[1,768]{1,0:T(1,128)} %get-tuple-element.197.g_ref, ...), custom_call_target="tpu_custom_call" | custom-call | flops 3623878656 | bytes 12582912 | tf_op jit(solution)/shard_map/qkv_forward/pallas_call | solution.py:454
  76.5 28.5 %self_forward.1 = (bf16[2048,384]{1,0:T(8,128)(2,1)}, f32[2048,384]{1,0:T(8,128)}) custom-call(s32[4]{0:T(128)} %and_select_fusion.3.count_ref, s32[4]{0:T(128)} %get-tuple-element.102.slot_ref, bf16[2048,384]{1,0:T(8,128)(2,1)} %get-tuple-element.106.q_ref, bf16[2048,384]{1,0:T(8,128)(2,1)} %get-tuple-element.107.k_ref, ...), custom_call_target="tpu_custom_call" | custom-call | flops 12884901888 | bytes 6291456 | tf_op jit(solution)/shard_map/self_forward/pallas_call | solution.py:358
  105.0 1.2 slice.45
  107.1 9.4 %enc_forward.1.k_ref.v_ref = bf16[2048,1536]{1,0:T(8,128)(2,1)} custom-call(bf16[1024,768]{1,0:T(8,128)(2,1)} %bitcast.99, bf16[1024,768]{1,0:T(8,128)(2,1)} %collective-permute-done.6.far_ref.refs_6_, bf16[768,3840]{1,0:T(8,128)(2,1)} %all-gather.3.cloned.1.call-done.w_ref.refs_2_.refs_3_.refs_5_.wc_ref.wq_ref.refs_0_.refs_1_.refs_11_.refs_12_.wk_ref.wv_ref), custom_call_target="tpu_custom_call" | custom-call | flops 4831838208 | bytes 12582912 | tf_op jit(solution)/shard_map/enc_forward/pallas_call | solution.py:488
  116.5 8.4 %collective-permute-done.5.refs_1_.refs_4_ = bf16[1024,384]{1,0:T(8,128)(2,1)S(1)} collective-permute-done((bf16[1024,384]{1,0:T(8,128)(2,1)S(1)}, bf16[1024,384]{1,0:T(8,128)(2,1)S(1)}, u32[]{:S(2)}, u32[]{:S(2)}) %collective-permute-start.5) | collective-permute-done | bytes 786464 | tf_op jit(solution)/shard_map/ppermute | solution.py:1299
  125.8 9.4 %after_self.1 = (f32[1024,768]{1,0:T(8,128)}, bf16[1024,768]{1,0:T(8,128)(2,1)}, bf16[1024,768]{1,0:T(8,128)(2,1)}, f32[8,768]{1,0:T(8,128)}) custom-call(s32[2]{0:T(128)} %and_select_fusion.5.turn_ref, bf16[1024,768]{1,0:T(8,128)(2,1)} %bitcast.67, bf16[2048,384]{1,0:T(8,128)(2,1)} %get-tuple-element.109.refs_0_.refs_3_.o_ref, ...), custom_call_target="tpu_custom_call" | custom-call | flops 2415919104 | bytes 11010048 | tf_op jit(solution)/shard_map/after_self/pallas_call | solution.py:536
  135.9 35.9 %cross_forward.1 = (bf16[1024,768]{1,0:T(8,128)(2,1)}, f32[1024,768]{1,0:T(8,128)}) custom-call(bf16[1024,768]{1,0:T(8,128)(2,1)} %get-tuple-element.112.q_ref, bf16[2048,1536]{1,0:T(8,128)(2,1)} %enc_forward.1.k_ref.v_ref, bf16[2048,1536]{1,0:T(8,128)(2,1)} %enc_forward.1.k_ref.v_ref, bf16[1024,128]{1,0:T(8,128)(2,1)} %broadcast_in_dim.93.qa_ref, ...), custom_call_target="tpu_custom_call" | custom-call | flops 25769803776 | bytes 6291456 | tf_op jit(solution)/shard_map/cross_forward/pallas_call | solution.py:243
  171.9 46.3 %feed_forward.1 = (bf16[1024,768]{1,0:T(8,128)(2,1)}, f32[1024,768]{1,0:T(8,128)}, bf16[1024,768]{1,0:T(8,128)(2,1)}, bf16[1024,768]{1,0:T(8,128)(2,1)}, f32[8,7...) custom-call(bf16[1024,768]{1,0:T(8,128)(2,1)} %get-tuple-element.114.o_ref.refs_9_, ...), custom_call_target="tpu_custom_call" | custom-call | flops 32614907904 | bytes 41943040 | tf_op jit(solution)/shard_map/feed_forward/pallas_call | solution.py:685
  219.7 78.4 %cross_backward.1 = (bf16[1024,768]{1,0:T(8,128)(2,1)}, bf16[2048,768]{1,0:T(8,128)(2,1)}, bf16[2048,768]{1,0:T(8,128)(2,1)}) custom-call(bf16[1024,768]{1,0:T(8,128)(2,1)} %get-tuple-element.112.q_ref, bf16[2048,1536]{1,0:T(8,128)(2,1)} %enc_forward.1.k_ref.v_ref, bf16[2048,1536]{1,0:T(8,128)(2,1)} %enc_forward.1.k_ref.v_ref, ...), custom_call_target="tpu_custom_call" | custom-call | flops 64424509440 | bytes 9437184 | tf_op jit(solution)/shard_map/cross_backward/pallas_call | solution.py:291
  298.2 10.1 %before_self.1 = (f32[1024,768]{1,0:T(8,128)}, bf16[1024,768]{1,0:T(8,128)(2,1)}, f32[8,768]{1,0:T(8,128)}, bf16[1024,384]{1,0:T(8,128)(2,1)}, bf16[1024,384]{1,0:T(8,128)(2,1)}) custom-call(s32[2]{0:T(128)} %and_select_fusion.5.turn_ref, bf16[1024,768]{1,0:T(8,128)(2,1)} %get-tuple-element.119.dq_ref.refs_1_, ...), custom_call_target="tpu_custom_call" | custom-call | flops 2415919104 | bytes 14155776 | tf_op jit(solution)/shard_map/before_self/pallas_call | solution.py:966
  310.1 1.2 collective-permute-start.7
  311.6 1.4 concatenate.20.refs_6_
  313.0 19.5 %mid_grads.1 = (bf16[768,3840]{1,0:T(8,128)(2,1)}, bf16[1024,768]{1,0:T(8,128)(2,1)}) custom-call(s32[2]{0:T(128)} %and_select_fusion.5.turn_ref, bf16[1024,768]{1,0:T(8,128)(2,1)} %get-tuple-element.123.refs_0_, bf16[1024,768]{1,0:T(8,128)(2,1)} %get-tuple-element.119.dq_ref.refs_1_, bf16[1024,768]{1,0:T(8,128)(2,1)} %get-tuple-element.124.refs_2_, ...), custom_call_target="tpu_custom_call" | custom-call | flops 10871635968 | bytes 31457280 | tf_op jit(solution)/shard_map/mid_grads/pallas_call | solution.py:883
  335.1 47.4 %self_backward.1 = (bf16[2048,384]{1,0:T(8,128)(2,1)}, bf16[2048,384]{1,0:T(8,128)(2,1)}, bf16[2048,384]{1,0:T(8,128)(2,1)}) custom-call(s32[4]{0:T(128)} %and_select_fusion.3.count_ref, s32[4]{0:T(128)} %get-tuple-element.102.slot_ref, bf16[2048,384]{1,0:T(8,128)(2,1)} %get-tuple-element.106.q_ref, bf16[2048,384]{1,0:T(8,128)(2,1)} %get-tuple-element.107.k_ref, ...), custom_call_target="tpu_custom_call" | custom-call | flops 6442450944 | bytes 1572864 | tf_op jit(solution)/shard_map/self_backward/pallas_call | solution.py:410
  382.5 1.2 add_convert_fusion
  383.8 11.5 %qkv_grads.1 = (bf16[8,48,1280]{2,1,0:T(8,128)(2,1)}, bf16[8,48,1280]{2,1,0:T(8,128)(2,1)}) custom-call(s32[1]{0:T(128)} %bitcast.6.core_ref, bf16[2048,384]{1,0:T(8,128)(2,1)} %get-tuple-element.152.refs_0_, bf16[2048,384]{1,0:T(8,128)(2,1)} %get-tuple-element.153.refs_1_, bf16[2048,384]{1,0:T(8,128)(2,1)} %get-tuple-element.154.refs_2_, ...), custom_call_target="tpu_custom_call" | custom-call | flops 1572864 | bytes 2048 | tf_op jit(solution)/shard_map/qkv_grads/pallas_call | solution.py:1034
  395.3 1.2 collective-permute-start.10
  396.5 6.2 %qkv_back.2 = bf16[1024,768]{1,0:T(8,128)(2,1)} custom-call(s32[4]{0:T(128)} %copy-done.21, bf16[2048,384]{1,0:T(8,128)(2,1)} %get-tuple-element.152.refs_0_, bf16[2048,384]{1,0:T(8,128)(2,1)} %get-tuple-element.153.refs_1_, bf16[2048,384]{1,0:T(8,128)(2,1)} %get-tuple-element.154.refs_2_, bf16[768,1152]{1,0:T(8,128)(2,1)} %get-tuple-element.105.w_ref.refs_4_.refs_3_), custom_call_target="tpu_custom_call" | custom-call | flops 786432 | bytes 1024 | tf_op jit(solution)/shard_map/qkv_back/pallas_call | solution.py:1063
  405.0 6.6 %enc_finish.1 = f32[1024,768]{1,0:T(8,128)} custom-call(bf16[2048,768]{1,0:T(8,128)(2,1)} %get-tuple-element.125.refs_7_.dk_ref, bf16[2048,768]{1,0:T(8,128)(2,1)} %get-tuple-element.126.refs_8_.dv_ref, bf16[768,3840]{1,0:T(8,128)(2,1)} %all-gather.3.cloned.1.call-done.w_ref.refs_2_.refs_3_.refs_5_.wc_ref.wq_ref.refs_0_.refs_1_.refs_11_.refs_12_.wk_ref.wv_ref, ...), custom_call_target="tpu_custom_call" | custom-call | flops 2415919104 | bytes 9437184 | tf_op jit(solution)/shard_map/enc_finish/pallas_call | solution.py:921
  411.6 6.6 %collective-permute-done.11 = bf16[4,48,1280]{2,1,0:T(8,128)(2,1)} collective-permute-done((bf16[4,48,1280]{2,1,0:T(8,128)(2,1)}, bf16[4,48,1280]{2,1,0:T(8,128)(2,1)}, u32[]{:S(2)}, u32[]{:S(2)}) %collective-permute-start.11) | collective-permute-done | bytes 491552 | tf_op jit(solution)/shard_map/ppermute | solution.py:1170
  419.4 1.3 collective-permute-start.12
  421.8 1.3 collective-permute-start.14
  423.0 6.5 %qkv_back.3.own_ref = f32[1024,768]{1,0:T(8,128)} custom-call(s32[4]{0:T(128)} %copy-done.21, bf16[2048,384]{1,0:T(8,128)(2,1)} %get-tuple-element.152.refs_0_, bf16[2048,384]{1,0:T(8,128)(2,1)} %get-tuple-element.153.refs_1_, bf16[2048,384]{1,0:T(8,128)(2,1)} %get-tuple-element.154.refs_2_, bf16[768,1152]{1,0:T(8,128)(2,1)} %get-tuple-element.105.w_ref.refs_4_.refs_3_), custom_call_target="tpu_custom_call" | custom-call | flops 786432 | bytes 1024 | tf_op jit(solution)/shard_map/qkv_back/pallas_call | solution.py:1063
  430.6 2.9 collective-permute-done.14
  433.6 6.4 %collective-permute-done.15.refs_0_ = bf16[1024,768]{1,0:T(8,128)(2,1)S(1)} collective-permute-done((bf16[1024,768]{1,0:T(8,128)(2,1)}, bf16[1024,768]{1,0:T(8,128)(2,1)S(1)}, u32[]{:S(2)}, u32[]{:S(2)}) %collective-permute-start.15) | collective-permute-done | bytes 1572896 | tf_op jit(solution)/shard_map/ppermute | solution.py:1359
  442.7 1.8 collective-permute-start.19
  444.5 6.4 %finish.1 = f32[1024,768]{1,0:T(8,128)} custom-call(bf16[1024,768]{1,0:T(8,128)(2,1)} %bitcast.68, f32[1024,768]{1,0:T(8,128)} %get-tuple-element.162.dh_ref, f32[1,768]{1,0:T(1,128)} %get-tuple-element.197.g_ref, f32[1024,768]{1,0:T(8,128)} %qkv_back.3.own_ref, bf16[1024,768]{1,0:T(8,128)(2,1)} %copy-done.8), custom_call_target="tpu_custom_call" | custom-call | flops 7864320 | bytes 12582912 | tf_op jit(solution)/shard_map/finish/pallas_call | solution.py:1091
  453.0 1.2 add_convert_fusion.4
  455.3 4.1 unpack.1
  459.5 3.6 collective-permute-start.20
  463.0 2.3 collective-permute-done.22
  465.5 3.0 collective-permute-start.23
  469.2 2.5 settle_qkv.1
  471.8 1.9 slice_reduce_fusion
  473.6 1.3 sqrt_bitcast_fusion
  475.8 3.1 settle_mid.1
  (161 shorter events, 39.1 us)
Async XLA Ops:
  7.2 7.4 %copy-start = (bf16[512,768]{1,0:T(8,128)(2,1)S(1)}, bf16[512,768]{1,0:T(8,128)(2,1)}, u32[]{:S(2)}) copy-start(bf16[512,768]{1,0:T(8,128)(2,1)} %param.35) | copy-start | bytes 2359300
  7.2 99.9 %all-gather.3.cloned.1.call-start = ((), (), s32[]{:S(2)}) async-start(), calls=%async_computation.2 | async-start | bytes 6266880 | tf_op jit(solution)/shard_map/all_gather | solution.py:1260
  12.5 159.3 %all-gather.5.cloned.1.call-start = ((), (), s32[]{:S(2)}) async-start(), calls=%async_computation.3 | async-start | bytes 10027008 | tf_op jit(solution)/shard_map/all_gather | solution.py:1269
  14.6 1.1 copy-start.23
  14.6 1.1 copy-start.24
  14.6 1.2 copy-start.25
  14.6 1.3 copy-start.17
  14.7 1.4 copy-start.18
  14.7 1.4 copy-start.19
  14.8 7.0 %copy-start.2 = (bf16[1,1024,768]{2,1,0:T(8,128)(2,1)S(1)}, bf16[1,1024,768]{2,1,0:T(8,128)(2,1)}, u32[]{:S(2)}) copy-start(bf16[1,1024,768]{2,1,0:T(8,128)(2,1)} %param.20) | copy-start | bytes 4718596
  14.8 8.7 %copy-start.16 = (s32[1,2048]{1,0:T(1,128)S(1)}, s32[1,2048]{1,0:T(1,128)}, u32[]{:S(2)}) copy-start(s32[1,2048]{1,0:T(1,128)} %param.22) | copy-start | bytes 24580
  14.8 11.8 %copy-start.26 = (s32[1,4]{1,0:T(1,128)S(1)}, s32[1,4]{1,0:T(1,128)}, u32[]{:S(2)}) copy-start(s32[1,4]{1,0:T(1,128)} %param.23) | copy-start | bytes 52
  15.7 316.9 %reduce-scatter.3.cloned.1.call-start = ((), (), s32[]{:S(2)}) async-start(), calls=%async_computation.4 | async-start | bytes 10027008 | tf_op jit(solution)/shard_map/reduce_scatter | solution.py:1314
  16.1 11.8 %collective-permute-start.3 = (bf16[96,1280]{1,0:T(8,128)(2,1)S(1)}, bf16[96,1280]{1,0:T(8,128)(2,1)S(1)}, u32[]{:S(2)}, u32[]{:S(2)}) collective-permute-start(bf16[96,1280]{1,0:T(8,128)(2,1)S(1)} %fusion.3), channel_id=1, source_target_pairs={{0,3},{1,0},{2,1},{3,2},{4,7},{5,4},{6,5},{7,6},{8,11},{9,8},{10,9... | collective-permute-start | bytes 737288 | tf_op jit(solution)/shard_map/ppermute | solution.py:1133
  16.2 19.7 %collective-permute-start.1 = (bf16[96,1280]{1,0:T(8,128)(2,1)S(1)}, bf16[96,1280]{1,0:T(8,128)(2,1)S(1)}, u32[]{:S(2)}, u32[]{:S(2)}) collective-permute-start(bf16[96,1280]{1,0:T(8,128)(2,1)S(1)} %fusion.3), channel_id=1, source_target_pairs={{0,1},{1,2},{2,3},{3,0},{4,5},{5,6},{6,7},{7,4},{8,9},{9,10},{10,1... | collective-permute-start | bytes 737288 | tf_op jit(solution)/shard_map/ppermute | solution.py:1133
  17.7 31.0 %collective-permute-start.2 = (bf16[96,1280]{1,0:T(8,128)(2,1)S(1)}, bf16[96,1280]{1,0:T(8,128)(2,1)S(1)}, u32[]{:S(2)}, u32[]{:S(2)}) collective-permute-start(bf16[96,1280]{1,0:T(8,128)(2,1)S(1)} %fusion.3), channel_id=1, source_target_pairs={{0,2},{1,3},{2,0},{3,1},{4,6},{5,7},{6,4},{7,5},{8,10},{9,11},{10,... | collective-permute-start | bytes 737288 | tf_op jit(solution)/shard_map/ppermute | solution.py:1133
  21.8 44.3 %collective-permute-start = (bf16[1024,768]{1,0:T(8,128)(2,1)S(1)}, bf16[1024,768]{1,0:T(8,128)(2,1)}, u32[]{:S(2)}, u32[]{:S(2)}) collective-permute-start(bf16[1024,768]{1,0:T(8,128)(2,1)S(1)} %bitcast.69), channel_id=1, source_target_pairs={{0,4},{4,0},{1,5},{5,1},{2,6},{6,2},{3,7},{7,3},{8,12},{12,8},{9,1... | collective-permute-start | bytes 4718600 | tf_op jit(solution)/shard_map/ppermute | solution.py:1239
  48.8 11.1 %copy-start.4 = (bf16[4,96,1280]{2,1,0:T(8,128)(2,1)}, bf16[4,96,1280]{2,1,0:T(8,128)(2,1)S(1)}, u32[]{:S(2)}) copy-start(bf16[4,96,1280]{2,1,0:T(8,128)(2,1)S(1)} %pad_maximum_fusion.1.near_ref) | copy-start | bytes 2949124
  48.8 11.1 %collective-permute-start.4 = (bf16[4,96,1280]{2,1,0:T(8,128)(2,1)S(1)}, bf16[4,96,1280]{2,1,0:T(8,128)(2,1)S(1)}, u32[]{:S(2)}, u32[]{:S(2)}) collective-permute-start(bf16[4,96,1280]{2,1,0:T(8,128)(2,1)S(1)} %pad_maximum_fusion.1.near_ref), channel_id=1, source_target_pairs={{0,8},{8,0},{16,24},{24,16},{1,9},{9,1},{17,25},{25,17},{2,10},{10... | collective-permute-start | bytes 2949128 | tf_op jit(solution)/shard_map/ppermute | solution.py:1135
  52.8 10.9 %copy-start.21 = (s32[4]{0:T(128)}, s32[4]{0:T(128)S(1)}, u32[]{:S(2)}) copy-start(s32[4]{0:T(128)S(1)} %dynamic_slice.66.order_ref) | copy-start | bytes 52
  66.0 41.1 %collective-permute-start.6 = (bf16[1024,768]{1,0:T(8,128)(2,1)}, bf16[1024,768]{1,0:T(8,128)(2,1)}, u32[]{:S(2)}, u32[]{:S(2)}) collective-permute-start(bf16[1024,768]{1,0:T(8,128)(2,1)} %bitcast.98), channel_id=1, source_target_pairs={{0,4},{4,0},{1,5},{5,1},{2,6},{6,2},{3,7},{7,3},{8,12},{12,8},{9,1... | collective-permute-start | bytes 4718600 | tf_op jit(solution)/shard_map/ppermute | solution.py:1239
  106.2 18.7 %collective-permute-start.5 = (bf16[1024,384]{1,0:T(8,128)(2,1)S(1)}, bf16[1024,384]{1,0:T(8,128)(2,1)S(1)}, u32[]{:S(2)}, u32[]{:S(2)}) collective-permute-start(bf16[1024,384]{1,0:T(8,128)(2,1)S(1)} %slice.45), channel_id=1, source_target_pairs={{0,4},{4,0},{1,5},{5,1},{2,6},{6,2},{3,7},{7,3},{8,12},{12,8},{9,1... | collective-permute-start | bytes 2359304 | tf_op jit(solution)/shard_map/ppermute | solution.py:1299
  218.2 221.9 %reduce-scatter.5.cloned.1.call-start = ((), (), s32[]{:S(2)}) async-start(), calls=%async_computation.5 | async-start | bytes 6266880 | tf_op jit(solution)/shard_map/reduce_scatter | solution.py:1346
  310.1 22.4 %collective-permute-start.7 = (bf16[1024,384]{1,0:T(8,128)(2,1)}, bf16[1024,384]{1,0:T(8,128)(2,1)S(1)}, u32[]{:S(2)}, u32[]{:S(2)}) collective-permute-start(bf16[1024,384]{1,0:T(8,128)(2,1)} %get-tuple-element.122), channel_id=1, source_target_pairs={{0,4},{4,0},{1,5},{5,1},{2,6},{6,2},{3,7},{7,3},{8,12},{12,8},{9,1... | collective-permute-start | bytes 2359304 | tf_op jit(solution)/shard_map/ppermute | solution.py:1320
  313.0 19.6 %copy-start.20 = (f32[768]{0:T(1024)S(1)}, f32[768]{0:T(1024)}, u32[]{:S(2)}) copy-start(f32[768]{0:T(1024)} %get-tuple-element.194) | copy-start | bytes 9220
  333.6 50.2 %collective-permute-start.9 = (bf16[1024,768]{1,0:T(8,128)(2,1)}, bf16[1024,768]{1,0:T(8,128)(2,1)S(1)}, u32[]{:S(2)}, u32[]{:S(2)}) collective-permute-start(bf16[1024,768]{1,0:T(8,128)(2,1)} %get-tuple-element.141), channel_id=1, source_target_pairs={{0,4},{4,0},{1,5},{5,1},{2,6},{6,2},{3,7},{7,3},{8,12},{12,8},{9,1... | collective-permute-start | bytes 4718600 | tf_op jit(solution)/shard_map/ppermute | solution.py:1349
  334.6 47.9 %collective-permute-start.8 = (bf16[2,3,64,768]{3,2,1,0:T(8,128)(2,1)S(1)}, bf16[2,3,64,768]{3,2,1,0:T(8,128)(2,1)}, u32[]{:S(2)}, u32[]{:S(2)}) collective-permute-start(bf16[2,3,64,768]{3,2,1,0:T(8,128)(2,1)S(1)} %bitcast.82), channel_id=1, source_target_pairs={{0,4},{4,0},{1,5},{5,1},{2,6},{6,2},{3,7},{7,3},{8,12},{12,8},{9,1... | collective-permute-start | bytes 1769480 | tf_op jit(solution)/shard_map/ppermute | solution.py:1181
  383.8 11.5 %copy-start.7 = (bf16[1024,768]{1,0:T(8,128)(2,1)}, bf16[1024,768]{1,0:T(8,128)(2,1)S(1)}, u32[]{:S(2)}) copy-start(bf16[1024,768]{1,0:T(8,128)(2,1)S(1)} %collective-permute-done.9.refs_0_) | copy-start | bytes 4718596
  395.3 7.4 %collective-permute-start.10 = (bf16[8,48,1280]{2,1,0:T(8,128)(2,1)}, bf16[8,48,1280]{2,1,0:T(8,128)(2,1)S(1)}, u32[]{:S(2)}, u32[]{:S(2)}) collective-permute-start(bf16[8,48,1280]{2,1,0:T(8,128)(2,1)} %get-tuple-element.151), channel_id=1, source_target_pairs={{0,8},{8,0},{16,24},{24,16},{1,9},{9,1},{17,25},{25,17},{2,10},{10... | collective-permute-start | bytes 2949128 | tf_op jit(solution)/shard_map/ppermute | solution.py:1164
  396.5 6.2 %copy-start.10 = (bf16[8,48,1280]{2,1,0:T(8,128)(2,1)S(1)}, bf16[8,48,1280]{2,1,0:T(8,128)(2,1)}, u32[]{:S(2)}) copy-start(bf16[8,48,1280]{2,1,0:T(8,128)(2,1)} %get-tuple-element.150) | copy-start | bytes 2949124
  403.7 14.5 %collective-permute-start.11 = (bf16[4,48,1280]{2,1,0:T(8,128)(2,1)}, bf16[4,48,1280]{2,1,0:T(8,128)(2,1)}, u32[]{:S(2)}, u32[]{:S(2)}) collective-permute-start(bf16[4,48,1280]{2,1,0:T(8,128)(2,1)} %get-tuple-element.156), channel_id=1, source_target_pairs={{0,16},{8,24},{16,0},{24,8},{1,17},{9,25},{17,1},{25,9},{2,18},{10... | collective-permute-start | bytes 1474568 | tf_op jit(solution)/shard_map/ppermute | solution.py:1170
  404.2 35.8 %collective-permute-start.15 = (bf16[1024,768]{1,0:T(8,128)(2,1)}, bf16[1024,768]{1,0:T(8,128)(2,1)S(1)}, u32[]{:S(2)}, u32[]{:S(2)}) collective-permute-start(bf16[1024,768]{1,0:T(8,128)(2,1)} %qkv_back.2), channel_id=1, source_target_pairs={{0,4},{4,0},{1,5},{5,1},{2,6},{6,2},{3,7},{7,3},{8,12},{12,8},{9,1... | collective-permute-start | bytes 4718600 | tf_op jit(solution)/shard_map/ppermute | solution.py:1359
  419.4 10.2 %collective-permute-start.12 = (bf16[48,1280]{1,0:T(8,128)(2,1)S(1)}, bf16[48,1280]{1,0:T(8,128)(2,1)S(1)}, u32[]{:S(2)}, u32[]{:S(2)}) collective-permute-start(bf16[48,1280]{1,0:T(8,128)(2,1)S(1)} %get-tuple-element.191), channel_id=1, source_target_pairs={{0,1},{1,2},{2,3},{3,0},{4,5},{5,6},{6,7},{7,4},{8,9},{9,10},{10,1... | collective-permute-start | bytes 368648 | tf_op jit(solution)/shard_map/ppermute | solution.py:1177
  420.6 10.0 %collective-permute-start.13 = (bf16[48,1280]{1,0:T(8,128)(2,1)S(1)}, bf16[48,1280]{1,0:T(8,128)(2,1)S(1)}, u32[]{:S(2)}, u32[]{:S(2)}) collective-permute-start(bf16[48,1280]{1,0:T(8,128)(2,1)S(1)} %get-tuple-element.193), channel_id=1, source_target_pairs={{0,2},{1,3},{2,0},{3,1},{4,6},{5,7},{6,4},{7,5},{8,10},{9,11},{10,... | collective-permute-start | bytes 368648 | tf_op jit(solution)/shard_map/ppermute | solution.py:1177
  421.8 11.8 %collective-permute-start.14 = (bf16[48,1280]{1,0:T(8,128)(2,1)S(1)}, bf16[48,1280]{1,0:T(8,128)(2,1)S(1)}, u32[]{:S(2)}, u32[]{:S(2)}) collective-permute-start(bf16[48,1280]{1,0:T(8,128)(2,1)S(1)} %get-tuple-element.192), channel_id=1, source_target_pairs={{0,3},{1,0},{2,1},{3,2},{4,7},{5,4},{6,5},{7,6},{8,11},{9,8},{10,9... | collective-permute-start | bytes 368648 | tf_op jit(solution)/shard_map/ppermute | solution.py:1177
  423.0 18.5 %collective-permute-start.18 = (bf16[2,3,64,768]{3,2,1,0:T(8,128)(2,1)S(1)}, bf16[2,3,64,768]{3,2,1,0:T(8,128)(2,1)}, u32[]{:S(2)}, u32[]{:S(2)}) collective-permute-start(bf16[2,3,64,768]{3,2,1,0:T(8,128)(2,1)S(1)} %add_convert_fusion), channel_id=1, source_target_pairs={{0,16},{8,24},{16,0},{24,8},{1,17},{9,25},{17,1},{25,9},{2,18},{10... | collective-permute-start | bytes 1769480 | tf_op jit(solution)/shard_map/ppermute | solution.py:1187
  440.1 4.5 copy-start.8
  440.1 12.9 %collective-permute-start.21 = (bf16[48,3840]{1,0:T(8,128)(2,1)}, bf16[48,3840]{1,0:T(8,128)(2,1)}, u32[]{:S(2)}, u32[]{:S(2)}) collective-permute-start(bf16[48,3840]{1,0:T(8,128)(2,1)} %reduce-scatter.5.cloned.1.call-done), channel_id=1, source_target_pairs={{0,4},{4,0},{1,5},{5,1},{2,6},{6,2},{3,7},{7,3},{8,12},{12,8},{9,1... | collective-permute-start | bytes 1105928 | tf_op jit(solution)/shard_map/ppermute | solution.py:1181
  440.8 11.1 %collective-permute-start.16 = (bf16[48,1280]{1,0:T(8,128)(2,1)S(1)}, bf16[48,1280]{1,0:T(8,128)(2,1)S(1)}, u32[]{:S(2)}, u32[]{:S(2)}) collective-permute-start(bf16[48,1280]{1,0:T(8,128)(2,1)S(1)} %fusion.8), channel_id=1, source_target_pairs={{0,4},{4,0},{1,5},{5,1},{2,6},{6,2},{3,7},{7,3},{8,12},{12,8},{9,1... | collective-permute-start | bytes 368648 | tf_op jit(solution)/shard_map/ppermute | solution.py:1184
  442.7 8.2 %copy-start.3 = (bf16[2,2,3,64,768]{4,3,2,1,0:T(8,128)(2,1)}, bf16[2,2,3,64,768]{4,3,2,1,0:T(8,128)(2,1)S(1)}, u32[]{:S(2)}) copy-start(bf16[2,2,3,64,768]{4,3,2,1,0:T(8,128)(2,1)S(1)} %pad_maximum_fusion.near_ref) | copy-start | bytes 3538948
  442.7 12.6 %collective-permute-start.19 = (bf16[2,2,3,64,768]{4,3,2,1,0:T(8,128)(2,1)S(1)}, bf16[2,2,3,64,768]{4,3,2,1,0:T(8,128)(2,1)}, u32[]{:S(2)}, u32[]{:S(2)}) collective-permute-start(bf16[2,2,3,64,768]{4,3,2,1,0:T(8,128)(2,1)S(1)} %pad_maximum_fusion.near_ref), channel_id=1, source_target_pairs={{0,8},{8,0},{16,24},{24,16},{1,9},{9,1},{17,25},{25,17},{2,10},{10... | collective-permute-start | bytes 3538952 | tf_op jit(solution)/shard_map/ppermute | solution.py:1190
  452.0 7.4 %collective-permute-start.17 = (bf16[2,48,1280]{2,1,0:T(8,128)(2,1)S(1)}, bf16[2,48,1280]{2,1,0:T(8,128)(2,1)S(1)}, u32[]{:S(2)}, u32[]{:S(2)}) collective-permute-start(bf16[2,48,1280]{2,1,0:T(8,128)(2,1)S(1)} %pad_maximum_fusion.5), channel_id=1, source_target_pairs={{0,16},{8,24},{16,0},{24,8},{1,17},{9,25},{17,1},{25,9},{2,18},{10... | collective-permute-start | bytes 737288 | tf_op jit(solution)/shard_map/ppermute | solution.py:1187
  454.2 11.2 %collective-permute-start.22 = (bf16[48,3840]{1,0:T(8,128)(2,1)S(1)}, bf16[48,3840]{1,0:T(8,128)(2,1)S(1)}, u32[]{:S(2)}, u32[]{:S(2)}) collective-permute-start(bf16[48,3840]{1,0:T(8,128)(2,1)S(1)} %add_convert_fusion.4), channel_id=1, source_target_pairs={{0,16},{8,24},{16,0},{24,8},{1,17},{9,25},{17,1},{25,9},{2,18},{10... | collective-permute-start | bytes 1105928 | tf_op jit(solution)/shard_map/ppermute | solution.py:1187
  459.4 9.0 %copy-start.6 = (bf16[2,2,48,1280]{3,2,1,0:T(8,128)(2,1)}, bf16[2,2,48,1280]{3,2,1,0:T(8,128)(2,1)S(1)}, u32[]{:S(2)}) copy-start(bf16[2,2,48,1280]{3,2,1,0:T(8,128)(2,1)S(1)} %pad_maximum_fusion.4.near_ref) | copy-start | bytes 1474564
  459.5 9.0 %collective-permute-start.20 = (bf16[2,2,48,1280]{3,2,1,0:T(8,128)(2,1)S(1)}, bf16[2,2,48,1280]{3,2,1,0:T(8,128)(2,1)S(1)}, u32[]{:S(2)}, u32[]{:S(2)}) collective-permute-start(bf16[2,2,48,1280]{3,2,1,0:T(8,128)(2,1)S(1)} %pad_maximum_fusion.4.near_ref), channel_id=1, source_target_pairs={{0,8},{8,0},{16,24},{24,16},{1,9},{9,1},{17,25},{25,17},{2,10},{10... | collective-permute-start | bytes 1474568 | tf_op jit(solution)/shard_map/ppermute | solution.py:1190
  465.4 13.5 %copy-start.1 = (bf16[512,768]{1,0:T(8,128)(2,1)S(1)}, bf16[512,768]{1,0:T(8,128)(2,1)}, u32[]{:S(2)}) copy-start(bf16[512,768]{1,0:T(8,128)(2,1)} %param.35) | copy-start | bytes 2359300
  465.5 9.5 %copy-start.5 = (bf16[2,48,3840]{2,1,0:T(8,128)(2,1)}, bf16[2,48,3840]{2,1,0:T(8,128)(2,1)S(1)}, u32[]{:S(2)}) copy-start(bf16[2,48,3840]{2,1,0:T(8,128)(2,1)S(1)} %pad_maximum_fusion.2.near_ref) | copy-start | bytes 2211844
  465.5 9.5 %collective-permute-start.23 = (bf16[2,48,3840]{2,1,0:T(8,128)(2,1)S(1)}, bf16[2,48,3840]{2,1,0:T(8,128)(2,1)S(1)}, u32[]{:S(2)}, u32[]{:S(2)}) collective-permute-start(bf16[2,48,3840]{2,1,0:T(8,128)(2,1)S(1)} %pad_maximum_fusion.2.near_ref), channel_id=1, source_target_pairs={{0,8},{8,0},{16,24},{24,16},{1,9},{9,1},{17,25},{25,17},{2,10},{10... | collective-permute-start | bytes 2211848 | tf_op jit(solution)/shard_map/ppermute | solution.py:1190
  (7 other events, 6.3 us)
Sparse Core Ops, SparseCore 0:
  12.7 76.1 all-gather.2
  91.7 79.1 all-gather.4
  218.3 112.4 reduce-scatter.2
  335.2 81.0 reduce-scatter.4

commit v7 on v6

--- a/solution.py
+++ b/solution.py
@@ -222,16 +222,34 @@
 
 
 def cross_forward_kernel(
-    q_ref, k_ref, v_ref, qa_ref, ka_ref, o_ref, lse_ref, kx, vx, s_scr, m_scr, a_scr
+    q_ref, k_ref, v_ref, qa_ref, ka_ref, o_ref, inv_ref, p_ref, kx, vx, s_scr, m_scr, a_scr
 ):
     @pl.when(pl.program_id(1) == 0)
     def _():
         forward_prep(k_ref, v_ref, ka_ref, kx, vx)
 
-    full = k_ref.shape[0] // CHUNK
-    forward_block(
-        0, full, None, CHUNK, False, q_ref, qa_ref, kx, vx, o_ref, lse_ref, s_scr, m_scr, a_scr, full
-    )
+    q = q_ref[...]
+    keys = k_ref.shape[0]
+    left = lanes(q.shape) < HEAD
+    sides = pair_of(q, qa_ref[...])
+    chunks = [pl.ds(c, CHUNK) for c in range(0, keys, CHUNK)]
+    m_scr[...] = jnp.full_like(m_scr, -BIG)
+    a_scr[...] = jnp.zeros_like(a_scr)
+    for at in chunks:
+        for h in range(2):
+            s = nt(sides[h], kx[h, at, :])
+            s_scr[h, :, at] = s
+            m_scr[h] = jnp.maximum(m_scr[h], lane_max(s))
+    tops = [jnp.max(m_scr[h], axis=1, keepdims=True) for h in range(2)]
+    for at in chunks:
+        for h in range(2):
+            p = jnp.exp2(s_scr[h, :, at] - tops[h]).astype(BF)
+            p_ref[:, pl.ds(h * keys + at.start, CHUNK)] = p
+            a_scr[h] += nn(p, vx[h, at, :])
+    wide = jnp.where(left, a_scr[0], a_scr[1])
+    inv = 1.0 / jnp.where(left, a_scr[1], a_scr[0])
+    o_ref[...] = (wide * pltpu.roll(inv, HEAD, 1)).astype(o_ref.dtype)
+    inv_ref[...] = inv
 
 
 def cross_forward(q, kv, qa, ka):
@@ -250,10 +268,11 @@
             pl.BlockSpec((block, 128), lambda h, i: (i, 0)),
             pl.BlockSpec((keys, 128), lambda h, i: (0, 0)),
         ],
-        out_specs=[row, row],
+        out_specs=[row, row, pl.BlockSpec((block, 2 * keys), lambda h, i: (i, h))],
         out_shape=[
             jax.ShapeDtypeStruct((rows, width), BF),
             jax.ShapeDtypeStruct((rows, width), F32),
+            jax.ShapeDtypeStruct((rows, 2 * pairs * keys), BF),
         ],
         scratch_shapes=forward_scratch(block, keys),
         compiler_params=params(),
@@ -263,17 +282,47 @@
 
 
 def cross_backward_kernel(
-    q_ref, k_ref, v_ref, do_ref, o_ref, lse_ref, qa_ref, ka_ref,
-    dq_ref, dk_ref, dv_ref, kx, vx, km, dk_acc, dv_acc, dq_acc,
+    q_ref, k_ref, v_ref, do_ref, o_ref, inv_ref, p_ref,
+    dq_ref, dk_ref, dv_ref, vx, km, dk_acc, dv_acc,
 ):
+    keys = k_ref.shape[0]
+
     @pl.when(pl.program_id(1) == 0)
     def _():
-        backward_prep(k_ref, v_ref, ka_ref, kx, vx, km, dk_acc, dv_acc)
-
-    backward_block(
-        0, k_ref.shape[0] // CHUNK, None, CHUNK, False, q_ref[...], do_ref[...], o_ref, lse_ref,
-        qa_ref, kx, vx, km, dq_ref, dk_acc, dv_acc, dq_acc, k_ref.shape[0] // CHUNK,
-    )
+        k, v = k_ref[...], v_ref[...]
+        spot = lanes(v.shape) % HEAD
+        neg = jnp.where((spot >= PART0) & (spot < PART0 + 3), -1.0, 0.0).astype(BF)
+        vx[0], vx[1] = pair_of(v, neg)
+        km[0], km[1] = pair_of(k, jnp.zeros_like(k))
+        dk_acc[...] = jnp.zeros_like(dk_acc)
+        dv_acc[...] = jnp.zeros_like(dv_acc)
+
+    q, do = q_ref[...], do_ref[...].astype(F32)
+    left = lanes(q.shape) < HEAD
+    zero = jnp.zeros_like(q)
+    inv = inv_ref[...]
+    product = do * o_ref[...].astype(F32)
+    first = jnp.sum(jnp.where(left, product, 0.0), axis=1, keepdims=True)
+    second = jnp.sum(jnp.where(left, 0.0, product), axis=1, keepdims=True)
+    delta = jnp.where(left, second, first) * inv
+    do = (do * pltpu.roll(inv, HEAD, 1)).astype(BF)
+    dx = pair_of(do, with_parts(zero, delta))
+    qm = pair_of(q, zero)
+    dm = pair_of(do, zero)
+    dq = None
+    for c in range(0, keys, CHUNK):
+        at = pl.ds(c, CHUNK)
+        dk = dv = None
+        for h in range(2):
+            p = p_ref[:, pl.ds(h * keys + c, CHUNK)]
+            ds = (p.astype(F32) * nt(dx[h], vx[h, at, :])).astype(BF)
+            tv, tk, tq = tn(p, dm[h]), tn(ds, qm[h]), nn(ds, km[h, at, :])
+            dv = tv if dv is None else dv + tv
+            dk = tk if dk is None else dk + tk
+            dq = tq if dq is None else dq + tq
+        dv_acc[at, :] += dv
+        dk_acc[at, :] += dk
+    dq_ref[...] = (dq * SCALE).astype(BF)
 
     @pl.when(pl.program_id(1) == pl.num_programs(1) - 1)
     def _():
@@ -281,7 +330,7 @@
         dv_ref[...] = dv_acc[...].astype(BF)
 
 
-def cross_backward(q, kv, do, o, lse, qa, ka):
+def cross_backward(q, kv, do, o, inv, p):
     rows, width = q.shape
     keys = kv.shape[0]
     block = min(512, rows)
@@ -298,8 +347,7 @@
             row,
             row,
             row,
-            pl.BlockSpec((block, 128), lambda h, i: (i, 0)),
-            pl.BlockSpec((keys, 128), lambda h, i: (0, 0)),
+            pl.BlockSpec((block, 2 * keys), lambda h, i: (i, h)),
         ],
         out_specs=[row, col, col],
         out_shape=[
@@ -307,11 +355,11 @@
             jax.ShapeDtypeStruct((keys, width), BF),
             jax.ShapeDtypeStruct((keys, width), BF),
         ],
-        scratch_shapes=backward_scratch(block, keys),
+        scratch_shapes=[pltpu.VMEM((2, keys, 128), BF)] * 2 + [pltpu.VMEM((keys, 128), F32)] * 2,
         compiler_params=params(),
-        cost_estimate=cost(40 * rows * keys * width, 12 * rows * width, rows * keys * 12),
+        cost_estimate=cost(32 * rows * keys * width, 12 * rows * width),
         name="cross_backward",
-    )(q, kv, kv, do, o, lse, qa, ka)
+    )(q, kv, kv, do, o, inv, p)
 
 
 def grain_of(block):
@@ -764,7 +812,10 @@
             out[pl.ds(row, size), :] = ref[:, m * dim : (m + 1) * dim].astype(F32)
 
 
-def settle_qkv_kernel(me_ref, near_ref, far_ref, q_ref, k_ref, v_ref, tail_ref):
+def settle_qkv_kernel(
+    me_ref, near_ref, far_ref, q_ref, k_ref, v_ref, self_ref, mlp_ref, cross_ref, rms_ref, tail_ref,
+    *, entries,
+):
     place = me_ref[2]
     size = near_ref.shape[2]
     width = q_ref.shape[1] // 2
@@ -778,15 +829,20 @@
             part = block[:, 3 * width :]
             tail = part if tail is None else tail + part
         tail_ref[at, :] = tail
-
-
-def settle(kernel, me, near, far, shapes):
+    rms_ref[...] = jnp.sqrt(pltpu.roll(tail_ref[0:8, :], 128 - 3, 1)[0:1, :4] / entries)
+    turned_tail = tail_ref[...].T
+    for i, ref in enumerate((self_ref, mlp_ref, cross_ref)):
+        ref[...] = turned_tail[i : i + 1, :]
+
+
+def settle(kernel, me, near, far, shapes, scratch=(), **given):
     vmem = pl.BlockSpec(memory_space=pltpu.VMEM)
     return pl.pallas_call(
-        kernel,
+        functools.partial(kernel, **given),
         in_specs=[pl.BlockSpec(memory_space=pltpu.SMEM), vmem, vmem],
         out_specs=[vmem] * len(shapes),
         out_shape=[jax.ShapeDtypeStruct(shape, F32) for shape in shapes],
+        scratch_shapes=scratch,
         compiler_params=params(),
         name=kernel.__name__[:-7],
     )(me, near, far)
@@ -997,8 +1053,8 @@
 
 def qkv_grads_kernel(core_ref, *refs, count, deal):
     d_refs = refs[:count]
-    n_ref, w_ref, gain_ref, extra_ref = refs[count : count + 4]
-    outs = refs[count + 4 :]
+    n_ref, w_ref, gain_ref, one_ref, two_ref, three_ref = refs[count : count + 6]
+    outs = refs[count + 6 :]
     acc, full = outs[-2:]
     i = pl.program_id(0)
     term = tn(n_ref[...], joined(d_refs))
@@ -1015,8 +1071,15 @@
     def _():
         width = acc.shape[1]
         grad = acc[...]
-        gains = jnp.sum(grad * w_ref[...].astype(F32), axis=1, keepdims=True) / gain_ref[:, :1]
-        extra = extra_ref[...]
+        dim = grad.shape[0]
+        totals = [
+            jnp.broadcast_to(jnp.sum(row, axis=1, keepdims=True), (1, dim))
+            for row in (one_ref[0:1, :], one_ref[1:2, :], two_ref[0:1, :], two_ref[1:2, :])
+        ]
+        lines = [gain_ref[...], two_ref[2:3, :], three_ref[0:1, :], *totals]
+        lines.append(jnp.zeros((128 - len(lines), dim), F32))
+        extra = jnp.concatenate(lines, axis=0).T
+        gains = jnp.sum(grad * w_ref[...].astype(F32), axis=1, keepdims=True) / extra[:, :1]
         full[:, :width] = grad.astype(BF)
         full[:, width:] = jnp.where(lanes(extra.shape) == 0, gains, extra).astype(BF)
         if deal:
@@ -1025,7 +1088,7 @@
             outs[0][...] = full[...]
 
 
-def qkv_grads(core, ds, n, w, gain, extra, deal):
+def qkv_grads(core, ds, n, w, gain, stats, deal):
     total, dim = n.shape
     block = min(512, total)
     width = w.shape[1]
@@ -1040,9 +1103,9 @@
             + [
                 pl.BlockSpec((block, dim), lambda i, c: (i, 0)),
                 pl.BlockSpec(w.shape, whole),
-                pl.BlockSpec((dim, 128), whole),
-                pl.BlockSpec((dim, 128), whole),
-            ],
+                pl.BlockSpec((1, dim), whole),
+            ]
+            + [pl.BlockSpec((8, dim), whole)] * 3,
             out_specs=specs,
             scratch_shapes=[pltpu.VMEM((dim, width), F32), pltpu.VMEM((dim, width + 128), BF)],
         ),
@@ -1050,7 +1113,7 @@
         compiler_params=params(),
         cost_estimate=cost(total * dim, total),
         name="qkv_grads",
-    )(core, *ds, n, w, gain, extra)
+    )(core, *ds, n, w, gain, *stats)
 
 
 def qkv_back_kernel(order_ref, *refs, count):
@@ -1109,7 +1172,7 @@
     return lax.dynamic_slice_in_dim(array, index * size, size, 0)
 
 
-def assemble_kernel(place_ref, near_ref, far_ref, w_ref, g_ref):
+def assemble_kernel(place_ref, near_ref, far_ref, w_ref, gain_ref, g_ref):
     z, core = place_ref[0], place_ref[1]
     count, size = near_ref.shape[0], near_ref.shape[1]
     width = w_ref.shape[1]
@@ -1118,7 +1181,8 @@
         for ref, half in ((near_ref, core), (far_ref, 1 - core)):
             at = pl.ds(pl.multiple_of(base + half * size, 16), size)
             w_ref[at, :] = ref[d, :, :width]
-            g_ref[at, :] = ref[d, :, width:]
+            g_ref[at, :] = ref[d, :, width:].astype(F32)
+    gain_ref[...] = g_ref[...].T[:8, :]
 
 
 def gather_first(own, z, part, n_fsdp, n_parts):
@@ -1126,7 +1190,7 @@
     width = own.shape[1] - 128
     if n_parts % 2 or size % 16:
         full = lax.all_gather(own, "fsdp", axis=0, tiled=True)
-        return full[:, :width], full[:, width:]
+        return full[:, :width], full[:, width : width + 8].astype(F32).T
     core = part % 2
     mine = lax.dynamic_slice_in_dim(own, core * size, size, 0)
     near = jnp.stack(
@@ -1141,8 +1205,9 @@
         out_specs=[vmem, vmem],
         out_shape=[
             jax.ShapeDtypeStruct((total, width), BF),
-            jax.ShapeDtypeStruct((total, 128), BF),
+            jax.ShapeDtypeStruct((8, total), F32),
         ],
+        scratch_shapes=[pltpu.VMEM((total, 128), F32)],
         compiler_params=params(),
         name="assemble",
     )(jnp.stack([z, core]).astype(jnp.int32), near, far)
@@ -1253,7 +1318,6 @@
         [own_heads(self_query), own_heads(self_key), own_heads(self_value), gain_cols], axis=1
     )
     w1, gains = gather_first(first, z, part, n_fsdp, n_parts)
-    gains = gains[:, :8].astype(F32).T
     gain_self, gain_cross, gain_mlp = (gains[i : i + 1] for i in range(3))
     mats = (self_output, cross_query, cross_key, cross_value, cross_output)
     if fast:
@@ -1307,7 +1371,7 @@
     where_key = (ring[:, None] * enc_rows + jnp.arange(enc_rows, dtype=jnp.int32)).reshape(-1, 1)
     len_q = jnp.where(spot == 0, jnp.ones((rows, 1), F32), 0.0).astype(BF)
     len_k = jnp.where((spot == 0) & (where_key >= prompt_len[0]), -BIG, minus).astype(BF)
-    o2, lse2 = cross_forward(q2, kv2, len_q, len_k)
+    o2, inv2, p2 = cross_forward(q2, kv2, len_q, len_k)
 
     layer_out, dh2, dc, do2, stat2, g_ff = feed_forward(o2, h1, w2, gain_mlp, cotangent[0], w3)
     if fast:
@@ -1315,7 +1379,7 @@
             g_ff.reshape(-1, dim), AROUND, scatter_dimension=0, tiled=True
         ).reshape(2, 3, 64, dim)
 
-    dq2, dk2, dv2 = cross_backward(q2, kv2, do2, o2, lse2, len_q, len_k)
+    dq2, dk2, dv2 = cross_backward(q2, kv2, do2, o2, inv2, p2)
     dh1, da, stat3, *do1 = before_self(turn, dq2, w2, h1, dh2, gain_cross, wo, width)
     do_far = [lax.ppermute(do1[i], "ctx", turned(n_ctx, -i)) for i in range(1, n_ctx)]
     do_far = do_far[0] if n_ctx == 2 else jnp.concatenate(do_far, axis=0)
@@ -1325,23 +1389,12 @@
         turn, pieces, da, n2, dq2, enc_own, enc_far, dk2, dv2, o2, dc, w2
     )
 
-    sums = jnp.sum(jnp.concatenate([stat1[:2], stat2[:2]], axis=0), axis=1)
-    extra = jnp.concatenate(
-        [
-            jnp.zeros((dim, 1), F32),
-            stat2[2][:, None],
-            stat3[0][:, None],
-            jnp.broadcast_to(sums[None], (dim, 4)),
-            jnp.zeros((dim, 121), F32),
-        ],
-        axis=1,
-    )
-    gain_wide = jnp.broadcast_to(gain_self.reshape(dim, 1), (dim, 128))
+    entries = float(n_parts * n_ctx * n_fsdp * rows * dim)
 
     if fast:
         net = Plane(part, place, z, n_parts, n_fsdp)
-        do_own, do_far, d_far, extra, gain_wide, g_mid, part_ff = lax.optimization_barrier(
-            (do_own, do_far, d_far, extra, gain_wide, g_mid, part_ff)
+        do_own, do_far, d_far, g_mid, part_ff = lax.optimization_barrier(
+            (do_own, do_far, d_far, g_mid, part_ff)
         )
         part_mid = lax.psum_scatter(g_mid, AROUND, scatter_dimension=0, tiled=True)
         sum_ff = net.over_ctx(part_ff)
@@ -1352,7 +1405,7 @@
     ds = self_backward(counts, slots, q, k, v, do_own, do_far, o1, lse1, seg_q, seg_k, block)
     if fast:
         ds, sum_ff, enc_got = lax.optimization_barrier((ds, sum_ff, enc_got))
-    g_qkv = qkv_grads(core, ds, n1, w1, gain_wide, extra, fast)
+    g_qkv = qkv_grads(core, ds, n1, w1, gain_self, (stat1, stat2, stat3), fast)
     ds, g_qkv = lax.optimization_barrier((ds, g_qkv))
     dn_far = qkv_back(order_here, per_dev, ds, w1, total - rows, BF, block)
     dn_got = [
@@ -1382,8 +1435,10 @@
         g_qkv, ff = lax.optimization_barrier((net.widen_x(g_qkv), ff))
         grad_gate, grad_up, grad_down = ff
         sum_mid = net.widen_x(net.over_ctx(part_mid))
-        *grads_qkv, tail = settle(
-            settle_qkv_kernel, me, g_qkv, net.from_core(g_qkv), [square] * 3 + [(shard, 128)]
+        *grads_qkv, grad_gself, grad_gmlp, grad_gcross, rms_values = settle(
+            settle_qkv_kernel, me, g_qkv, net.from_core(g_qkv),
+            [square] * 3 + [(1, shard)] * 3 + [(1, 4)],
+            [pltpu.VMEM((shard, 128), F32)], entries=entries,
         )
         mids = settle(settle_mid_kernel, me, sum_mid, net.from_core(sum_mid), [square] * 5)
     else:
@@ -1410,9 +1465,8 @@
         ]
         tail = jnp.sum(every[:, :, 3 * width :], axis=0)
         mids = [sum_mid[:, i * dim : (i + 1) * dim] for i in range(5)]
-    grad_gself, grad_gmlp, grad_gcross = tail[:, 0], tail[:, 1], tail[:, 2]
-    entries = float(n_parts * n_ctx * n_fsdp * rows * dim)
-    rms_values = jnp.sqrt(tail[0, 3:7] / entries)
+        grad_gself, grad_gmlp, grad_gcross = tail[:, 0], tail[:, 1], tail[:, 2]
+        rms_values = jnp.sqrt(tail[0, 3:7] / entries)
     return (
         layer_out[None],
         decoder_grad[None],
@@ -1422,10 +1476,10 @@
         grad_gate,
         grad_up,
         grad_down,
-        grad_gself,
-        grad_gcross,
-        grad_gmlp,
-        rms_values,
+        grad_gself.reshape(shard),
+        grad_gcross.reshape(shard),
+        grad_gmlp.reshape(shard),
+        rms_values.reshape(4),
     )
 
 

time: 491 us -> 481 us (0.980)
  waiting for transfers between devices: 49.6 us -> 67 us
  local copies, waits for them, and re-layouts: 26.4 us -> 15.4 us
  Pallas kernels: 344 us -> 335 us
  other arithmetic: 19.4 us -> 13 us
    ppermute x2, waiting for transfers between devices: 0.01 us -> 7.8 us  [over_ctx(): lax.ppermute(g, 'ctx', turned(2, 1)).astype(F32)]
    reduce_scatter x1, waiting for transfers between devices: 0.02 us -> 6.9 us  [local(): lax.psum_scatter(g_ff.reshape(-1, dim), AROUND, scatter_dimension=0, tile...]
    pallas_call x1, Pallas kernels: 78.4 us -> 73.5 us  [cross_backward(): pl.pallas_call(cross_backward_kernel, grid=(pairs, rows // block), in_spe...]
  transfers between devices with their start and end apart: 28 -> 28, of which waited for: 9 -> 12; matrix products, arithmetic and copies ran while one was open for 7% -> 4% of each run, Pallas kernels for 61% -> 60%
where the time goes in v7:
time: 481 us; the launch traced here: 476 us
  Pallas kernels  335 us (70%)
  waiting for transfers between devices  67 us (14%)
  starting transfers between devices  30.7 us (6%)
  local copies, waits for them, and re-layouts  15.4 us (3%)
  between operations  15.3 us (3%)
  other arithmetic  13 us (3%)
    pallas_call x1, Pallas kernels, cross_backward(): pl.pallas_call(cross_backward_kernel, grid=(pairs, rows // block), in_spe...  73.5 us
    pallas_call x1, Pallas kernels, feed_forward(): pl.pallas_call(mlp_kernel, grid=(steps,), in_specs=[full, full, pl.BlockS...  46.4 us
    pallas_call x1, Pallas kernels, self_backward(): pl.pallas_call(functools.partial(self_backward_kernel, per_dev=per_dev),...  43.8 us
    pallas_call x1, Pallas kernels, cross_forward(): pl.pallas_call(cross_forward_kernel, grid=(pairs, rows // block), in_spec...  37.3 us
    pallas_call x1, Pallas kernels, self_forward(): pl.pallas_call(self_forward_kernel, grid_spec=pltpu.PrefetchScalarGridSpe...  26.4 us
    ppermute x3, waiting for transfers between devices, gather_first(): lax.ppermute(mine, 'fsdp', turned(n_fsdp, d))  22.7 us
    pallas_call x1, Pallas kernels, mid_grads(): pl.pallas_call(functools.partial(mid_grads_kernel, count=len(pieces)), gr...  19.4 us
    pallas_call x2, Pallas kernels, qkv_back(): pl.pallas_call(functools.partial(qkv_back_kernel, count=len(ds)), grid_sp...  12.7 us
  transfers between devices with their start and end apart: 28, of which 12 were waited for; matrix products, arithmetic and copies ran while one was open for 4% of the time, Pallas kernels for 60%

profile of v7, /device:TPU:9, one launch (start us, length us, event | category | flops | bytes accessed | tf_op | source)
XLA Modules:
  0.0 476.2 jit_solution(12208136036729210891)
XLA Ops:
  16.2 1.5 collective-permute-start.1
  17.7 4.1 collective-permute-start.2
  21.8 1.2 collective-permute-start
  25.9 10.0 %collective-permute-done.1 = bf16[96,1280]{1,0:T(8,128)(2,1)S(1)} collective-permute-done((bf16[96,1280]{1,0:T(8,128)(2,1)S(1)}, bf16[96,1280]{1,0:T(8,128)(2,1)S(1)}, u32[]{:S(2)}, u32[]{:S(2)}) %collective-permute-start.1) | collective-permute-done | bytes 245792 | tf_op jit(solution)/shard_map/ppermute | solution.py:1197
  35.9 12.7 %collective-permute-done.2 = bf16[96,1280]{1,0:T(8,128)(2,1)} collective-permute-done((bf16[96,1280]{1,0:T(8,128)(2,1)S(1)}, bf16[96,1280]{1,0:T(8,128)(2,1)}, u32[]{:S(2)}, u32[]{:S(2)}) %collective-permute-start.2) | collective-permute-done | bytes 245792 | tf_op jit(solution)/shard_map/ppermute | solution.py:1197
  49.7 2.7 collective-permute-start.4
  55.0 2.6 select_convert_fusion
  57.6 3.6 assemble.1
  61.1 1.4 fusion.12
  62.6 1.3 collective-permute-start.6
  63.9 9.2 %qkv_forward.1 = (bf16[2048,768]{1,0:T(8,128)(2,1)}, bf16[2048,384]{1,0:T(8,128)(2,1)}, bf16[2048,384]{1,0:T(8,128)(2,1)}, bf16[2048,384]{1,0:T(8,128)(2,1)}) custom-call(s32[4]{0:T(128)} %copy-done.19, bf16[1024,768]{1,0:T(8,128)(2,1)} %bitcast.62, bf16[1024,768]{1,0:T(8,128)(2,1)} %collective-permute-done.far_ref, ...), custom_call_target="tpu_custom_call" | custom-call | flops 3623878656 | bytes 12582912 | tf_op jit(solution)/shard_map/qkv_forward/pallas_call | solution.py:502
  73.0 26.4 %self_forward.1 = (bf16[2048,384]{1,0:T(8,128)(2,1)}, f32[2048,384]{1,0:T(8,128)}) custom-call(s32[4]{0:T(128)} %and_select_fusion.3.count_ref, s32[4]{0:T(128)} %get-tuple-element.104.slot_ref, bf16[2048,384]{1,0:T(8,128)(2,1)} %get-tuple-element.108.q_ref, bf16[2048,384]{1,0:T(8,128)(2,1)} %get-tuple-element.109.k_ref, ...), custom_call_target="tpu_custom_call" | custom-call | flops 12884901888 | bytes 6291456 | tf_op jit(solution)/shard_map/self_forward/pallas_call | solution.py:406
  99.4 1.3 slice.17
  101.6 1.2 copy-done.20
  102.7 9.3 %enc_forward.1.k_ref.v_ref = bf16[2048,1536]{1,0:T(8,128)(2,1)} custom-call(bf16[1024,768]{1,0:T(8,128)(2,1)} %bitcast.93, bf16[1024,768]{1,0:T(8,128)(2,1)} %copy-done.20, bf16[768,3840]{1,0:T(8,128)(2,1)} %all-gather.3.cloned.1.call-done.w_ref.refs_2_.refs_3_.refs_5_.wc_ref.wq_ref.refs_0_.refs_1_.refs_11_.refs_12_.wk_ref.wv_ref), custom_call_target="tpu_custom_call" | custom-call | flops 4831838208 | bytes 12582912 | tf_op jit(solution)/shard_map/enc_forward/pallas_call | solution.py:536
  112.0 7.5 %collective-permute-done.5.refs_1_.refs_4_ = bf16[1024,384]{1,0:T(8,128)(2,1)S(1)} collective-permute-done((bf16[1024,384]{1,0:T(8,128)(2,1)S(1)}, bf16[1024,384]{1,0:T(8,128)(2,1)S(1)}, u32[]{:S(2)}, u32[]{:S(2)}) %collective-permute-start.5) | collective-permute-done | bytes 786464 | tf_op jit(solution)/shard_map/ppermute | solution.py:1363
  120.4 9.2 %after_self.1 = (f32[1024,768]{1,0:T(8,128)}, bf16[1024,768]{1,0:T(8,128)(2,1)}, bf16[1024,768]{1,0:T(8,128)(2,1)}, f32[8,768]{1,0:T(8,128)}) custom-call(s32[2]{0:T(128)} %and_select_fusion.5.turn_ref, bf16[1024,768]{1,0:T(8,128)(2,1)} %bitcast.63, bf16[2048,384]{1,0:T(8,128)(2,1)} %get-tuple-element.111.refs_0_.refs_3_.o_ref, ...), custom_call_target="tpu_custom_call" | custom-call | flops 2415919104 | bytes 11010048 | tf_op jit(solution)/shard_map/after_self/pallas_call | solution.py:584
  130.3 37.3 %cross_forward.1 = (bf16[1024,768]{1,0:T(8,128)(2,1)}, f32[1024,768]{1,0:T(8,128)}, bf16[1024,24576]{1,0:T(8,128)(2,1)}) custom-call(bf16[1024,768]{1,0:T(8,128)(2,1)} %get-tuple-element.114.q_ref, bf16[2048,1536]{1,0:T(8,128)(2,1)} %enc_forward.1.k_ref.v_ref, bf16[2048,1536]{1,0:T(8,128)(2,1)} %enc_forward.1.k_ref.v_ref, ...), custom_call_target="tpu_custom_call" | custom-call | flops 25769803776 | bytes 6291456 | tf_op jit(solution)/shard_map/cross_forward/pallas_call | solution.py:261
  167.6 3.3 all-gather.5.cloned.1.call-done
  170.9 46.4 %feed_forward.1 = (bf16[1024,768]{1,0:T(8,128)(2,1)}, f32[1024,768]{1,0:T(8,128)}, bf16[1024,768]{1,0:T(8,128)(2,1)}, bf16[1024,768]{1,0:T(8,128)(2,1)}, f32[8,7...) custom-call(bf16[1024,768]{1,0:T(8,128)(2,1)} %get-tuple-element.116.o_ref.refs_9_, ...), custom_call_target="tpu_custom_call" | custom-call | flops 32614907904 | bytes 41943040 | tf_op jit(solution)/shard_map/feed_forward/pallas_call | solution.py:733
  217.3 73.5 %cross_backward.1 = (bf16[1024,768]{1,0:T(8,128)(2,1)}, bf16[2048,768]{1,0:T(8,128)(2,1)}, bf16[2048,768]{1,0:T(8,128)(2,1)}) custom-call(bf16[1024,768]{1,0:T(8,128)(2,1)} %get-tuple-element.114.q_ref, bf16[2048,1536]{1,0:T(8,128)(2,1)} %enc_forward.1.k_ref.v_ref, bf16[2048,1536]{1,0:T(8,128)(2,1)} %enc_forward.1.k_ref.v_ref, ...), custom_call_target="tpu_custom_call" | custom-call | flops 51539607552 | bytes 9437184 | tf_op jit(solution)/shard_map/cross_backward/pallas_call | solution.py:340
  290.8 10.2 %before_self.1 = (f32[1024,768]{1,0:T(8,128)}, bf16[1024,768]{1,0:T(8,128)(2,1)}, f32[8,768]{1,0:T(8,128)}, bf16[1024,384]{1,0:T(8,128)(2,1)}, bf16[1024,384]{1,0:T(8,128)(2,1)}) custom-call(s32[2]{0:T(128)} %and_select_fusion.5.turn_ref, bf16[1024,768]{1,0:T(8,128)(2,1)} %get-tuple-element.122.dq_ref.refs_1_, ...), custom_call_target="tpu_custom_call" | custom-call | flops 2415919104 | bytes 14155776 | tf_op jit(solution)/shard_map/before_self/pallas_call | solution.py:1022
  301.0 1.2 collective-permute-start.7
  302.2 19.4 %mid_grads.1 = (bf16[768,3840]{1,0:T(8,128)(2,1)}, bf16[1024,768]{1,0:T(8,128)(2,1)}) custom-call(s32[2]{0:T(128)} %and_select_fusion.5.turn_ref, bf16[1024,768]{1,0:T(8,128)(2,1)} %get-tuple-element.126.refs_0_, bf16[1024,768]{1,0:T(8,128)(2,1)} %get-tuple-element.122.dq_ref.refs_1_, bf16[1024,768]{1,0:T(8,128)(2,1)} %get-tuple-element.127.refs_2_, ...), custom_call_target="tpu_custom_call" | custom-call | flops 10871635968 | bytes 31457280 | tf_op jit(solution)/shard_map/mid_grads/pallas_call | solution.py:939
  321.6 6.9 %reduce-scatter.3.cloned.1.call-done = bf16[384,768]{1,0:T(8,128)(2,1)} async-done(((bf16[6144,768]{1,0:T(8,128)(2,1)}), bf16[384,768]{1,0:T(8,128)(2,1)}) %reduce-scatter.3.cloned.1.call-update) | async-done | bytes 589840 | tf_op jit(solution)/shard_map/reduce_scatter | solution.py:1378
  328.6 1.3 collective-permute-start.9
  330.8 43.8 %self_backward.1 = (bf16[2048,384]{1,0:T(8,128)(2,1)}, bf16[2048,384]{1,0:T(8,128)(2,1)}, bf16[2048,384]{1,0:T(8,128)(2,1)}) custom-call(s32[4]{0:T(128)} %and_select_fusion.3.count_ref, s32[4]{0:T(128)} %get-tuple-element.104.slot_ref, bf16[2048,384]{1,0:T(8,128)(2,1)} %get-tuple-element.108.q_ref, bf16[2048,384]{1,0:T(8,128)(2,1)} %get-tuple-element.109.k_ref, ...), custom_call_target="tpu_custom_call" | custom-call | flops 6442450944 | bytes 1572864 | tf_op jit(solution)/shard_map/self_backward/pallas_call | solution.py:458
  374.6 2.0 collective-permute-done.8
  376.8 11.2 %qkv_grads.1 = (bf16[8,48,1280]{2,1,0:T(8,128)(2,1)}, bf16[8,48,1280]{2,1,0:T(8,128)(2,1)}) custom-call(s32[1]{0:T(128)} %bitcast.6.core_ref, bf16[2048,384]{1,0:T(8,128)(2,1)} %get-tuple-element.153.refs_0_, bf16[2048,384]{1,0:T(8,128)(2,1)} %get-tuple-element.154.refs_1_, bf16[2048,384]{1,0:T(8,128)(2,1)} %get-tuple-element.155.refs_2_, ...), custom_call_target="tpu_custom_call" | custom-call | flops 1572864 | bytes 2048 | tf_op jit(solution)/shard_map/qkv_grads/pallas_call | solution.py:1097
  388.1 1.7 collective-permute-start.10
  389.7 6.2 %qkv_back.2 = bf16[1024,768]{1,0:T(8,128)(2,1)} custom-call(s32[4]{0:T(128)} %copy-done.19, bf16[2048,384]{1,0:T(8,128)(2,1)} %get-tuple-element.153.refs_0_, bf16[2048,384]{1,0:T(8,128)(2,1)} %get-tuple-element.154.refs_1_, bf16[2048,384]{1,0:T(8,128)(2,1)} %get-tuple-element.155.refs_2_, bf16[768,1152]{1,0:T(8,128)(2,1)} %get-tuple-element.107.w_ref.refs_4_.refs_3_), custom_call_target="tpu_custom_call" | custom-call | flops 786432 | bytes 1024 | tf_op jit(solution)/shard_map/qkv_back/pallas_call | solution.py:1126
  396.2 2.3 collective-permute-start.11
  399.2 6.7 %enc_finish.1 = f32[1024,768]{1,0:T(8,128)} custom-call(bf16[2048,768]{1,0:T(8,128)(2,1)} %get-tuple-element.128.refs_7_.dk_ref, bf16[2048,768]{1,0:T(8,128)(2,1)} %get-tuple-element.129.refs_8_.dv_ref, bf16[768,3840]{1,0:T(8,128)(2,1)} %all-gather.3.cloned.1.call-done.w_ref.refs_2_.refs_3_.refs_5_.wc_ref.wq_ref.refs_0_.refs_1_.refs_11_.refs_12_.wk_ref.wv_ref, ...), custom_call_target="tpu_custom_call" | custom-call | flops 2415919104 | bytes 9437184 | tf_op jit(solution)/shard_map/enc_finish/pallas_call | solution.py:977
  406.0 8.2 %collective-permute-done.11 = bf16[4,48,1280]{2,1,0:T(8,128)(2,1)} collective-permute-done((bf16[4,48,1280]{2,1,0:T(8,128)(2,1)S(1)}, bf16[4,48,1280]{2,1,0:T(8,128)(2,1)}, u32[]{:S(2)}, u32[]{:S(2)}) %collective-permute-start.11) | collective-permute-done | bytes 491552 | tf_op jit(solution)/shard_map/ppermute | solution.py:1235
  416.2 1.4 collective-permute-start.13
  417.6 1.4 collective-permute-start.18
  419.0 6.5 %qkv_back.3.own_ref = f32[1024,768]{1,0:T(8,128)} custom-call(s32[4]{0:T(128)} %copy-done.19, bf16[2048,384]{1,0:T(8,128)(2,1)} %get-tuple-element.153.refs_0_, bf16[2048,384]{1,0:T(8,128)(2,1)} %get-tuple-element.154.refs_1_, bf16[2048,384]{1,0:T(8,128)(2,1)} %get-tuple-element.155.refs_2_, bf16[768,1152]{1,0:T(8,128)(2,1)} %get-tuple-element.107.w_ref.refs_4_.refs_3_), custom_call_target="tpu_custom_call" | custom-call | flops 786432 | bytes 1024 | tf_op jit(solution)/shard_map/qkv_back/pallas_call | solution.py:1126
  426.1 3.2 collective-permute-done.14
  429.4 5.0 %collective-permute-done.15.refs_0_ = bf16[1024,768]{1,0:T(8,128)(2,1)S(1)} collective-permute-done((bf16[1024,768]{1,0:T(8,128)(2,1)}, bf16[1024,768]{1,0:T(8,128)(2,1)S(1)}, u32[]{:S(2)}, u32[]{:S(2)}) %collective-permute-start.15) | collective-permute-done | bytes 1572896 | tf_op jit(solution)/shard_map/ppermute | solution.py:1412
  435.1 1.2 pad_maximum_fusion.near_ref
  436.3 1.5 collective-permute-start.19
  437.8 5.8 %collective-permute-done.21 = bf16[48,3840]{1,0:T(8,128)(2,1)S(1)} collective-permute-done((bf16[48,3840]{1,0:T(8,128)(2,1)}, bf16[48,3840]{1,0:T(8,128)(2,1)S(1)}, u32[]{:S(2)}, u32[]{:S(2)}) %collective-permute-start.21) | collective-permute-done | bytes 368672 | tf_op jit(solution)/shard_map/ppermute | solution.py:1246
  445.2 6.3 %finish.1 = f32[1024,768]{1,0:T(8,128)} custom-call(bf16[1024,768]{1,0:T(8,128)(2,1)} %bitcast.64, f32[1024,768]{1,0:T(8,128)} %get-tuple-element.163.dh_ref, f32[1,768]{1,0:T(1,128)} %get-tuple-element.197.g_ref.refs_5_, f32[1024,768]{1,0:T(8,128)} %qkv_back.3.own_ref, bf16[1024,768]{1,0:T(8,128)(2,1)} %copy-done.8), custom_call_target="tpu_custom_call" | custom-call | flops 7864320 | bytes 12582912 | tf_op jit(solution)/shard_map/finish/pallas_call | solution.py:1154
  453.4 3.0 collective-permute-start.23
  457.0 4.1 unpack.1
  461.3 1.7 collective-permute-done.20.far_ref
  463.8 2.5 settle_qkv.1
  466.3 3.1 settle_mid.1
  (143 shorter events, 27.8 us)
Async XLA Ops:
  7.2 7.4 %copy-start = (bf16[512,768]{1,0:T(8,128)(2,1)S(1)}, bf16[512,768]{1,0:T(8,128)(2,1)}, u32[]{:S(2)}) copy-start(bf16[512,768]{1,0:T(8,128)(2,1)} %param.35) | copy-start | bytes 2359300
  7.2 94.4 %all-gather.3.cloned.1.call-start = ((), (), s32[]{:S(2)}) async-start(), calls=%async_computation.2 | async-start | bytes 6266880 | tf_op jit(solution)/shard_map/all_gather | solution.py:1324
  12.5 158.3 %all-gather.5.cloned.1.call-start = ((), (), s32[]{:S(2)}) async-start(), calls=%async_computation.3 | async-start | bytes 10027008 | tf_op jit(solution)/shard_map/all_gather | solution.py:1333
  14.6 1.3 copy-start.16
  14.7 1.4 copy-start.17
  14.7 1.4 copy-start.18
  14.8 7.0 %copy-start.2 = (bf16[1,1024,768]{2,1,0:T(8,128)(2,1)S(1)}, bf16[1,1024,768]{2,1,0:T(8,128)(2,1)}, u32[]{:S(2)}) copy-start(bf16[1,1024,768]{2,1,0:T(8,128)(2,1)} %param.20) | copy-start | bytes 4718596
  14.8 9.4 %copy-start.15 = (s32[1,2048]{1,0:T(1,128)S(1)}, s32[1,2048]{1,0:T(1,128)}, u32[]{:S(2)}) copy-start(s32[1,2048]{1,0:T(1,128)} %param.22) | copy-start | bytes 24580
  14.8 11.0 %copy-start.25 = (s32[1,4]{1,0:T(1,128)S(1)}, s32[1,4]{1,0:T(1,128)}, u32[]{:S(2)}) copy-start(s32[1,4]{1,0:T(1,128)} %param.23) | copy-start | bytes 52
  15.7 312.9 %reduce-scatter.3.cloned.1.call-start = ((), (), s32[]{:S(2)}) async-start(), calls=%async_computation.4 | async-start | bytes 10027008 | tf_op jit(solution)/shard_map/reduce_scatter | solution.py:1378
  16.1 9.8 %collective-permute-start.3 = (bf16[96,1280]{1,0:T(8,128)(2,1)S(1)}, bf16[96,1280]{1,0:T(8,128)(2,1)S(1)}, u32[]{:S(2)}, u32[]{:S(2)}) collective-permute-start(bf16[96,1280]{1,0:T(8,128)(2,1)S(1)} %fusion.3), channel_id=1, source_target_pairs={{0,3},{1,0},{2,1},{3,2},{4,7},{5,4},{6,5},{7,6},{8,11},{9,8},{10,9... | collective-permute-start | bytes 737288 | tf_op jit(solution)/shard_map/ppermute | solution.py:1197
  16.2 19.7 %collective-permute-start.1 = (bf16[96,1280]{1,0:T(8,128)(2,1)S(1)}, bf16[96,1280]{1,0:T(8,128)(2,1)S(1)}, u32[]{:S(2)}, u32[]{:S(2)}) collective-permute-start(bf16[96,1280]{1,0:T(8,128)(2,1)S(1)} %fusion.3), channel_id=1, source_target_pairs={{0,1},{1,2},{2,3},{3,0},{4,5},{5,6},{6,7},{7,4},{8,9},{9,10},{10,1... | collective-permute-start | bytes 737288 | tf_op jit(solution)/shard_map/ppermute | solution.py:1197
  17.7 31.0 %collective-permute-start.2 = (bf16[96,1280]{1,0:T(8,128)(2,1)S(1)}, bf16[96,1280]{1,0:T(8,128)(2,1)}, u32[]{:S(2)}, u32[]{:S(2)}) collective-permute-start(bf16[96,1280]{1,0:T(8,128)(2,1)S(1)} %fusion.3), channel_id=1, source_target_pairs={{0,2},{1,3},{2,0},{3,1},{4,6},{5,7},{6,4},{7,5},{8,10},{9,11},{10,... | collective-permute-start | bytes 737288 | tf_op jit(solution)/shard_map/ppermute | solution.py:1197
  21.8 40.8 %collective-permute-start = (bf16[1024,768]{1,0:T(8,128)(2,1)S(1)}, bf16[1024,768]{1,0:T(8,128)(2,1)}, u32[]{:S(2)}, u32[]{:S(2)}) collective-permute-start(bf16[1024,768]{1,0:T(8,128)(2,1)S(1)} %bitcast.65), channel_id=1, source_target_pairs={{0,4},{4,0},{1,5},{5,1},{2,6},{6,2},{3,7},{7,3},{8,12},{12,8},{9,1... | collective-permute-start | bytes 4718600 | tf_op jit(solution)/shard_map/ppermute | solution.py:1304
  49.7 7.9 %copy-start.4 = (bf16[4,96,1280]{2,1,0:T(8,128)(2,1)}, bf16[4,96,1280]{2,1,0:T(8,128)(2,1)S(1)}, u32[]{:S(2)}) copy-start(bf16[4,96,1280]{2,1,0:T(8,128)(2,1)S(1)} %pad_maximum_fusion.1.near_ref) | copy-start | bytes 2949124
  49.7 7.9 %collective-permute-start.4 = (bf16[4,96,1280]{2,1,0:T(8,128)(2,1)S(1)}, bf16[4,96,1280]{2,1,0:T(8,128)(2,1)}, u32[]{:S(2)}, u32[]{:S(2)}) collective-permute-start(bf16[4,96,1280]{2,1,0:T(8,128)(2,1)S(1)} %pad_maximum_fusion.1.near_ref), channel_id=1, source_target_pairs={{0,8},{8,0},{16,24},{24,16},{1,9},{9,1},{17,25},{25,17},{2,10},{10... | collective-permute-start | bytes 2949128 | tf_op jit(solution)/shard_map/ppermute | solution.py:1199
  53.1 8.0 %copy-start.19 = (s32[4]{0:T(128)}, s32[4]{0:T(128)S(1)}, u32[]{:S(2)}) copy-start(s32[4]{0:T(128)S(1)} %dynamic_slice.66.order_ref) | copy-start | bytes 52
  62.6 38.9 %collective-permute-start.6 = (bf16[1024,768]{1,0:T(8,128)(2,1)}, bf16[1024,768]{1,0:T(8,128)(2,1)S(1)}, u32[]{:S(2)}, u32[]{:S(2)}) collective-permute-start(bf16[1024,768]{1,0:T(8,128)(2,1)} %bitcast.92), channel_id=1, source_target_pairs={{0,4},{4,0},{1,5},{5,1},{2,6},{6,2},{3,7},{7,3},{8,12},{12,8},{9,1... | collective-permute-start | bytes 4718600 | tf_op jit(solution)/shard_map/ppermute | solution.py:1304
  100.7 18.8 %collective-permute-start.5 = (bf16[1024,384]{1,0:T(8,128)(2,1)S(1)}, bf16[1024,384]{1,0:T(8,128)(2,1)S(1)}, u32[]{:S(2)}, u32[]{:S(2)}) collective-permute-start(bf16[1024,384]{1,0:T(8,128)(2,1)S(1)} %slice.17), channel_id=1, source_target_pairs={{0,4},{4,0},{1,5},{5,1},{2,6},{6,2},{3,7},{7,3},{8,12},{12,8},{9,1... | collective-permute-start | bytes 2359304 | tf_op jit(solution)/shard_map/ppermute | solution.py:1363
  101.5 1.2 copy-start.20
  217.3 217.1 %reduce-scatter.5.cloned.1.call-start = ((), (), s32[]{:S(2)}) async-start(), calls=%async_computation.5 | async-start | bytes 6266880 | tf_op jit(solution)/shard_map/reduce_scatter | solution.py:1399
  301.0 20.6 %collective-permute-start.7 = (bf16[1024,384]{1,0:T(8,128)(2,1)}, bf16[1024,384]{1,0:T(8,128)(2,1)S(1)}, u32[]{:S(2)}, u32[]{:S(2)}) collective-permute-start(bf16[1024,384]{1,0:T(8,128)(2,1)} %get-tuple-element.125), channel_id=1, source_target_pairs={{0,4},{4,0},{1,5},{5,1},{2,6},{6,2},{3,7},{7,3},{8,12},{12,8},{9,1... | collective-permute-start | bytes 2359304 | tf_op jit(solution)/shard_map/ppermute | solution.py:1384
  321.6 6.9 %copy-start.21 = (bf16[1024,384]{1,0:T(8,128)(2,1)}, bf16[1024,384]{1,0:T(8,128)(2,1)S(1)}, u32[]{:S(2)}) copy-start(bf16[1024,384]{1,0:T(8,128)(2,1)S(1)} %collective-permute-done.7.far_ref) | copy-start | bytes 2359300
  328.5 1.3 copy-start.11
  328.6 48.2 %collective-permute-start.9 = (bf16[1024,768]{1,0:T(8,128)(2,1)}, bf16[1024,768]{1,0:T(8,128)(2,1)S(1)}, u32[]{:S(2)}, u32[]{:S(2)}) collective-permute-start(bf16[1024,768]{1,0:T(8,128)(2,1)} %get-tuple-element.141), channel_id=1, source_target_pairs={{0,4},{4,0},{1,5},{5,1},{2,6},{6,2},{3,7},{7,3},{8,12},{12,8},{9,1... | collective-permute-start | bytes 4718600 | tf_op jit(solution)/shard_map/ppermute | solution.py:1402
  329.8 46.8 %collective-permute-start.8 = (bf16[2,3,64,768]{3,2,1,0:T(8,128)(2,1)S(1)}, bf16[2,3,64,768]{3,2,1,0:T(8,128)(2,1)S(1)}, u32[]{:S(2)}, u32[]{:S(2)}) collective-permute-start(bf16[2,3,64,768]{3,2,1,0:T(8,128)(2,1)S(1)} %bitcast.78), channel_id=1, source_target_pairs={{0,4},{4,0},{1,5},{5,1},{2,6},{6,2},{3,7},{7,3},{8,12},{12,8},{9,1... | collective-permute-start | bytes 1769480 | tf_op jit(solution)/shard_map/ppermute | solution.py:1246
  376.8 11.2 %copy-start.7 = (bf16[1024,768]{1,0:T(8,128)(2,1)}, bf16[1024,768]{1,0:T(8,128)(2,1)S(1)}, u32[]{:S(2)}) copy-start(bf16[1024,768]{1,0:T(8,128)(2,1)S(1)} %collective-permute-done.9.refs_0_) | copy-start | bytes 4718596
  388.1 7.9 %collective-permute-start.10 = (bf16[8,48,1280]{2,1,0:T(8,128)(2,1)}, bf16[8,48,1280]{2,1,0:T(8,128)(2,1)S(1)}, u32[]{:S(2)}, u32[]{:S(2)}) collective-permute-start(bf16[8,48,1280]{2,1,0:T(8,128)(2,1)} %get-tuple-element.152), channel_id=1, source_target_pairs={{0,8},{8,0},{16,24},{24,16},{1,9},{9,1},{17,25},{25,17},{2,10},{10... | collective-permute-start | bytes 2949128 | tf_op jit(solution)/shard_map/ppermute | solution.py:1229
  389.7 6.2 %copy-start.9 = (bf16[8,48,1280]{2,1,0:T(8,128)(2,1)S(1)}, bf16[8,48,1280]{2,1,0:T(8,128)(2,1)}, u32[]{:S(2)}) copy-start(bf16[8,48,1280]{2,1,0:T(8,128)(2,1)} %get-tuple-element.151) | copy-start | bytes 2949124
  396.2 17.9 %collective-permute-start.11 = (bf16[4,48,1280]{2,1,0:T(8,128)(2,1)S(1)}, bf16[4,48,1280]{2,1,0:T(8,128)(2,1)}, u32[]{:S(2)}, u32[]{:S(2)}) collective-permute-start(bf16[4,48,1280]{2,1,0:T(8,128)(2,1)S(1)} %get-tuple-element.157), channel_id=1, source_target_pairs={{0,16},{8,24},{16,0},{24,8},{1,17},{9,25},{17,1},{25,9},{2,18},{10... | collective-permute-start | bytes 1474568 | tf_op jit(solution)/shard_map/ppermute | solution.py:1235
  398.5 35.9 %collective-permute-start.15 = (bf16[1024,768]{1,0:T(8,128)(2,1)}, bf16[1024,768]{1,0:T(8,128)(2,1)S(1)}, u32[]{:S(2)}, u32[]{:S(2)}) collective-permute-start(bf16[1024,768]{1,0:T(8,128)(2,1)} %qkv_back.2), channel_id=1, source_target_pairs={{0,4},{4,0},{1,5},{5,1},{2,6},{6,2},{3,7},{7,3},{8,12},{12,8},{9,1... | collective-permute-start | bytes 4718600 | tf_op jit(solution)/shard_map/ppermute | solution.py:1412
  415.3 10.2 %collective-permute-start.12 = (bf16[48,1280]{1,0:T(8,128)(2,1)S(1)}, bf16[48,1280]{1,0:T(8,128)(2,1)S(1)}, u32[]{:S(2)}, u32[]{:S(2)}) collective-permute-start(bf16[48,1280]{1,0:T(8,128)(2,1)S(1)} %get-tuple-element.192), channel_id=1, source_target_pairs={{0,1},{1,2},{2,3},{3,0},{4,5},{5,6},{6,7},{7,4},{8,9},{9,10},{10,1... | collective-permute-start | bytes 368648 | tf_op jit(solution)/shard_map/ppermute | solution.py:1242
  416.2 9.9 %collective-permute-start.13 = (bf16[48,1280]{1,0:T(8,128)(2,1)S(1)}, bf16[48,1280]{1,0:T(8,128)(2,1)S(1)}, u32[]{:S(2)}, u32[]{:S(2)}) collective-permute-start(bf16[48,1280]{1,0:T(8,128)(2,1)S(1)} %get-tuple-element.194), channel_id=1, source_target_pairs={{0,2},{1,3},{2,0},{3,1},{4,6},{5,7},{6,4},{7,5},{8,10},{9,11},{10,... | collective-permute-start | bytes 368648 | tf_op jit(solution)/shard_map/ppermute | solution.py:1242
  417.6 11.8 %collective-permute-start.14 = (bf16[48,1280]{1,0:T(8,128)(2,1)S(1)}, bf16[48,1280]{1,0:T(8,128)(2,1)S(1)}, u32[]{:S(2)}, u32[]{:S(2)}) collective-permute-start(bf16[48,1280]{1,0:T(8,128)(2,1)S(1)} %get-tuple-element.193), channel_id=1, source_target_pairs={{0,3},{1,0},{2,1},{3,2},{4,7},{5,4},{6,5},{7,6},{8,11},{9,8},{10,9... | collective-permute-start | bytes 368648 | tf_op jit(solution)/shard_map/ppermute | solution.py:1242
  417.6 17.5 %collective-permute-start.18 = (bf16[2,3,64,768]{3,2,1,0:T(8,128)(2,1)S(1)}, bf16[2,3,64,768]{3,2,1,0:T(8,128)(2,1)}, u32[]{:S(2)}, u32[]{:S(2)}) collective-permute-start(bf16[2,3,64,768]{3,2,1,0:T(8,128)(2,1)S(1)} %add_convert_fusion), channel_id=1, source_target_pairs={{0,16},{8,24},{16,0},{24,8},{1,17},{9,25},{17,1},{25,9},{2,18},{10... | collective-permute-start | bytes 1769480 | tf_op jit(solution)/shard_map/ppermute | solution.py:1252
  434.4 9.3 %copy-start.8 = (bf16[1024,768]{1,0:T(8,128)(2,1)}, bf16[1024,768]{1,0:T(8,128)(2,1)S(1)}, u32[]{:S(2)}) copy-start(bf16[1024,768]{1,0:T(8,128)(2,1)S(1)} %collective-permute-done.15.refs_0_) | copy-start | bytes 4718596
  434.4 9.2 %copy-start.14 = (bf16[48,3840]{1,0:T(8,128)(2,1)S(1)}, bf16[48,3840]{1,0:T(8,128)(2,1)}, u32[]{:S(2)}) copy-start(bf16[48,3840]{1,0:T(8,128)(2,1)} %reduce-scatter.5.cloned.1.call-done) | copy-start | bytes 1105924
  434.4 9.2 %collective-permute-start.21 = (bf16[48,3840]{1,0:T(8,128)(2,1)}, bf16[48,3840]{1,0:T(8,128)(2,1)S(1)}, u32[]{:S(2)}, u32[]{:S(2)}) collective-permute-start(bf16[48,3840]{1,0:T(8,128)(2,1)} %reduce-scatter.5.cloned.1.call-done), channel_id=1, source_target_pairs={{0,4},{4,0},{1,5},{5,1},{2,6},{6,2},{3,7},{7,3},{8,12},{12,8},{9,1... | collective-permute-start | bytes 1105928 | tf_op jit(solution)/shard_map/ppermute | solution.py:1246
  436.3 15.2 %copy-start.3 = (bf16[2,2,3,64,768]{4,3,2,1,0:T(8,128)(2,1)}, bf16[2,2,3,64,768]{4,3,2,1,0:T(8,128)(2,1)S(1)}, u32[]{:S(2)}) copy-start(bf16[2,2,3,64,768]{4,3,2,1,0:T(8,128)(2,1)S(1)} %pad_maximum_fusion.near_ref) | copy-start | bytes 3538948
  436.3 20.7 %collective-permute-start.19 = (bf16[2,2,3,64,768]{4,3,2,1,0:T(8,128)(2,1)S(1)}, bf16[2,2,3,64,768]{4,3,2,1,0:T(8,128)(2,1)}, u32[]{:S(2)}, u32[]{:S(2)}) collective-permute-start(bf16[2,2,3,64,768]{4,3,2,1,0:T(8,128)(2,1)S(1)} %pad_maximum_fusion.near_ref), channel_id=1, source_target_pairs={{0,8},{8,0},{16,24},{24,16},{1,9},{9,1},{17,25},{25,17},{2,10},{10... | collective-permute-start | bytes 3538952 | tf_op jit(solution)/shard_map/ppermute | solution.py:1255
  443.7 8.6 %collective-permute-start.22 = (bf16[48,3840]{1,0:T(8,128)(2,1)S(1)}, bf16[48,3840]{1,0:T(8,128)(2,1)}, u32[]{:S(2)}, u32[]{:S(2)}) collective-permute-start(bf16[48,3840]{1,0:T(8,128)(2,1)S(1)} %add_convert_fusion.4), channel_id=1, source_target_pairs={{0,16},{8,24},{16,0},{24,8},{1,17},{9,25},{17,1},{25,9},{2,18},{10... | collective-permute-start | bytes 1105928 | tf_op jit(solution)/shard_map/ppermute | solution.py:1252
  444.5 7.0 %collective-permute-start.16 = (bf16[48,1280]{1,0:T(8,128)(2,1)S(1)}, bf16[48,1280]{1,0:T(8,128)(2,1)S(1)}, u32[]{:S(2)}, u32[]{:S(2)}) collective-permute-start(bf16[48,1280]{1,0:T(8,128)(2,1)S(1)} %fusion.8), channel_id=1, source_target_pairs={{0,4},{4,0},{1,5},{5,1},{2,6},{6,2},{3,7},{7,3},{8,12},{12,8},{9,1... | collective-permute-start | bytes 368648 | tf_op jit(solution)/shard_map/ppermute | solution.py:1249
  451.5 9.5 %collective-permute-start.17 = (bf16[2,48,1280]{2,1,0:T(8,128)(2,1)S(1)}, bf16[2,48,1280]{2,1,0:T(8,128)(2,1)S(1)}, u32[]{:S(2)}, u32[]{:S(2)}) collective-permute-start(bf16[2,48,1280]{2,1,0:T(8,128)(2,1)S(1)} %pad_maximum_fusion.5), channel_id=1, source_target_pairs={{0,16},{8,24},{16,0},{24,8},{1,17},{9,25},{17,1},{25,9},{2,18},{10... | collective-permute-start | bytes 737288 | tf_op jit(solution)/shard_map/ppermute | solution.py:1252
  453.4 7.7 %copy-start.5 = (bf16[2,48,3840]{2,1,0:T(8,128)(2,1)}, bf16[2,48,3840]{2,1,0:T(8,128)(2,1)S(1)}, u32[]{:S(2)}) copy-start(bf16[2,48,3840]{2,1,0:T(8,128)(2,1)S(1)} %pad_maximum_fusion.2.near_ref) | copy-start | bytes 2211844
  453.4 13.0 %collective-permute-start.23 = (bf16[2,48,3840]{2,1,0:T(8,128)(2,1)S(1)}, bf16[2,48,3840]{2,1,0:T(8,128)(2,1)}, u32[]{:S(2)}, u32[]{:S(2)}) collective-permute-start(bf16[2,48,3840]{2,1,0:T(8,128)(2,1)S(1)} %pad_maximum_fusion.2.near_ref), channel_id=1, source_target_pairs={{0,8},{8,0},{16,24},{24,16},{1,9},{9,1},{17,25},{25,17},{2,10},{10... | collective-permute-start | bytes 2211848 | tf_op jit(solution)/shard_map/ppermute | solution.py:1255
  461.1 8.4 %copy-start.1 = (bf16[512,768]{1,0:T(8,128)(2,1)S(1)}, bf16[512,768]{1,0:T(8,128)(2,1)}, u32[]{:S(2)}) copy-start(bf16[512,768]{1,0:T(8,128)(2,1)} %param.35) | copy-start | bytes 2359300
  461.1 1.9 copy-start.6
  461.1 1.9 collective-permute-start.20
  (6 other events, 5.8 us)
Sparse Core Ops, SparseCore 0:
  12.7 76.1 all-gather.2
  91.7 79.1 all-gather.4
  217.4 111.0 reduce-scatter.2
  332.8 85.1 reduce-scatter.4

commit v8 on v7

--- a/solution.py
+++ b/solution.py
@@ -1235,12 +1235,11 @@
         got = lax.ppermute(send, "parts", self.swap_x)
         return (keep.astype(F32) + got.astype(F32)).astype(BF)
 
-    def over_fsdp(self, g):
-        total = pick(g, self.z, 0).astype(F32)
-        for d in range(1, self.n_fsdp):
-            piece = pick(g, (self.z + d) % self.n_fsdp, 0)
-            total = total + lax.ppermute(piece, "fsdp", turned(self.n_fsdp, d)).astype(F32)
-        return total.astype(BF)
+    def from_fsdp(self, g):
+        return [pick(g, self.z, 0)] + [
+            lax.ppermute(pick(g, (self.z + d) % self.n_fsdp, 0), "fsdp", turned(self.n_fsdp, d))
+            for d in range(1, self.n_fsdp)
+        ]
 
     def over_ctx(self, g):
         return (g.astype(F32) + lax.ppermute(g, "ctx", turned(2, 1)).astype(F32)).astype(BF)
@@ -1417,11 +1416,16 @@
     if fast:
         send, keep = net.over_core(*g_qkv)
         send, keep, dn_far = lax.optimization_barrier((send, keep, dn_far))
+        g_qkv, enc_grad, sum_ff, dn_own = lax.optimization_barrier(
+            (net.over_x(send, keep), enc_grad, sum_ff, dn_own)
+        )
         sum_ff = net.widen_x(sum_ff)
-        g_qkv, enc_grad = lax.optimization_barrier((net.over_x(send, keep), enc_grad))
-        g_qkv = net.over_fsdp(g_qkv)
-        dn_got, part_mid, dn_own = lax.optimization_barrier((dn_got, part_mid, dn_own))
-        g_qkv, part_mid = lax.optimization_barrier((g_qkv, part_mid))
+        shares = net.from_fsdp(g_qkv)
+        shares[1], part_mid = lax.optimization_barrier((shares[1], part_mid))
+        got_mid = lax.ppermute(part_mid, "ctx", turned(2, 1))
+        g_qkv = functools.reduce(jnp.add, [share.astype(F32) for share in shares]).astype(BF)
+        g_qkv, dn_got, got_mid = lax.optimization_barrier((g_qkv, dn_got, got_mid))
+        part_mid = (part_mid.astype(F32) + got_mid.astype(F32)).astype(BF)
     decoder_grad = finish(x_own, dh1, gain_self, dn_own, dn_got)
 
     if fast:
@@ -1434,7 +1438,7 @@
         g_qkv, decoder_grad = lax.optimization_barrier((net.widen_ctx(g_qkv), decoder_grad))
         g_qkv, ff = lax.optimization_barrier((net.widen_x(g_qkv), ff))
         grad_gate, grad_up, grad_down = ff
-        sum_mid = net.widen_x(net.over_ctx(part_mid))
+        sum_mid = net.widen_x(part_mid)
         *grads_qkv, grad_gself, grad_gmlp, grad_gcross, rms_values = settle(
             settle_qkv_kernel, me, g_qkv, net.from_core(g_qkv),
             [square] * 3 + [(1, shard)] * 3 + [(1, 4)],

time: 481 us -> 485 us (level)
  waiting for transfers between devices: 67 us -> 57.6 us
  Pallas kernels: 335 us -> 340 us
    ppermute x3, waiting for transfers between devices: 0.01 us -> 8.16 us  [widen_x(): return jnp.stack([g, lax.ppermute(g, 'parts', self.swap_x)])]
    ppermute x2 -> x1, waiting for transfers between devices: 7.8 us -> 0.01 us  [over_ctx(): lax.ppermute(g, 'ctx', turned(2, 1)).astype(F32)]
    ppermute x1, waiting for transfers between devices: 8.16 us -> 1.08 us  [over_x(): got = lax.ppermute(send, 'parts', self.swap_x)]
    unnamed x58 -> x56, local copies, waits for them, and re-layouts: 7.91 us -> 9.86 us
  transfers between devices with their start and end apart: 28 -> 28, of which waited for: 12 -> 9; matrix products, arithmetic and copies ran while one was open for 4% -> 5% of each run, Pallas kernels for 60% -> 61%
where the time goes in v8:
time: 485 us; the launch traced here: 480 us
  Pallas kernels  340 us (70%)
  waiting for transfers between devices  57.6 us (12%)
  starting transfers between devices  30.1 us (6%)
  local copies, waits for them, and re-layouts  19.2 us (4%)
  other arithmetic  17 us (4%)
  between operations  15.2 us (3%)
    pallas_call x1, Pallas kernels, cross_backward(): pl.pallas_call(cross_backward_kernel, grid=(pairs, rows // block), in_spe...  73.5 us
    pallas_call x1, Pallas kernels, self_backward(): pl.pallas_call(functools.partial(self_backward_kernel, per_dev=per_dev),...  47.4 us
    pallas_call x1, Pallas kernels, feed_forward(): pl.pallas_call(mlp_kernel, grid=(steps,), in_specs=[full, full, pl.BlockS...  46.4 us
    pallas_call x1, Pallas kernels, cross_forward(): pl.pallas_call(cross_forward_kernel, grid=(pairs, rows // block), in_spec...  37.2 us
    pallas_call x1, Pallas kernels, self_forward(): pl.pallas_call(self_forward_kernel, grid_spec=pltpu.PrefetchScalarGridSpe...  28.6 us
    ppermute x3, waiting for transfers between devices, gather_first(): lax.ppermute(mine, 'fsdp', turned(n_fsdp, d))  20.7 us
    pallas_call x1, Pallas kernels, mid_grads(): pl.pallas_call(functools.partial(mid_grads_kernel, count=len(pieces)), gr...  19.4 us
    pallas_call x2, Pallas kernels, qkv_back(): pl.pallas_call(functools.partial(qkv_back_kernel, count=len(ds)), grid_sp...  12.6 us
  transfers between devices with their start and end apart: 28, of which 9 were waited for; matrix products, arithmetic and copies ran while one was open for 5% of the time, Pallas kernels for 61%

profile of v8, /device:TPU:9, one launch (start us, length us, event | category | flops | bytes accessed | tf_op | source)
XLA Modules:
  0.0 479.5 jit_solution(16691586936645703132)
XLA Ops:
  16.2 1.5 collective-permute-start.1
  17.7 4.1 collective-permute-start.2
  21.8 1.2 collective-permute-start
  27.9 8.0 %collective-permute-done.1 = bf16[96,1280]{1,0:T(8,128)(2,1)S(1)} collective-permute-done((bf16[96,1280]{1,0:T(8,128)(2,1)S(1)}, bf16[96,1280]{1,0:T(8,128)(2,1)S(1)}, u32[]{:S(2)}, u32[]{:S(2)}) %collective-permute-start.1) | collective-permute-done | bytes 245792 | tf_op jit(solution)/shard_map/ppermute | solution.py:1197
  35.9 12.7 %collective-permute-done.2 = bf16[96,1280]{1,0:T(8,128)(2,1)S(1)} collective-permute-done((bf16[96,1280]{1,0:T(8,128)(2,1)S(1)}, bf16[96,1280]{1,0:T(8,128)(2,1)S(1)}, u32[]{:S(2)}, u32[]{:S(2)}) %collective-permute-start.2) | collective-permute-done | bytes 245792 | tf_op jit(solution)/shard_map/ppermute | solution.py:1197
  48.8 2.7 collective-permute-start.4
  53.3 1.4 sort.17
  54.7 1.8 select_convert_fusion.2.qa_ref
  56.5 3.3 select_convert_fusion
  60.8 3.0 assemble.1
  63.7 1.4 fusion.12
  65.2 1.3 collective-permute-start.6
  66.5 9.2 %qkv_forward.1 = (bf16[2048,768]{1,0:T(8,128)(2,1)}, bf16[2048,384]{1,0:T(8,128)(2,1)}, bf16[2048,384]{1,0:T(8,128)(2,1)}, bf16[2048,384]{1,0:T(8,128)(2,1)}) custom-call(s32[4]{0:T(128)} %copy-done.19, bf16[1024,768]{1,0:T(8,128)(2,1)} %bitcast.62, bf16[1024,768]{1,0:T(8,128)(2,1)} %collective-permute-done.far_ref, ...), custom_call_target="tpu_custom_call" | custom-call | flops 3623878656 | bytes 12582912 | tf_op jit(solution)/shard_map/qkv_forward/pallas_call | solution.py:502
  75.6 28.6 %self_forward.1 = (bf16[2048,384]{1,0:T(8,128)(2,1)}, f32[2048,384]{1,0:T(8,128)}) custom-call(s32[4]{0:T(128)} %and_select_fusion.3.count_ref, s32[4]{0:T(128)} %get-tuple-element.106.slot_ref, bf16[2048,384]{1,0:T(8,128)(2,1)} %get-tuple-element.110.q_ref, bf16[2048,384]{1,0:T(8,128)(2,1)} %get-tuple-element.111.k_ref, ...), custom_call_target="tpu_custom_call" | custom-call | flops 12884901888 | bytes 6291456 | tf_op jit(solution)/shard_map/self_forward/pallas_call | solution.py:406
  104.3 1.2 slice.17
  106.1 1.2 copy-done.20
  107.3 9.3 %enc_forward.1.k_ref.v_ref = bf16[2048,1536]{1,0:T(8,128)(2,1)} custom-call(bf16[1024,768]{1,0:T(8,128)(2,1)} %bitcast.94, bf16[1024,768]{1,0:T(8,128)(2,1)} %copy-done.20, bf16[768,3840]{1,0:T(8,128)(2,1)} %all-gather.3.cloned.1.call-done.w_ref.refs_2_.refs_3_.refs_5_.wc_ref.wq_ref.refs_0_.refs_1_.refs_11_.refs_12_.wk_ref.wv_ref), custom_call_target="tpu_custom_call" | custom-call | flops 4831838208 | bytes 12582912 | tf_op jit(solution)/shard_map/enc_forward/pallas_call | solution.py:536
  116.6 7.0 %collective-permute-done.5.refs_1_.refs_4_ = bf16[1024,384]{1,0:T(8,128)(2,1)S(1)} collective-permute-done((bf16[1024,384]{1,0:T(8,128)(2,1)S(1)}, bf16[1024,384]{1,0:T(8,128)(2,1)S(1)}, u32[]{:S(2)}, u32[]{:S(2)}) %collective-permute-start.5) | collective-permute-done | bytes 786464 | tf_op jit(solution)/shard_map/ppermute | solution.py:1362
  124.5 10.0 %after_self.1 = (f32[1024,768]{1,0:T(8,128)}, bf16[1024,768]{1,0:T(8,128)(2,1)}, bf16[1024,768]{1,0:T(8,128)(2,1)}, f32[8,768]{1,0:T(8,128)}) custom-call(s32[2]{0:T(128)} %and_select_fusion.5.turn_ref, bf16[1024,768]{1,0:T(8,128)(2,1)} %bitcast.63, bf16[2048,384]{1,0:T(8,128)(2,1)} %get-tuple-element.113.refs_0_.refs_3_.o_ref, ...), custom_call_target="tpu_custom_call" | custom-call | flops 2415919104 | bytes 11010048 | tf_op jit(solution)/shard_map/after_self/pallas_call | solution.py:584
  135.3 37.2 %cross_forward.1 = (bf16[1024,768]{1,0:T(8,128)(2,1)}, f32[1024,768]{1,0:T(8,128)}, bf16[1024,24576]{1,0:T(8,128)(2,1)}) custom-call(bf16[1024,768]{1,0:T(8,128)(2,1)} %get-tuple-element.116.q_ref, bf16[2048,1536]{1,0:T(8,128)(2,1)} %enc_forward.1.k_ref.v_ref, bf16[2048,1536]{1,0:T(8,128)(2,1)} %enc_forward.1.k_ref.v_ref, ...), custom_call_target="tpu_custom_call" | custom-call | flops 25769803776 | bytes 6291456 | tf_op jit(solution)/shard_map/cross_forward/pallas_call | solution.py:261
  172.4 46.4 %feed_forward.1 = (bf16[1024,768]{1,0:T(8,128)(2,1)}, f32[1024,768]{1,0:T(8,128)}, bf16[1024,768]{1,0:T(8,128)(2,1)}, bf16[1024,768]{1,0:T(8,128)(2,1)}, f32[8,7...) custom-call(bf16[1024,768]{1,0:T(8,128)(2,1)} %get-tuple-element.118.o_ref.refs_9_, ...), custom_call_target="tpu_custom_call" | custom-call | flops 32614907904 | bytes 41943040 | tf_op jit(solution)/shard_map/feed_forward/pallas_call | solution.py:733
  218.9 73.5 %cross_backward.1 = (bf16[1024,768]{1,0:T(8,128)(2,1)}, bf16[2048,768]{1,0:T(8,128)(2,1)}, bf16[2048,768]{1,0:T(8,128)(2,1)}) custom-call(bf16[1024,768]{1,0:T(8,128)(2,1)} %get-tuple-element.116.q_ref, bf16[2048,1536]{1,0:T(8,128)(2,1)} %enc_forward.1.k_ref.v_ref, bf16[2048,1536]{1,0:T(8,128)(2,1)} %enc_forward.1.k_ref.v_ref, ...), custom_call_target="tpu_custom_call" | custom-call | flops 51539607552 | bytes 9437184 | tf_op jit(solution)/shard_map/cross_backward/pallas_call | solution.py:340
  292.4 10.2 %before_self.1 = (f32[1024,768]{1,0:T(8,128)}, bf16[1024,768]{1,0:T(8,128)(2,1)}, f32[8,768]{1,0:T(8,128)}, bf16[1024,384]{1,0:T(8,128)(2,1)}, bf16[1024,384]{1,0:T(8,128)(2,1)}) custom-call(s32[2]{0:T(128)} %and_select_fusion.5.turn_ref, bf16[1024,768]{1,0:T(8,128)(2,1)} %get-tuple-element.124.dq_ref.refs_1_, ...), custom_call_target="tpu_custom_call" | custom-call | flops 2415919104 | bytes 14155776 | tf_op jit(solution)/shard_map/before_self/pallas_call | solution.py:1022
  302.7 19.4 %mid_grads.1 = (bf16[768,3840]{1,0:T(8,128)(2,1)}, bf16[1024,768]{1,0:T(8,128)(2,1)}) custom-call(s32[2]{0:T(128)} %and_select_fusion.5.turn_ref, bf16[1024,768]{1,0:T(8,128)(2,1)} %get-tuple-element.128.refs_0_, bf16[1024,768]{1,0:T(8,128)(2,1)} %get-tuple-element.124.dq_ref.refs_1_, bf16[1024,768]{1,0:T(8,128)(2,1)} %get-tuple-element.129.refs_2_, ...), custom_call_target="tpu_custom_call" | custom-call | flops 10871635968 | bytes 31457280 | tf_op jit(solution)/shard_map/mid_grads/pallas_call | solution.py:939
  322.0 9.6 %reduce-scatter.3.cloned.1.call-done = bf16[384,768]{1,0:T(8,128)(2,1)} async-done(((bf16[6144,768]{1,0:T(8,128)(2,1)}), bf16[384,768]{1,0:T(8,128)(2,1)}) %reduce-scatter.3.cloned.1.call-update) | async-done | bytes 589840 | tf_op jit(solution)/shard_map/reduce_scatter | solution.py:1377
  331.7 1.3 collective-permute-start.9
  333.9 47.4 %self_backward.1 = (bf16[2048,384]{1,0:T(8,128)(2,1)}, bf16[2048,384]{1,0:T(8,128)(2,1)}, bf16[2048,384]{1,0:T(8,128)(2,1)}) custom-call(s32[4]{0:T(128)} %and_select_fusion.3.count_ref, s32[4]{0:T(128)} %get-tuple-element.106.slot_ref, bf16[2048,384]{1,0:T(8,128)(2,1)} %get-tuple-element.110.q_ref, bf16[2048,384]{1,0:T(8,128)(2,1)} %get-tuple-element.111.k_ref, ...), custom_call_target="tpu_custom_call" | custom-call | flops 6442450944 | bytes 1572864 | tf_op jit(solution)/shard_map/self_backward/pallas_call | solution.py:458
  381.5 11.2 %qkv_grads.1 = (bf16[8,48,1280]{2,1,0:T(8,128)(2,1)}, bf16[8,48,1280]{2,1,0:T(8,128)(2,1)}) custom-call(s32[1]{0:T(128)} %bitcast.6.core_ref, bf16[2048,384]{1,0:T(8,128)(2,1)} %get-tuple-element.155.refs_0_, bf16[2048,384]{1,0:T(8,128)(2,1)} %get-tuple-element.156.refs_1_, bf16[2048,384]{1,0:T(8,128)(2,1)} %get-tuple-element.157.refs_2_, ...), custom_call_target="tpu_custom_call" | custom-call | flops 1572864 | bytes 2048 | tf_op jit(solution)/shard_map/qkv_grads/pallas_call | solution.py:1097
  392.8 6.2 %qkv_back.2 = bf16[1024,768]{1,0:T(8,128)(2,1)} custom-call(s32[4]{0:T(128)} %copy-done.19, bf16[2048,384]{1,0:T(8,128)(2,1)} %get-tuple-element.155.refs_0_, bf16[2048,384]{1,0:T(8,128)(2,1)} %get-tuple-element.156.refs_1_, bf16[2048,384]{1,0:T(8,128)(2,1)} %get-tuple-element.157.refs_2_, bf16[768,1152]{1,0:T(8,128)(2,1)} %get-tuple-element.109.w_ref.refs_4_.refs_3_), custom_call_target="tpu_custom_call" | custom-call | flops 786432 | bytes 1024 | tf_op jit(solution)/shard_map/qkv_back/pallas_call | solution.py:1126
  399.3 1.2 collective-permute-start.11
  400.5 1.2 collective-permute-start.15
  401.7 6.4 %qkv_back.3.own_ref = f32[1024,768]{1,0:T(8,128)} custom-call(s32[4]{0:T(128)} %copy-done.19, bf16[2048,384]{1,0:T(8,128)(2,1)} %get-tuple-element.155.refs_0_, bf16[2048,384]{1,0:T(8,128)(2,1)} %get-tuple-element.156.refs_1_, bf16[2048,384]{1,0:T(8,128)(2,1)} %get-tuple-element.157.refs_2_, bf16[768,1152]{1,0:T(8,128)(2,1)} %get-tuple-element.109.w_ref.refs_4_.refs_3_), custom_call_target="tpu_custom_call" | custom-call | flops 786432 | bytes 1024 | tf_op jit(solution)/shard_map/qkv_back/pallas_call | solution.py:1126
  408.1 6.6 %enc_finish.1 = f32[1024,768]{1,0:T(8,128)} custom-call(bf16[2048,768]{1,0:T(8,128)(2,1)} %get-tuple-element.130.refs_7_.dk_ref, bf16[2048,768]{1,0:T(8,128)(2,1)} %get-tuple-element.131.refs_8_.dv_ref, bf16[768,3840]{1,0:T(8,128)(2,1)} %all-gather.3.cloned.1.call-done.w_ref.refs_2_.refs_3_.refs_5_.wc_ref.wq_ref.refs_0_.refs_1_.refs_11_.refs_12_.wk_ref.wv_ref, ...), custom_call_target="tpu_custom_call" | custom-call | flops 2415919104 | bytes 9437184 | tf_op jit(solution)/shard_map/enc_finish/pallas_call | solution.py:977
  415.9 1.2 collective-permute-start.19
  418.9 1.7 collective-permute-start.13
  421.6 8.2 %collective-permute-done.19 = bf16[2,3,64,768]{3,2,1,0:T(8,128)(2,1)S(1)} collective-permute-done((bf16[2,3,64,768]{3,2,1,0:T(8,128)(2,1)S(1)}, bf16[2,3,64,768]{3,2,1,0:T(8,128)(2,1)S(1)}, u32[]{:S(2)}, u32[]{:S(2)}) %collective-permute-start.19) | collective-permute-done | bytes 589856 | tf_op jit(solution)/shard_map/ppermute | solution.py:1251
  429.9 2.0 collective-permute-start.20
  431.9 1.6 collective-permute-start.16
  434.7 1.4 collective-permute-done.15.refs_0_
  436.0 7.8 %collective-permute-done.16 = bf16[48,3840]{1,0:T(8,128)(2,1)S(1)} collective-permute-done((bf16[48,3840]{1,0:T(8,128)(2,1)}, bf16[48,3840]{1,0:T(8,128)(2,1)S(1)}, u32[]{:S(2)}, u32[]{:S(2)}) %collective-permute-start.16) | collective-permute-done | bytes 368672 | tf_op jit(solution)/shard_map/ppermute | solution.py:1425
  445.3 1.6 collective-permute-start.17
  447.0 6.3 %finish.1 = f32[1024,768]{1,0:T(8,128)} custom-call(bf16[1024,768]{1,0:T(8,128)(2,1)} %bitcast.64, f32[1024,768]{1,0:T(8,128)} %get-tuple-element.167.dh_ref, f32[1,768]{1,0:T(1,128)} %get-tuple-element.201.g_ref.refs_5_, f32[1024,768]{1,0:T(8,128)} %qkv_back.3.own_ref, bf16[1024,768]{1,0:T(8,128)(2,1)} %collective-permute-done.15.refs_0_), custom_call_target="tpu_custom_call" | custom-call | flops 7864320 | bytes 12582912 | tf_op jit(solution)/shard_map/finish/pallas_call | solution.py:1154
  453.3 1.2 collective-permute-start.18
  455.6 2.1 collective-permute-start.23
  459.3 4.1 unpack.1
  464.6 1.8 collective-permute-done.21.far_ref
  467.2 2.5 settle_qkv.1
  469.7 3.1 settle_mid.1
  (141 shorter events, 31.2 us)
Async XLA Ops:
  7.2 7.4 %copy-start = (bf16[512,768]{1,0:T(8,128)(2,1)S(1)}, bf16[512,768]{1,0:T(8,128)(2,1)}, u32[]{:S(2)}) copy-start(bf16[512,768]{1,0:T(8,128)(2,1)} %param.35) | copy-start | bytes 2359300
  7.2 98.9 %all-gather.3.cloned.1.call-start = ((), (), s32[]{:S(2)}) async-start(), calls=%async_computation.2 | async-start | bytes 6266880 | tf_op jit(solution)/shard_map/all_gather | solution.py:1323
  12.5 159.9 %all-gather.5.cloned.1.call-start = ((), (), s32[]{:S(2)}) async-start(), calls=%async_computation.3 | async-start | bytes 10027008 | tf_op jit(solution)/shard_map/all_gather | solution.py:1332
  14.6 1.1 copy-start.21
  14.6 1.1 copy-start.22
  14.6 1.2 copy-start.23
  14.6 1.3 copy-start.16
  14.7 1.4 copy-start.17
  14.7 1.4 copy-start.18
  14.8 7.0 %copy-start.2 = (bf16[1,1024,768]{2,1,0:T(8,128)(2,1)S(1)}, bf16[1,1024,768]{2,1,0:T(8,128)(2,1)}, u32[]{:S(2)}) copy-start(bf16[1,1024,768]{2,1,0:T(8,128)(2,1)} %param.20) | copy-start | bytes 4718596
  14.8 9.4 %copy-start.15 = (s32[1,2048]{1,0:T(1,128)S(1)}, s32[1,2048]{1,0:T(1,128)}, u32[]{:S(2)}) copy-start(s32[1,2048]{1,0:T(1,128)} %param.22) | copy-start | bytes 24580
  14.8 12.6 %copy-start.24 = (s32[1,4]{1,0:T(1,128)S(1)}, s32[1,4]{1,0:T(1,128)}, u32[]{:S(2)}) copy-start(s32[1,4]{1,0:T(1,128)} %param.23) | copy-start | bytes 52
  15.7 316.0 %reduce-scatter.3.cloned.1.call-start = ((), (), s32[]{:S(2)}) async-start(), calls=%async_computation.4 | async-start | bytes 10027008 | tf_op jit(solution)/shard_map/reduce_scatter | solution.py:1377
  16.1 11.8 %collective-permute-start.3 = (bf16[96,1280]{1,0:T(8,128)(2,1)S(1)}, bf16[96,1280]{1,0:T(8,128)(2,1)S(1)}, u32[]{:S(2)}, u32[]{:S(2)}) collective-permute-start(bf16[96,1280]{1,0:T(8,128)(2,1)S(1)} %fusion.3), channel_id=1, source_target_pairs={{0,3},{1,0},{2,1},{3,2},{4,7},{5,4},{6,5},{7,6},{8,11},{9,8},{10,9... | collective-permute-start | bytes 737288 | tf_op jit(solution)/shard_map/ppermute | solution.py:1197
  16.2 19.7 %collective-permute-start.1 = (bf16[96,1280]{1,0:T(8,128)(2,1)S(1)}, bf16[96,1280]{1,0:T(8,128)(2,1)S(1)}, u32[]{:S(2)}, u32[]{:S(2)}) collective-permute-start(bf16[96,1280]{1,0:T(8,128)(2,1)S(1)} %fusion.3), channel_id=1, source_target_pairs={{0,1},{1,2},{2,3},{3,0},{4,5},{5,6},{6,7},{7,4},{8,9},{9,10},{10,1... | collective-permute-start | bytes 737288 | tf_op jit(solution)/shard_map/ppermute | solution.py:1197
  17.7 31.0 %collective-permute-start.2 = (bf16[96,1280]{1,0:T(8,128)(2,1)S(1)}, bf16[96,1280]{1,0:T(8,128)(2,1)S(1)}, u32[]{:S(2)}, u32[]{:S(2)}) collective-permute-start(bf16[96,1280]{1,0:T(8,128)(2,1)S(1)} %fusion.3), channel_id=1, source_target_pairs={{0,2},{1,3},{2,0},{3,1},{4,6},{5,7},{6,4},{7,5},{8,10},{9,11},{10,... | collective-permute-start | bytes 737288 | tf_op jit(solution)/shard_map/ppermute | solution.py:1197
  21.8 43.4 %collective-permute-start = (bf16[1024,768]{1,0:T(8,128)(2,1)S(1)}, bf16[1024,768]{1,0:T(8,128)(2,1)}, u32[]{:S(2)}, u32[]{:S(2)}) collective-permute-start(bf16[1024,768]{1,0:T(8,128)(2,1)S(1)} %bitcast.65), channel_id=1, source_target_pairs={{0,4},{4,0},{1,5},{5,1},{2,6},{6,2},{3,7},{7,3},{8,12},{12,8},{9,1... | collective-permute-start | bytes 4718600 | tf_op jit(solution)/shard_map/ppermute | solution.py:1303
  48.8 11.1 %copy-start.4 = (bf16[4,96,1280]{2,1,0:T(8,128)(2,1)}, bf16[4,96,1280]{2,1,0:T(8,128)(2,1)S(1)}, u32[]{:S(2)}) copy-start(bf16[4,96,1280]{2,1,0:T(8,128)(2,1)S(1)} %pad_maximum_fusion.1.near_ref) | copy-start | bytes 2949124
  48.8 11.0 %collective-permute-start.4 = (bf16[4,96,1280]{2,1,0:T(8,128)(2,1)S(1)}, bf16[4,96,1280]{2,1,0:T(8,128)(2,1)S(1)}, u32[]{:S(2)}, u32[]{:S(2)}) collective-permute-start(bf16[4,96,1280]{2,1,0:T(8,128)(2,1)S(1)} %pad_maximum_fusion.1.near_ref), channel_id=1, source_target_pairs={{0,8},{8,0},{16,24},{24,16},{1,9},{9,1},{17,25},{25,17},{2,10},{10... | collective-permute-start | bytes 2949128 | tf_op jit(solution)/shard_map/ppermute | solution.py:1199
  52.8 10.9 %copy-start.19 = (s32[4]{0:T(128)}, s32[4]{0:T(128)S(1)}, u32[]{:S(2)}) copy-start(s32[4]{0:T(128)S(1)} %dynamic_slice.66.order_ref) | copy-start | bytes 52
  65.2 40.9 %collective-permute-start.6 = (bf16[1024,768]{1,0:T(8,128)(2,1)}, bf16[1024,768]{1,0:T(8,128)(2,1)S(1)}, u32[]{:S(2)}, u32[]{:S(2)}) collective-permute-start(bf16[1024,768]{1,0:T(8,128)(2,1)} %bitcast.93), channel_id=1, source_target_pairs={{0,4},{4,0},{1,5},{5,1},{2,6},{6,2},{3,7},{7,3},{8,12},{12,8},{9,1... | collective-permute-start | bytes 4718600 | tf_op jit(solution)/shard_map/ppermute | solution.py:1303
  105.5 18.2 %collective-permute-start.5 = (bf16[1024,384]{1,0:T(8,128)(2,1)S(1)}, bf16[1024,384]{1,0:T(8,128)(2,1)S(1)}, u32[]{:S(2)}, u32[]{:S(2)}) collective-permute-start(bf16[1024,384]{1,0:T(8,128)(2,1)S(1)} %slice.17), channel_id=1, source_target_pairs={{0,4},{4,0},{1,5},{5,1},{2,6},{6,2},{3,7},{7,3},{8,12},{12,8},{9,1... | collective-permute-start | bytes 2359304 | tf_op jit(solution)/shard_map/ppermute | solution.py:1362
  106.1 1.2 copy-start.20
  218.9 213.1 %reduce-scatter.5.cloned.1.call-start = ((), (), s32[]{:S(2)}) async-start(), calls=%async_computation.5 | async-start | bytes 6266880 | tf_op jit(solution)/shard_map/reduce_scatter | solution.py:1398
  302.6 19.4 %collective-permute-start.7 = (bf16[1024,384]{1,0:T(8,128)(2,1)}, bf16[1024,384]{1,0:T(8,128)(2,1)}, u32[]{:S(2)}, u32[]{:S(2)}) collective-permute-start(bf16[1024,384]{1,0:T(8,128)(2,1)} %get-tuple-element.127), channel_id=1, source_target_pairs={{0,4},{4,0},{1,5},{5,1},{2,6},{6,2},{3,7},{7,3},{8,12},{12,8},{9,1... | collective-permute-start | bytes 2359304 | tf_op jit(solution)/shard_map/ppermute | solution.py:1383
  331.6 1.3 copy-start.12
  331.7 49.8 %collective-permute-start.9 = (bf16[1024,768]{1,0:T(8,128)(2,1)}, bf16[1024,768]{1,0:T(8,128)(2,1)S(1)}, u32[]{:S(2)}, u32[]{:S(2)}) collective-permute-start(bf16[1024,768]{1,0:T(8,128)(2,1)} %get-tuple-element.143), channel_id=1, source_target_pairs={{0,4},{4,0},{1,5},{5,1},{2,6},{6,2},{3,7},{7,3},{8,12},{12,8},{9,1... | collective-permute-start | bytes 4718600 | tf_op jit(solution)/shard_map/ppermute | solution.py:1401
  332.9 48.3 %collective-permute-start.8 = (bf16[2,3,64,768]{3,2,1,0:T(8,128)(2,1)S(1)}, bf16[2,3,64,768]{3,2,1,0:T(8,128)(2,1)S(1)}, u32[]{:S(2)}, u32[]{:S(2)}) collective-permute-start(bf16[2,3,64,768]{3,2,1,0:T(8,128)(2,1)S(1)} %bitcast.78), channel_id=1, source_target_pairs={{0,4},{4,0},{1,5},{5,1},{2,6},{6,2},{3,7},{7,3},{8,12},{12,8},{9,1... | collective-permute-start | bytes 1769480 | tf_op jit(solution)/shard_map/ppermute | solution.py:1245
  381.4 11.2 %copy-start.7 = (bf16[1024,768]{1,0:T(8,128)(2,1)}, bf16[1024,768]{1,0:T(8,128)(2,1)S(1)}, u32[]{:S(2)}) copy-start(bf16[1024,768]{1,0:T(8,128)(2,1)S(1)} %collective-permute-done.9.refs_0_) | copy-start | bytes 4718596
  392.7 6.4 %collective-permute-start.10 = (bf16[8,48,1280]{2,1,0:T(8,128)(2,1)}, bf16[8,48,1280]{2,1,0:T(8,128)(2,1)S(1)}, u32[]{:S(2)}, u32[]{:S(2)}) collective-permute-start(bf16[8,48,1280]{2,1,0:T(8,128)(2,1)} %get-tuple-element.154), channel_id=1, source_target_pairs={{0,8},{8,0},{16,24},{24,16},{1,9},{9,1},{17,25},{25,17},{2,10},{10... | collective-permute-start | bytes 2949128 | tf_op jit(solution)/shard_map/ppermute | solution.py:1229
  392.8 6.2 %copy-start.10 = (bf16[8,48,1280]{2,1,0:T(8,128)(2,1)S(1)}, bf16[8,48,1280]{2,1,0:T(8,128)(2,1)}, u32[]{:S(2)}) copy-start(bf16[8,48,1280]{2,1,0:T(8,128)(2,1)} %get-tuple-element.153) | copy-start | bytes 2949124
  399.3 16.5 %collective-permute-start.11 = (bf16[4,48,1280]{2,1,0:T(8,128)(2,1)S(1)}, bf16[4,48,1280]{2,1,0:T(8,128)(2,1)S(1)}, u32[]{:S(2)}, u32[]{:S(2)}) collective-permute-start(bf16[4,48,1280]{2,1,0:T(8,128)(2,1)S(1)} %get-tuple-element.159), channel_id=1, source_target_pairs={{0,16},{8,24},{16,0},{24,8},{1,17},{9,25},{17,1},{25,9},{2,18},{10... | collective-permute-start | bytes 1474568 | tf_op jit(solution)/shard_map/ppermute | solution.py:1235
  400.5 35.5 %collective-permute-start.15 = (bf16[1024,768]{1,0:T(8,128)(2,1)}, bf16[1024,768]{1,0:T(8,128)(2,1)}, u32[]{:S(2)}, u32[]{:S(2)}) collective-permute-start(bf16[1024,768]{1,0:T(8,128)(2,1)} %qkv_back.2), channel_id=1, source_target_pairs={{0,4},{4,0},{1,5},{5,1},{2,6},{6,2},{3,7},{7,3},{8,12},{12,8},{9,1... | collective-permute-start | bytes 4718600 | tf_op jit(solution)/shard_map/ppermute | solution.py:1411
  415.9 13.9 %collective-permute-start.19 = (bf16[2,3,64,768]{3,2,1,0:T(8,128)(2,1)S(1)}, bf16[2,3,64,768]{3,2,1,0:T(8,128)(2,1)S(1)}, u32[]{:S(2)}, u32[]{:S(2)}) collective-permute-start(bf16[2,3,64,768]{3,2,1,0:T(8,128)(2,1)S(1)} %add_convert_fusion), channel_id=1, source_target_pairs={{0,16},{8,24},{16,0},{24,8},{1,17},{9,25},{17,1},{25,9},{2,18},{10... | collective-permute-start | bytes 1769480 | tf_op jit(solution)/shard_map/ppermute | solution.py:1251
  417.8 14.1 %collective-permute-start.12 = (bf16[48,1280]{1,0:T(8,128)(2,1)S(1)}, bf16[48,1280]{1,0:T(8,128)(2,1)}, u32[]{:S(2)}, u32[]{:S(2)}) collective-permute-start(bf16[48,1280]{1,0:T(8,128)(2,1)S(1)} %get-tuple-element.196), channel_id=1, source_target_pairs={{0,1},{1,2},{2,3},{3,0},{4,5},{5,6},{6,7},{7,4},{8,9},{9,10},{10,1... | collective-permute-start | bytes 368648 | tf_op jit(solution)/shard_map/ppermute | solution.py:1240
  418.9 14.7 %collective-permute-start.13 = (bf16[48,1280]{1,0:T(8,128)(2,1)}, bf16[48,1280]{1,0:T(8,128)(2,1)}, u32[]{:S(2)}, u32[]{:S(2)}) collective-permute-start(bf16[48,1280]{1,0:T(8,128)(2,1)} %get-tuple-element.198), channel_id=1, source_target_pairs={{0,2},{1,3},{2,0},{3,1},{4,6},{5,7},{6,4},{7,5},{8,10},{9,11},{10,... | collective-permute-start | bytes 368648 | tf_op jit(solution)/shard_map/ppermute | solution.py:1240
  420.6 13.0 %collective-permute-start.14 = (bf16[48,1280]{1,0:T(8,128)(2,1)}, bf16[48,1280]{1,0:T(8,128)(2,1)}, u32[]{:S(2)}, u32[]{:S(2)}) collective-permute-start(bf16[48,1280]{1,0:T(8,128)(2,1)} %get-tuple-element.197), channel_id=1, source_target_pairs={{0,3},{1,0},{2,1},{3,2},{4,7},{5,4},{6,5},{7,6},{8,11},{9,8},{10,9... | collective-permute-start | bytes 368648 | tf_op jit(solution)/shard_map/ppermute | solution.py:1240
  429.9 23.3 %copy-start.3 = (bf16[2,2,3,64,768]{4,3,2,1,0:T(8,128)(2,1)}, bf16[2,2,3,64,768]{4,3,2,1,0:T(8,128)(2,1)S(1)}, u32[]{:S(2)}) copy-start(bf16[2,2,3,64,768]{4,3,2,1,0:T(8,128)(2,1)S(1)} %pad_maximum_fusion.near_ref) | copy-start | bytes 3538948
  429.9 28.3 %collective-permute-start.20 = (bf16[2,2,3,64,768]{4,3,2,1,0:T(8,128)(2,1)S(1)}, bf16[2,2,3,64,768]{4,3,2,1,0:T(8,128)(2,1)S(1)}, u32[]{:S(2)}, u32[]{:S(2)}) collective-permute-start(bf16[2,2,3,64,768]{4,3,2,1,0:T(8,128)(2,1)S(1)} %pad_maximum_fusion.near_ref), channel_id=1, source_target_pairs={{0,8},{8,0},{16,24},{24,16},{1,9},{9,1},{17,25},{25,17},{2,10},{10... | collective-permute-start | bytes 3538952 | tf_op jit(solution)/shard_map/ppermute | solution.py:1254
  431.9 11.9 %collective-permute-start.16 = (bf16[48,3840]{1,0:T(8,128)(2,1)}, bf16[48,3840]{1,0:T(8,128)(2,1)S(1)}, u32[]{:S(2)}, u32[]{:S(2)}) collective-permute-start(bf16[48,3840]{1,0:T(8,128)(2,1)} %reduce-scatter.5.cloned.1.call-done), channel_id=1, source_target_pairs={{0,4},{4,0},{1,5},{5,1},{2,6},{6,2},{3,7},{7,3},{8,12},{12,8},{9,1... | collective-permute-start | bytes 1105928 | tf_op jit(solution)/shard_map/ppermute | solution.py:1425
  444.9 9.6 %collective-permute-start.22 = (bf16[48,3840]{1,0:T(8,128)(2,1)S(1)}, bf16[48,3840]{1,0:T(8,128)(2,1)}, u32[]{:S(2)}, u32[]{:S(2)}) collective-permute-start(bf16[48,3840]{1,0:T(8,128)(2,1)S(1)} %add_convert_fusion.4), channel_id=1, source_target_pairs={{0,16},{8,24},{16,0},{24,8},{1,17},{9,25},{17,1},{25,9},{2,18},{10... | collective-permute-start | bytes 1105928 | tf_op jit(solution)/shard_map/ppermute | solution.py:1251
  445.3 7.9 %collective-permute-start.17 = (bf16[48,1280]{1,0:T(8,128)(2,1)S(1)}, bf16[48,1280]{1,0:T(8,128)(2,1)S(1)}, u32[]{:S(2)}, u32[]{:S(2)}) collective-permute-start(bf16[48,1280]{1,0:T(8,128)(2,1)S(1)} %fusion.8), channel_id=1, source_target_pairs={{0,4},{4,0},{1,5},{5,1},{2,6},{6,2},{3,7},{7,3},{8,12},{12,8},{9,1... | collective-permute-start | bytes 368648 | tf_op jit(solution)/shard_map/ppermute | solution.py:1248
  453.3 10.1 %collective-permute-start.18 = (bf16[2,48,1280]{2,1,0:T(8,128)(2,1)S(1)}, bf16[2,48,1280]{2,1,0:T(8,128)(2,1)}, u32[]{:S(2)}, u32[]{:S(2)}) collective-permute-start(bf16[2,48,1280]{2,1,0:T(8,128)(2,1)S(1)} %pad_maximum_fusion.5), channel_id=1, source_target_pairs={{0,16},{8,24},{16,0},{24,8},{1,17},{9,25},{17,1},{25,9},{2,18},{10... | collective-permute-start | bytes 737288 | tf_op jit(solution)/shard_map/ppermute | solution.py:1251
  455.6 8.9 %copy-start.5 = (bf16[2,48,3840]{2,1,0:T(8,128)(2,1)}, bf16[2,48,3840]{2,1,0:T(8,128)(2,1)S(1)}, u32[]{:S(2)}) copy-start(bf16[2,48,3840]{2,1,0:T(8,128)(2,1)S(1)} %pad_maximum_fusion.2.near_ref) | copy-start | bytes 2211844
  455.6 14.1 %collective-permute-start.23 = (bf16[2,48,3840]{2,1,0:T(8,128)(2,1)S(1)}, bf16[2,48,3840]{2,1,0:T(8,128)(2,1)}, u32[]{:S(2)}, u32[]{:S(2)}) collective-permute-start(bf16[2,48,3840]{2,1,0:T(8,128)(2,1)S(1)} %pad_maximum_fusion.2.near_ref), channel_id=1, source_target_pairs={{0,8},{8,0},{16,24},{24,16},{1,9},{9,1},{17,25},{25,17},{2,10},{10... | collective-permute-start | bytes 2211848 | tf_op jit(solution)/shard_map/ppermute | solution.py:1254
  463.4 9.4 %copy-start.1 = (bf16[512,768]{1,0:T(8,128)(2,1)S(1)}, bf16[512,768]{1,0:T(8,128)(2,1)}, u32[]{:S(2)}) copy-start(bf16[512,768]{1,0:T(8,128)(2,1)} %param.35) | copy-start | bytes 2359300
  464.5 1.9 copy-start.6
  464.5 1.9 collective-permute-start.21
  (5 other events, 4.4 us)
Sparse Core Ops, SparseCore 0:
  12.7 76.1 all-gather.2
  91.7 79.1 all-gather.4
  219.0 112.6 reduce-scatter.2
  335.9 85.2 reduce-scatter.4

commit v9 on v8

--- a/solution.py
+++ b/solution.py
@@ -987,7 +987,7 @@
         out_specs=row,
         out_shape=jax.ShapeDtypeStruct((rows, dim), F32),
         compiler_params=params(),
-        cost_estimate=cost(4 * rows * dim * dim, 12 * rows * dim),
+        cost_estimate=cost(rows * dim, rows),
         name="enc_finish",
     )(dk, dv, w2, w2, *got)
 
@@ -1158,7 +1158,7 @@
         out_specs=row,
         out_shape=jax.ShapeDtypeStruct((rows, dim), F32),
         compiler_params=params(),
-        cost_estimate=cost(10 * rows * dim, 16 * rows * dim),
+        cost_estimate=cost(rows * dim, rows),
         name="finish",
     )(x, dh1, gain, own, *got)
 
@@ -1424,7 +1424,7 @@
         shares[1], part_mid = lax.optimization_barrier((shares[1], part_mid))
         got_mid = lax.ppermute(part_mid, "ctx", turned(2, 1))
         g_qkv = functools.reduce(jnp.add, [share.astype(F32) for share in shares]).astype(BF)
-        g_qkv, dn_got, got_mid = lax.optimization_barrier((g_qkv, dn_got, got_mid))
+        g_qkv, dn_got, got_mid = lax.optimization_barrier((net.widen_ctx(g_qkv), dn_got, got_mid))
         part_mid = (part_mid.astype(F32) + got_mid.astype(F32)).astype(BF)
     decoder_grad = finish(x_own, dh1, gain_self, dn_own, dn_got)
 
@@ -1435,8 +1435,7 @@
             unpack_kernel, me, sum_ff, net.from_core(sum_ff),
             [(shard, hidden), (shard, hidden), (hidden // n_fsdp, dim)],
         )
-        g_qkv, decoder_grad = lax.optimization_barrier((net.widen_ctx(g_qkv), decoder_grad))
-        g_qkv, ff = lax.optimization_barrier((net.widen_x(g_qkv), ff))
+        g_qkv, ff, decoder_grad = lax.optimization_barrier((net.widen_x(g_qkv), ff, decoder_grad))
         grad_gate, grad_up, grad_down = ff
         sum_mid = net.widen_x(part_mid)
         *grads_qkv, grad_gself, grad_gmlp, grad_gcross, rms_values = settle(

time: 485 us -> 495 us (1.021)
  waiting for transfers between devices: 57.6 us -> 68.8 us
    ppermute x3, waiting for transfers between devices: 0.01 us -> 9.91 us  [from_fsdp(): lax.ppermute(pick(g, (self.z + d) % self.n_fsdp, 0), 'fsdp', turned(self....]
  transfers between devices with their start and end apart: 28 -> 28, of which waited for: 9 -> 15; matrix products, arithmetic and copies ran while one was open for 5% -> 5% of each run, Pallas kernels for 61% -> 59%
where the time goes in v9:
time: 495 us; the launch traced here: 490 us
  Pallas kernels  337 us (68%)
  waiting for transfers between devices  68.8 us (14%)
  starting transfers between devices  33 us (7%)
  local copies, waits for them, and re-layouts  18.3 us (4%)
  other arithmetic  18.3 us (4%)
  between operations  15.3 us (3%)
    pallas_call x1, Pallas kernels, cross_backward(): pl.pallas_call(cross_backward_kernel, grid=(pairs, rows // block), in_spe...  73.5 us
    pallas_call x1, Pallas kernels, feed_forward(): pl.pallas_call(mlp_kernel, grid=(steps,), in_specs=[full, full, pl.BlockS...  46.4 us
    pallas_call x1, Pallas kernels, self_backward(): pl.pallas_call(functools.partial(self_backward_kernel, per_dev=per_dev),...  45.6 us
    pallas_call x1, Pallas kernels, cross_forward(): pl.pallas_call(cross_forward_kernel, grid=(pairs, rows // block), in_spec...  37.2 us
    pallas_call x1, Pallas kernels, self_forward(): pl.pallas_call(self_forward_kernel, grid_spec=pltpu.PrefetchScalarGridSpe...  27.6 us
    ppermute x3, waiting for transfers between devices, gather_first(): lax.ppermute(mine, 'fsdp', turned(n_fsdp, d))  20.7 us
    pallas_call x1, Pallas kernels, mid_grads(): pl.pallas_call(functools.partial(mid_grads_kernel, count=len(pieces)), gr...  19.3 us
    pallas_call x2, Pallas kernels, qkv_back(): pl.pallas_call(functools.partial(qkv_back_kernel, count=len(ds)), grid_sp...  12.5 us
  transfers between devices with their start and end apart: 28, of which 15 were waited for; matrix products, arithmetic and copies ran while one was open for 5% of the time, Pallas kernels for 59%

profile of v9, /device:TPU:9, one launch (start us, length us, event | category | flops | bytes accessed | tf_op | source)
XLA Modules:
  0.0 490.3 jit_solution(1915214498126008411)
XLA Ops:
  16.2 1.5 collective-permute-start.1
  17.7 4.1 collective-permute-start.2
  21.8 1.2 collective-permute-start
  27.9 8.0 %collective-permute-done.1 = bf16[96,1280]{1,0:T(8,128)(2,1)S(1)} collective-permute-done((bf16[96,1280]{1,0:T(8,128)(2,1)S(1)}, bf16[96,1280]{1,0:T(8,128)(2,1)S(1)}, u32[]{:S(2)}, u32[]{:S(2)}) %collective-permute-start.1) | collective-permute-done | bytes 245792 | tf_op jit(solution)/shard_map/ppermute | solution.py:1197
  35.9 12.7 %collective-permute-done.2 = bf16[96,1280]{1,0:T(8,128)(2,1)S(1)} collective-permute-done((bf16[96,1280]{1,0:T(8,128)(2,1)S(1)}, bf16[96,1280]{1,0:T(8,128)(2,1)S(1)}, u32[]{:S(2)}, u32[]{:S(2)}) %collective-permute-start.2) | collective-permute-done | bytes 245792 | tf_op jit(solution)/shard_map/ppermute | solution.py:1197
  48.8 2.7 collective-permute-start.4
  53.3 1.4 sort.17
  54.7 1.8 select_convert_fusion.2.qa_ref
  56.5 3.3 select_convert_fusion
  60.8 3.0 assemble.1
  63.8 1.4 fusion.12
  65.3 1.3 collective-permute-start.6
  66.5 9.2 %qkv_forward.1 = (bf16[2048,768]{1,0:T(8,128)(2,1)}, bf16[2048,384]{1,0:T(8,128)(2,1)}, bf16[2048,384]{1,0:T(8,128)(2,1)}, bf16[2048,384]{1,0:T(8,128)(2,1)}) custom-call(s32[4]{0:T(128)} %copy-done.21, bf16[1024,768]{1,0:T(8,128)(2,1)} %bitcast.62, bf16[1024,768]{1,0:T(8,128)(2,1)} %collective-permute-done.far_ref, ...), custom_call_target="tpu_custom_call" | custom-call | flops 3623878656 | bytes 12582912 | tf_op jit(solution)/shard_map/qkv_forward/pallas_call | solution.py:502
  75.7 27.6 %self_forward.1 = (bf16[2048,384]{1,0:T(8,128)(2,1)}, f32[2048,384]{1,0:T(8,128)}) custom-call(s32[4]{0:T(128)} %and_select_fusion.3.count_ref, s32[4]{0:T(128)} %get-tuple-element.105.slot_ref, bf16[2048,384]{1,0:T(8,128)(2,1)} %get-tuple-element.109.q_ref, bf16[2048,384]{1,0:T(8,128)(2,1)} %get-tuple-element.110.k_ref, ...), custom_call_target="tpu_custom_call" | custom-call | flops 12884901888 | bytes 6291456 | tf_op jit(solution)/shard_map/self_forward/pallas_call | solution.py:406
  106.3 9.3 %enc_forward.1.k_ref.v_ref = bf16[2048,1536]{1,0:T(8,128)(2,1)} custom-call(bf16[1024,768]{1,0:T(8,128)(2,1)} %bitcast.94, bf16[1024,768]{1,0:T(8,128)(2,1)} %copy-done.22, bf16[768,3840]{1,0:T(8,128)(2,1)} %all-gather.3.cloned.1.call-done.w_ref.refs_2_.refs_3_.refs_5_.wc_ref.wq_ref.refs_0_.refs_1_.refs_11_.refs_12_.wk_ref.wv_ref), custom_call_target="tpu_custom_call" | custom-call | flops 4831838208 | bytes 12582912 | tf_op jit(solution)/shard_map/enc_forward/pallas_call | solution.py:536
  115.6 6.6 %collective-permute-done.5.refs_1_.refs_4_ = bf16[1024,384]{1,0:T(8,128)(2,1)S(1)} collective-permute-done((bf16[1024,384]{1,0:T(8,128)(2,1)S(1)}, bf16[1024,384]{1,0:T(8,128)(2,1)S(1)}, u32[]{:S(2)}, u32[]{:S(2)}) %collective-permute-start.5) | collective-permute-done | bytes 786464 | tf_op jit(solution)/shard_map/ppermute | solution.py:1362
  123.0 9.1 %after_self.1 = (f32[1024,768]{1,0:T(8,128)}, bf16[1024,768]{1,0:T(8,128)(2,1)}, bf16[1024,768]{1,0:T(8,128)(2,1)}, f32[8,768]{1,0:T(8,128)}) custom-call(s32[2]{0:T(128)} %and_select_fusion.5.turn_ref, bf16[1024,768]{1,0:T(8,128)(2,1)} %bitcast.63, bf16[2048,384]{1,0:T(8,128)(2,1)} %get-tuple-element.112.refs_0_.refs_3_.o_ref, ...), custom_call_target="tpu_custom_call" | custom-call | flops 2415919104 | bytes 11010048 | tf_op jit(solution)/shard_map/after_self/pallas_call | solution.py:584
  132.9 37.2 %cross_forward.1 = (bf16[1024,768]{1,0:T(8,128)(2,1)}, f32[1024,768]{1,0:T(8,128)}, bf16[1024,24576]{1,0:T(8,128)(2,1)}) custom-call(bf16[1024,768]{1,0:T(8,128)(2,1)} %get-tuple-element.115.q_ref, bf16[2048,1536]{1,0:T(8,128)(2,1)} %enc_forward.1.k_ref.v_ref, bf16[2048,1536]{1,0:T(8,128)(2,1)} %enc_forward.1.k_ref.v_ref, ...), custom_call_target="tpu_custom_call" | custom-call | flops 25769803776 | bytes 6291456 | tf_op jit(solution)/shard_map/cross_forward/pallas_call | solution.py:261
  170.9 46.4 %feed_forward.1 = (bf16[1024,768]{1,0:T(8,128)(2,1)}, f32[1024,768]{1,0:T(8,128)}, bf16[1024,768]{1,0:T(8,128)(2,1)}, bf16[1024,768]{1,0:T(8,128)(2,1)}, f32[8,7...) custom-call(bf16[1024,768]{1,0:T(8,128)(2,1)} %get-tuple-element.117.o_ref.refs_9_, ...), custom_call_target="tpu_custom_call" | custom-call | flops 32614907904 | bytes 41943040 | tf_op jit(solution)/shard_map/feed_forward/pallas_call | solution.py:733
  217.3 73.5 %cross_backward.1 = (bf16[1024,768]{1,0:T(8,128)(2,1)}, bf16[2048,768]{1,0:T(8,128)(2,1)}, bf16[2048,768]{1,0:T(8,128)(2,1)}) custom-call(bf16[1024,768]{1,0:T(8,128)(2,1)} %get-tuple-element.115.q_ref, bf16[2048,1536]{1,0:T(8,128)(2,1)} %enc_forward.1.k_ref.v_ref, bf16[2048,1536]{1,0:T(8,128)(2,1)} %enc_forward.1.k_ref.v_ref, ...), custom_call_target="tpu_custom_call" | custom-call | flops 51539607552 | bytes 9437184 | tf_op jit(solution)/shard_map/cross_backward/pallas_call | solution.py:340
  290.8 10.1 %before_self.1 = (f32[1024,768]{1,0:T(8,128)}, bf16[1024,768]{1,0:T(8,128)(2,1)}, f32[8,768]{1,0:T(8,128)}, bf16[1024,384]{1,0:T(8,128)(2,1)}, bf16[1024,384]{1,0:T(8,128)(2,1)}) custom-call(s32[2]{0:T(128)} %and_select_fusion.5.turn_ref, bf16[1024,768]{1,0:T(8,128)(2,1)} %get-tuple-element.123.dq_ref.refs_1_, ...), custom_call_target="tpu_custom_call" | custom-call | flops 2415919104 | bytes 14155776 | tf_op jit(solution)/shard_map/before_self/pallas_call | solution.py:1022
  302.1 19.3 %mid_grads.1 = (bf16[768,3840]{1,0:T(8,128)(2,1)}, bf16[1024,768]{1,0:T(8,128)(2,1)}) custom-call(s32[2]{0:T(128)} %and_select_fusion.5.turn_ref, bf16[1024,768]{1,0:T(8,128)(2,1)} %get-tuple-element.127.refs_0_, bf16[1024,768]{1,0:T(8,128)(2,1)} %get-tuple-element.123.dq_ref.refs_1_, bf16[1024,768]{1,0:T(8,128)(2,1)} %get-tuple-element.128.refs_2_, ...), custom_call_target="tpu_custom_call" | custom-call | flops 10871635968 | bytes 31457280 | tf_op jit(solution)/shard_map/mid_grads/pallas_call | solution.py:939
  321.5 9.3 %reduce-scatter.3.cloned.1.call-done = bf16[384,768]{1,0:T(8,128)(2,1)} async-done(((bf16[6144,768]{1,0:T(8,128)(2,1)}), bf16[384,768]{1,0:T(8,128)(2,1)}) %reduce-scatter.3.cloned.1.call-update) | async-done | bytes 589840 | tf_op jit(solution)/shard_map/reduce_scatter | solution.py:1377
  330.8 1.3 collective-permute-start.9
  333.0 45.6 %self_backward.1 = (bf16[2048,384]{1,0:T(8,128)(2,1)}, bf16[2048,384]{1,0:T(8,128)(2,1)}, bf16[2048,384]{1,0:T(8,128)(2,1)}) custom-call(s32[4]{0:T(128)} %and_select_fusion.3.count_ref, s32[4]{0:T(128)} %get-tuple-element.105.slot_ref, bf16[2048,384]{1,0:T(8,128)(2,1)} %get-tuple-element.109.q_ref, bf16[2048,384]{1,0:T(8,128)(2,1)} %get-tuple-element.110.k_ref, ...), custom_call_target="tpu_custom_call" | custom-call | flops 6442450944 | bytes 1572864 | tf_op jit(solution)/shard_map/self_backward/pallas_call | solution.py:458
  380.1 11.2 %qkv_grads.1 = (bf16[8,48,1280]{2,1,0:T(8,128)(2,1)}, bf16[8,48,1280]{2,1,0:T(8,128)(2,1)}) custom-call(s32[1]{0:T(128)} %bitcast.6.core_ref, bf16[2048,384]{1,0:T(8,128)(2,1)} %get-tuple-element.154.refs_0_, bf16[2048,384]{1,0:T(8,128)(2,1)} %get-tuple-element.155.refs_1_, bf16[2048,384]{1,0:T(8,128)(2,1)} %get-tuple-element.156.refs_2_, ...), custom_call_target="tpu_custom_call" | custom-call | flops 1572864 | bytes 2048 | tf_op jit(solution)/shard_map/qkv_grads/pallas_call | solution.py:1097
  391.3 2.7 collective-permute-start.10
  394.0 6.2 %qkv_back.2 = bf16[1024,768]{1,0:T(8,128)(2,1)} custom-call(s32[4]{0:T(128)} %copy-done.21, bf16[2048,384]{1,0:T(8,128)(2,1)} %get-tuple-element.154.refs_0_, bf16[2048,384]{1,0:T(8,128)(2,1)} %get-tuple-element.155.refs_1_, bf16[2048,384]{1,0:T(8,128)(2,1)} %get-tuple-element.156.refs_2_, bf16[768,1152]{1,0:T(8,128)(2,1)} %get-tuple-element.108.w_ref.refs_4_.refs_3_), custom_call_target="tpu_custom_call" | custom-call | flops 786432 | bytes 1024 | tf_op jit(solution)/shard_map/qkv_back/pallas_call | solution.py:1126
  400.2 2.3 fusion.1
  402.5 1.4 collective-permute-start.11
  404.6 6.3 %qkv_back.3.own_ref = f32[1024,768]{1,0:T(8,128)} custom-call(s32[4]{0:T(128)} %copy-done.21, bf16[2048,384]{1,0:T(8,128)(2,1)} %get-tuple-element.154.refs_0_, bf16[2048,384]{1,0:T(8,128)(2,1)} %get-tuple-element.155.refs_1_, bf16[2048,384]{1,0:T(8,128)(2,1)} %get-tuple-element.156.refs_2_, bf16[768,1152]{1,0:T(8,128)(2,1)} %get-tuple-element.108.w_ref.refs_4_.refs_3_), custom_call_target="tpu_custom_call" | custom-call | flops 786432 | bytes 1024 | tf_op jit(solution)/shard_map/qkv_back/pallas_call | solution.py:1126
  410.9 6.7 %enc_finish.1 = f32[1024,768]{1,0:T(8,128)} custom-call(bf16[2048,768]{1,0:T(8,128)(2,1)} %get-tuple-element.129.refs_7_.dk_ref, bf16[2048,768]{1,0:T(8,128)(2,1)} %get-tuple-element.130.refs_8_.dv_ref, bf16[768,3840]{1,0:T(8,128)(2,1)} %all-gather.3.cloned.1.call-done.w_ref.refs_2_.refs_3_.refs_5_.wc_ref.wq_ref.refs_0_.refs_1_.refs_11_.refs_12_.wk_ref.wv_ref, ...), custom_call_target="tpu_custom_call" | custom-call | flops 786432 | bytes 1024 | tf_op jit(solution)/shard_map/enc_finish/pallas_call | solution.py:977
  421.5 1.4 collective-permute-start.14
  423.7 6.7 %collective-permute-done.13 = bf16[48,1280]{1,0:T(8,128)(2,1)S(1)} collective-permute-done((bf16[48,1280]{1,0:T(8,128)(2,1)S(1)}, bf16[48,1280]{1,0:T(8,128)(2,1)S(1)}, u32[]{:S(2)}, u32[]{:S(2)}) %collective-permute-start.13) | collective-permute-done | bytes 122912 | tf_op jit(solution)/shard_map/ppermute | solution.py:1240
  430.4 2.8 collective-permute-done.14
  433.3 1.4 collective-permute-start.15
  434.9 1.4 collective-permute-done.19
  437.5 2.5 collective-permute-start.20
  439.9 2.2 collective-permute-done.15
  442.2 7.9 %collective-permute-done.17 = bf16[48,3840]{1,0:T(8,128)(2,1)S(1)} collective-permute-done((bf16[48,3840]{1,0:T(8,128)(2,1)}, bf16[48,3840]{1,0:T(8,128)(2,1)S(1)}, u32[]{:S(2)}, u32[]{:S(2)}) %collective-permute-start.17) | collective-permute-done | bytes 368672 | tf_op jit(solution)/shard_map/ppermute | solution.py:1425
  450.4 1.3 collective-permute-start.18
  451.7 7.4 %collective-permute-done.22 = bf16[48,3840]{1,0:T(8,128)(2,1)S(1)} collective-permute-done((bf16[48,3840]{1,0:T(8,128)(2,1)S(1)}, bf16[48,3840]{1,0:T(8,128)(2,1)S(1)}, u32[]{:S(2)}, u32[]{:S(2)}) %collective-permute-start.22) | collective-permute-done | bytes 368672 | tf_op jit(solution)/shard_map/ppermute | solution.py:1251
  459.2 3.9 collective-permute-start.23
  463.8 4.1 unpack.1
  467.9 6.4 %finish.1 = f32[1024,768]{1,0:T(8,128)} custom-call(bf16[1024,768]{1,0:T(8,128)(2,1)} %bitcast.64, f32[1024,768]{1,0:T(8,128)} %get-tuple-element.170.dh_ref, f32[1,768]{1,0:T(1,128)} %get-tuple-element.199.g_ref.refs_5_, f32[1024,768]{1,0:T(8,128)} %qkv_back.3.own_ref, bf16[1024,768]{1,0:T(8,128)(2,1)} %collective-permute-done.16.refs_0_), custom_call_target="tpu_custom_call" | custom-call | flops 786432 | bytes 1024 | tf_op jit(solution)/shard_map/finish/pallas_call | solution.py:1154
  474.5 1.7 collective-permute-done.21.far_ref
  477.1 2.5 settle_qkv.1
  480.4 3.1 settle_mid.1
  (147 shorter events, 34.8 us)
Async XLA Ops:
  7.2 7.4 %copy-start = (bf16[512,768]{1,0:T(8,128)(2,1)S(1)}, bf16[512,768]{1,0:T(8,128)(2,1)}, u32[]{:S(2)}) copy-start(bf16[512,768]{1,0:T(8,128)(2,1)} %param.35) | copy-start | bytes 2359300
  7.2 98.0 %all-gather.3.cloned.1.call-start = ((), (), s32[]{:S(2)}) async-start(), calls=%async_computation.2 | async-start | bytes 6266880 | tf_op jit(solution)/shard_map/all_gather | solution.py:1323
  12.5 158.4 %all-gather.5.cloned.1.call-start = ((), (), s32[]{:S(2)}) async-start(), calls=%async_computation.3 | async-start | bytes 10027008 | tf_op jit(solution)/shard_map/all_gather | solution.py:1332
  14.6 1.3 copy-start.18
  14.7 1.4 copy-start.19
  14.7 1.4 copy-start.20
  14.8 7.0 %copy-start.2 = (bf16[1,1024,768]{2,1,0:T(8,128)(2,1)S(1)}, bf16[1,1024,768]{2,1,0:T(8,128)(2,1)}, u32[]{:S(2)}) copy-start(bf16[1,1024,768]{2,1,0:T(8,128)(2,1)} %param.20) | copy-start | bytes 4718596
  14.8 9.4 %copy-start.17 = (s32[1,2048]{1,0:T(1,128)S(1)}, s32[1,2048]{1,0:T(1,128)}, u32[]{:S(2)}) copy-start(s32[1,2048]{1,0:T(1,128)} %param.22) | copy-start | bytes 24580
  14.8 12.6 %copy-start.27 = (s32[1,4]{1,0:T(1,128)S(1)}, s32[1,4]{1,0:T(1,128)}, u32[]{:S(2)}) copy-start(s32[1,4]{1,0:T(1,128)} %param.23) | copy-start | bytes 52
  15.7 315.1 %reduce-scatter.3.cloned.1.call-start = ((), (), s32[]{:S(2)}) async-start(), calls=%async_computation.4 | async-start | bytes 10027008 | tf_op jit(solution)/shard_map/reduce_scatter | solution.py:1377
  16.1 11.8 %collective-permute-start.3 = (bf16[96,1280]{1,0:T(8,128)(2,1)S(1)}, bf16[96,1280]{1,0:T(8,128)(2,1)S(1)}, u32[]{:S(2)}, u32[]{:S(2)}) collective-permute-start(bf16[96,1280]{1,0:T(8,128)(2,1)S(1)} %fusion.3), channel_id=1, source_target_pairs={{0,3},{1,0},{2,1},{3,2},{4,7},{5,4},{6,5},{7,6},{8,11},{9,8},{10,9... | collective-permute-start | bytes 737288 | tf_op jit(solution)/shard_map/ppermute | solution.py:1197
  16.2 19.7 %collective-permute-start.1 = (bf16[96,1280]{1,0:T(8,128)(2,1)S(1)}, bf16[96,1280]{1,0:T(8,128)(2,1)S(1)}, u32[]{:S(2)}, u32[]{:S(2)}) collective-permute-start(bf16[96,1280]{1,0:T(8,128)(2,1)S(1)} %fusion.3), channel_id=1, source_target_pairs={{0,1},{1,2},{2,3},{3,0},{4,5},{5,6},{6,7},{7,4},{8,9},{9,10},{10,1... | collective-permute-start | bytes 737288 | tf_op jit(solution)/shard_map/ppermute | solution.py:1197
  17.7 31.0 %collective-permute-start.2 = (bf16[96,1280]{1,0:T(8,128)(2,1)S(1)}, bf16[96,1280]{1,0:T(8,128)(2,1)S(1)}, u32[]{:S(2)}, u32[]{:S(2)}) collective-permute-start(bf16[96,1280]{1,0:T(8,128)(2,1)S(1)} %fusion.3), channel_id=1, source_target_pairs={{0,2},{1,3},{2,0},{3,1},{4,6},{5,7},{6,4},{7,5},{8,10},{9,11},{10,... | collective-permute-start | bytes 737288 | tf_op jit(solution)/shard_map/ppermute | solution.py:1197
  21.8 43.5 %collective-permute-start = (bf16[1024,768]{1,0:T(8,128)(2,1)S(1)}, bf16[1024,768]{1,0:T(8,128)(2,1)}, u32[]{:S(2)}, u32[]{:S(2)}) collective-permute-start(bf16[1024,768]{1,0:T(8,128)(2,1)S(1)} %bitcast.65), channel_id=1, source_target_pairs={{0,4},{4,0},{1,5},{5,1},{2,6},{6,2},{3,7},{7,3},{8,12},{12,8},{9,1... | collective-permute-start | bytes 4718600 | tf_op jit(solution)/shard_map/ppermute | solution.py:1303
  48.8 11.1 %copy-start.4 = (bf16[4,96,1280]{2,1,0:T(8,128)(2,1)}, bf16[4,96,1280]{2,1,0:T(8,128)(2,1)S(1)}, u32[]{:S(2)}) copy-start(bf16[4,96,1280]{2,1,0:T(8,128)(2,1)S(1)} %pad_maximum_fusion.1.near_ref) | copy-start | bytes 2949124
  48.8 11.1 %collective-permute-start.4 = (bf16[4,96,1280]{2,1,0:T(8,128)(2,1)S(1)}, bf16[4,96,1280]{2,1,0:T(8,128)(2,1)S(1)}, u32[]{:S(2)}, u32[]{:S(2)}) collective-permute-start(bf16[4,96,1280]{2,1,0:T(8,128)(2,1)S(1)} %pad_maximum_fusion.1.near_ref), channel_id=1, source_target_pairs={{0,8},{8,0},{16,24},{24,16},{1,9},{9,1},{17,25},{25,17},{2,10},{10... | collective-permute-start | bytes 2949128 | tf_op jit(solution)/shard_map/ppermute | solution.py:1199
  52.8 11.0 %copy-start.21 = (s32[4]{0:T(128)}, s32[4]{0:T(128)S(1)}, u32[]{:S(2)}) copy-start(s32[4]{0:T(128)S(1)} %dynamic_slice.66.order_ref) | copy-start | bytes 52
  65.3 39.9 %collective-permute-start.6 = (bf16[1024,768]{1,0:T(8,128)(2,1)}, bf16[1024,768]{1,0:T(8,128)(2,1)S(1)}, u32[]{:S(2)}, u32[]{:S(2)}) collective-permute-start(bf16[1024,768]{1,0:T(8,128)(2,1)} %bitcast.93), channel_id=1, source_target_pairs={{0,4},{4,0},{1,5},{5,1},{2,6},{6,2},{3,7},{7,3},{8,12},{12,8},{9,1... | collective-permute-start | bytes 4718600 | tf_op jit(solution)/shard_map/ppermute | solution.py:1303
  104.5 17.7 %collective-permute-start.5 = (bf16[1024,384]{1,0:T(8,128)(2,1)S(1)}, bf16[1024,384]{1,0:T(8,128)(2,1)S(1)}, u32[]{:S(2)}, u32[]{:S(2)}) collective-permute-start(bf16[1024,384]{1,0:T(8,128)(2,1)S(1)} %slice.17), channel_id=1, source_target_pairs={{0,4},{4,0},{1,5},{5,1},{2,6},{6,2},{3,7},{7,3},{8,12},{12,8},{9,1... | collective-permute-start | bytes 2359304 | tf_op jit(solution)/shard_map/ppermute | solution.py:1362
  105.2 1.2 copy-start.22
  217.3 206.4 %reduce-scatter.5.cloned.1.call-start = ((), (), s32[]{:S(2)}) async-start(), calls=%async_computation.5 | async-start | bytes 6266880 | tf_op jit(solution)/shard_map/reduce_scatter | solution.py:1398
  300.9 20.5 %collective-permute-start.7 = (bf16[1024,384]{1,0:T(8,128)(2,1)}, bf16[1024,384]{1,0:T(8,128)(2,1)S(1)}, u32[]{:S(2)}, u32[]{:S(2)}) collective-permute-start(bf16[1024,384]{1,0:T(8,128)(2,1)} %get-tuple-element.126), channel_id=1, source_target_pairs={{0,4},{4,0},{1,5},{5,1},{2,6},{6,2},{3,7},{7,3},{8,12},{12,8},{9,1... | collective-permute-start | bytes 2359304 | tf_op jit(solution)/shard_map/ppermute | solution.py:1383
  321.5 9.3 %copy-start.23 = (bf16[1024,384]{1,0:T(8,128)(2,1)}, bf16[1024,384]{1,0:T(8,128)(2,1)S(1)}, u32[]{:S(2)}) copy-start(bf16[1024,384]{1,0:T(8,128)(2,1)S(1)} %collective-permute-done.7.far_ref) | copy-start | bytes 2359300
  330.7 1.3 copy-start.13
  330.8 49.3 %collective-permute-start.9 = (bf16[1024,768]{1,0:T(8,128)(2,1)}, bf16[1024,768]{1,0:T(8,128)(2,1)S(1)}, u32[]{:S(2)}, u32[]{:S(2)}) collective-permute-start(bf16[1024,768]{1,0:T(8,128)(2,1)} %get-tuple-element.142), channel_id=1, source_target_pairs={{0,4},{4,0},{1,5},{5,1},{2,6},{6,2},{3,7},{7,3},{8,12},{12,8},{9,1... | collective-permute-start | bytes 4718600 | tf_op jit(solution)/shard_map/ppermute | solution.py:1401
  332.1 46.8 %collective-permute-start.8 = (bf16[2,3,64,768]{3,2,1,0:T(8,128)(2,1)S(1)}, bf16[2,3,64,768]{3,2,1,0:T(8,128)(2,1)}, u32[]{:S(2)}, u32[]{:S(2)}) collective-permute-start(bf16[2,3,64,768]{3,2,1,0:T(8,128)(2,1)S(1)} %bitcast.77), channel_id=1, source_target_pairs={{0,4},{4,0},{1,5},{5,1},{2,6},{6,2},{3,7},{7,3},{8,12},{12,8},{9,1... | collective-permute-start | bytes 1769480 | tf_op jit(solution)/shard_map/ppermute | solution.py:1245
  380.1 11.2 %copy-start.7 = (bf16[1024,768]{1,0:T(8,128)(2,1)}, bf16[1024,768]{1,0:T(8,128)(2,1)S(1)}, u32[]{:S(2)}) copy-start(bf16[1024,768]{1,0:T(8,128)(2,1)S(1)} %collective-permute-done.9.refs_0_) | copy-start | bytes 4718596
  391.3 8.9 %collective-permute-start.10 = (bf16[8,48,1280]{2,1,0:T(8,128)(2,1)}, bf16[8,48,1280]{2,1,0:T(8,128)(2,1)}, u32[]{:S(2)}, u32[]{:S(2)}) collective-permute-start(bf16[8,48,1280]{2,1,0:T(8,128)(2,1)} %get-tuple-element.153), channel_id=1, source_target_pairs={{0,8},{8,0},{16,24},{24,16},{1,9},{9,1},{17,25},{25,17},{2,10},{10... | collective-permute-start | bytes 2949128 | tf_op jit(solution)/shard_map/ppermute | solution.py:1229
  394.0 6.2 %copy-start.10 = (bf16[8,48,1280]{2,1,0:T(8,128)(2,1)S(1)}, bf16[8,48,1280]{2,1,0:T(8,128)(2,1)}, u32[]{:S(2)}) copy-start(bf16[8,48,1280]{2,1,0:T(8,128)(2,1)} %get-tuple-element.152) | copy-start | bytes 2949124
  400.2 3.7 copy-start.8
  402.5 15.5 %collective-permute-start.11 = (bf16[4,48,1280]{2,1,0:T(8,128)(2,1)}, bf16[4,48,1280]{2,1,0:T(8,128)(2,1)}, u32[]{:S(2)}, u32[]{:S(2)}) collective-permute-start(bf16[4,48,1280]{2,1,0:T(8,128)(2,1)} %get-tuple-element.158), channel_id=1, source_target_pairs={{0,16},{8,24},{16,0},{24,8},{1,17},{9,25},{17,1},{25,9},{2,18},{10... | collective-permute-start | bytes 1474568 | tf_op jit(solution)/shard_map/ppermute | solution.py:1235
  403.9 38.3 %collective-permute-start.16 = (bf16[1024,768]{1,0:T(8,128)(2,1)S(1)}, bf16[1024,768]{1,0:T(8,128)(2,1)}, u32[]{:S(2)}, u32[]{:S(2)}) collective-permute-start(bf16[1024,768]{1,0:T(8,128)(2,1)S(1)} %copy-done.8), channel_id=1, source_target_pairs={{0,4},{4,0},{1,5},{5,1},{2,6},{6,2},{3,7},{7,3},{8,12},{12,8},{9,1... | collective-permute-start | bytes 4718600 | tf_op jit(solution)/shard_map/ppermute | solution.py:1411
  419.2 4.5 collective-permute-start.12
  420.5 10.0 %collective-permute-start.13 = (bf16[48,1280]{1,0:T(8,128)(2,1)S(1)}, bf16[48,1280]{1,0:T(8,128)(2,1)S(1)}, u32[]{:S(2)}, u32[]{:S(2)}) collective-permute-start(bf16[48,1280]{1,0:T(8,128)(2,1)S(1)} %get-tuple-element.196), channel_id=1, source_target_pairs={{0,2},{1,3},{2,0},{3,1},{4,6},{5,7},{6,4},{7,5},{8,10},{9,11},{10,... | collective-permute-start | bytes 368648 | tf_op jit(solution)/shard_map/ppermute | solution.py:1240
  421.5 11.8 %collective-permute-start.14 = (bf16[48,1280]{1,0:T(8,128)(2,1)S(1)}, bf16[48,1280]{1,0:T(8,128)(2,1)S(1)}, u32[]{:S(2)}, u32[]{:S(2)}) collective-permute-start(bf16[48,1280]{1,0:T(8,128)(2,1)S(1)} %get-tuple-element.195), channel_id=1, source_target_pairs={{0,3},{1,0},{2,1},{3,2},{4,7},{5,4},{6,5},{7,6},{8,11},{9,8},{10,9... | collective-permute-start | bytes 368648 | tf_op jit(solution)/shard_map/ppermute | solution.py:1240
  422.8 13.5 %collective-permute-start.19 = (bf16[2,3,64,768]{3,2,1,0:T(8,128)(2,1)S(1)}, bf16[2,3,64,768]{3,2,1,0:T(8,128)(2,1)}, u32[]{:S(2)}, u32[]{:S(2)}) collective-permute-start(bf16[2,3,64,768]{3,2,1,0:T(8,128)(2,1)S(1)} %add_convert_fusion), channel_id=1, source_target_pairs={{0,16},{8,24},{16,0},{24,8},{1,17},{9,25},{17,1},{25,9},{2,18},{10... | collective-permute-start | bytes 1769480 | tf_op jit(solution)/shard_map/ppermute | solution.py:1251
  433.3 16.7 %copy-start.16 = (bf16[48,3840]{1,0:T(8,128)(2,1)S(1)}, bf16[48,3840]{1,0:T(8,128)(2,1)}, u32[]{:S(2)}) copy-start(bf16[48,3840]{1,0:T(8,128)(2,1)} %reduce-scatter.5.cloned.1.call-done) | copy-start | bytes 1105924
  433.3 8.8 %collective-permute-start.15 = (bf16[48,1280]{1,0:T(8,128)(2,1)S(1)}, bf16[48,1280]{1,0:T(8,128)(2,1)S(1)}, u32[]{:S(2)}, u32[]{:S(2)}) collective-permute-start(bf16[48,1280]{1,0:T(8,128)(2,1)S(1)} %fusion.8), channel_id=1, source_target_pairs={{0,4},{4,0},{1,5},{5,1},{2,6},{6,2},{3,7},{7,3},{8,12},{12,8},{9,1... | collective-permute-start | bytes 368648 | tf_op jit(solution)/shard_map/ppermute | solution.py:1248
  434.8 15.3 %collective-permute-start.17 = (bf16[48,3840]{1,0:T(8,128)(2,1)}, bf16[48,3840]{1,0:T(8,128)(2,1)S(1)}, u32[]{:S(2)}, u32[]{:S(2)}) collective-permute-start(bf16[48,3840]{1,0:T(8,128)(2,1)} %reduce-scatter.5.cloned.1.call-done), channel_id=1, source_target_pairs={{0,4},{4,0},{1,5},{5,1},{2,6},{6,2},{3,7},{7,3},{8,12},{12,8},{9,1... | collective-permute-start | bytes 1105928 | tf_op jit(solution)/shard_map/ppermute | solution.py:1425
  437.5 26.3 %copy-start.3 = (bf16[2,2,3,64,768]{4,3,2,1,0:T(8,128)(2,1)}, bf16[2,2,3,64,768]{4,3,2,1,0:T(8,128)(2,1)S(1)}, u32[]{:S(2)}) copy-start(bf16[2,2,3,64,768]{4,3,2,1,0:T(8,128)(2,1)S(1)} %pad_maximum_fusion.near_ref) | copy-start | bytes 3538948
  437.5 26.3 %collective-permute-start.20 = (bf16[2,2,3,64,768]{4,3,2,1,0:T(8,128)(2,1)S(1)}, bf16[2,2,3,64,768]{4,3,2,1,0:T(8,128)(2,1)}, u32[]{:S(2)}, u32[]{:S(2)}) collective-permute-start(bf16[2,2,3,64,768]{4,3,2,1,0:T(8,128)(2,1)S(1)} %pad_maximum_fusion.near_ref), channel_id=1, source_target_pairs={{0,8},{8,0},{16,24},{24,16},{1,9},{9,1},{17,25},{25,17},{2,10},{10... | collective-permute-start | bytes 3538952 | tf_op jit(solution)/shard_map/ppermute | solution.py:1254
  450.2 9.0 %collective-permute-start.22 = (bf16[48,3840]{1,0:T(8,128)(2,1)S(1)}, bf16[48,3840]{1,0:T(8,128)(2,1)S(1)}, u32[]{:S(2)}, u32[]{:S(2)}) collective-permute-start(bf16[48,3840]{1,0:T(8,128)(2,1)S(1)} %add_convert_fusion.4), channel_id=1, source_target_pairs={{0,16},{8,24},{16,0},{24,8},{1,17},{9,25},{17,1},{25,9},{2,18},{10... | collective-permute-start | bytes 1105928 | tf_op jit(solution)/shard_map/ppermute | solution.py:1251
  450.4 23.9 %collective-permute-start.18 = (bf16[2,48,1280]{2,1,0:T(8,128)(2,1)S(1)}, bf16[2,48,1280]{2,1,0:T(8,128)(2,1)S(1)}, u32[]{:S(2)}, u32[]{:S(2)}) collective-permute-start(bf16[2,48,1280]{2,1,0:T(8,128)(2,1)S(1)} %pad_maximum_fusion.5), channel_id=1, source_target_pairs={{0,16},{8,24},{16,0},{24,8},{1,17},{9,25},{17,1},{25,9},{2,18},{10... | collective-permute-start | bytes 737288 | tf_op jit(solution)/shard_map/ppermute | solution.py:1251
  459.2 15.0 %copy-start.5 = (bf16[2,48,3840]{2,1,0:T(8,128)(2,1)}, bf16[2,48,3840]{2,1,0:T(8,128)(2,1)S(1)}, u32[]{:S(2)}) copy-start(bf16[2,48,3840]{2,1,0:T(8,128)(2,1)S(1)} %pad_maximum_fusion.2.near_ref) | copy-start | bytes 2211844
  459.2 20.3 %collective-permute-start.23 = (bf16[2,48,3840]{2,1,0:T(8,128)(2,1)S(1)}, bf16[2,48,3840]{2,1,0:T(8,128)(2,1)S(1)}, u32[]{:S(2)}, u32[]{:S(2)}) collective-permute-start(bf16[2,48,3840]{2,1,0:T(8,128)(2,1)S(1)} %pad_maximum_fusion.2.near_ref), channel_id=1, source_target_pairs={{0,8},{8,0},{16,24},{24,16},{1,9},{9,1},{17,25},{25,17},{2,10},{10... | collective-permute-start | bytes 2211848 | tf_op jit(solution)/shard_map/ppermute | solution.py:1254
  474.3 9.2 %copy-start.1 = (bf16[512,768]{1,0:T(8,128)(2,1)S(1)}, bf16[512,768]{1,0:T(8,128)(2,1)}, u32[]{:S(2)}) copy-start(bf16[512,768]{1,0:T(8,128)(2,1)} %param.35) | copy-start | bytes 2359300
  474.3 1.9 copy-start.6
  474.3 1.9 collective-permute-start.21
  (8 other events, 7.6 us)
Sparse Core Ops, SparseCore 0:
  12.7 76.1 all-gather.2
  91.7 79.1 all-gather.4
  217.4 113.2 reduce-scatter.2
  335.0 84.9 reduce-scatter.4
